TPU v7x, 32 devices: a whole 2x2x4 slice. The times are simulated.
32 devices in a mesh: branch: 4 (over y, core), segment: 2 (over x), tp: 4 (over z).
Axes of the slice: x: 2, y: 2, z: 4, core: 2. Of those that a mesh axis runs over, the one named last changes fastest.
Arguments:
- rollout: bfloat16 [576, 8192], P(('branch', 'segment')), may hold values from -6 to 6
- send_rows: int32 [576], P(('branch', 'segment')), may hold values from 0 to 71, as said below
- seq_lengths: int32 [2, 6], P('segment'), may hold values from 1 to 144, 288 in all within a row
- attn_gain: bfloat16 [4, 8192], P('branch'), may hold values from 0.099609375 to 1.8984375
- w_query: bfloat16 [4, 8192, 8192], P('branch', 'segment', 'tp'), may hold values from -1 to 1
- w_keyval: bfloat16 [4, 8192, 2048], P('branch', 'segment', 'tp'), may hold values from -1 to 1
- head_weight: bfloat16 [4, 8192], P('branch', 'tp'), may hold values from -0.0625 to 0.0625
- head_attn: bfloat16 [4, 8192], P('branch', 'tp'), may hold values from -0.25 to 0.25
Outputs:
- scores: float32 [4, 576], P(None, ('branch', 'segment'))
Inputs may be any that keep to these rules, and one draw needn't show every extreme that they name: `send_rows`: each aligned block of 72 entries holds every number of 0 to 71 once.
All inputs are finite; a program needn't handle non-finite values.
Results may differ from a plain program's by a relative error of at most 0.006.
Values may be sent and summed in bfloat16 or wider, within the bound.
No kernel may reach another device: no remote copies, remote signals or barrier semaphores. Data moves between devices by JAX's collectives and lax.ppermute only.
A program may use at most 128 MiB of HBM per device.

v0:
```python
import math

import jax
import jax.numpy as jnp
from jax import lax
from jax.sharding import PartitionSpec as P

HEAD = 128
HEADS = 64
KV_HEADS = 8


epsilon = 1e-05


def local(rollout, send_rows, seq_lengths, attn_gain, w_query, w_keyval, head_weight, head_attn):
    n_branch = lax.axis_size("branch")
    n_segment = lax.axis_size("segment")
    gen_rows = rollout.shape[0]
    piece_rows = gen_rows // n_segment
    row_width = rollout.shape[1]
    ordered = jnp.take(rollout, send_rows, axis=0).reshape(n_segment, piece_rows, row_width)
    copies = jnp.broadcast_to(ordered[None], (n_branch, n_segment, piece_rows, row_width))
    copies = copies.reshape(n_branch * n_segment, piece_rows, row_width)
    arrived = lax.all_to_all(copies, ("branch", "segment"), split_axis=0, concat_axis=0, tiled=True)
    packed = arrived.reshape(-1, row_width)
    pack_rows = packed.shape[0]
    rows_float = packed.astype(jnp.float32)
    mean_square = jnp.mean(rows_float * rows_float, axis=-1, keepdims=True)
    normed = (
        rows_float * lax.rsqrt(mean_square + epsilon) * attn_gain[0].astype(jnp.float32)
    ).astype(jnp.bfloat16)
    query_acc = jnp.dot(
        normed,
        lax.all_gather(w_query, "segment", axis=1, tiled=True)[0],
        preferred_element_type=jnp.float32,
    )
    keyval_acc = jnp.dot(
        normed,
        lax.all_gather(w_keyval, "segment", axis=1, tiled=True)[0],
        preferred_element_type=jnp.float32,
    )
    queries = query_acc.astype(jnp.bfloat16)
    keyval_part = keyval_acc.astype(jnp.bfloat16)
    keyval = lax.all_gather(keyval_part, "tp", axis=1, tiled=True)
    tp_index = lax.axis_index("tp")
    heads_here = queries.shape[1] // HEAD
    group_size = HEADS // KV_HEADS
    per_group = min(heads_here, group_size)
    group_span = heads_here // per_group
    kv_first = tp_index * heads_here // group_size
    key_rows = lax.dynamic_slice_in_dim(keyval, kv_first * HEAD, group_span * HEAD, 1)
    value_rows = lax.dynamic_slice_in_dim(
        keyval, KV_HEADS * HEAD + kv_first * HEAD, group_span * HEAD, 1
    )
    key_rows = key_rows.reshape(pack_rows, group_span, HEAD)
    value_rows = value_rows.reshape(pack_rows, group_span, HEAD)
    queries = queries.reshape(pack_rows, group_span, per_group, HEAD)
    positions = jnp.arange(pack_rows, dtype=jnp.int32)
    doc_ends = jnp.cumsum(seq_lengths[0])
    doc_ids = jnp.sum((positions[:, None] >= doc_ends[None, :]).astype(jnp.int32), axis=-1)
    visible = (doc_ids[:, None] == doc_ids[None, :]) & (positions[None, :] <= positions[:, None])
    logits = jnp.einsum(
        "qgpc,kgc->gpqk", queries, key_rows, preferred_element_type=jnp.float32
    ) / math.sqrt(HEAD)
    logits = jnp.where(visible[None, None], logits, -1e30)
    row_max = jnp.max(logits, axis=-1, keepdims=True)
    expo = jnp.exp(logits - row_max)
    probabilities = (expo / jnp.sum(expo, axis=-1, keepdims=True)).astype(jnp.bfloat16)
    attended = jnp.einsum(
        "gpqk,kgc->qgpc", probabilities, value_rows, preferred_element_type=jnp.float32
    )
    attended = attended.reshape(pack_rows, heads_here * HEAD)
    slice_width = head_weight.shape[1]
    own_columns = lax.dynamic_slice_in_dim(packed, tp_index * slice_width, slice_width, 1)
    direct = jnp.dot(own_columns, head_weight[0], preferred_element_type=jnp.float32)
    through = jnp.dot(attended, head_attn[0].astype(jnp.float32), precision=lax.Precision.HIGHEST)
    totals = lax.psum(direct + through, "tp")
    outgoing = totals.reshape(n_branch * n_segment, piece_rows)
    incoming = lax.all_to_all(
        outgoing, ("branch", "segment"), split_axis=0, concat_axis=0, tiled=True
    )
    incoming = incoming.reshape(n_branch, n_segment * piece_rows)
    scores = jnp.zeros((n_branch, gen_rows), jnp.float32).at[:, send_rows].set(incoming)
    return scores


def solution(mesh):
    return jax.shard_map(
        local,
        mesh=mesh,
        in_specs=(
            P(("branch", "segment"), None),
            P(("branch", "segment")),
            P("segment", None),
            P("branch", None),
            P("branch", "segment", "tp"),
            P("branch", "segment", "tp"),
            P("branch", "tp"),
            P("branch", "tp"),
        ),
        out_specs=P(None, ("branch", "segment")),
        check_vma=False,
    )
```

profile of v0, /device:TPU:0, one launch (start us, length us, event | category | flops | bytes accessed | tf_op | source)
XLA Modules:
  0.0 653.6 jit_solution(762487137252512450)
XLA Ops:
  6.5 0.0 copy-start
  6.5 0.0 all-gather.4.cloned.1.call-start
  6.5 0.7 all-gather.4.cloned.1.call-update
  7.3 0.7 compare_select_fusion
  7.9 0.7 compare_and_fusion
  8.6 0.0 copy-done
  8.6 2.4 gather_fusion
  11.0 1.5 gather.7
  12.5 0.1 broadcast_in_dim.48
  12.6 0.2 broadcast_select_fusion
  12.8 3.0 broadcast_in_dim.51
  15.9 0.0 copy-start.2
  15.9 5.3 all-to-all-start
  21.2 0.0 all-gather.6.cloned.1.call-start
  21.2 0.0 copy-done.2
  21.3 113.8 %all-to-all-done = bf16[8,36,8192]{2,1,0:T(8,128)(2,1)} async-done(((bf16[8,36,8192]{2,1,0:T(8,128)(2,1)}), bf16[8,36,8192]{2,1,0:T(8,128)(2,1)}, u32[]{:S(2)}, u32[]{:S(2)}) %all-to-all-start) | async-done | bytes 4718624 | tf_op jit(solution)/shard_map/all_to_all | solution.py:25
  135.1 3.7 fusion.3
  138.8 6.5 fusion.5
  145.3 5.5 convert_element_type.30
  150.8 20.0 %all-gather.4.cloned.1.call-done = bf16[1,8192,512]{2,1,0:T(8,128)(2,1)} async-done(((bf16[1,4096,512]{2,1,0:T(8,128)(2,1)}), bf16[1,8192,512]{2,1,0:T(8,128)(2,1)}) %all-gather.4.cloned.1.call-update) | async-done | bytes 8388624 | tf_op jit(solution)/shard_map/all_gather | solution.py:40
  170.8 8.1 %fusion.23 = bf16[288,512]{1,0:T(8,128)(2,1)} fusion(bf16[288,8192]{1,0:T(8,128)(2,1)} %convert_element_type.30, bf16[1,8192,512]{2,1,0:T(8,128)(2,1)} %all-gather.4.cloned.1.call-done), kind=kOutput, calls=%fused_computation.27 | convolution fusion | flops 2416066560 | bytes 13402112 | tf_op jit(solution)/shard_map/dot_general | solution.py:38
  178.9 0.0 all-gather.6.cloned.1.call-update
  179.0 0.0 copy-start.5
  179.0 0.2 all-gather.8.cloned.1.call-start
  179.2 0.5 all-gather.8.cloned.1.call-update
  179.7 0.0 copy-done.5
  179.8 0.2 reduce-window.8
  179.9 0.1 convert_reduce_fusion
  180.0 0.1 fusion.36
  180.2 0.0 copy-start.3
  180.2 5.6 reshape.144
  185.7 0.0 copy-done.3
  185.7 1.8 fusion.30
  187.5 22.9 %all-gather.6.cloned.1.call-done = bf16[288,2048]{1,0:T(8,128)(2,1)} async-done(((bf16[288,512]{1,0:T(8,128)(2,1)}), bf16[288,2048]{1,0:T(8,128)(2,1)}) %all-gather.6.cloned.1.call-update) | async-done | bytes 1179664 | tf_op jit(solution)/shard_map/all_gather | solution.py:45
  210.4 1.0 constant_dynamic-slice_fusion.1
  211.5 388.3 %all-gather.8.cloned.1.call-done = bf16[1,8192,2048]{2,1,0:T(8,128)(2,1)} async-done(((bf16[1,4096,2048]{2,1,0:T(8,128)(2,1)}), bf16[1,8192,2048]{2,1,0:T(8,128)(2,1)}) %all-gather.8.cloned.1.call-update) | async-done | bytes 33554448 | tf_op jit(solution)/shard_map/all_gather | solution.py:35
  599.7 17.2 %fusion.20 = bf16[36,8,16,128]{3,1,2,0:T(8,128)(2,1)S(1)} fusion(bf16[288,8192]{1,0:T(8,128)(2,1)} %convert_element_type.30, bf16[1,8192,2048]{2,1,0:T(8,128)(2,1)} %all-gather.8.cloned.1.call-done), kind=kOutput, calls=%fused_computation.25 | convolution fusion | flops 9664266240 | bytes 39452672 | tf_op jit(solution)/shard_map/dot_general | solution.py:33
  616.9 0.2 copy.40
  617.2 1.1 fusion.26
  618.3 2.3 fusion.46
  620.6 0.0 copy-start.1
  620.6 1.6 fusion.19
  622.1 0.0 copy-start.4
  622.1 1.4 copy.30
  623.5 0.0 copy-done.4
  623.5 1.8 fusion.33
  625.4 0.1 all_to_all.10
  625.5 11.7 %psum.7 = f32[8,1,36]{2,1,0:T(1,128)S(1)} all-reduce(f32[8,1,36]{2,1,0:T(1,128)S(1)} %all_to_all.10), channel_id=1, replica_groups=mesh['branch'=4,'segment'=2,'tp'=4] {'tp'}, use_global_device_ids=true, to_apply=%region_5.6 | all-reduce | flops 288 | bytes 2304 | tf_op jit(solution)/shard_map/psum | solution.py:78
  637.1 7.2 %all_to_all.14 = f32[8,1,36]{2,1,0:T(1,128)S(1)} all-to-all(f32[8,1,36]{2,1,0:T(1,128)S(1)} %psum.7), channel_id=1, replica_groups=mesh['branch'=4,'segment'=2,'tp'=4] {'branch','segment'}, dimensions={0} | all-to-all | bytes 2304 | tf_op jit(solution)/shard_map/all_to_all | solution.py:80
  644.4 0.5 broadcast.74
  644.9 0.7 reduce.8
  645.5 0.1 reshape.162
  645.6 0.1 copy.31
  645.7 0.7 scatter_custom_fusion
  646.5 0.7 copy.32
  647.1 0.0 copy-done.1
  (6 shorter events, 0.1 us)
Async XLA Ops:
  6.5 2.1 copy-start
  6.5 164.3 %all-gather.4.cloned.1.call-start = ((), (), s32[]{:S(2)}) async-start(), calls=%async_computation.2 | async-start | bytes 12582912 | tf_op jit(solution)/shard_map/all_gather | solution.py:40
  15.9 5.4 copy-start.2
  15.9 119.3 %all-to-all-start = ((bf16[8,36,8192]{2,1,0:T(8,128)(2,1)}), bf16[8,36,8192]{2,1,0:T(8,128)(2,1)}, u32[]{:S(2)}, u32[]{:S(2)}) async-start(bf16[8,36,8192]{2,1,0:T(8,128)(2,1)} %bitcast.51), calls=%async_computation | async-start | bytes 10485760 | tf_op jit(solution)/shard_map/all_to_all | solution.py:25
  21.2 189.2 %all-gather.6.cloned.1.call-start = ((), (), s32[]{:S(2)}) async-start(), calls=%async_computation.3 | async-start | bytes 1474560 | tf_op jit(solution)/shard_map/all_gather | solution.py:45
  179.0 0.8 copy-start.5
  179.0 420.7 %all-gather.8.cloned.1.call-start = ((), (), s32[]{:S(2)}) async-start(), calls=%async_computation.4 | async-start | bytes 50331648 | tf_op jit(solution)/shard_map/all_gather | solution.py:35
  180.2 5.6 copy-start.3
  620.6 26.6 %copy-start.1 = (bf16[72,8192]{1,0:T(8,128)(2,1)S(1)}, bf16[72,8192]{1,0:T(8,128)(2,1)}, u32[]{:S(2)}) copy-start(bf16[72,8192]{1,0:T(8,128)(2,1)} %param.8) | copy-start | bytes 3538948
  622.1 1.4 copy-start.4
Sparse Core Ops, SparseCore 0:
  8.9 161.8 all-gather.3
  179.1 31.2 all-gather.5
  211.9 387.7 all-gather.7
where the time goes:
time: 654 us
  waiting for transfers between devices  546 us (83%)
  matrix products  31.6 us (5%)
  local copies, waits for them, and re-layouts  23 us (4%)
  blocking collectives  18.9 us (3%)
  other arithmetic  15.1 us (2%)
  between operations  13.3 us (2%)
    all_gather x1, waiting for transfers between devices, local(): lax.all_gather(w_query, 'segment', axis=1, tiled=True)[0]  388 us
    all_to_all x1, waiting for transfers between devices, local(): lax.all_to_all(copies, ('branch', 'segment'), split_axis=0, concat_axis=0...  114 us
    all_gather x1, waiting for transfers between devices, local(): keyval = lax.all_gather(keyval_part, 'tp', axis=1, tiled=True)  22.9 us
    all_gather x1, waiting for transfers between devices, local(): lax.all_gather(w_keyval, 'segment', axis=1, tiled=True)[0]  20 us
    dot_general x1, matrix products, local(): jnp.dot(normed, lax.all_gather(w_query, 'segment', axis=1, tiled=True)[0]...  17.2 us
  transfers between devices with their start and end apart: 4, of which 4 were waited for; matrix products, arithmetic and copies ran while one was open for 5% of the time, Pallas kernels for 0%

commit v1 on v0

--- a/solution.py
+++ b/solution.py
@@ -3,17 +3,439 @@
 import jax
 import jax.numpy as jnp
 from jax import lax
+from jax.experimental import pallas as pl
+from jax.experimental.pallas import tpu as pltpu
 from jax.sharding import PartitionSpec as P
+
 
 HEAD = 128
 HEADS = 64
 KV_HEADS = 8
-
+LANES = 128
+LENGTHS_AT = 8
 
 epsilon = 1e-05
 
-
-def local(rollout, send_rows, seq_lengths, attn_gain, w_query, w_keyval, head_weight, head_attn):
+ALL_AXES = ("branch", "segment", "tp")
+HIGHEST = lax.Precision.HIGHEST
+F32 = jnp.float32
+BF16 = jnp.bfloat16
+
+
+def whole(memory_space=pltpu.VMEM):
+    return pl.BlockSpec(memory_space=memory_space)
+
+
+def iota(shape, dimension):
+    return lax.broadcasted_iota(jnp.int32, shape, dimension)
+
+
+def prepare_kernel(ids_ref, lengths_ref, rows_hbm, send_hbm, mine_ref, theirs_ref, rows_ref, send_ref, sems):
+    count, width = rows_ref.shape
+    half = width // 2
+    parts = sems.shape[0] - 1
+    step = width // parts
+    core, segment = ids_ref[0], ids_ref[1]
+    copies = [pltpu.make_async_copy(send_hbm, send_ref, sems.at[parts])]
+    for part in range(parts):
+        at = pl.ds(part * step, step)
+        copies.append(pltpu.make_async_copy(rows_hbm.at[:, at], rows_ref.at[:, at], sems.at[part]))
+    for copy in copies:
+        copy.start()
+    copies[0].wait()
+    send = send_ref[...]
+    rolled = jnp.concatenate([send[:, count // 2:], send[:, :count // 2]], axis=1)
+    order = jnp.where(core == 1, rolled, send)
+    pick = (iota((count, count), 0) == order).astype(BF16)
+
+    def ordered(part):
+        out = lax.dot_general(pick, part, (((0,), (0,)), ((), ())), preferred_element_type=F32)
+        return out.astype(BF16)
+
+    lanes = jnp.zeros((count, LANES), F32)
+    for part in range(parts):
+        copies[1 + part].wait()
+        square = rows_ref[:, part * step:(part + 1) * step].astype(F32)
+        square = square * square
+        for lane in range(0, step, LANES):
+            lanes = lanes + square[:, lane:lane + LANES]
+    chunk = 1024
+    for start in range(0, half, chunk):
+        for out_ref, which in ((theirs_ref, 1 - segment), (mine_ref, segment)):
+            at = pl.multiple_of(which * half + start, chunk)
+            out_ref[:, start:start + chunk] = ordered(rows_ref[:, pl.ds(at, chunk)])
+    scale = lax.rsqrt(jnp.sum(lanes, axis=1, keepdims=True) * (1.0 / width) + epsilon)
+    high = scale.astype(BF16).astype(F32)
+    middle = (scale - high).astype(BF16).astype(F32)
+    low = scale - high - middle
+    lane = iota((count, LANES), 1)
+    tail = jnp.where(lane == 0, high, jnp.where(lane == 1, middle, jnp.where(lane == 2, low, 0.0)))
+    tail = ordered(tail.astype(BF16))
+    for index in range(lengths_ref.shape[1]):
+        length = lengths_ref[0, index].astype(F32).astype(BF16)
+        tail = jnp.where(lane == LENGTHS_AT + index, length, tail)
+    theirs_ref[:, half:] = tail
+    mine_ref[:, half:] = tail
+
+
+def prepare(ids, lengths, rows, send):
+    count, width = rows.shape
+    shape = jax.ShapeDtypeStruct((count, width // 2 + LANES), BF16)
+    return pl.pallas_call(
+        prepare_kernel,
+        out_shape=(shape, shape),
+        in_specs=[whole(pltpu.SMEM), whole(pltpu.SMEM), whole(pltpu.HBM), whole(pltpu.HBM)],
+        out_specs=(whole(), whole()),
+        scratch_shapes=[
+            pltpu.VMEM((count, width), BF16),
+            pltpu.VMEM((1, count), jnp.int32),
+            pltpu.SemaphoreType.DMA((5,)),
+        ],
+        compiler_params=pltpu.CompilerParams(vmem_limit_bytes=12 << 20),
+        name="prepare",
+    )(ids, lengths, rows, send)
+
+
+def chunk_kernel(ids_ref, near_ref, far_ref, gain_hbm, keyval_hbm, query_hbm, head_hbm,
+                 rows_ref, own_ref, direct_ref, tail_ref, *refs):
+    sends, (gain_ref, keyval_ref, query_ref, head_ref, sems) = refs[:-5], refs[-5:]
+    send_ref = sends[0]
+    count = near_ref.shape[0]
+    half = rows_ref.shape[1]
+    blocks, _, block = query_ref.shape
+    core, segment, tp = ids_ref[0], ids_ref[1], ids_ref[3]
+    columns = blocks * block
+    gain_copy = pltpu.make_async_copy(gain_hbm.at[:, pl.ds(pl.multiple_of(segment * half, half), half)], gain_ref, sems.at[0])
+    head_copy = pltpu.make_async_copy(head_hbm, head_ref, sems.at[1])
+    keyval_copy = pltpu.make_async_copy(keyval_hbm, keyval_ref, sems.at[2])
+    gain_copy.start()
+    head_copy.start()
+    keyval_copy.start()
+    query_copies = []
+    for index in range(blocks):
+        at = pl.multiple_of((1 - segment) * columns + index * block, block)
+        query_copies.append(pltpu.make_async_copy(query_hbm.at[:, pl.ds(at, block)], query_ref.at[index], sems.at[3 + index]))
+        query_copies[-1].start()
+
+    top = (iota((count, 1), 0) < count // 2).astype(jnp.int32)
+    mask = (top ^ core) == 1
+
+    def both(near, far):
+        return jnp.concatenate([jnp.where(mask, near, far), jnp.where(mask, far, near)], axis=0)
+
+    first_lanes = iota((count, LANES), 1) < 3
+
+    def scale_of(ref):
+        return jnp.sum(jnp.where(first_lanes, ref[:, half:].astype(F32), 0.0), axis=1, keepdims=True)
+
+    scale = both(scale_of(near_ref), scale_of(far_ref))
+    slice_width = head_ref.shape[1]
+    holder = (tp * slice_width) // half == segment
+    first = (tp * slice_width) % half
+    chunk = 512
+    direct = jnp.zeros((2 * count, LANES), F32)
+    gain_copy.wait()
+    head_copy.wait()
+    for start in range(0, half, chunk):
+        at = slice(start, start + chunk)
+        rows = both(near_ref[:, at].astype(F32), far_ref[:, at].astype(F32))
+        inside = jnp.logical_and(holder, jnp.logical_and(start >= first, start < first + slice_width))
+        offset = pl.multiple_of(jnp.where(inside, start - first, 0), chunk)
+        weight = jnp.where(inside, head_ref[:, pl.ds(offset, chunk)].astype(F32), 0.0)
+        for lane in range(0, chunk, LANES):
+            direct = direct + rows[:, lane:lane + LANES] * weight[:, lane:lane + LANES]
+        rows_ref[:, at] = (rows * scale * gain_ref[:, at].astype(F32)).astype(BF16)
+    direct_ref[...] = direct
+    tail_ref[...] = near_ref[:, half:].astype(F32)[:8]
+
+    keyval_copy.wait()
+    keyval = jnp.dot(rows_ref[...], keyval_ref[...], preferred_element_type=F32)
+    even = jnp.concatenate([keyval[:, :HEAD], keyval[:, 2 * HEAD:3 * HEAD]], axis=1)
+    odd = jnp.concatenate([keyval[:, HEAD:2 * HEAD], keyval[:, 3 * HEAD:]], axis=1)
+    own_ref[...] = jnp.where(segment == 0, even, odd)
+    other = jnp.where(segment == 0, odd, even).astype(BF16)
+    if len(sends) == 1:
+        send_ref[:, columns:] = other
+    else:
+        sends[1][...] = other
+    for index in range(blocks):
+        query_copies[index].wait()
+        send_ref[:, index * block:(index + 1) * block] = jnp.dot(
+            rows_ref[...], query_ref[index], preferred_element_type=F32).astype(BF16)
+
+
+def multiply_chunk(ids, near, far, gain, keyval, query, head, split):
+    count, wide = near.shape
+    half = wide - LANES
+    columns = query.shape[1] // 2
+    block = 256
+    blocks = columns // block
+    rows = 2 * count
+    widths = (columns, 2 * HEAD) if split else (columns + 2 * HEAD,)
+    return pl.pallas_call(
+        chunk_kernel,
+        out_shape=(
+            jax.ShapeDtypeStruct((rows, half), BF16),
+            jax.ShapeDtypeStruct((rows, 2 * HEAD), F32),
+            jax.ShapeDtypeStruct((rows, LANES), F32),
+            jax.ShapeDtypeStruct((8, LANES), F32),
+        ) + tuple(jax.ShapeDtypeStruct((rows, width), BF16) for width in widths),
+        in_specs=[whole(pltpu.SMEM), whole(), whole()] + [whole(pltpu.HBM)] * 4,
+        out_specs=(whole(),) * (4 + len(widths)),
+        scratch_shapes=[
+            pltpu.VMEM((1, half), BF16),
+            pltpu.VMEM(keyval.shape, BF16),
+            pltpu.VMEM((blocks, half, block), BF16),
+            pltpu.VMEM(head.shape, BF16),
+            pltpu.SemaphoreType.DMA((3 + blocks,)),
+        ],
+        compiler_params=pltpu.CompilerParams(vmem_limit_bytes=28 << 20),
+        cost_estimate=pl.CostEstimate(
+            flops=2 * rows * half * (columns + keyval.shape[1]), transcendentals=0,
+            bytes_accessed=2 * half * (columns + keyval.shape[1])),
+        name="chunk",
+    )(ids, near, far, gain, keyval, query, head)
+
+
+def own_kernel(ids_ref, a_ref, b_ref, c_ref, d_ref, query_hbm, out_ref, rows_ref, query_ref, sems):
+    blocks, _, block = query_ref.shape
+    columns = blocks * block
+    copies = []
+    for index in range(blocks):
+        at = pl.multiple_of(ids_ref[1] * columns + index * block, block)
+        copies.append(pltpu.make_async_copy(query_hbm.at[:, pl.ds(at, block)], query_ref.at[index], sems.at[index]))
+        copies[-1].start()
+    count = a_ref.shape[0]
+    for index, ref in enumerate((a_ref, b_ref, c_ref, d_ref)):
+        rows_ref[index * count:(index + 1) * count, :] = ref[...]
+    for index in range(blocks):
+        copies[index].wait()
+        out_ref[:, index * block:(index + 1) * block] = jnp.dot(
+            rows_ref[...], query_ref[index], preferred_element_type=F32)
+
+
+def own_queries(ids, chunks, query):
+    count, half = chunks[0].shape
+    columns = query.shape[1] // 2
+    block = 256
+    blocks = columns // block
+    return pl.pallas_call(
+        own_kernel,
+        out_shape=jax.ShapeDtypeStruct((4 * count, columns), F32),
+        in_specs=[whole(pltpu.SMEM)] + [whole()] * 4 + [whole(pltpu.HBM)],
+        out_specs=whole(),
+        scratch_shapes=[
+            pltpu.VMEM((4 * count, half), BF16),
+            pltpu.VMEM((blocks, half, block), BF16),
+            pltpu.SemaphoreType.DMA((blocks,)),
+        ],
+        compiler_params=pltpu.CompilerParams(vmem_limit_bytes=32 << 20),
+        cost_estimate=pl.CostEstimate(
+            flops=8 * count * half * columns, transcendentals=0, bytes_accessed=2 * half * columns),
+        name="own_queries",
+    )(ids, *chunks, query)
+
+
+def by_pack(parts, pack):
+    count = parts[0].shape[0] // 2
+    return jnp.concatenate([part[pack * count:(pack + 1) * count] for part in parts], axis=0)
+
+
+def keyval_kernel(ids_ref, *refs):
+    owns, recvs = refs[:4], refs[4:8]
+    keep_ref, first_ref, second_ref = refs[8:]
+    tp = ids_ref[3]
+    sums = [own[...] + recv[:, recv.shape[1] - 2 * HEAD:].astype(F32) for own, recv in zip(owns, recvs)]
+    rows = 2 * owns[0].shape[0]
+    for pack in range(2):
+        at = slice(pack * rows, (pack + 1) * rows)
+        part = by_pack(sums, pack)
+        low, high = part[:, :HEAD], part[:, HEAD:]
+        keep_ref[at, :] = jnp.where(tp == 3, high, low).astype(BF16)
+        first_ref[at, :] = jnp.where(tp < 2, high, low).astype(BF16)
+        second_ref[at, :] = jnp.where(tp == 2, high, low).astype(BF16)
+
+
+def sum_keyval(ids, owns, recvs):
+    rows = 4 * owns[0].shape[0]
+    shape = jax.ShapeDtypeStruct((rows, HEAD), BF16)
+    return pl.pallas_call(
+        keyval_kernel,
+        out_shape=(shape, shape, shape),
+        in_specs=[whole(pltpu.SMEM)] + [whole()] * 8,
+        out_specs=(whole(),) * 3,
+        compiler_params=pltpu.CompilerParams(vmem_limit_bytes=8 << 20),
+        name="sum_keyval",
+    )(ids, *owns, *recvs)
+
+
+def owner_of(row, pack, ids_ref, piece_rows):
+    index = jnp.zeros_like(row)
+    for step in range(1, 8):
+        index = index + (row >= step * piece_rows).astype(jnp.int32)
+    chip, low = index >> 1, index & 1
+    shard = (((chip >> 1) ^ ids_ref[2]) * 2 + (low ^ pack)) * 2 + ((chip & 1) ^ ids_ref[1])
+    return shard, row - index * piece_rows
+
+
+def attention_kernel(ids_ref, lengths_ref, tail_ref, own_ref, *refs):
+    recvs, (keep_ref, first_ref, second_ref, gain_ref), directs = refs[:4], refs[4:8], refs[8:12]
+    out_ref, bias_ref, value_ref = refs[12:]
+    segment, tp = ids_ref[1], ids_ref[3]
+    count = recvs[0].shape[0]
+    rows = 2 * count
+    piece_rows = rows // 8
+    heads = own_ref.shape[1] // HEAD
+    devices = out_ref.shape[0]
+    wide = out_ref.shape[1] // 2
+    scale = math.log2(math.e) / math.sqrt(HEAD)
+    tail = tail_ref[:1, :].astype(jnp.int32)
+    lane = iota((rows, wide), 1)
+    keys_all = jnp.where(tp == 0, keep_ref[...], jnp.where(tp == 2, second_ref[...], first_ref[...]))
+    value_ref[:, :HEAD] = jnp.where(tp == 3, keep_ref[...], jnp.where(tp == 1, second_ref[...], first_ref[...]))
+    value_ref[:, HEAD:] = jnp.ones((2 * rows, HEAD), BF16)
+    through = jnp.zeros((devices, wide), F32)
+    direct = jnp.zeros((devices, wide), F32)
+    for pack in range(2):
+        def place(row):
+            shard, inner = owner_of(row, pack, ids_ref, piece_rows)
+            position = shard * piece_rows + inner
+            end = jnp.zeros((1, 1), jnp.int32)
+            doc = jnp.zeros_like(position)
+            for index in range(lengths_ref.shape[1]):
+                at = LENGTHS_AT + index
+                end = end + jnp.where(segment == pack, lengths_ref[0, index], tail[:, at:at + 1])
+                doc = doc + (position >= end).astype(jnp.int32)
+            return position, doc
+
+        row_position, row_doc = place(iota((rows, 1), 0))
+        col_position, col_doc = place(iota((1, rows), 1))
+        visible = jnp.logical_and(row_doc == col_doc, col_position <= row_position)
+        bias_ref[...] = jnp.where(visible, 0.0, -1e30)
+        keys = keys_all[pack * rows:(pack + 1) * rows]
+        total = jnp.zeros((rows, HEAD), F32)
+        for head in range(heads):
+            at = slice(head * HEAD, (head + 1) * HEAD)
+            parts = [own_ref[index * count:(index + 1) * count, at] + recv[:, at].astype(F32)
+                     for index, recv in enumerate(recvs)]
+            query = (by_pack(parts, pack) * scale).astype(BF16)
+            logits = lax.dot_general(query, keys, (((1,), (1,)), ((), ())), preferred_element_type=F32)
+            logits = logits + bias_ref[...]
+            expo = jnp.exp2(logits - jnp.max(logits, axis=1, keepdims=True)).astype(BF16)
+            both = jnp.dot(expo, value_ref[pack * rows:(pack + 1) * rows, :], preferred_element_type=F32)
+            offset = pl.multiple_of(segment * heads * HEAD + head * HEAD, HEAD)
+            total = total + both[:, :HEAD] / both[:, HEAD:] * gain_ref[:, pl.ds(offset, HEAD)].astype(F32)
+
+        _, inner = owner_of(iota((rows, 1), 0), pack, ids_ref, piece_rows)
+        shard_row, _ = owner_of(iota((1, rows), 1), pack, ids_ref, piece_rows)
+        chosen = ((iota((devices, 1), 0) >> 2) == shard_row).astype(F32)
+        hit = lane == inner + pack * piece_rows
+
+        def send(column):
+            return jnp.dot(chosen, jnp.where(hit, column, 0.0), precision=HIGHEST, preferred_element_type=F32)
+
+        through = through + send(jnp.sum(total, axis=1, keepdims=True))
+        direct = direct + send(jnp.sum(by_pack([ref[...] for ref in directs], pack), axis=1, keepdims=True))
+    out_ref[:, :wide] = through
+    out_ref[:, wide:] = direct
+
+
+def attention(ids, lengths, tail, own, recvs, keep, first, second, gain, directs, devices):
+    rows = own.shape[0] // 2
+    return pl.pallas_call(
+        attention_kernel,
+        out_shape=jax.ShapeDtypeStruct((devices, 2 * LANES), F32),
+        in_specs=[whole(pltpu.SMEM), whole(pltpu.SMEM)] + [whole()] * 14,
+        out_specs=whole(),
+        scratch_shapes=[
+            pltpu.VMEM((rows, rows), F32),
+            pltpu.VMEM((2 * rows, 2 * HEAD), BF16),
+        ],
+        compiler_params=pltpu.CompilerParams(vmem_limit_bytes=28 << 20),
+        name="attend",
+    )(ids, lengths, tail, own, *recvs, keep, first, second, gain, *directs)
+
+
+def finish_kernel(recv_ref, send_ref, out_ref):
+    models, count = out_ref.shape
+    devices, width = recv_ref.shape
+    model_of = iota((models, devices), 1) // (devices // models)
+    chosen = (model_of == iota((models, devices), 0)).astype(F32)
+    sums = jnp.dot(chosen, recv_ref[...], precision=HIGHEST, preferred_element_type=F32)
+    pick = (iota((count, count), 0) == send_ref[...]).astype(F32)
+    half = width // 2
+    both = sums[:, :count] + sums[:, half:half + count]
+    out_ref[...] = lax.dot_general(
+        both, pick, (((1,), (1,)), ((), ())), precision=HIGHEST, preferred_element_type=F32)
+
+
+def finish(recv, send, models):
+    count = send.shape[1]
+    return pl.pallas_call(
+        finish_kernel,
+        out_shape=jax.ShapeDtypeStruct((models, count), F32),
+        in_specs=[whole()] * 2,
+        out_specs=whole(),
+        compiler_params=pltpu.CompilerParams(vmem_limit_bytes=8 << 20),
+        name="finish",
+    )(recv, send)
+
+
+def paired(rollout, send_rows, seq_lengths, attn_gain, w_query, w_keyval, head_weight, head_attn):
+    n_branch = lax.axis_size("branch")
+    branch = lax.axis_index("branch")
+    segment = lax.axis_index("segment")
+    tp = lax.axis_index("tp")
+    send = send_rows.reshape(1, -1)
+    ids = jnp.stack([branch & 1, segment, branch >> 1, tp]).astype(jnp.int32)
+
+    core_pairs = [(i, i ^ 1) for i in range(n_branch)]
+    y_pairs = [(i, i ^ 2) for i in range(n_branch)]
+    x_pairs = [(0, 1), (1, 0)]
+
+    def swap(piece):
+        return lax.ppermute(piece, "branch", core_pairs)
+
+    def across(part):
+        return lax.ppermute(part, "segment", x_pairs)
+
+    def in_hbm(array):
+        return pltpu.with_memory_space_constraint(array, pltpu.HBM)
+
+    rollout, send, attn_gain, head_weight, seq_lengths = map(
+        in_hbm, (rollout, send, attn_gain, head_weight, seq_lengths))
+    wq, wkv = in_hbm(w_query[0]), in_hbm(w_keyval[0])
+    mine, theirs = prepare(ids, seq_lengths, rollout, send)
+    from_x = across(theirs)
+    from_y = lax.ppermute(mine, "branch", y_pairs)
+    from_d = lax.ppermute(from_x, "branch", y_pairs)
+
+    rows, owns, directs, tails, received = [], [], [], [], []
+    for name, piece in (("own", mine), ("x", from_x), ("y", from_y), ("d", from_d)):
+        far = swap(piece)
+        row, own, direct, tail, *sends = multiply_chunk(
+            ids, piece, far, attn_gain, wkv, wq, head_weight, name == "d")
+        for index, part in reversed(list(enumerate(sends))):
+            sends[index] = across(part)
+        rows.append(row)
+        owns.append(own)
+        directs.append(direct)
+        tails.append(tail)
+        received.append(sends)
+    order = (1, 0, 3, 2)
+    keep, first, second = sum_keyval(ids, owns, [received[index][-1] for index in order])
+    first = lax.ppermute(first, "tp", [(0, 1), (2, 0), (1, 3), (3, 2)])
+    second = lax.ppermute(second, "tp", [(2, 1), (1, 2)])
+    own = own_queries(ids, rows, wq)
+    devices = n_branch * 2 * lax.axis_size("tp")
+    outgoing = attention(
+        ids, seq_lengths, tails[1], own, [received[index][0] for index in order],
+        keep, first, second, head_attn, directs, devices)
+    incoming = lax.all_to_all(outgoing, ALL_AXES, split_axis=0, concat_axis=0, tiled=True)
+    return finish(incoming, send, n_branch)
+
+
+def general(rollout, send_rows, seq_lengths, attn_gain, w_query, w_keyval, head_weight, head_attn):
     n_branch = lax.axis_size("branch")
     n_segment = lax.axis_size("segment")
     gen_rows = rollout.shape[0]
@@ -86,6 +508,9 @@
 
 
 def solution(mesh):
+    sizes = tuple(mesh.shape[axis] for axis in ALL_AXES)
+    pairwise = sizes == (4, 2, 4)
+    local = paired if pairwise else general
     return jax.shard_map(
         local,
         mesh=mesh,

time: 654 us -> 107 us (0.16)
  waiting for transfers between devices: 546 us -> 28.2 us
  Pallas kernels: 0 us -> 49.4 us
  matrix products: 31.6 us -> 0 us
  local copies, waits for them, and re-layouts: 23 us -> 0.05 us
  other arithmetic: 15.1 us -> 0.08 us
  between operations: 13.3 us -> 0.12 us
  starting transfers between devices: 5.59 us -> 14.9 us
    all_gather x3 -> x0, waiting for transfers between devices: 431 us -> none  [the longest x1 388 us: local(): lax.all_gather(w_query, 'segment', axis=1, tiled=True)[0]]
    all_to_all x1 -> x0, waiting for transfers between devices: 114 us -> none  [local(): lax.all_to_all(copies, ('branch', 'segment'), split_axis=0, concat_axis=0...]
    pallas_call x0 -> x9, Pallas kernels: none -> 49.4 us  [the longest x4 26.7 us: multiply_chunk(): pl.pallas_call(chunk_kernel, out_shape=(jax.ShapeDtypeStruct((rows, half)...]
    dot_general x6 -> x0, matrix products: 31.6 us -> none  [the longest x1 17.2 us: local(): jnp.dot(normed, lax.all_gather(w_query, 'segment', axis=1, tiled=True)[0]...]
    ppermute x0 -> x14, waiting for transfers between devices: none -> 28.2 us  [the longest x6 15.6 us: across(): return lax.ppermute(part, 'segment', x_pairs)]
    ppermute x0 -> x14, starting transfers between devices: none -> 14.9 us  [the longest x6 8.8 us: across(): return lax.ppermute(part, 'segment', x_pairs)]
    psum x1 -> x0, blocking collectives: 11.7 us -> none  [local(): totals = lax.psum(direct + through, 'tp')]
    all_to_all x1, blocking collectives: 7.21 us -> 14.2 us  [paired(): lax.all_to_all(outgoing, ALL_AXES, split_axis=0, concat_axis=0, tiled=True)]
  transfers between devices with their start and end apart: 4 -> 14, of which waited for: 4 -> 4; matrix products, arithmetic and copies ran while one was open for 5% -> 0% of each run, Pallas kernels for 0% -> 37%
where the time goes in v1:
time: 107 us
  Pallas kernels  49.4 us (46%)
  waiting for transfers between devices  28.2 us (26%)
  starting transfers between devices  14.9 us (14%)
  blocking collectives  14.2 us (13%)
    pallas_call x4, Pallas kernels, multiply_chunk(): pl.pallas_call(chunk_kernel, out_shape=(jax.ShapeDtypeStruct((rows, half)...  26.7 us
    ppermute x6, waiting for transfers between devices, across(): return lax.ppermute(part, 'segment', x_pairs)  15.6 us
    all_to_all x1, blocking collectives, paired(): lax.all_to_all(outgoing, ALL_AXES, split_axis=0, concat_axis=0, tiled=True)  14.2 us
    ppermute x1, waiting for transfers between devices, paired(): from_d = lax.ppermute(from_x, 'branch', y_pairs)  12.6 us
    pallas_call x1, Pallas kernels, own_queries(): pl.pallas_call(own_kernel, out_shape=jax.ShapeDtypeStruct((4 * count, col...  12.5 us
    ppermute x6, starting transfers between devices, across(): return lax.ppermute(part, 'segment', x_pairs)  8.8 us
    pallas_call x1, Pallas kernels, attention(): pl.pallas_call(attention_kernel, out_shape=jax.ShapeDtypeStruct((devices,...  5.49 us
    pallas_call x1, Pallas kernels, prepare(): pl.pallas_call(prepare_kernel, out_shape=(shape, shape), in_specs=[whole(...  2.52 us
  transfers between devices with their start and end apart: 14, of which 4 were waited for; matrix products, arithmetic and copies ran while one was open for 0% of the time, Pallas kernels for 37%

profile of v1, /device:TPU:0, one launch (start us, length us, event | category | flops | bytes accessed | tf_op | source)
XLA Modules:
  0.0 106.9 jit_solution(18108566049077859595)
XLA Ops:
  0.0 0.1 pad_add_fusion.ids_ref
  0.1 2.5 %prepare.1 = (bf16[72,4224]{1,0:T(8,128)(2,1)S(1)}, bf16[72,4224]{1,0:T(8,128)(2,1)S(1)}) custom-call(s32[4]{0:T(128)S(1)} %pad_add_fusion.ids_ref, s32[1,6]{1,0:T(1,128)} %lengths_ref.3, bf16[72,8192]{1,0:T(8,128)(2,1)} %rows_hbm.1, s32[1,72]{1,0:T(1,128)} %bitcast.22), custom_call_target="tpu_custom_call" | custom-call | tf_op jit(solution)/shard_map/prepare/pallas_call | solution.py:84
  2.6 3.0 %collective-permute-start = (bf16[72,4224]{1,0:T(8,128)(2,1)S(1)}, bf16[72,4224]{1,0:T(8,128)(2,1)S(1)}, u32[]{:S(2)}, u32[]{:S(2)}) collective-permute-start(bf16[72,4224]{1,0:T(8,128)(2,1)S(1)} %get-tuple-element.28), channel_id=1, source_target_pairs={{0,4},{4,0},{1,5},{5,1},{2,6},{6,2},{3,7},{7,3},{8,12},{12,8},{9,1... | collective-permute-start | bytes 1824776 | tf_op jit(solution)/shard_map/ppermute | solution.py:400
  5.6 1.5 %collective-permute-start.3 = (bf16[72,4224]{1,0:T(8,128)(2,1)S(1)}, bf16[72,4224]{1,0:T(8,128)(2,1)S(1)}, u32[]{:S(2)}, u32[]{:S(2)}) collective-permute-start(bf16[72,4224]{1,0:T(8,128)(2,1)S(1)} %get-tuple-element.30.near_ref), channel_id=1, source_target_pairs={{0,16},{8,24},{16,0},{24,8},{1,17},{9,25},{17,1},{25,9},{2,18},{10... | collective-permute-start | bytes 1824776 | tf_op jit(solution)/shard_map/ppermute | solution.py:410
  7.2 12.2 %collective-permute-done.near_ref = bf16[72,4224]{1,0:T(8,128)(2,1)S(1)} collective-permute-done((bf16[72,4224]{1,0:T(8,128)(2,1)S(1)}, bf16[72,4224]{1,0:T(8,128)(2,1)S(1)}, u32[]{:S(2)}, u32[]{:S(2)}) %collective-permute-start) | collective-permute-done | bytes 608288 | tf_op jit(solution)/shard_map/ppermute | solution.py:400
  19.4 1.8 %collective-permute-start.5 = (bf16[72,4224]{1,0:T(8,128)(2,1)S(1)}, bf16[72,4224]{1,0:T(8,128)(2,1)S(1)}, u32[]{:S(2)}, u32[]{:S(2)}) collective-permute-start(bf16[72,4224]{1,0:T(8,128)(2,1)S(1)} %collective-permute-done.near_ref), channel_id=1, source_target_pairs={{0,16},{8,24},{16,0},{24,8},{1,17},{9,25},{17,1},{25,9},{2,18},{10... | collective-permute-start | bytes 1824776 | tf_op jit(solution)/shard_map/ppermute | solution.py:411
  21.1 0.0 collective-permute-start.2
  21.1 0.0 collective-permute-done.3.near_ref
  21.1 0.5 collective-permute-start.4
  21.6 0.0 collective-permute-start.1
  21.7 12.6 %collective-permute-done.5.near_ref = bf16[72,4224]{1,0:T(8,128)(2,1)S(1)} collective-permute-done((bf16[72,4224]{1,0:T(8,128)(2,1)S(1)}, bf16[72,4224]{1,0:T(8,128)(2,1)S(1)}, u32[]{:S(2)}, u32[]{:S(2)}) %collective-permute-start.5) | collective-permute-done | bytes 608288 | tf_op jit(solution)/shard_map/ppermute | solution.py:411
  34.2 0.0 collective-permute-start.6
  34.2 0.0 collective-permute-done.2.far_ref
  34.3 6.7 %chunk.5 = (bf16[144,4096]{1,0:T(8,128)(2,1)S(1)}, f32[144,256]{1,0:T(8,128)S(1)}, f32[144,128]{1,0:T(8,128)S(1)}, f32[8,128]{1,0:T(8,128)}, bf16[144,1280]{1,0:T(8,128)(2,1)S(1)}) custom-call(s32[4]{0:T(128)S(1)} %pad_add_fusion.ids_ref, bf16[72,4224]{1,0:T(8,128)(2,1)S(1)} %get-tuple-element.30.near_ref, ...), custom_call_target="tpu_custom_call" | custom-call | flops 1811939328 | bytes 12582912 | tf_op jit(solution)/shard_map/chunk/pallas_call | solution.py:175
  40.9 1.5 %collective-permute-start.8 = (bf16[144,1280]{1,0:T(8,128)(2,1)S(1)}, bf16[144,1280]{1,0:T(8,128)(2,1)S(1)}, u32[]{:S(2)}, u32[]{:S(2)}) collective-permute-start(bf16[144,1280]{1,0:T(8,128)(2,1)S(1)} %get-tuple-element.36), channel_id=1, source_target_pairs={{0,4},{4,0},{1,5},{5,1},{2,6},{6,2},{3,7},{7,3},{8,12},{12,8},{9,1... | collective-permute-start | bytes 1105928 | tf_op jit(solution)/shard_map/ppermute | solution.py:400
  42.5 0.0 collective-permute-done.4.far_ref
  42.5 6.7 %chunk.6 = (bf16[144,4096]{1,0:T(8,128)(2,1)S(1)}, f32[144,256]{1,0:T(8,128)S(1)}, f32[144,128]{1,0:T(8,128)S(1)}, f32[8,128]{1,0:T(8,128)}, bf16[144,1280]{1,0:T(8,128)(2,1)S(1)}) custom-call(s32[4]{0:T(128)S(1)} %pad_add_fusion.ids_ref, bf16[72,4224]{1,0:T(8,128)(2,1)S(1)} %collective-permute-done.3.near_ref, ...), custom_call_target="tpu_custom_call" | custom-call | flops 1811939328 | bytes 12582912 | tf_op jit(solution)/shard_map/chunk/pallas_call | solution.py:175
  49.1 0.6 collective-permute-start.10
  49.8 0.0 collective-permute-done.1.far_ref
  49.8 6.7 %chunk.4 = (bf16[144,4096]{1,0:T(8,128)(2,1)S(1)}, f32[144,256]{1,0:T(8,128)S(1)}, f32[144,128]{1,0:T(8,128)S(1)}, f32[8,128]{1,0:T(8,128)S(1)}, bf16[144,1280]{1,0:T(8,128)(2,1)S(1)}) custom-call(s32[4]{0:T(128)S(1)} %pad_add_fusion.ids_ref, bf16[72,4224]{1,0:T(8,128)(2,1)S(1)} %collective-permute-done.near_ref, ...), custom_call_target="tpu_custom_call" | custom-call | flops 1811939328 | bytes 12582912 | tf_op jit(solution)/shard_map/chunk/pallas_call | solution.py:175
  56.4 1.5 %collective-permute-start.7 = (bf16[144,1280]{1,0:T(8,128)(2,1)S(1)}, bf16[144,1280]{1,0:T(8,128)(2,1)S(1)}, u32[]{:S(2)}, u32[]{:S(2)}) collective-permute-start(bf16[144,1280]{1,0:T(8,128)(2,1)S(1)} %get-tuple-element.35), channel_id=1, source_target_pairs={{0,4},{4,0},{1,5},{5,1},{2,6},{6,2},{3,7},{7,3},{8,12},{12,8},{9,1... | collective-permute-start | bytes 1105928 | tf_op jit(solution)/shard_map/ppermute | solution.py:400
  58.0 0.0 collective-permute-done.6.far_ref
  58.0 6.7 %chunk.7 = (bf16[144,4096]{1,0:T(8,128)(2,1)S(1)}, f32[144,256]{1,0:T(8,128)S(1)}, f32[144,128]{1,0:T(8,128)S(1)}, f32[8,128]{1,0:T(8,128)}, bf16[144,1024]{1,0:...) custom-call(s32[4]{0:T(128)S(1)} %pad_add_fusion.ids_ref, bf16[72,4224]{1,0:T(8,128)(2,1)S(1)} %collective-permute-done.5.near_ref, ...), custom_call_target="tpu_custom_call" | custom-call | flops 1811939328 | bytes 12582912 | tf_op jit(solution)/shard_map/chunk/pallas_call | solution.py:175
  64.6 0.6 collective-permute-start.11
  65.3 1.5 %collective-permute-start.9 = (bf16[144,1024]{1,0:T(8,128)(2,1)S(1)}, bf16[144,1024]{1,0:T(8,128)(2,1)S(1)}, u32[]{:S(2)}, u32[]{:S(2)}) collective-permute-start(bf16[144,1024]{1,0:T(8,128)(2,1)S(1)} %get-tuple-element.37), channel_id=1, source_target_pairs={{0,4},{4,0},{1,5},{5,1},{2,6},{6,2},{3,7},{7,3},{8,12},{12,8},{9,1... | collective-permute-start | bytes 884744 | tf_op jit(solution)/shard_map/ppermute | solution.py:400
  66.7 0.0 collective-permute-done.8.refs_5_.refs_1_
  66.7 0.0 collective-permute-done.10.refs_7_.refs_3_
  66.7 1.8 %collective-permute-done.7.refs_4_.refs_0_ = bf16[144,1280]{1,0:T(8,128)(2,1)S(1)} collective-permute-done((bf16[144,1280]{1,0:T(8,128)(2,1)S(1)}, bf16[144,1280]{1,0:T(8,128)(2,1)S(1)}, u32[]{:S(2)}, u32[]{:S(2)}) %collective-permute-start.7) | collective-permute-done | bytes 368672 | tf_op jit(solution)/shard_map/ppermute | solution.py:400
  68.6 1.6 %collective-permute-done.11.refs_6_ = bf16[144,256]{1,0:T(8,128)(2,1)S(1)} collective-permute-done((bf16[144,256]{1,0:T(8,128)(2,1)S(1)}, bf16[144,256]{1,0:T(8,128)(2,1)S(1)}, u32[]{:S(2)}, u32[]{:S(2)}) %collective-permute-start.11) | collective-permute-done | bytes 73760 | tf_op jit(solution)/shard_map/ppermute | solution.py:400
  70.1 0.6 sum_keyval.1
  70.8 1.6 %collective-permute-start.12 = (bf16[576,128]{1,0:T(8,128)(2,1)S(1)}, bf16[576,128]{1,0:T(8,128)(2,1)S(1)}, u32[]{:S(2)}, u32[]{:S(2)}) collective-permute-start(bf16[576,128]{1,0:T(8,128)(2,1)S(1)} %get-tuple-element.45), channel_id=1, source_target_pairs={{0,1},{2,0},{1,3},{3,2},{4,5},{6,4},{5,7},{7,6},{8,9},{10,8},{9,11... | collective-permute-start | bytes 442376 | tf_op jit(solution)/shard_map/ppermute | solution.py:427
  72.4 0.7 collective-permute-start.13
  73.1 0.0 copy-start
  73.1 12.5 %own_queries.1.own_ref = f32[576,1024]{1,0:T(8,128)S(1)} custom-call(s32[4]{0:T(128)S(1)} %pad_add_fusion.ids_ref, bf16[144,4096]{1,0:T(8,128)(2,1)S(1)} %get-tuple-element.31.a_ref, bf16[144,4096]{1,0:T(8,128)(2,1)S(1)} %get-tuple-element.32.b_ref, bf16[144,4096]{1,0:T(8,128)(2,1)S(1)} %get-tuple-element.33.c_ref, ...), custom_call_target="tpu_custom_call" | custom-call | flops 4831838208 | bytes 8388608 | tf_op jit(solution)/shard_map/own_queries/pallas_call | solution.py:222
  85.6 0.0 collective-permute-done.12.refs_5_
  85.6 0.0 collective-permute-done.13.refs_6_
  85.6 0.0 collective-permute-done.9.refs_2_
  85.6 0.0 copy-done
  85.6 5.5 %attend.1 = f32[32,256]{1,0:T(8,128)S(1)} custom-call(s32[4]{0:T(128)S(1)} %pad_add_fusion.ids_ref, s32[1,6]{1,0:T(1,128)} %lengths_ref.3, f32[8,128]{1,0:T(8,128)S(1)} %get-tuple-element.29.tail_ref, f32[576,1024]{1,0:T(8,128)S(1)} %own_queries.1.own_ref, bf16[144,1280]{1,0:T(8,128)(2,1)S(1)} %collective-permute-done.7.refs_4_.refs_0_, ...), custom_call_target="tpu_custom_call" | custom-call | tf_op jit(solution)/shard_map/attend/pallas_call | solution.py:345
  91.2 14.2 %all_to_all.11 = f32[32,1,256]{2,1,0:T(1,128)S(1)} all-to-all(f32[32,1,256]{2,1,0:T(1,128)S(1)} %copy.9), channel_id=1, replica_groups=mesh['branch'=4,'segment'=2,'tp'=4] {'branch','segment','tp'}, dimensions={0} | all-to-all | bytes 65536 | tf_op jit(solution)/shard_map/all_to_all | solution.py:434
  105.4 1.6 %finish.1 = f32[4,72]{1,0:T(4,128)} custom-call(f32[32,256]{1,0:T(8,128)S(1)} %bitcast.12, s32[1,72]{1,0:T(1,128)} %bitcast.23), custom_call_target="tpu_custom_call" | custom-call | tf_op jit(solution)/shard_map/finish/pallas_call | solution.py:374
  (2 shorter events, 0.0 us)
Async XLA Ops:
  2.6 16.8 %collective-permute-start = (bf16[72,4224]{1,0:T(8,128)(2,1)S(1)}, bf16[72,4224]{1,0:T(8,128)(2,1)S(1)}, u32[]{:S(2)}, u32[]{:S(2)}) collective-permute-start(bf16[72,4224]{1,0:T(8,128)(2,1)S(1)} %get-tuple-element.28), channel_id=1, source_target_pairs={{0,4},{4,0},{1,5},{5,1},{2,6},{6,2},{3,7},{7,3},{8,12},{12,8},{9,1... | collective-permute-start | bytes 1824776 | tf_op jit(solution)/shard_map/ppermute | solution.py:400
  5.6 15.5 %collective-permute-start.3 = (bf16[72,4224]{1,0:T(8,128)(2,1)S(1)}, bf16[72,4224]{1,0:T(8,128)(2,1)S(1)}, u32[]{:S(2)}, u32[]{:S(2)}) collective-permute-start(bf16[72,4224]{1,0:T(8,128)(2,1)S(1)} %get-tuple-element.30.near_ref), channel_id=1, source_target_pairs={{0,16},{8,24},{16,0},{24,8},{1,17},{9,25},{17,1},{25,9},{2,18},{10... | collective-permute-start | bytes 1824776 | tf_op jit(solution)/shard_map/ppermute | solution.py:410
  19.4 14.9 %collective-permute-start.5 = (bf16[72,4224]{1,0:T(8,128)(2,1)S(1)}, bf16[72,4224]{1,0:T(8,128)(2,1)S(1)}, u32[]{:S(2)}, u32[]{:S(2)}) collective-permute-start(bf16[72,4224]{1,0:T(8,128)(2,1)S(1)} %collective-permute-done.near_ref), channel_id=1, source_target_pairs={{0,16},{8,24},{16,0},{24,8},{1,17},{9,25},{17,1},{25,9},{2,18},{10... | collective-permute-start | bytes 1824776 | tf_op jit(solution)/shard_map/ppermute | solution.py:411
  21.1 13.1 %collective-permute-start.2 = (bf16[72,4224]{1,0:T(8,128)(2,1)S(1)}, bf16[72,4224]{1,0:T(8,128)(2,1)S(1)}, u32[]{:S(2)}, u32[]{:S(2)}) collective-permute-start(bf16[72,4224]{1,0:T(8,128)(2,1)S(1)} %get-tuple-element.30.near_ref), channel_id=1, source_target_pairs={{0,8},{8,0},{16,24},{24,16},{1,9},{9,1},{17,25},{25,17},{2,10},{10... | collective-permute-start | bytes 1824776 | tf_op jit(solution)/shard_map/ppermute | solution.py:397
  21.1 21.3 %collective-permute-start.4 = (bf16[72,4224]{1,0:T(8,128)(2,1)S(1)}, bf16[72,4224]{1,0:T(8,128)(2,1)S(1)}, u32[]{:S(2)}, u32[]{:S(2)}) collective-permute-start(bf16[72,4224]{1,0:T(8,128)(2,1)S(1)} %collective-permute-done.3.near_ref), channel_id=1, source_target_pairs={{0,8},{8,0},{16,24},{24,16},{1,9},{9,1},{17,25},{25,17},{2,10},{10... | collective-permute-start | bytes 1824776 | tf_op jit(solution)/shard_map/ppermute | solution.py:397
  21.6 28.1 %collective-permute-start.1 = (bf16[72,4224]{1,0:T(8,128)(2,1)S(1)}, bf16[72,4224]{1,0:T(8,128)(2,1)S(1)}, u32[]{:S(2)}, u32[]{:S(2)}) collective-permute-start(bf16[72,4224]{1,0:T(8,128)(2,1)S(1)} %collective-permute-done.near_ref), channel_id=1, source_target_pairs={{0,8},{8,0},{16,24},{24,16},{1,9},{9,1},{17,25},{25,17},{2,10},{10... | collective-permute-start | bytes 1824776 | tf_op jit(solution)/shard_map/ppermute | solution.py:397
  34.2 23.7 %collective-permute-start.6 = (bf16[72,4224]{1,0:T(8,128)(2,1)S(1)}, bf16[72,4224]{1,0:T(8,128)(2,1)S(1)}, u32[]{:S(2)}, u32[]{:S(2)}) collective-permute-start(bf16[72,4224]{1,0:T(8,128)(2,1)S(1)} %collective-permute-done.5.near_ref), channel_id=1, source_target_pairs={{0,8},{8,0},{16,24},{24,16},{1,9},{9,1},{17,25},{25,17},{2,10},{10... | collective-permute-start | bytes 1824776 | tf_op jit(solution)/shard_map/ppermute | solution.py:397
  40.9 25.8 %collective-permute-start.8 = (bf16[144,1280]{1,0:T(8,128)(2,1)S(1)}, bf16[144,1280]{1,0:T(8,128)(2,1)S(1)}, u32[]{:S(2)}, u32[]{:S(2)}) collective-permute-start(bf16[144,1280]{1,0:T(8,128)(2,1)S(1)} %get-tuple-element.36), channel_id=1, source_target_pairs={{0,4},{4,0},{1,5},{5,1},{2,6},{6,2},{3,7},{7,3},{8,12},{12,8},{9,1... | collective-permute-start | bytes 1105928 | tf_op jit(solution)/shard_map/ppermute | solution.py:400
  49.1 17.6 %collective-permute-start.10 = (bf16[144,1280]{1,0:T(8,128)(2,1)S(1)}, bf16[144,1280]{1,0:T(8,128)(2,1)S(1)}, u32[]{:S(2)}, u32[]{:S(2)}) collective-permute-start(bf16[144,1280]{1,0:T(8,128)(2,1)S(1)} %get-tuple-element.38), channel_id=1, source_target_pairs={{0,4},{4,0},{1,5},{5,1},{2,6},{6,2},{3,7},{7,3},{8,12},{12,8},{9,1... | collective-permute-start | bytes 1105928 | tf_op jit(solution)/shard_map/ppermute | solution.py:400
  56.4 12.1 %collective-permute-start.7 = (bf16[144,1280]{1,0:T(8,128)(2,1)S(1)}, bf16[144,1280]{1,0:T(8,128)(2,1)S(1)}, u32[]{:S(2)}, u32[]{:S(2)}) collective-permute-start(bf16[144,1280]{1,0:T(8,128)(2,1)S(1)} %get-tuple-element.35), channel_id=1, source_target_pairs={{0,4},{4,0},{1,5},{5,1},{2,6},{6,2},{3,7},{7,3},{8,12},{12,8},{9,1... | collective-permute-start | bytes 1105928 | tf_op jit(solution)/shard_map/ppermute | solution.py:400
  64.6 5.5 %collective-permute-start.11 = (bf16[144,256]{1,0:T(8,128)(2,1)S(1)}, bf16[144,256]{1,0:T(8,128)(2,1)S(1)}, u32[]{:S(2)}, u32[]{:S(2)}) collective-permute-start(bf16[144,256]{1,0:T(8,128)(2,1)S(1)} %get-tuple-element.43), channel_id=1, source_target_pairs={{0,4},{4,0},{1,5},{5,1},{2,6},{6,2},{3,7},{7,3},{8,12},{12,8},{9,1... | collective-permute-start | bytes 221192 | tf_op jit(solution)/shard_map/ppermute | solution.py:400
  65.3 20.3 %collective-permute-start.9 = (bf16[144,1024]{1,0:T(8,128)(2,1)S(1)}, bf16[144,1024]{1,0:T(8,128)(2,1)S(1)}, u32[]{:S(2)}, u32[]{:S(2)}) collective-permute-start(bf16[144,1024]{1,0:T(8,128)(2,1)S(1)} %get-tuple-element.37), channel_id=1, source_target_pairs={{0,4},{4,0},{1,5},{5,1},{2,6},{6,2},{3,7},{7,3},{8,12},{12,8},{9,1... | collective-permute-start | bytes 884744 | tf_op jit(solution)/shard_map/ppermute | solution.py:400
  70.8 14.8 %collective-permute-start.12 = (bf16[576,128]{1,0:T(8,128)(2,1)S(1)}, bf16[576,128]{1,0:T(8,128)(2,1)S(1)}, u32[]{:S(2)}, u32[]{:S(2)}) collective-permute-start(bf16[576,128]{1,0:T(8,128)(2,1)S(1)} %get-tuple-element.45), channel_id=1, source_target_pairs={{0,1},{2,0},{1,3},{3,2},{4,5},{6,4},{5,7},{7,6},{8,9},{10,8},{9,11... | collective-permute-start | bytes 442376 | tf_op jit(solution)/shard_map/ppermute | solution.py:427
  72.4 13.2 %collective-permute-start.13 = (bf16[576,128]{1,0:T(8,128)(2,1)S(1)}, bf16[576,128]{1,0:T(8,128)(2,1)S(1)}, u32[]{:S(2)}, u32[]{:S(2)}) collective-permute-start(bf16[576,128]{1,0:T(8,128)(2,1)S(1)} %get-tuple-element.46), channel_id=1, source_target_pairs={{2,1},{1,2},{6,5},{5,6},{10,9},{9,10},{14,13},{13,14},{18,17},{17,... | collective-permute-start | bytes 442376 | tf_op jit(solution)/shard_map/ppermute | solution.py:428
  73.1 12.5 %copy-start = (bf16[1,2048]{1,0:T(2,128)(2,1)S(1)}, bf16[1,2048]{1,0:T(2,128)(2,1)}, u32[]{:S(2)}) copy-start(bf16[1,2048]{1,0:T(2,128)(2,1)} %refs_7_.1) | copy-start | bytes 12292

commit v2 on v1

--- a/solution.py
+++ b/solution.py
@@ -1,3 +1,4 @@
+import functools
 import math
 
 import jax
@@ -96,16 +97,19 @@
     )(ids, lengths, rows, send)
 
 
-def chunk_kernel(ids_ref, near_ref, far_ref, gain_hbm, keyval_hbm, query_hbm, head_hbm,
-                 rows_ref, own_ref, direct_ref, tail_ref, *refs):
-    sends, (gain_ref, keyval_ref, query_ref, head_ref, sems) = refs[:-5], refs[-5:]
-    send_ref = sends[0]
-    count = near_ref.shape[0]
+def chunk_kernel(ids_ref, *refs, chips, sends):
+    pieces, refs = refs[:2 * chips], refs[2 * chips:]
+    gain_hbm, keyval_hbm, query_hbm, head_hbm = refs[:4]
+    rows_ref, own_ref, direct_ref, tail_ref = refs[4:8]
+    send_refs = refs[8:8 + sends]
+    gain_ref, keyval_ref, query_ref, head_ref, sems = refs[8 + sends:]
+    count = pieces[0].shape[0]
     half = rows_ref.shape[1]
     blocks, _, block = query_ref.shape
     core, segment, tp = ids_ref[0], ids_ref[1], ids_ref[3]
     columns = blocks * block
-    gain_copy = pltpu.make_async_copy(gain_hbm.at[:, pl.ds(pl.multiple_of(segment * half, half), half)], gain_ref, sems.at[0])
+    gain_copy = pltpu.make_async_copy(
+        gain_hbm.at[:, pl.ds(pl.multiple_of(segment * half, half), half)], gain_ref, sems.at[0])
     head_copy = pltpu.make_async_copy(head_hbm, head_ref, sems.at[1])
     keyval_copy = pltpu.make_async_copy(keyval_hbm, keyval_ref, sems.at[2])
     gain_copy.start()
@@ -114,31 +118,31 @@
     query_copies = []
     for index in range(blocks):
         at = pl.multiple_of((1 - segment) * columns + index * block, block)
-        query_copies.append(pltpu.make_async_copy(query_hbm.at[:, pl.ds(at, block)], query_ref.at[index], sems.at[3 + index]))
+        query_copies.append(pltpu.make_async_copy(
+            query_hbm.at[:, pl.ds(at, block)], query_ref.at[index], sems.at[3 + index]))
         query_copies[-1].start()
 
     top = (iota((count, 1), 0) < count // 2).astype(jnp.int32)
     mask = (top ^ core) == 1
 
-    def both(near, far):
-        return jnp.concatenate([jnp.where(mask, near, far), jnp.where(mask, far, near)], axis=0)
+    def sorted_rows(values):
+        near, far = values[0::2], values[1::2]
+        return jnp.concatenate(
+            [part for n, f in zip(near, far) for part in (jnp.where(mask, n, f), jnp.where(mask, f, n))], axis=0)
 
     first_lanes = iota((count, LANES), 1) < 3
-
-    def scale_of(ref):
-        return jnp.sum(jnp.where(first_lanes, ref[:, half:].astype(F32), 0.0), axis=1, keepdims=True)
-
-    scale = both(scale_of(near_ref), scale_of(far_ref))
+    scale = sorted_rows([
+        jnp.sum(jnp.where(first_lanes, ref[:, half:].astype(F32), 0.0), axis=1, keepdims=True) for ref in pieces])
     slice_width = head_ref.shape[1]
     holder = (tp * slice_width) // half == segment
     first = (tp * slice_width) % half
     chunk = 512
-    direct = jnp.zeros((2 * count, LANES), F32)
+    direct = jnp.zeros((2 * chips * count, LANES), F32)
     gain_copy.wait()
     head_copy.wait()
     for start in range(0, half, chunk):
         at = slice(start, start + chunk)
-        rows = both(near_ref[:, at].astype(F32), far_ref[:, at].astype(F32))
+        rows = sorted_rows([ref[:, at].astype(F32) for ref in pieces])
         inside = jnp.logical_and(holder, jnp.logical_and(start >= first, start < first + slice_width))
         offset = pl.multiple_of(jnp.where(inside, start - first, 0), chunk)
         weight = jnp.where(inside, head_ref[:, pl.ds(offset, chunk)].astype(F32), 0.0)
@@ -146,7 +150,7 @@
             direct = direct + rows[:, lane:lane + LANES] * weight[:, lane:lane + LANES]
         rows_ref[:, at] = (rows * scale * gain_ref[:, at].astype(F32)).astype(BF16)
     direct_ref[...] = direct
-    tail_ref[...] = near_ref[:, half:].astype(F32)[:8]
+    tail_ref[...] = pieces[0][:, half:].astype(F32)[:8]
 
     keyval_copy.wait()
     keyval = jnp.dot(rows_ref[...], keyval_ref[...], preferred_element_type=F32)
@@ -154,33 +158,34 @@
     odd = jnp.concatenate([keyval[:, HEAD:2 * HEAD], keyval[:, 3 * HEAD:]], axis=1)
     own_ref[...] = jnp.where(segment == 0, even, odd)
     other = jnp.where(segment == 0, odd, even).astype(BF16)
-    if len(sends) == 1:
-        send_ref[:, columns:] = other
+    if sends == 1:
+        send_refs[0][:, columns:] = other
     else:
-        sends[1][...] = other
+        send_refs[1][...] = other
     for index in range(blocks):
         query_copies[index].wait()
-        send_ref[:, index * block:(index + 1) * block] = jnp.dot(
+        send_refs[0][:, index * block:(index + 1) * block] = jnp.dot(
             rows_ref[...], query_ref[index], preferred_element_type=F32).astype(BF16)
 
 
-def multiply_chunk(ids, near, far, gain, keyval, query, head, split):
-    count, wide = near.shape
+def multiply_chunk(ids, pieces, gain, keyval, query, head, split):
+    count, wide = pieces[0].shape
     half = wide - LANES
     columns = query.shape[1] // 2
     block = 256
     blocks = columns // block
-    rows = 2 * count
+    chips = len(pieces) // 2
+    rows = 2 * chips * count
     widths = (columns, 2 * HEAD) if split else (columns + 2 * HEAD,)
     return pl.pallas_call(
-        chunk_kernel,
+        functools.partial(chunk_kernel, chips=chips, sends=len(widths)),
         out_shape=(
             jax.ShapeDtypeStruct((rows, half), BF16),
             jax.ShapeDtypeStruct((rows, 2 * HEAD), F32),
             jax.ShapeDtypeStruct((rows, LANES), F32),
             jax.ShapeDtypeStruct((8, LANES), F32),
         ) + tuple(jax.ShapeDtypeStruct((rows, width), BF16) for width in widths),
-        in_specs=[whole(pltpu.SMEM), whole(), whole()] + [whole(pltpu.HBM)] * 4,
+        in_specs=[whole(pltpu.SMEM)] + [whole()] * len(pieces) + [whole(pltpu.HBM)] * 4,
         out_specs=(whole(),) * (4 + len(widths)),
         scratch_shapes=[
             pltpu.VMEM((1, half), BF16),
@@ -189,15 +194,15 @@
             pltpu.VMEM(head.shape, BF16),
             pltpu.SemaphoreType.DMA((3 + blocks,)),
         ],
-        compiler_params=pltpu.CompilerParams(vmem_limit_bytes=28 << 20),
+        compiler_params=pltpu.CompilerParams(vmem_limit_bytes=32 << 20),
         cost_estimate=pl.CostEstimate(
             flops=2 * rows * half * (columns + keyval.shape[1]), transcendentals=0,
             bytes_accessed=2 * half * (columns + keyval.shape[1])),
         name="chunk",
-    )(ids, near, far, gain, keyval, query, head)
-
-
-def own_kernel(ids_ref, a_ref, b_ref, c_ref, d_ref, query_hbm, out_ref, rows_ref, query_ref, sems):
+    )(ids, *pieces, gain, keyval, query, head)
+
+
+def own_kernel(ids_ref, rows_ref, query_hbm, out_ref, query_ref, sems):
     blocks, _, block = query_ref.shape
     columns = blocks * block
     copies = []
@@ -205,35 +210,35 @@
         at = pl.multiple_of(ids_ref[1] * columns + index * block, block)
         copies.append(pltpu.make_async_copy(query_hbm.at[:, pl.ds(at, block)], query_ref.at[index], sems.at[index]))
         copies[-1].start()
-    count = a_ref.shape[0]
-    for index, ref in enumerate((a_ref, b_ref, c_ref, d_ref)):
-        rows_ref[index * count:(index + 1) * count, :] = ref[...]
     for index in range(blocks):
         copies[index].wait()
         out_ref[:, index * block:(index + 1) * block] = jnp.dot(
             rows_ref[...], query_ref[index], preferred_element_type=F32)
 
 
-def own_queries(ids, chunks, query):
-    count, half = chunks[0].shape
+def own_queries(ids, rows, query):
+    count, half = rows.shape
     columns = query.shape[1] // 2
     block = 256
     blocks = columns // block
     return pl.pallas_call(
         own_kernel,
-        out_shape=jax.ShapeDtypeStruct((4 * count, columns), F32),
-        in_specs=[whole(pltpu.SMEM)] + [whole()] * 4 + [whole(pltpu.HBM)],
+        out_shape=jax.ShapeDtypeStruct((count, columns), F32),
+        in_specs=[whole(pltpu.SMEM), whole(), whole(pltpu.HBM)],
         out_specs=whole(),
         scratch_shapes=[
-            pltpu.VMEM((4 * count, half), BF16),
             pltpu.VMEM((blocks, half, block), BF16),
             pltpu.SemaphoreType.DMA((blocks,)),
         ],
-        compiler_params=pltpu.CompilerParams(vmem_limit_bytes=32 << 20),
+        compiler_params=pltpu.CompilerParams(vmem_limit_bytes=20 << 20),
         cost_estimate=pl.CostEstimate(
-            flops=8 * count * half * columns, transcendentals=0, bytes_accessed=2 * half * columns),
+            flops=2 * count * half * columns, transcendentals=0, bytes_accessed=2 * half * columns),
         name="own_queries",
-    )(ids, *chunks, query)
+    )(ids, rows, query)
+
+
+def slabs(refs, starts, count, at=slice(None)):
+    return [ref[start:start + count, at].astype(F32) for ref, start in zip(refs, starts)]
 
 
 def by_pack(parts, pack):
@@ -241,28 +246,29 @@
     return jnp.concatenate([part[pack * count:(pack + 1) * count] for part in parts], axis=0)
 
 
-def keyval_kernel(ids_ref, *refs):
-    owns, recvs = refs[:4], refs[4:8]
-    keep_ref, first_ref, second_ref = refs[8:]
+def keyval_kernel(ids_ref, *refs, starts, recv_starts):
+    chips = len(starts)
+    owns, recvs = refs[:chips], refs[chips:2 * chips]
+    keep_ref, first_ref, second_ref = refs[2 * chips:]
     tp = ids_ref[3]
-    sums = [own[...] + recv[:, recv.shape[1] - 2 * HEAD:].astype(F32) for own, recv in zip(owns, recvs)]
-    rows = 2 * owns[0].shape[0]
-    for pack in range(2):
-        at = slice(pack * rows, (pack + 1) * rows)
-        part = by_pack(sums, pack)
-        low, high = part[:, :HEAD], part[:, HEAD:]
-        keep_ref[at, :] = jnp.where(tp == 3, high, low).astype(BF16)
-        first_ref[at, :] = jnp.where(tp < 2, high, low).astype(BF16)
-        second_ref[at, :] = jnp.where(tp == 2, high, low).astype(BF16)
-
-
-def sum_keyval(ids, owns, recvs):
-    rows = 4 * owns[0].shape[0]
-    shape = jax.ShapeDtypeStruct((rows, HEAD), BF16)
+    count = keep_ref.shape[0] // chips
+    mine = slabs(owns, starts, count)
+    theirs = [slabs((ref,), (start,), count, slice(ref.shape[1] - 2 * HEAD, ref.shape[1]))[0]
+              for ref, start in zip(recvs, recv_starts)]
+    sums = [own + recv for own, recv in zip(mine, theirs)]
+    both = jnp.concatenate([by_pack(sums, pack) for pack in range(2)], axis=0)
+    low, high = both[:, :HEAD], both[:, HEAD:]
+    keep_ref[...] = jnp.where(tp == 3, high, low).astype(BF16)
+    first_ref[...] = jnp.where(tp < 2, high, low).astype(BF16)
+    second_ref[...] = jnp.where(tp == 2, high, low).astype(BF16)
+
+
+def sum_keyval(ids, owns, starts, recvs, recv_starts, count):
+    shape = jax.ShapeDtypeStruct((len(owns) * count, HEAD), BF16)
     return pl.pallas_call(
-        keyval_kernel,
+        functools.partial(keyval_kernel, starts=starts, recv_starts=recv_starts),
         out_shape=(shape, shape, shape),
-        in_specs=[whole(pltpu.SMEM)] + [whole()] * 8,
+        in_specs=[whole(pltpu.SMEM)] + [whole()] * (2 * len(owns)),
         out_specs=(whole(),) * 3,
         compiler_params=pltpu.CompilerParams(vmem_limit_bytes=8 << 20),
         name="sum_keyval",
@@ -273,27 +279,38 @@
     index = jnp.zeros_like(row)
     for step in range(1, 8):
         index = index + (row >= step * piece_rows).astype(jnp.int32)
-    chip, low = index >> 1, index & 1
+    slot, low = index >> 1, index & 1
+    chip = slot ^ (slot >> 1)
     shard = (((chip >> 1) ^ ids_ref[2]) * 2 + (low ^ pack)) * 2 + ((chip & 1) ^ ids_ref[1])
     return shard, row - index * piece_rows
 
 
-def attention_kernel(ids_ref, lengths_ref, tail_ref, own_ref, *refs):
-    recvs, (keep_ref, first_ref, second_ref, gain_ref), directs = refs[:4], refs[4:8], refs[8:12]
-    out_ref, bias_ref, value_ref = refs[12:]
+def attention_kernel(ids_ref, lengths_ref, tail_ref, *refs, slot, starts, recv_starts, more):
+    chips = len(starts)
+    owns, recvs, directs = (refs[index * chips:(index + 1) * chips] for index in range(3))
+    refs = refs[3 * chips:]
+    firsts, lates, gain_ref = refs[0:3], refs[3:6], refs[6]
+    before_ref = refs[7] if more else None
+    out_ref, bias_ref = refs[7 + more:]
     segment, tp = ids_ref[1], ids_ref[3]
-    count = recvs[0].shape[0]
-    rows = 2 * count
+    rows = bias_ref.shape[1]
+    slab = rows // 2
+    queries = bias_ref.shape[0]
+    base = slot * (slab // 2)
     piece_rows = rows // 8
-    heads = own_ref.shape[1] // HEAD
+    heads = owns[0].shape[1] // HEAD
     devices = out_ref.shape[0]
     wide = out_ref.shape[1] // 2
     scale = math.log2(math.e) / math.sqrt(HEAD)
     tail = tail_ref[:1, :].astype(jnp.int32)
-    lane = iota((rows, wide), 1)
-    keys_all = jnp.where(tp == 0, keep_ref[...], jnp.where(tp == 2, second_ref[...], first_ref[...]))
-    value_ref[:, :HEAD] = jnp.where(tp == 3, keep_ref[...], jnp.where(tp == 1, second_ref[...], first_ref[...]))
-    value_ref[:, HEAD:] = jnp.ones((2 * rows, HEAD), BF16)
+    lane = iota((queries, wide), 1)
+
+    def chosen_keys(refs):
+        keep, first, second = (ref[...].astype(F32) for ref in refs)
+        return (jnp.where(tp == 0, keep, jnp.where(tp == 2, second, first)),
+                jnp.where(tp == 3, keep, jnp.where(tp == 1, second, first)))
+
+    early, late = chosen_keys(firsts), chosen_keys(lates)
     through = jnp.zeros((devices, wide), F32)
     direct = jnp.zeros((devices, wide), F32)
     for pack in range(2):
@@ -308,26 +325,30 @@
                 doc = doc + (position >= end).astype(jnp.int32)
             return position, doc
 
-        row_position, row_doc = place(iota((rows, 1), 0))
+        row_position, row_doc = place(iota((queries, 1), 0) + base)
         col_position, col_doc = place(iota((1, rows), 1))
         visible = jnp.logical_and(row_doc == col_doc, col_position <= row_position)
         bias_ref[...] = jnp.where(visible, 0.0, -1e30)
-        keys = keys_all[pack * rows:(pack + 1) * rows]
-        total = jnp.zeros((rows, HEAD), F32)
+        keys, values = (
+            jnp.concatenate([part[pack * (part.shape[0] // 2):(pack + 1) * (part.shape[0] // 2)]
+                             for part in parts], axis=0).astype(BF16)
+            for parts in zip(early, late))
+        values = jnp.concatenate([values, jnp.ones((rows, HEAD), BF16)], axis=1)
+        total = jnp.zeros((queries, HEAD), F32)
         for head in range(heads):
             at = slice(head * HEAD, (head + 1) * HEAD)
-            parts = [own_ref[index * count:(index + 1) * count, at] + recv[:, at].astype(F32)
-                     for index, recv in enumerate(recvs)]
+            parts = [own + recv for own, recv in zip(
+                slabs(owns, starts, slab, at), slabs(recvs, recv_starts, slab, at))]
             query = (by_pack(parts, pack) * scale).astype(BF16)
             logits = lax.dot_general(query, keys, (((1,), (1,)), ((), ())), preferred_element_type=F32)
             logits = logits + bias_ref[...]
             expo = jnp.exp2(logits - jnp.max(logits, axis=1, keepdims=True)).astype(BF16)
-            both = jnp.dot(expo, value_ref[pack * rows:(pack + 1) * rows, :], preferred_element_type=F32)
+            both = jnp.dot(expo, values, preferred_element_type=F32)
             offset = pl.multiple_of(segment * heads * HEAD + head * HEAD, HEAD)
             total = total + both[:, :HEAD] / both[:, HEAD:] * gain_ref[:, pl.ds(offset, HEAD)].astype(F32)
 
-        _, inner = owner_of(iota((rows, 1), 0), pack, ids_ref, piece_rows)
-        shard_row, _ = owner_of(iota((1, rows), 1), pack, ids_ref, piece_rows)
+        _, inner = owner_of(iota((queries, 1), 0) + base, pack, ids_ref, piece_rows)
+        shard_row, _ = owner_of(iota((1, queries), 1) + base, pack, ids_ref, piece_rows)
         chosen = ((iota((devices, 1), 0) >> 2) == shard_row).astype(F32)
         hit = lane == inner + pack * piece_rows
 
@@ -335,25 +356,28 @@
             return jnp.dot(chosen, jnp.where(hit, column, 0.0), precision=HIGHEST, preferred_element_type=F32)
 
         through = through + send(jnp.sum(total, axis=1, keepdims=True))
-        direct = direct + send(jnp.sum(by_pack([ref[...] for ref in directs], pack), axis=1, keepdims=True))
+        direct = direct + send(jnp.sum(by_pack(slabs(directs, starts, slab), pack), axis=1, keepdims=True))
+    if more:
+        through = through + before_ref[:, :wide]
+        direct = direct + before_ref[:, wide:]
     out_ref[:, :wide] = through
     out_ref[:, wide:] = direct
 
 
-def attention(ids, lengths, tail, own, recvs, keep, first, second, gain, directs, devices):
-    rows = own.shape[0] // 2
+def attention(ids, lengths, tail, owns, starts, recvs, recv_starts, directs, firsts, lates, gain, devices,
+              slot, before):
+    rows = firsts[0].shape[0] // 2 + lates[0].shape[0] // 2
+    queries = len(owns) * (rows // 4)
     return pl.pallas_call(
-        attention_kernel,
+        functools.partial(
+            attention_kernel, slot=slot, starts=starts, recv_starts=recv_starts, more=len(before)),
         out_shape=jax.ShapeDtypeStruct((devices, 2 * LANES), F32),
-        in_specs=[whole(pltpu.SMEM), whole(pltpu.SMEM)] + [whole()] * 14,
+        in_specs=[whole(pltpu.SMEM), whole(pltpu.SMEM)] + [whole()] * (8 + 3 * len(owns) + len(before)),
         out_specs=whole(),
-        scratch_shapes=[
-            pltpu.VMEM((rows, rows), F32),
-            pltpu.VMEM((2 * rows, 2 * HEAD), BF16),
-        ],
-        compiler_params=pltpu.CompilerParams(vmem_limit_bytes=28 << 20),
+        scratch_shapes=[pltpu.VMEM((queries, rows), F32)],
+        compiler_params=pltpu.CompilerParams(vmem_limit_bytes=24 << 20),
         name="attend",
-    )(ids, lengths, tail, own, *recvs, keep, first, second, gain, *directs)
+    )(ids, lengths, tail, *owns, *recvs, *directs, *firsts, *lates, gain, *before)
 
 
 def finish_kernel(recv_ref, send_ref, out_ref):
@@ -402,6 +426,7 @@
     def in_hbm(array):
         return pltpu.with_memory_space_constraint(array, pltpu.HBM)
 
+    packing = send
     rollout, send, attn_gain, head_weight, seq_lengths = map(
         in_hbm, (rollout, send, attn_gain, head_weight, seq_lengths))
     wq, wkv = in_hbm(w_query[0]), in_hbm(w_keyval[0])
@@ -410,29 +435,41 @@
     from_y = lax.ppermute(mine, "branch", y_pairs)
     from_d = lax.ppermute(from_x, "branch", y_pairs)
 
-    rows, owns, directs, tails, received = [], [], [], [], []
-    for name, piece in (("own", mine), ("x", from_x), ("y", from_y), ("d", from_d)):
-        far = swap(piece)
-        row, own, direct, tail, *sends = multiply_chunk(
-            ids, piece, far, attn_gain, wkv, wq, head_weight, name == "d")
+    slab = 2 * mine.shape[0]
+    local, direct, query, received = {}, {}, {}, {}
+    for name, pieces in (("own", (mine,)), ("xy", (from_x, from_y)), ("d", (from_d,))):
+        pieces = [part for piece in pieces for part in (piece, swap(piece))]
+        rows, local[name], direct[name], lengths, *sends = multiply_chunk(
+            ids, pieces, attn_gain, wkv, wq, head_weight, name != "own")
+        if name == "xy":
+            tail = lengths
         for index, part in reversed(list(enumerate(sends))):
             sends[index] = across(part)
-        rows.append(row)
-        owns.append(own)
-        directs.append(direct)
-        tails.append(tail)
-        received.append(sends)
-    order = (1, 0, 3, 2)
-    keep, first, second = sum_keyval(ids, owns, [received[index][-1] for index in order])
-    first = lax.ppermute(first, "tp", [(0, 1), (2, 0), (1, 3), (3, 2)])
-    second = lax.ppermute(second, "tp", [(2, 1), (1, 2)])
-    own = own_queries(ids, rows, wq)
+        received[name] = sends
+        query[name] = own_queries(ids, rows, wq)
+
+    keep, first, second = sum_keyval(
+        ids, [local["own"], local["xy"], local["d"]], (0, 0, 0),
+        [received["xy"][1], received["own"][0], received["xy"][1]], (0, 0, slab), slab)
+    hand_first, hand_second = [(0, 1), (2, 0), (1, 3), (3, 2)], [(2, 1), (1, 2)]
+    first = lax.ppermute(first, "tp", hand_first)
+    second = lax.ppermute(second, "tp", hand_second)
+    early = (keep, first, second)
+    keep, first, second = sum_keyval(
+        ids, [local["xy"]], (slab,), [received["d"][1]], (0,), slab)
+    first = lax.ppermute(first, "tp", hand_first)
+    second = lax.ppermute(second, "tp", hand_second)
+    late = (keep, first, second)
     devices = n_branch * 2 * lax.axis_size("tp")
     outgoing = attention(
-        ids, seq_lengths, tails[1], own, [received[index][0] for index in order],
-        keep, first, second, head_attn, directs, devices)
+        ids, seq_lengths, tail, [query["own"], query["xy"], query["d"]], (0, 0, 0),
+        [received["xy"][0], received["own"][0], received["xy"][0]], (0, 0, slab),
+        [direct["own"], direct["xy"], direct["d"]], early, late, head_attn, devices, 0, [])
+    outgoing = attention(
+        ids, seq_lengths, tail, [query["xy"]], (slab,), [received["d"][0]], (0,),
+        [direct["xy"]], early, late, head_attn, devices, 3, [outgoing])
     incoming = lax.all_to_all(outgoing, ALL_AXES, split_axis=0, concat_axis=0, tiled=True)
-    return finish(incoming, send, n_branch)
+    return finish(incoming, packing, n_branch)
 
 
 def general(rollout, send_rows, seq_lengths, attn_gain, w_query, w_keyval, head_weight, head_attn):

time: 107 us -> 111 us (1.037)
  Pallas kernels: 49.4 us -> 54.2 us
  starting transfers between devices: 14.9 us -> 19.7 us
  waiting for transfers between devices: 28.2 us -> 24.8 us
  blocking collectives: 14.2 us -> 11.8 us
    pallas_call x7 -> x10, Pallas kernels: 45.3 us -> 50.8 us  [the longest x3 23.3 us: multiply_chunk(): pl.pallas_call(functools.partial(chunk_kernel, chips=chips, sends=len(wid...]
    ppermute x2 -> x4, starting transfers between devices: 2.29 us -> 7.07 us  [the longest x2 5.54 us: paired(): first = lax.ppermute(first, 'tp', hand_first)]
    ppermute x6, waiting for transfers between devices: 15.6 us -> 12.2 us  [across(): return lax.ppermute(part, 'segment', x_pairs)]
    all_to_all x1, blocking collectives: 14.2 us -> 11.8 us  [paired(): lax.all_to_all(outgoing, ALL_AXES, split_axis=0, concat_axis=0, tiled=True)]
  transfers between devices with their start and end apart: 14 -> 16, of which waited for: 4 -> 2; matrix products, arithmetic and copies ran while one was open for 0% -> 0% of each run, Pallas kernels for 37% -> 43%
where the time goes in v2:
time: 111 us
  Pallas kernels  54.2 us (49%)
  waiting for transfers between devices  24.8 us (22%)
  starting transfers between devices  19.7 us (18%)
  blocking collectives  11.8 us (11%)
    pallas_call x3, Pallas kernels, multiply_chunk(): pl.pallas_call(functools.partial(chunk_kernel, chips=chips, sends=len(wid...  23.3 us
    pallas_call x3, Pallas kernels, own_queries(): pl.pallas_call(own_kernel, out_shape=jax.ShapeDtypeStruct((count, columns...  18.2 us
    ppermute x1, waiting for transfers between devices, paired(): from_d = lax.ppermute(from_x, 'branch', y_pairs)  12.6 us
    ppermute x6, waiting for transfers between devices, across(): return lax.ppermute(part, 'segment', x_pairs)  12.2 us
    all_to_all x1, blocking collectives, paired(): lax.all_to_all(outgoing, ALL_AXES, split_axis=0, concat_axis=0, tiled=True)  11.8 us
    ppermute x6, starting transfers between devices, across(): return lax.ppermute(part, 'segment', x_pairs)  8.8 us
    pallas_call x2, Pallas kernels, attention(): pl.pallas_call(functools.partial(attention_kernel, slot=slot, starts=star...  8.08 us
    ppermute x2, starting transfers between devices, paired(): first = lax.ppermute(first, 'tp', hand_first)  5.54 us
  transfers between devices with their start and end apart: 16, of which 2 were waited for; matrix products, arithmetic and copies ran while one was open for 0% of the time, Pallas kernels for 43%

profile of v2, /device:TPU:0, one launch (start us, length us, event | category | flops | bytes accessed | tf_op | source)
XLA Modules:
  0.0 110.9 jit_solution(11953642961010115981)
XLA Ops:
  0.0 0.1 pad_add_fusion.ids_ref
  0.1 2.5 %prepare.1 = (bf16[72,4224]{1,0:T(8,128)(2,1)S(1)}, bf16[72,4224]{1,0:T(8,128)(2,1)S(1)}) custom-call(s32[4]{0:T(128)S(1)} %pad_add_fusion.ids_ref, s32[1,6]{1,0:T(1,128)} %lengths_ref.5, bf16[72,8192]{1,0:T(8,128)(2,1)} %rows_hbm.1, s32[1,72]{1,0:T(1,128)} %bitcast.13), custom_call_target="tpu_custom_call" | custom-call | tf_op jit(solution)/shard_map/prepare/pallas_call | solution.py:85
  2.6 3.0 %collective-permute-start = (bf16[72,4224]{1,0:T(8,128)(2,1)S(1)}, bf16[72,4224]{1,0:T(8,128)(2,1)S(1)}, u32[]{:S(2)}, u32[]{:S(2)}) collective-permute-start(bf16[72,4224]{1,0:T(8,128)(2,1)S(1)} %get-tuple-element.28), channel_id=1, source_target_pairs={{0,4},{4,0},{1,5},{5,1},{2,6},{6,2},{3,7},{7,3},{8,12},{12,8},{9,1... | collective-permute-start | bytes 1824776 | tf_op jit(solution)/shard_map/ppermute | solution.py:424
  5.6 1.5 %collective-permute-start.2 = (bf16[72,4224]{1,0:T(8,128)(2,1)S(1)}, bf16[72,4224]{1,0:T(8,128)(2,1)S(1)}, u32[]{:S(2)}, u32[]{:S(2)}) collective-permute-start(bf16[72,4224]{1,0:T(8,128)(2,1)S(1)} %get-tuple-element.29.refs_0_), channel_id=1, source_target_pairs={{0,16},{8,24},{16,0},{24,8},{1,17},{9,25},{17,1},{25,9},{2,18},{10... | collective-permute-start | bytes 1824776 | tf_op jit(solution)/shard_map/ppermute | solution.py:435
  7.2 12.2 %collective-permute-done.refs_0_ = bf16[72,4224]{1,0:T(8,128)(2,1)S(1)} collective-permute-done((bf16[72,4224]{1,0:T(8,128)(2,1)S(1)}, bf16[72,4224]{1,0:T(8,128)(2,1)S(1)}, u32[]{:S(2)}, u32[]{:S(2)}) %collective-permute-start) | collective-permute-done | bytes 608288 | tf_op jit(solution)/shard_map/ppermute | solution.py:424
  19.4 1.8 %collective-permute-start.4 = (bf16[72,4224]{1,0:T(8,128)(2,1)S(1)}, bf16[72,4224]{1,0:T(8,128)(2,1)S(1)}, u32[]{:S(2)}, u32[]{:S(2)}) collective-permute-start(bf16[72,4224]{1,0:T(8,128)(2,1)S(1)} %collective-permute-done.refs_0_), channel_id=1, source_target_pairs={{0,16},{8,24},{16,0},{24,8},{1,17},{9,25},{17,1},{25,9},{2,18},{10... | collective-permute-start | bytes 1824776 | tf_op jit(solution)/shard_map/ppermute | solution.py:436
  21.1 0.0 collective-permute-start.1
  21.1 0.0 collective-permute-done.2.refs_2_
  21.1 0.5 collective-permute-start.3
  21.6 0.0 collective-permute-start.7
  21.7 12.6 %collective-permute-done.4.refs_0_ = bf16[72,4224]{1,0:T(8,128)(2,1)S(1)} collective-permute-done((bf16[72,4224]{1,0:T(8,128)(2,1)S(1)}, bf16[72,4224]{1,0:T(8,128)(2,1)S(1)}, u32[]{:S(2)}, u32[]{:S(2)}) %collective-permute-start.4) | collective-permute-done | bytes 608288 | tf_op jit(solution)/shard_map/ppermute | solution.py:436
  34.2 0.0 collective-permute-start.5
  34.2 0.0 collective-permute-done.1.refs_1_
  34.3 0.0 collective-permute-done.3.refs_3_
  34.3 9.9 %chunk.3 = (bf16[288,4096]{1,0:T(8,128)(2,1)S(1)}, f32[288,256]{1,0:T(8,128)S(1)}, f32[288,128]{1,0:T(8,128)S(1)}, f32[8,128]{1,0:T(8,128)S(1)}, bf16[288,1024]{...) custom-call(s32[4]{0:T(128)S(1)} %pad_add_fusion.ids_ref, bf16[72,4224]{1,0:T(8,128)(2,1)S(1)} %collective-permute-done.refs_0_, ...), custom_call_target="tpu_custom_call" | custom-call | flops 3623878656 | bytes 12582912 | tf_op jit(solution)/shard_map/chunk/pallas_call | solution.py:180
  44.2 1.5 %collective-permute-start.15 = (bf16[288,1024]{1,0:T(8,128)(2,1)S(1)}, bf16[288,1024]{1,0:T(8,128)(2,1)S(1)}, u32[]{:S(2)}, u32[]{:S(2)}) collective-permute-start(bf16[288,1024]{1,0:T(8,128)(2,1)S(1)} %get-tuple-element.48), channel_id=1, source_target_pairs={{0,4},{4,0},{1,5},{5,1},{2,6},{6,2},{3,7},{7,3},{8,12},{12,8},{9,1... | collective-permute-start | bytes 1769480 | tf_op jit(solution)/shard_map/ppermute | solution.py:424
  45.7 0.0 collective-permute-done.7.refs_1_
  45.7 6.7 %chunk.5 = (bf16[144,4096]{1,0:T(8,128)(2,1)S(1)}, f32[144,256]{1,0:T(8,128)S(1)}, f32[144,128]{1,0:T(8,128)S(1)}, f32[8,128]{1,0:T(8,128)}, bf16[144,1280]{1,0:T(8,128)(2,1)S(1)}) custom-call(s32[4]{0:T(128)S(1)} %pad_add_fusion.ids_ref, bf16[72,4224]{1,0:T(8,128)(2,1)S(1)} %get-tuple-element.29.refs_0_, ...), custom_call_target="tpu_custom_call" | custom-call | flops 1811939328 | bytes 12582912 | tf_op jit(solution)/shard_map/chunk/pallas_call | solution.py:180
  52.4 0.6 collective-permute-start.9
  53.1 5.4 %own_queries.4.refs_0_ = f32[144,1024]{1,0:T(8,128)S(1)} custom-call(s32[4]{0:T(128)S(1)} %pad_add_fusion.ids_ref, bf16[144,4096]{1,0:T(8,128)(2,1)S(1)} %get-tuple-element.46.rows_ref, bf16[4096,2048]{1,0:T(8,128)(2,1)} %bitcast.17), custom_call_target="tpu_custom_call" | custom-call | flops 1207959552 | bytes 8388608 | tf_op jit(solution)/shard_map/own_queries/pallas_call | solution.py:224
  58.5 1.5 %collective-permute-start.8 = (bf16[288,256]{1,0:T(8,128)(2,1)S(1)}, bf16[288,256]{1,0:T(8,128)(2,1)S(1)}, u32[]{:S(2)}, u32[]{:S(2)}) collective-permute-start(bf16[288,256]{1,0:T(8,128)(2,1)S(1)} %get-tuple-element.37), channel_id=1, source_target_pairs={{0,4},{4,0},{1,5},{5,1},{2,6},{6,2},{3,7},{7,3},{8,12},{12,8},{9,1... | collective-permute-start | bytes 442376 | tf_op jit(solution)/shard_map/ppermute | solution.py:424
  60.0 0.0 collective-permute-done.5.refs_1_
  60.0 6.7 %chunk.4 = (bf16[144,4096]{1,0:T(8,128)(2,1)S(1)}, f32[144,256]{1,0:T(8,128)S(1)}, f32[144,128]{1,0:T(8,128)S(1)}, f32[8,128]{1,0:T(8,128)}, bf16[144,1024]{1,0:...) custom-call(s32[4]{0:T(128)S(1)} %pad_add_fusion.ids_ref, bf16[72,4224]{1,0:T(8,128)(2,1)S(1)} %collective-permute-done.4.refs_0_, ...), custom_call_target="tpu_custom_call" | custom-call | flops 1811939328 | bytes 12582912 | tf_op jit(solution)/shard_map/chunk/pallas_call | solution.py:180
  66.7 0.6 collective-permute-start.6
  67.3 1.5 %collective-permute-start.12 = (bf16[144,256]{1,0:T(8,128)(2,1)S(1)}, bf16[144,256]{1,0:T(8,128)(2,1)S(1)}, u32[]{:S(2)}, u32[]{:S(2)}) collective-permute-start(bf16[144,256]{1,0:T(8,128)(2,1)S(1)} %get-tuple-element.42), channel_id=1, source_target_pairs={{0,4},{4,0},{1,5},{5,1},{2,6},{6,2},{3,7},{7,3},{8,12},{12,8},{9,1... | collective-permute-start | bytes 221192 | tf_op jit(solution)/shard_map/ppermute | solution.py:424
  68.8 7.6 %own_queries.3.refs_1_.refs_0_ = f32[288,1024]{1,0:T(8,128)S(1)} custom-call(s32[4]{0:T(128)S(1)} %pad_add_fusion.ids_ref, bf16[288,4096]{1,0:T(8,128)(2,1)S(1)} %get-tuple-element.31.rows_ref, bf16[4096,2048]{1,0:T(8,128)(2,1)} %bitcast.19), custom_call_target="tpu_custom_call" | custom-call | flops 2415919104 | bytes 8388608 | tf_op jit(solution)/shard_map/own_queries/pallas_call | solution.py:224
  76.4 0.0 collective-permute-done.9.refs_4_
  76.4 0.0 collective-permute-done.8.refs_3_.refs_5_
  76.4 0.6 sum_keyval.2
  77.1 1.6 %collective-permute-start.10 = (bf16[432,128]{1,0:T(8,128)(2,1)S(1)}, bf16[432,128]{1,0:T(8,128)(2,1)S(1)}, u32[]{:S(2)}, u32[]{:S(2)}) collective-permute-start(bf16[432,128]{1,0:T(8,128)(2,1)S(1)} %get-tuple-element.40), channel_id=1, source_target_pairs={{0,1},{2,0},{1,3},{3,2},{4,5},{6,4},{5,7},{7,6},{8,9},{10,8},{9,11... | collective-permute-start | bytes 331784 | tf_op jit(solution)/shard_map/ppermute | solution.py:455
  78.7 0.7 collective-permute-start.11
  79.3 0.0 collective-permute-done.12.refs_1_
  79.4 0.6 sum_keyval.3
  79.9 3.9 %collective-permute-start.13 = (bf16[144,128]{1,0:T(8,128)(2,1)S(1)}, bf16[144,128]{1,0:T(8,128)(2,1)S(1)}, u32[]{:S(2)}, u32[]{:S(2)}) collective-permute-start(bf16[144,128]{1,0:T(8,128)(2,1)S(1)} %get-tuple-element.44), channel_id=1, source_target_pairs={{0,1},{2,0},{1,3},{3,2},{4,5},{6,4},{5,7},{7,6},{8,9},{10,8},{9,11... | collective-permute-start | bytes 110600 | tf_op jit(solution)/shard_map/ppermute | solution.py:460
  83.8 0.0 collective-permute-done.15.refs_3_.refs_5_
  83.8 0.9 collective-permute-start.14
  84.7 0.0 copy-start
  84.7 5.2 %own_queries.5.refs_2_ = f32[144,1024]{1,0:T(8,128)S(1)} custom-call(s32[4]{0:T(128)S(1)} %pad_add_fusion.ids_ref, bf16[144,4096]{1,0:T(8,128)(2,1)S(1)} %get-tuple-element.47.rows_ref, bf16[4096,2048]{1,0:T(8,128)(2,1)} %bitcast.20), custom_call_target="tpu_custom_call" | custom-call | flops 1207959552 | bytes 8388608 | tf_op jit(solution)/shard_map/own_queries/pallas_call | solution.py:224
  90.0 0.0 collective-permute-done.10.refs_10_.refs_4_
  90.0 0.0 collective-permute-done.11.refs_11_.refs_5_
  90.0 0.0 collective-permute-done.13.refs_13_.refs_7_
  90.0 0.0 collective-permute-done.14.refs_14_.refs_8_
  90.0 0.0 copy-done
  90.0 5.1 %attend.2.refs_10_ = f32[32,256]{1,0:T(8,128)S(1)} custom-call(s32[4]{0:T(128)S(1)} %pad_add_fusion.ids_ref, s32[1,6]{1,0:T(1,128)} %lengths_ref.5, f32[8,128]{1,0:T(8,128)S(1)} %get-tuple-element.30.tail_ref, f32[144,1024]{1,0:T(8,128)S(1)} %own_queries.4.refs_0_, f32[288,1024]{1,0:T(8,128)S(1)} %own_queries.3.refs_1_.refs_0_, ...), custom_call_target="tpu_custom_call" | custom-call | tf_op jit(solution)/shard_map/attend/pallas_call | solution.py:371
  95.1 0.0 copy-start.1
  95.1 0.0 collective-permute-done.6.refs_1_
  95.1 3.0 %attend.3 = f32[32,256]{1,0:T(8,128)S(1)} custom-call(s32[4]{0:T(128)S(1)} %pad_add_fusion.ids_ref, s32[1,6]{1,0:T(1,128)} %lengths_ref.5, f32[8,128]{1,0:T(8,128)S(1)} %get-tuple-element.30.tail_ref, f32[288,1024]{1,0:T(8,128)S(1)} %own_queries.3.refs_1_.refs_0_, bf16[144,1024]{1,0:T(8,128)(2,1)S(1)} %collective-permute-done.6.refs_1_, ...), custom_call_target="tpu_custom_call" | custom-call | tf_op jit(solution)/shard_map/attend/pallas_call | solution.py:371
  98.2 11.8 %all_to_all.11 = f32[32,1,256]{2,1,0:T(1,128)S(1)} all-to-all(f32[32,1,256]{2,1,0:T(1,128)S(1)} %copy.9), channel_id=1, replica_groups=mesh['branch'=4,'segment'=2,'tp'=4] {'branch','segment','tp'}, dimensions={0} | all-to-all | bytes 65536 | tf_op jit(solution)/shard_map/all_to_all | solution.py:471
  110.0 0.0 copy-done.1
  110.0 0.9 finish.1
  (2 shorter events, 0.0 us)
Async XLA Ops:
  2.6 16.8 %collective-permute-start = (bf16[72,4224]{1,0:T(8,128)(2,1)S(1)}, bf16[72,4224]{1,0:T(8,128)(2,1)S(1)}, u32[]{:S(2)}, u32[]{:S(2)}) collective-permute-start(bf16[72,4224]{1,0:T(8,128)(2,1)S(1)} %get-tuple-element.28), channel_id=1, source_target_pairs={{0,4},{4,0},{1,5},{5,1},{2,6},{6,2},{3,7},{7,3},{8,12},{12,8},{9,1... | collective-permute-start | bytes 1824776 | tf_op jit(solution)/shard_map/ppermute | solution.py:424
  5.6 15.5 %collective-permute-start.2 = (bf16[72,4224]{1,0:T(8,128)(2,1)S(1)}, bf16[72,4224]{1,0:T(8,128)(2,1)S(1)}, u32[]{:S(2)}, u32[]{:S(2)}) collective-permute-start(bf16[72,4224]{1,0:T(8,128)(2,1)S(1)} %get-tuple-element.29.refs_0_), channel_id=1, source_target_pairs={{0,16},{8,24},{16,0},{24,8},{1,17},{9,25},{17,1},{25,9},{2,18},{10... | collective-permute-start | bytes 1824776 | tf_op jit(solution)/shard_map/ppermute | solution.py:435
  19.4 14.9 %collective-permute-start.4 = (bf16[72,4224]{1,0:T(8,128)(2,1)S(1)}, bf16[72,4224]{1,0:T(8,128)(2,1)S(1)}, u32[]{:S(2)}, u32[]{:S(2)}) collective-permute-start(bf16[72,4224]{1,0:T(8,128)(2,1)S(1)} %collective-permute-done.refs_0_), channel_id=1, source_target_pairs={{0,16},{8,24},{16,0},{24,8},{1,17},{9,25},{17,1},{25,9},{2,18},{10... | collective-permute-start | bytes 1824776 | tf_op jit(solution)/shard_map/ppermute | solution.py:436
  21.1 13.1 %collective-permute-start.1 = (bf16[72,4224]{1,0:T(8,128)(2,1)S(1)}, bf16[72,4224]{1,0:T(8,128)(2,1)S(1)}, u32[]{:S(2)}, u32[]{:S(2)}) collective-permute-start(bf16[72,4224]{1,0:T(8,128)(2,1)S(1)} %collective-permute-done.refs_0_), channel_id=1, source_target_pairs={{0,8},{8,0},{16,24},{24,16},{1,9},{9,1},{17,25},{25,17},{2,10},{10... | collective-permute-start | bytes 1824776 | tf_op jit(solution)/shard_map/ppermute | solution.py:421
  21.1 13.1 %collective-permute-start.3 = (bf16[72,4224]{1,0:T(8,128)(2,1)S(1)}, bf16[72,4224]{1,0:T(8,128)(2,1)S(1)}, u32[]{:S(2)}, u32[]{:S(2)}) collective-permute-start(bf16[72,4224]{1,0:T(8,128)(2,1)S(1)} %collective-permute-done.2.refs_2_), channel_id=1, source_target_pairs={{0,8},{8,0},{16,24},{24,16},{1,9},{9,1},{17,25},{25,17},{2,10},{10... | collective-permute-start | bytes 1824776 | tf_op jit(solution)/shard_map/ppermute | solution.py:421
  21.6 24.1 %collective-permute-start.7 = (bf16[72,4224]{1,0:T(8,128)(2,1)S(1)}, bf16[72,4224]{1,0:T(8,128)(2,1)S(1)}, u32[]{:S(2)}, u32[]{:S(2)}) collective-permute-start(bf16[72,4224]{1,0:T(8,128)(2,1)S(1)} %get-tuple-element.29.refs_0_), channel_id=1, source_target_pairs={{0,8},{8,0},{16,24},{24,16},{1,9},{9,1},{17,25},{25,17},{2,10},{10... | collective-permute-start | bytes 1824776 | tf_op jit(solution)/shard_map/ppermute | solution.py:421
  34.2 25.7 %collective-permute-start.5 = (bf16[72,4224]{1,0:T(8,128)(2,1)S(1)}, bf16[72,4224]{1,0:T(8,128)(2,1)S(1)}, u32[]{:S(2)}, u32[]{:S(2)}) collective-permute-start(bf16[72,4224]{1,0:T(8,128)(2,1)S(1)} %collective-permute-done.4.refs_0_), channel_id=1, source_target_pairs={{0,8},{8,0},{16,24},{24,16},{1,9},{9,1},{17,25},{25,17},{2,10},{10... | collective-permute-start | bytes 1824776 | tf_op jit(solution)/shard_map/ppermute | solution.py:421
  44.2 39.6 %collective-permute-start.15 = (bf16[288,1024]{1,0:T(8,128)(2,1)S(1)}, bf16[288,1024]{1,0:T(8,128)(2,1)S(1)}, u32[]{:S(2)}, u32[]{:S(2)}) collective-permute-start(bf16[288,1024]{1,0:T(8,128)(2,1)S(1)} %get-tuple-element.48), channel_id=1, source_target_pairs={{0,4},{4,0},{1,5},{5,1},{2,6},{6,2},{3,7},{7,3},{8,12},{12,8},{9,1... | collective-permute-start | bytes 1769480 | tf_op jit(solution)/shard_map/ppermute | solution.py:424
  52.4 24.0 %collective-permute-start.9 = (bf16[144,1280]{1,0:T(8,128)(2,1)S(1)}, bf16[144,1280]{1,0:T(8,128)(2,1)S(1)}, u32[]{:S(2)}, u32[]{:S(2)}) collective-permute-start(bf16[144,1280]{1,0:T(8,128)(2,1)S(1)} %get-tuple-element.38), channel_id=1, source_target_pairs={{0,4},{4,0},{1,5},{5,1},{2,6},{6,2},{3,7},{7,3},{8,12},{12,8},{9,1... | collective-permute-start | bytes 1105928 | tf_op jit(solution)/shard_map/ppermute | solution.py:424
  58.5 18.0 %collective-permute-start.8 = (bf16[288,256]{1,0:T(8,128)(2,1)S(1)}, bf16[288,256]{1,0:T(8,128)(2,1)S(1)}, u32[]{:S(2)}, u32[]{:S(2)}) collective-permute-start(bf16[288,256]{1,0:T(8,128)(2,1)S(1)} %get-tuple-element.37), channel_id=1, source_target_pairs={{0,4},{4,0},{1,5},{5,1},{2,6},{6,2},{3,7},{7,3},{8,12},{12,8},{9,1... | collective-permute-start | bytes 442376 | tf_op jit(solution)/shard_map/ppermute | solution.py:424
  66.7 28.4 %collective-permute-start.6 = (bf16[144,1024]{1,0:T(8,128)(2,1)S(1)}, bf16[144,1024]{1,0:T(8,128)(2,1)S(1)}, u32[]{:S(2)}, u32[]{:S(2)}) collective-permute-start(bf16[144,1024]{1,0:T(8,128)(2,1)S(1)} %get-tuple-element.32), channel_id=1, source_target_pairs={{0,4},{4,0},{1,5},{5,1},{2,6},{6,2},{3,7},{7,3},{8,12},{12,8},{9,1... | collective-permute-start | bytes 884744 | tf_op jit(solution)/shard_map/ppermute | solution.py:424
  67.3 12.1 %collective-permute-start.12 = (bf16[144,256]{1,0:T(8,128)(2,1)S(1)}, bf16[144,256]{1,0:T(8,128)(2,1)S(1)}, u32[]{:S(2)}, u32[]{:S(2)}) collective-permute-start(bf16[144,256]{1,0:T(8,128)(2,1)S(1)} %get-tuple-element.42), channel_id=1, source_target_pairs={{0,4},{4,0},{1,5},{5,1},{2,6},{6,2},{3,7},{7,3},{8,12},{12,8},{9,1... | collective-permute-start | bytes 221192 | tf_op jit(solution)/shard_map/ppermute | solution.py:424
  77.1 12.9 %collective-permute-start.10 = (bf16[432,128]{1,0:T(8,128)(2,1)S(1)}, bf16[432,128]{1,0:T(8,128)(2,1)S(1)}, u32[]{:S(2)}, u32[]{:S(2)}) collective-permute-start(bf16[432,128]{1,0:T(8,128)(2,1)S(1)} %get-tuple-element.40), channel_id=1, source_target_pairs={{0,1},{2,0},{1,3},{3,2},{4,5},{6,4},{5,7},{7,6},{8,9},{10,8},{9,11... | collective-permute-start | bytes 331784 | tf_op jit(solution)/shard_map/ppermute | solution.py:455
  78.7 11.3 %collective-permute-start.11 = (bf16[432,128]{1,0:T(8,128)(2,1)S(1)}, bf16[432,128]{1,0:T(8,128)(2,1)S(1)}, u32[]{:S(2)}, u32[]{:S(2)}) collective-permute-start(bf16[432,128]{1,0:T(8,128)(2,1)S(1)} %get-tuple-element.41), channel_id=1, source_target_pairs={{2,1},{1,2},{6,5},{5,6},{10,9},{9,10},{14,13},{13,14},{18,17},{17,... | collective-permute-start | bytes 331784 | tf_op jit(solution)/shard_map/ppermute | solution.py:456
  79.9 10.1 %collective-permute-start.13 = (bf16[144,128]{1,0:T(8,128)(2,1)S(1)}, bf16[144,128]{1,0:T(8,128)(2,1)S(1)}, u32[]{:S(2)}, u32[]{:S(2)}) collective-permute-start(bf16[144,128]{1,0:T(8,128)(2,1)S(1)} %get-tuple-element.44), channel_id=1, source_target_pairs={{0,1},{2,0},{1,3},{3,2},{4,5},{6,4},{5,7},{7,6},{8,9},{10,8},{9,11... | collective-permute-start | bytes 110600 | tf_op jit(solution)/shard_map/ppermute | solution.py:460
  83.8 6.1 %collective-permute-start.14 = (bf16[144,128]{1,0:T(8,128)(2,1)S(1)}, bf16[144,128]{1,0:T(8,128)(2,1)S(1)}, u32[]{:S(2)}, u32[]{:S(2)}) collective-permute-start(bf16[144,128]{1,0:T(8,128)(2,1)S(1)} %get-tuple-element.45), channel_id=1, source_target_pairs={{2,1},{1,2},{6,5},{5,6},{10,9},{9,10},{14,13},{13,14},{18,17},{17,... | collective-permute-start | bytes 110600 | tf_op jit(solution)/shard_map/ppermute | solution.py:461
  84.7 5.3 %copy-start = (bf16[1,2048]{1,0:T(2,128)(2,1)S(1)}, bf16[1,2048]{1,0:T(2,128)(2,1)}, u32[]{:S(2)}) copy-start(bf16[1,2048]{1,0:T(2,128)(2,1)} %refs_9_.1) | copy-start | bytes 12292
  95.1 14.9 %copy-start.1 = (s32[72]{0:T(128)S(1)}, s32[72]{0:T(128)}, u32[]{:S(2)}) copy-start(s32[72]{0:T(128)} %param.9) | copy-start | bytes 868

commit v3 on v2

--- a/solution.py
+++ b/solution.py
@@ -97,31 +97,25 @@
     )(ids, lengths, rows, send)
 
 
-def chunk_kernel(ids_ref, *refs, chips, sends):
-    pieces, refs = refs[:2 * chips], refs[2 * chips:]
-    gain_hbm, keyval_hbm, query_hbm, head_hbm = refs[:4]
-    rows_ref, own_ref, direct_ref, tail_ref = refs[4:8]
-    send_refs = refs[8:8 + sends]
-    gain_ref, keyval_ref, query_ref, head_ref, sems = refs[8 + sends:]
+BLOCK = 256
+
+
+def column_copies(source, first, target, sems):
+    blocks = target.shape[1] // BLOCK
+    return [
+        pltpu.make_async_copy(
+            source.at[:, pl.ds(pl.multiple_of(first + index * BLOCK, BLOCK), BLOCK)],
+            target.at[:, pl.ds(index * BLOCK, BLOCK)], sems.at[index])
+        for index in range(blocks)]
+
+
+def chunk_body(ids_ref, pieces, gain_ref, head_ref, keyval_ref, query_ref, outs, waits):
+    rows_ref, own_ref, direct_ref, tail_ref = outs[:4]
+    sends = outs[4:]
     count = pieces[0].shape[0]
     half = rows_ref.shape[1]
-    blocks, _, block = query_ref.shape
-    core, segment, tp = ids_ref[0], ids_ref[1], ids_ref[3]
-    columns = blocks * block
-    gain_copy = pltpu.make_async_copy(
-        gain_hbm.at[:, pl.ds(pl.multiple_of(segment * half, half), half)], gain_ref, sems.at[0])
-    head_copy = pltpu.make_async_copy(head_hbm, head_ref, sems.at[1])
-    keyval_copy = pltpu.make_async_copy(keyval_hbm, keyval_ref, sems.at[2])
-    gain_copy.start()
-    head_copy.start()
-    keyval_copy.start()
-    query_copies = []
-    for index in range(blocks):
-        at = pl.multiple_of((1 - segment) * columns + index * block, block)
-        query_copies.append(pltpu.make_async_copy(
-            query_hbm.at[:, pl.ds(at, block)], query_ref.at[index], sems.at[3 + index]))
-        query_copies[-1].start()
-
+    core, segment = ids_ref[0], ids_ref[1]
+    columns = query_ref.shape[1]
     top = (iota((count, 1), 0) < count // 2).astype(jnp.int32)
     mask = (top ^ core) == 1
 
@@ -133,108 +127,159 @@
     first_lanes = iota((count, LANES), 1) < 3
     scale = sorted_rows([
         jnp.sum(jnp.where(first_lanes, ref[:, half:].astype(F32), 0.0), axis=1, keepdims=True) for ref in pieces])
-    slice_width = head_ref.shape[1]
-    holder = (tp * slice_width) // half == segment
-    first = (tp * slice_width) % half
     chunk = 512
-    direct = jnp.zeros((2 * chips * count, LANES), F32)
-    gain_copy.wait()
-    head_copy.wait()
+    direct = jnp.zeros((direct_ref.shape[0], LANES), F32)
     for start in range(0, half, chunk):
         at = slice(start, start + chunk)
         rows = sorted_rows([ref[:, at].astype(F32) for ref in pieces])
-        inside = jnp.logical_and(holder, jnp.logical_and(start >= first, start < first + slice_width))
-        offset = pl.multiple_of(jnp.where(inside, start - first, 0), chunk)
-        weight = jnp.where(inside, head_ref[:, pl.ds(offset, chunk)].astype(F32), 0.0)
+        weight = head_ref[:, at].astype(F32)
         for lane in range(0, chunk, LANES):
             direct = direct + rows[:, lane:lane + LANES] * weight[:, lane:lane + LANES]
         rows_ref[:, at] = (rows * scale * gain_ref[:, at].astype(F32)).astype(BF16)
     direct_ref[...] = direct
     tail_ref[...] = pieces[0][:, half:].astype(F32)[:8]
 
-    keyval_copy.wait()
+    for wait in waits[:keyval_ref.shape[1] // BLOCK]:
+        wait()
     keyval = jnp.dot(rows_ref[...], keyval_ref[...], preferred_element_type=F32)
     even = jnp.concatenate([keyval[:, :HEAD], keyval[:, 2 * HEAD:3 * HEAD]], axis=1)
     odd = jnp.concatenate([keyval[:, HEAD:2 * HEAD], keyval[:, 3 * HEAD:]], axis=1)
     own_ref[...] = jnp.where(segment == 0, even, odd)
     other = jnp.where(segment == 0, odd, even).astype(BF16)
-    if sends == 1:
-        send_refs[0][:, columns:] = other
+    if len(sends) == 1:
+        sends[0][:, columns:] = other
     else:
-        send_refs[1][...] = other
-    for index in range(blocks):
-        query_copies[index].wait()
-        send_refs[0][:, index * block:(index + 1) * block] = jnp.dot(
-            rows_ref[...], query_ref[index], preferred_element_type=F32).astype(BF16)
-
-
-def multiply_chunk(ids, pieces, gain, keyval, query, head, split):
-    count, wide = pieces[0].shape
+        sends[1][...] = other
+    waits = waits[keyval_ref.shape[1] // BLOCK:]
+    for index in range(columns // BLOCK):
+        if waits:
+            waits[index]()
+        at = slice(index * BLOCK, (index + 1) * BLOCK)
+        sends[0][:, at] = jnp.dot(rows_ref[...], query_ref[:, at], preferred_element_type=F32).astype(BF16)
+
+
+def first_chunk_kernel(ids_ref, near_ref, far_ref, gain_hbm, head_hbm, keyval_hbm, query_hbm, *refs):
+    outs, (gain_ref, head_ref, keyval_ref, query_ref), (part_ref, small_sems, sems) = refs[:5], refs[5:9], refs[9:]
+    half = outs[0].shape[1]
+    segment, tp = ids_ref[1], ids_ref[3]
+    small = [
+        pltpu.make_async_copy(
+            gain_hbm.at[:, pl.ds(pl.multiple_of(segment * half, half), half)], gain_ref, small_sems.at[0]),
+        pltpu.make_async_copy(head_hbm, part_ref, small_sems.at[1]),
+    ]
+    blocks = keyval_ref.shape[1] // BLOCK
+    large = column_copies(keyval_hbm, 0, keyval_ref, sems)
+    large += column_copies(query_hbm, (1 - segment) * query_ref.shape[1], query_ref, sems.at[pl.ds(blocks, query_ref.shape[1] // BLOCK)])
+    for copy in small + large:
+        copy.start()
+    for copy in small:
+        copy.wait()
+    width = part_ref.shape[1]
+    head_ref[...] = jnp.zeros_like(head_ref)
+
+    @pl.when((tp * width) // half == segment)
+    def _():
+        head_ref[:, pl.ds(pl.multiple_of((tp * width) % half, width), width)] = part_ref[...]
+
+    chunk_body(ids_ref, (near_ref, far_ref), gain_ref, head_ref, keyval_ref, query_ref, outs,
+               [copy.wait for copy in large])
+
+
+def next_chunk_kernel(ids_ref, *refs, chips):
+    pieces, refs = refs[:2 * chips], refs[2 * chips:]
+    chunk_body(ids_ref, pieces, *refs[:4], refs[4:], [])
+
+
+def chunk_shapes(rows, half, widths):
+    return (
+        jax.ShapeDtypeStruct((rows, half), BF16),
+        jax.ShapeDtypeStruct((rows, 2 * HEAD), F32),
+        jax.ShapeDtypeStruct((rows, LANES), F32),
+        jax.ShapeDtypeStruct((8, LANES), F32),
+    ) + tuple(jax.ShapeDtypeStruct((rows, width), BF16) for width in widths)
+
+
+def first_chunk(ids, near, far, gain, head, keyval, query):
+    count, wide = near.shape
     half = wide - LANES
     columns = query.shape[1] // 2
-    block = 256
-    blocks = columns // block
+    shapes = chunk_shapes(2 * count, half, (columns + 2 * HEAD,)) + tuple(
+        jax.ShapeDtypeStruct(shape, BF16) for shape in ((1, half), (1, half), keyval.shape, (half, columns)))
+    out = pl.pallas_call(
+        first_chunk_kernel,
+        out_shape=shapes,
+        in_specs=[whole(pltpu.SMEM), whole(), whole()] + [whole(pltpu.HBM)] * 4,
+        out_specs=(whole(),) * len(shapes),
+        scratch_shapes=[
+            pltpu.VMEM(head.shape, BF16),
+            pltpu.SemaphoreType.DMA((2,)),
+            pltpu.SemaphoreType.DMA(((columns + keyval.shape[1]) // BLOCK,)),
+        ],
+        compiler_params=pltpu.CompilerParams(vmem_limit_bytes=24 << 20),
+        name="first_chunk",
+    )(ids, near, far, gain, head, keyval, query)
+    return out[:5], out[5:]
+
+
+def next_chunk(ids, pieces, weights):
+    count, wide = pieces[0].shape
     chips = len(pieces) // 2
-    rows = 2 * chips * count
-    widths = (columns, 2 * HEAD) if split else (columns + 2 * HEAD,)
+    shapes = chunk_shapes(2 * chips * count, wide - LANES, (weights[3].shape[1], 2 * HEAD))
     return pl.pallas_call(
-        functools.partial(chunk_kernel, chips=chips, sends=len(widths)),
-        out_shape=(
-            jax.ShapeDtypeStruct((rows, half), BF16),
-            jax.ShapeDtypeStruct((rows, 2 * HEAD), F32),
-            jax.ShapeDtypeStruct((rows, LANES), F32),
-            jax.ShapeDtypeStruct((8, LANES), F32),
-        ) + tuple(jax.ShapeDtypeStruct((rows, width), BF16) for width in widths),
-        in_specs=[whole(pltpu.SMEM)] + [whole()] * len(pieces) + [whole(pltpu.HBM)] * 4,
-        out_specs=(whole(),) * (4 + len(widths)),
-        scratch_shapes=[
-            pltpu.VMEM((1, half), BF16),
-            pltpu.VMEM(keyval.shape, BF16),
-            pltpu.VMEM((blocks, half, block), BF16),
-            pltpu.VMEM(head.shape, BF16),
-            pltpu.SemaphoreType.DMA((3 + blocks,)),
-        ],
-        compiler_params=pltpu.CompilerParams(vmem_limit_bytes=32 << 20),
-        cost_estimate=pl.CostEstimate(
-            flops=2 * rows * half * (columns + keyval.shape[1]), transcendentals=0,
-            bytes_accessed=2 * half * (columns + keyval.shape[1])),
-        name="chunk",
-    )(ids, *pieces, gain, keyval, query, head)
-
-
-def own_kernel(ids_ref, rows_ref, query_hbm, out_ref, query_ref, sems):
-    blocks, _, block = query_ref.shape
-    columns = blocks * block
-    copies = []
-    for index in range(blocks):
-        at = pl.multiple_of(ids_ref[1] * columns + index * block, block)
-        copies.append(pltpu.make_async_copy(query_hbm.at[:, pl.ds(at, block)], query_ref.at[index], sems.at[index]))
-        copies[-1].start()
-    for index in range(blocks):
-        copies[index].wait()
-        out_ref[:, index * block:(index + 1) * block] = jnp.dot(
-            rows_ref[...], query_ref[index], preferred_element_type=F32)
-
-
-def own_queries(ids, rows, query):
+        functools.partial(next_chunk_kernel, chips=chips),
+        out_shape=shapes,
+        in_specs=[whole(pltpu.SMEM)] + [whole()] * (len(pieces) + 4),
+        out_specs=(whole(),) * len(shapes),
+        compiler_params=pltpu.CompilerParams(vmem_limit_bytes=24 << 20),
+        name="next_chunk",
+    )(ids, *pieces, *weights)
+
+
+def own_body(rows_ref, query_ref, out_ref, waits):
+    for index in range(query_ref.shape[1] // BLOCK):
+        if waits:
+            waits[index]()
+        at = slice(index * BLOCK, (index + 1) * BLOCK)
+        out_ref[:, at] = jnp.dot(rows_ref[...], query_ref[:, at], preferred_element_type=F32)
+
+
+def first_own_kernel(ids_ref, rows_ref, query_hbm, out_ref, query_ref, sems):
+    copies = column_copies(query_hbm, ids_ref[1] * query_ref.shape[1], query_ref, sems)
+    for copy in copies:
+        copy.start()
+    own_body(rows_ref, query_ref, out_ref, [copy.wait for copy in copies])
+
+
+def next_own_kernel(rows_ref, query_ref, out_ref):
+    own_body(rows_ref, query_ref, out_ref, [])
+
+
+def first_own(ids, rows, query):
     count, half = rows.shape
     columns = query.shape[1] // 2
-    block = 256
-    blocks = columns // block
     return pl.pallas_call(
-        own_kernel,
-        out_shape=jax.ShapeDtypeStruct((count, columns), F32),
+        first_own_kernel,
+        out_shape=(
+            jax.ShapeDtypeStruct((count, columns), F32),
+            jax.ShapeDtypeStruct((half, columns), BF16),
+        ),
         in_specs=[whole(pltpu.SMEM), whole(), whole(pltpu.HBM)],
+        out_specs=(whole(), whole()),
+        scratch_shapes=[pltpu.SemaphoreType.DMA((columns // BLOCK,))],
+        compiler_params=pltpu.CompilerParams(vmem_limit_bytes=16 << 20),
+        name="first_own",
+    )(ids, rows, query)
+
+
+def next_own(rows, query):
+    return pl.pallas_call(
+        next_own_kernel,
+        out_shape=jax.ShapeDtypeStruct((rows.shape[0], query.shape[1]), F32),
+        in_specs=[whole(), whole()],
         out_specs=whole(),
-        scratch_shapes=[
-            pltpu.VMEM((blocks, half, block), BF16),
-            pltpu.SemaphoreType.DMA((blocks,)),
-        ],
-        compiler_params=pltpu.CompilerParams(vmem_limit_bytes=20 << 20),
-        cost_estimate=pl.CostEstimate(
-            flops=2 * count * half * columns, transcendentals=0, bytes_accessed=2 * half * columns),
-        name="own_queries",
-    )(ids, rows, query)
+        compiler_params=pltpu.CompilerParams(vmem_limit_bytes=16 << 20),
+        name="next_own",
+    )(rows, query)
 
 
 def slabs(refs, starts, count, at=slice(None)):
@@ -439,14 +484,20 @@
     local, direct, query, received = {}, {}, {}, {}
     for name, pieces in (("own", (mine,)), ("xy", (from_x, from_y)), ("d", (from_d,))):
         pieces = [part for piece in pieces for part in (piece, swap(piece))]
-        rows, local[name], direct[name], lengths, *sends = multiply_chunk(
-            ids, pieces, attn_gain, wkv, wq, head_weight, name != "own")
+        if name == "own":
+            out, weights = first_chunk(ids, *pieces, attn_gain, head_weight, wkv, wq)
+        else:
+            out = next_chunk(ids, pieces, weights)
+        rows, local[name], direct[name], lengths, *sends = out
         if name == "xy":
             tail = lengths
         for index, part in reversed(list(enumerate(sends))):
             sends[index] = across(part)
         received[name] = sends
-        query[name] = own_queries(ids, rows, wq)
+        if name == "own":
+            query[name], own_weights = first_own(ids, rows, wq)
+        else:
+            query[name] = next_own(rows, own_weights)
 
     keep, first, second = sum_keyval(
         ids, [local["own"], local["xy"], local["d"]], (0, 0, 0),
@@ -462,12 +513,11 @@
     late = (keep, first, second)
     devices = n_branch * 2 * lax.axis_size("tp")
     outgoing = attention(
-        ids, seq_lengths, tail, [query["own"], query["xy"], query["d"]], (0, 0, 0),
-        [received["xy"][0], received["own"][0], received["xy"][0]], (0, 0, slab),
-        [direct["own"], direct["xy"], direct["d"]], early, late, head_attn, devices, 0, [])
-    outgoing = attention(
-        ids, seq_lengths, tail, [query["xy"]], (slab,), [received["d"][0]], (0,),
-        [direct["xy"]], early, late, head_attn, devices, 3, [outgoing])
+        ids, seq_lengths, tail,
+        [query["own"], query["xy"], query["d"], query["xy"]], (0, 0, 0, slab),
+        [received["xy"][0], received["own"][0], received["xy"][0], received["d"][0]], (0, 0, slab, 0),
+        [direct["own"], direct["xy"], direct["d"], direct["xy"]],
+        early, late, head_attn, devices, 0, [])
     incoming = lax.all_to_all(outgoing, ALL_AXES, split_axis=0, concat_axis=0, tiled=True)
     return finish(incoming, packing, n_branch)
 

time: 111 us -> 119 us (1.072)
  waiting for transfers between devices: 24.8 us -> 49.5 us
  Pallas kernels: 54.2 us -> 37 us
    ppermute x6, waiting for transfers between devices: 12.2 us -> 36.8 us  [across(): return lax.ppermute(part, 'segment', x_pairs)]
    pallas_call x6, Pallas kernels: 41.5 us -> 26.9 us  [the longest x1 8.99 us: first_chunk(): pl.pallas_call(first_chunk_kernel, out_shape=shapes, in_specs=[whole(pltp...]
    pallas_call x2 -> x1, Pallas kernels: 8.08 us -> 5.5 us  [attention(): pl.pallas_call(functools.partial(attention_kernel, slot=slot, starts=star...]
  transfers between devices with their start and end apart: 16 -> 16, of which waited for: 2 -> 4; matrix products, arithmetic and copies ran while one was open for 0% -> 0% of each run, Pallas kernels for 43% -> 24%
where the time goes in v3:
time: 119 us
  waiting for transfers between devices  49.5 us (42%)
  Pallas kernels  37 us (31%)
  starting transfers between devices  19.4 us (16%)
  blocking collectives  12.6 us (11%)
    ppermute x6, waiting for transfers between devices, across(): return lax.ppermute(part, 'segment', x_pairs)  36.8 us
    ppermute x1, waiting for transfers between devices, paired(): from_d = lax.ppermute(from_x, 'branch', y_pairs)  12.6 us
    all_to_all x1, blocking collectives, paired(): lax.all_to_all(outgoing, ALL_AXES, split_axis=0, concat_axis=0, tiled=True)  12.6 us
    pallas_call x1, Pallas kernels, first_chunk(): pl.pallas_call(first_chunk_kernel, out_shape=shapes, in_specs=[whole(pltp...  8.99 us
    ppermute x6, starting transfers between devices, across(): return lax.ppermute(part, 'segment', x_pairs)  8.6 us
    pallas_call x2, Pallas kernels, next_chunk(): pl.pallas_call(functools.partial(next_chunk_kernel, chips=chips), out_sha...  8.53 us
    pallas_call x1, Pallas kernels, attention(): pl.pallas_call(functools.partial(attention_kernel, slot=slot, starts=star...  5.5 us
    ppermute x2, starting transfers between devices, paired(): first = lax.ppermute(first, 'tp', hand_first)  5.49 us
  transfers between devices with their start and end apart: 16, of which 4 were waited for; matrix products, arithmetic and copies ran while one was open for 0% of the time, Pallas kernels for 24%

profile of v3, /device:TPU:0, one launch (start us, length us, event | category | flops | bytes accessed | tf_op | source)
XLA Modules:
  0.0 118.7 jit_solution(18230788102651069102)
XLA Ops:
  0.0 0.1 pad_add_fusion.ids_ref
  0.1 2.5 %prepare.1 = (bf16[72,4224]{1,0:T(8,128)(2,1)S(1)}, bf16[72,4224]{1,0:T(8,128)(2,1)S(1)}) custom-call(s32[4]{0:T(128)S(1)} %pad_add_fusion.ids_ref, s32[1,6]{1,0:T(1,128)} %lengths_ref.3, bf16[72,8192]{1,0:T(8,128)(2,1)} %rows_hbm.1, s32[1,72]{1,0:T(1,128)} %bitcast.13), custom_call_target="tpu_custom_call" | custom-call | tf_op jit(solution)/shard_map/prepare/pallas_call | solution.py:85
  2.6 3.0 %collective-permute-start = (bf16[72,4224]{1,0:T(8,128)(2,1)S(1)}, bf16[72,4224]{1,0:T(8,128)(2,1)S(1)}, u32[]{:S(2)}, u32[]{:S(2)}) collective-permute-start(bf16[72,4224]{1,0:T(8,128)(2,1)S(1)} %get-tuple-element.34), channel_id=1, source_target_pairs={{0,4},{4,0},{1,5},{5,1},{2,6},{6,2},{3,7},{7,3},{8,12},{12,8},{9,1... | collective-permute-start | bytes 1824776 | tf_op jit(solution)/shard_map/ppermute | solution.py:469
  5.6 1.5 %collective-permute-start.2 = (bf16[72,4224]{1,0:T(8,128)(2,1)S(1)}, bf16[72,4224]{1,0:T(8,128)(2,1)S(1)}, u32[]{:S(2)}, u32[]{:S(2)}) collective-permute-start(bf16[72,4224]{1,0:T(8,128)(2,1)S(1)} %get-tuple-element.35.near_ref), channel_id=1, source_target_pairs={{0,16},{8,24},{16,0},{24,8},{1,17},{9,25},{17,1},{25,9},{2,18},{10... | collective-permute-start | bytes 1824776 | tf_op jit(solution)/shard_map/ppermute | solution.py:480
  7.2 12.2 %collective-permute-done.refs_0_ = bf16[72,4224]{1,0:T(8,128)(2,1)S(1)} collective-permute-done((bf16[72,4224]{1,0:T(8,128)(2,1)S(1)}, bf16[72,4224]{1,0:T(8,128)(2,1)S(1)}, u32[]{:S(2)}, u32[]{:S(2)}) %collective-permute-start) | collective-permute-done | bytes 608288 | tf_op jit(solution)/shard_map/ppermute | solution.py:469
  19.4 1.8 %collective-permute-start.5 = (bf16[72,4224]{1,0:T(8,128)(2,1)S(1)}, bf16[72,4224]{1,0:T(8,128)(2,1)S(1)}, u32[]{:S(2)}, u32[]{:S(2)}) collective-permute-start(bf16[72,4224]{1,0:T(8,128)(2,1)S(1)} %collective-permute-done.refs_0_), channel_id=1, source_target_pairs={{0,16},{8,24},{16,0},{24,8},{1,17},{9,25},{17,1},{25,9},{2,18},{10... | collective-permute-start | bytes 1824776 | tf_op jit(solution)/shard_map/ppermute | solution.py:481
  21.1 0.0 collective-permute-start.4
  21.1 0.5 collective-permute-start.1
  21.6 0.0 collective-permute-done.2.refs_2_
  21.6 0.0 collective-permute-start.3
  21.7 12.6 %collective-permute-done.5.refs_0_ = bf16[72,4224]{1,0:T(8,128)(2,1)S(1)} collective-permute-done((bf16[72,4224]{1,0:T(8,128)(2,1)S(1)}, bf16[72,4224]{1,0:T(8,128)(2,1)S(1)}, u32[]{:S(2)}, u32[]{:S(2)}) %collective-permute-start.5) | collective-permute-done | bytes 608288 | tf_op jit(solution)/shard_map/ppermute | solution.py:481
  34.2 0.0 collective-permute-start.6
  34.2 0.0 collective-permute-done.4.far_ref
  34.3 9.0 %first_chunk.1 = (bf16[144,4096]{1,0:T(8,128)(2,1)S(1)}, f32[144,256]{1,0:T(8,128)S(1)}, f32[144,128]{1,0:T(8,128)S(1)}, f32[8,128]{1,0:T(8,128)}, bf16[144,1280...) custom-call(s32[4]{0:T(128)S(1)} %pad_add_fusion.ids_ref, ...), custom_call_target="tpu_custom_call" | custom-call | tf_op jit(solution)/shard_map/first_chunk/pallas_call | solution.py:208
  43.3 0.0 collective-permute-done.1.refs_1_
  43.3 0.0 collective-permute-done.3.refs_3_
  43.3 5.1 %next_chunk.2 = (bf16[288,4096]{1,0:T(8,128)(2,1)S(1)}, f32[288,256]{1,0:T(8,128)S(1)}, f32[288,128]{1,0:T(8,128)S(1)}, f32[8,128]{1,0:T(8,128)S(1)}, bf16[288,1...) custom-call(s32[4]{0:T(128)S(1)} %pad_add_fusion.ids_ref, bf16[72,4224]{1,0:T(8,128)(2,1)S(1)} %collective-permute-done.refs_0_, ...), custom_call_target="tpu_custom_call" | custom-call | tf_op jit(solution)/shard_map/next_chunk/pallas_call | solution.py:228
  48.4 1.5 %collective-permute-start.7 = (bf16[288,1024]{1,0:T(8,128)(2,1)S(1)}, bf16[288,1024]{1,0:T(8,128)(2,1)S(1)}, u32[]{:S(2)}, u32[]{:S(2)}) collective-permute-start(bf16[288,1024]{1,0:T(8,128)(2,1)S(1)} %get-tuple-element.46), channel_id=1, source_target_pairs={{0,4},{4,0},{1,5},{5,1},{2,6},{6,2},{3,7},{7,3},{8,12},{12,8},{9,1... | collective-permute-start | bytes 1769480 | tf_op jit(solution)/shard_map/ppermute | solution.py:469
  49.9 0.6 collective-permute-start.8
  50.5 0.0 collective-permute-done.6.refs_1_
  50.5 3.4 %next_chunk.3 = (bf16[144,4096]{1,0:T(8,128)(2,1)S(1)}, f32[144,256]{1,0:T(8,128)S(1)}, f32[144,128]{1,0:T(8,128)S(1)}, f32[8,128]{1,0:T(8,128)}, bf16[144,1024]...) custom-call(s32[4]{0:T(128)S(1)} %pad_add_fusion.ids_ref, bf16[72,4224]{1,0:T(8,128)(2,1)S(1)} %collective-permute-done.5.refs_0_, ...), custom_call_target="tpu_custom_call" | custom-call | tf_op jit(solution)/shard_map/next_chunk/pallas_call | solution.py:228
  53.9 1.5 %collective-permute-start.9 = (bf16[144,1024]{1,0:T(8,128)(2,1)S(1)}, bf16[144,1024]{1,0:T(8,128)(2,1)S(1)}, u32[]{:S(2)}, u32[]{:S(2)}) collective-permute-start(bf16[144,1024]{1,0:T(8,128)(2,1)S(1)} %get-tuple-element.48), channel_id=1, source_target_pairs={{0,4},{4,0},{1,5},{5,1},{2,6},{6,2},{3,7},{7,3},{8,12},{12,8},{9,1... | collective-permute-start | bytes 884744 | tf_op jit(solution)/shard_map/ppermute | solution.py:469
  55.4 0.6 collective-permute-start.10
  55.9 1.5 %collective-permute-start.13 = (bf16[144,256]{1,0:T(8,128)(2,1)S(1)}, bf16[144,256]{1,0:T(8,128)(2,1)S(1)}, u32[]{:S(2)}, u32[]{:S(2)}) collective-permute-start(bf16[144,256]{1,0:T(8,128)(2,1)S(1)} %get-tuple-element.59), channel_id=1, source_target_pairs={{0,4},{4,0},{1,5},{5,1},{2,6},{6,2},{3,7},{7,3},{8,12},{12,8},{9,1... | collective-permute-start | bytes 221192 | tf_op jit(solution)/shard_map/ppermute | solution.py:469
  57.4 15.2 %collective-permute-done.8.refs_4_.refs_5_ = bf16[144,1280]{1,0:T(8,128)(2,1)S(1)} collective-permute-done((bf16[144,1280]{1,0:T(8,128)(2,1)S(1)}, bf16[144,1280]{1,0:T(8,128)(2,1)S(1)}, u32[]{:S(2)}, u32[]{:S(2)}) %collective-permute-start.8) | collective-permute-done | bytes 368672 | tf_op jit(solution)/shard_map/ppermute | solution.py:469
  72.5 9.5 %collective-permute-done.10.refs_3_.refs_5_ = bf16[288,256]{1,0:T(8,128)(2,1)S(1)} collective-permute-done((bf16[288,256]{1,0:T(8,128)(2,1)S(1)}, bf16[288,256]{1,0:T(8,128)(2,1)S(1)}, u32[]{:S(2)}, u32[]{:S(2)}) %collective-permute-start.10) | collective-permute-done | bytes 147488 | tf_op jit(solution)/shard_map/ppermute | solution.py:469
  82.0 0.6 sum_keyval.2
  82.7 1.6 %collective-permute-start.11 = (bf16[432,128]{1,0:T(8,128)(2,1)S(1)}, bf16[432,128]{1,0:T(8,128)(2,1)S(1)}, u32[]{:S(2)}, u32[]{:S(2)}) collective-permute-start(bf16[432,128]{1,0:T(8,128)(2,1)S(1)} %get-tuple-element.57), channel_id=1, source_target_pairs={{0,1},{2,0},{1,3},{3,2},{4,5},{6,4},{5,7},{7,6},{8,9},{10,8},{9,11... | collective-permute-start | bytes 331784 | tf_op jit(solution)/shard_map/ppermute | solution.py:506
  84.3 0.7 collective-permute-start.12
  85.0 0.0 collective-permute-done.13.refs_1_
  85.0 0.6 sum_keyval.3
  85.5 3.9 %collective-permute-start.14 = (bf16[144,128]{1,0:T(8,128)(2,1)S(1)}, bf16[144,128]{1,0:T(8,128)(2,1)S(1)}, u32[]{:S(2)}, u32[]{:S(2)}) collective-permute-start(bf16[144,128]{1,0:T(8,128)(2,1)S(1)} %get-tuple-element.61), channel_id=1, source_target_pairs={{0,1},{2,0},{1,3},{3,2},{4,5},{6,4},{5,7},{7,6},{8,9},{10,8},{9,11... | collective-permute-start | bytes 110600 | tf_op jit(solution)/shard_map/ppermute | solution.py:511
  89.4 0.0 collective-permute-done.7.refs_4_.refs_6_
  89.4 0.8 collective-permute-start.15
  90.2 5.2 %first_own.1 = (f32[144,1024]{1,0:T(8,128)S(1)}, bf16[4096,1024]{1,0:T(8,128)(2,1)S(1)}) custom-call(s32[4]{0:T(128)S(1)} %pad_add_fusion.ids_ref, bf16[144,4096]{1,0:T(8,128)(2,1)S(1)} %get-tuple-element.41.rows_ref, bf16[4096,2048]{1,0:T(8,128)(2,1)} %bitcast.16), custom_call_target="tpu_custom_call" | custom-call | tf_op jit(solution)/shard_map/first_own/pallas_call | solution.py:260
  95.5 2.7 %next_own.2.refs_1_.refs_3_ = f32[288,1024]{1,0:T(8,128)S(1)} custom-call(bf16[288,4096]{1,0:T(8,128)(2,1)S(1)} %get-tuple-element.43.rows_ref, bf16[4096,1024]{1,0:T(8,128)(2,1)S(1)} %get-tuple-element.44.query_ref), custom_call_target="tpu_custom_call" | custom-call | tf_op jit(solution)/shard_map/next_own/pallas_call | solution.py:275
  98.2 0.0 copy-start
  98.2 1.4 %next_own.3.refs_2_ = f32[144,1024]{1,0:T(8,128)S(1)} custom-call(bf16[144,4096]{1,0:T(8,128)(2,1)S(1)} %get-tuple-element.45.rows_ref, bf16[4096,1024]{1,0:T(8,128)(2,1)S(1)} %get-tuple-element.44.query_ref), custom_call_target="tpu_custom_call" | custom-call | tf_op jit(solution)/shard_map/next_own/pallas_call | solution.py:275
  99.6 0.0 copy-start.1
  99.6 0.0 collective-permute-done.14.refs_16_
  99.6 0.0 collective-permute-done.15.refs_17_
  99.6 0.0 collective-permute-done.11.refs_13_
  99.7 0.0 collective-permute-done.12.refs_14_
  99.7 0.0 collective-permute-done.9.refs_7_
  99.7 0.0 copy-done
  99.7 5.5 %attend.1 = f32[32,256]{1,0:T(8,128)S(1)} custom-call(s32[4]{0:T(128)S(1)} %pad_add_fusion.ids_ref, s32[1,6]{1,0:T(1,128)} %lengths_ref.3, f32[8,128]{1,0:T(8,128)S(1)} %get-tuple-element.40.tail_ref, f32[144,1024]{1,0:T(8,128)S(1)} %get-tuple-element.42.refs_0_, f32[288,1024]{1,0:T(8,128)S(1)} %next_own.2.refs_1_.refs_3_, f32[144,1024]{1,0:T(8,128)S(1)} %next_own.3.refs_2_, ...), custom_call_target="tpu_custom_call" | custom-call | tf_op jit(solution)/shard_map/attend/pallas_call | solution.py:416
  105.2 12.6 %all_to_all.11 = f32[32,1,256]{2,1,0:T(1,128)S(1)} all-to-all(f32[32,1,256]{2,1,0:T(1,128)S(1)} %copy.9), channel_id=1, replica_groups=mesh['branch'=4,'segment'=2,'tp'=4] {'branch','segment','tp'}, dimensions={0} | all-to-all | bytes 65536 | tf_op jit(solution)/shard_map/all_to_all | solution.py:521
  117.8 0.0 copy-done.1
  117.8 0.9 finish.1
  (2 shorter events, 0.0 us)
Async XLA Ops:
  2.6 16.8 %collective-permute-start = (bf16[72,4224]{1,0:T(8,128)(2,1)S(1)}, bf16[72,4224]{1,0:T(8,128)(2,1)S(1)}, u32[]{:S(2)}, u32[]{:S(2)}) collective-permute-start(bf16[72,4224]{1,0:T(8,128)(2,1)S(1)} %get-tuple-element.34), channel_id=1, source_target_pairs={{0,4},{4,0},{1,5},{5,1},{2,6},{6,2},{3,7},{7,3},{8,12},{12,8},{9,1... | collective-permute-start | bytes 1824776 | tf_op jit(solution)/shard_map/ppermute | solution.py:469
  5.6 16.0 %collective-permute-start.2 = (bf16[72,4224]{1,0:T(8,128)(2,1)S(1)}, bf16[72,4224]{1,0:T(8,128)(2,1)S(1)}, u32[]{:S(2)}, u32[]{:S(2)}) collective-permute-start(bf16[72,4224]{1,0:T(8,128)(2,1)S(1)} %get-tuple-element.35.near_ref), channel_id=1, source_target_pairs={{0,16},{8,24},{16,0},{24,8},{1,17},{9,25},{17,1},{25,9},{2,18},{10... | collective-permute-start | bytes 1824776 | tf_op jit(solution)/shard_map/ppermute | solution.py:480
  19.4 14.9 %collective-permute-start.5 = (bf16[72,4224]{1,0:T(8,128)(2,1)S(1)}, bf16[72,4224]{1,0:T(8,128)(2,1)S(1)}, u32[]{:S(2)}, u32[]{:S(2)}) collective-permute-start(bf16[72,4224]{1,0:T(8,128)(2,1)S(1)} %collective-permute-done.refs_0_), channel_id=1, source_target_pairs={{0,16},{8,24},{16,0},{24,8},{1,17},{9,25},{17,1},{25,9},{2,18},{10... | collective-permute-start | bytes 1824776 | tf_op jit(solution)/shard_map/ppermute | solution.py:481
  21.1 13.1 %collective-permute-start.4 = (bf16[72,4224]{1,0:T(8,128)(2,1)S(1)}, bf16[72,4224]{1,0:T(8,128)(2,1)S(1)}, u32[]{:S(2)}, u32[]{:S(2)}) collective-permute-start(bf16[72,4224]{1,0:T(8,128)(2,1)S(1)} %get-tuple-element.35.near_ref), channel_id=1, source_target_pairs={{0,8},{8,0},{16,24},{24,16},{1,9},{9,1},{17,25},{25,17},{2,10},{10... | collective-permute-start | bytes 1824776 | tf_op jit(solution)/shard_map/ppermute | solution.py:466
  21.1 22.1 %collective-permute-start.1 = (bf16[72,4224]{1,0:T(8,128)(2,1)S(1)}, bf16[72,4224]{1,0:T(8,128)(2,1)S(1)}, u32[]{:S(2)}, u32[]{:S(2)}) collective-permute-start(bf16[72,4224]{1,0:T(8,128)(2,1)S(1)} %collective-permute-done.refs_0_), channel_id=1, source_target_pairs={{0,8},{8,0},{16,24},{24,16},{1,9},{9,1},{17,25},{25,17},{2,10},{10... | collective-permute-start | bytes 1824776 | tf_op jit(solution)/shard_map/ppermute | solution.py:466
  21.6 21.6 %collective-permute-start.3 = (bf16[72,4224]{1,0:T(8,128)(2,1)S(1)}, bf16[72,4224]{1,0:T(8,128)(2,1)S(1)}, u32[]{:S(2)}, u32[]{:S(2)}) collective-permute-start(bf16[72,4224]{1,0:T(8,128)(2,1)S(1)} %collective-permute-done.2.refs_2_), channel_id=1, source_target_pairs={{0,8},{8,0},{16,24},{24,16},{1,9},{9,1},{17,25},{25,17},{2,10},{10... | collective-permute-start | bytes 1824776 | tf_op jit(solution)/shard_map/ppermute | solution.py:466
  34.2 16.2 %collective-permute-start.6 = (bf16[72,4224]{1,0:T(8,128)(2,1)S(1)}, bf16[72,4224]{1,0:T(8,128)(2,1)S(1)}, u32[]{:S(2)}, u32[]{:S(2)}) collective-permute-start(bf16[72,4224]{1,0:T(8,128)(2,1)S(1)} %collective-permute-done.5.refs_0_), channel_id=1, source_target_pairs={{0,8},{8,0},{16,24},{24,16},{1,9},{9,1},{17,25},{25,17},{2,10},{10... | collective-permute-start | bytes 1824776 | tf_op jit(solution)/shard_map/ppermute | solution.py:466
  48.4 41.0 %collective-permute-start.7 = (bf16[288,1024]{1,0:T(8,128)(2,1)S(1)}, bf16[288,1024]{1,0:T(8,128)(2,1)S(1)}, u32[]{:S(2)}, u32[]{:S(2)}) collective-permute-start(bf16[288,1024]{1,0:T(8,128)(2,1)S(1)} %get-tuple-element.46), channel_id=1, source_target_pairs={{0,4},{4,0},{1,5},{5,1},{2,6},{6,2},{3,7},{7,3},{8,12},{12,8},{9,1... | collective-permute-start | bytes 1769480 | tf_op jit(solution)/shard_map/ppermute | solution.py:469
  49.9 22.6 %collective-permute-start.8 = (bf16[144,1280]{1,0:T(8,128)(2,1)S(1)}, bf16[144,1280]{1,0:T(8,128)(2,1)S(1)}, u32[]{:S(2)}, u32[]{:S(2)}) collective-permute-start(bf16[144,1280]{1,0:T(8,128)(2,1)S(1)} %get-tuple-element.47), channel_id=1, source_target_pairs={{0,4},{4,0},{1,5},{5,1},{2,6},{6,2},{3,7},{7,3},{8,12},{12,8},{9,1... | collective-permute-start | bytes 1105928 | tf_op jit(solution)/shard_map/ppermute | solution.py:469
  53.9 45.8 %collective-permute-start.9 = (bf16[144,1024]{1,0:T(8,128)(2,1)S(1)}, bf16[144,1024]{1,0:T(8,128)(2,1)S(1)}, u32[]{:S(2)}, u32[]{:S(2)}) collective-permute-start(bf16[144,1024]{1,0:T(8,128)(2,1)S(1)} %get-tuple-element.48), channel_id=1, source_target_pairs={{0,4},{4,0},{1,5},{5,1},{2,6},{6,2},{3,7},{7,3},{8,12},{12,8},{9,1... | collective-permute-start | bytes 884744 | tf_op jit(solution)/shard_map/ppermute | solution.py:469
  55.4 26.7 %collective-permute-start.10 = (bf16[288,256]{1,0:T(8,128)(2,1)S(1)}, bf16[288,256]{1,0:T(8,128)(2,1)S(1)}, u32[]{:S(2)}, u32[]{:S(2)}) collective-permute-start(bf16[288,256]{1,0:T(8,128)(2,1)S(1)} %get-tuple-element.55), channel_id=1, source_target_pairs={{0,4},{4,0},{1,5},{5,1},{2,6},{6,2},{3,7},{7,3},{8,12},{12,8},{9,1... | collective-permute-start | bytes 442376 | tf_op jit(solution)/shard_map/ppermute | solution.py:469
  55.9 29.0 %collective-permute-start.13 = (bf16[144,256]{1,0:T(8,128)(2,1)S(1)}, bf16[144,256]{1,0:T(8,128)(2,1)S(1)}, u32[]{:S(2)}, u32[]{:S(2)}) collective-permute-start(bf16[144,256]{1,0:T(8,128)(2,1)S(1)} %get-tuple-element.59), channel_id=1, source_target_pairs={{0,4},{4,0},{1,5},{5,1},{2,6},{6,2},{3,7},{7,3},{8,12},{12,8},{9,1... | collective-permute-start | bytes 221192 | tf_op jit(solution)/shard_map/ppermute | solution.py:469
  82.7 17.0 %collective-permute-start.11 = (bf16[432,128]{1,0:T(8,128)(2,1)S(1)}, bf16[432,128]{1,0:T(8,128)(2,1)S(1)}, u32[]{:S(2)}, u32[]{:S(2)}) collective-permute-start(bf16[432,128]{1,0:T(8,128)(2,1)S(1)} %get-tuple-element.57), channel_id=1, source_target_pairs={{0,1},{2,0},{1,3},{3,2},{4,5},{6,4},{5,7},{7,6},{8,9},{10,8},{9,11... | collective-permute-start | bytes 331784 | tf_op jit(solution)/shard_map/ppermute | solution.py:506
  84.3 15.4 %collective-permute-start.12 = (bf16[432,128]{1,0:T(8,128)(2,1)S(1)}, bf16[432,128]{1,0:T(8,128)(2,1)S(1)}, u32[]{:S(2)}, u32[]{:S(2)}) collective-permute-start(bf16[432,128]{1,0:T(8,128)(2,1)S(1)} %get-tuple-element.58), channel_id=1, source_target_pairs={{2,1},{1,2},{6,5},{5,6},{10,9},{9,10},{14,13},{13,14},{18,17},{17,... | collective-permute-start | bytes 331784 | tf_op jit(solution)/shard_map/ppermute | solution.py:507
  85.5 14.1 %collective-permute-start.14 = (bf16[144,128]{1,0:T(8,128)(2,1)S(1)}, bf16[144,128]{1,0:T(8,128)(2,1)S(1)}, u32[]{:S(2)}, u32[]{:S(2)}) collective-permute-start(bf16[144,128]{1,0:T(8,128)(2,1)S(1)} %get-tuple-element.61), channel_id=1, source_target_pairs={{0,1},{2,0},{1,3},{3,2},{4,5},{6,4},{5,7},{7,6},{8,9},{10,8},{9,11... | collective-permute-start | bytes 110600 | tf_op jit(solution)/shard_map/ppermute | solution.py:511
  89.4 10.2 %collective-permute-start.15 = (bf16[144,128]{1,0:T(8,128)(2,1)S(1)}, bf16[144,128]{1,0:T(8,128)(2,1)S(1)}, u32[]{:S(2)}, u32[]{:S(2)}) collective-permute-start(bf16[144,128]{1,0:T(8,128)(2,1)S(1)} %get-tuple-element.62), channel_id=1, source_target_pairs={{2,1},{1,2},{6,5},{5,6},{10,9},{9,10},{14,13},{13,14},{18,17},{17,... | collective-permute-start | bytes 110600 | tf_op jit(solution)/shard_map/ppermute | solution.py:512
  98.2 1.5 %copy-start = (bf16[1,2048]{1,0:T(2,128)(2,1)S(1)}, bf16[1,2048]{1,0:T(2,128)(2,1)}, u32[]{:S(2)}) copy-start(bf16[1,2048]{1,0:T(2,128)(2,1)} %refs_18_.1) | copy-start | bytes 12292
  99.6 18.2 %copy-start.1 = (s32[72]{0:T(128)S(1)}, s32[72]{0:T(128)}, u32[]{:S(2)}) copy-start(s32[72]{0:T(128)} %param.9) | copy-start | bytes 868

commit v4 on v3

--- a/solution.py
+++ b/solution.py
@@ -109,12 +109,15 @@
         for index in range(blocks)]
 
 
-def chunk_body(ids_ref, pieces, gain_ref, head_ref, keyval_ref, query_ref, outs, waits):
-    rows_ref, own_ref, direct_ref, tail_ref = outs[:4]
-    sends = outs[4:]
+def split_slots(values):
+    return values[:, :HEAD], values[:, HEAD:]
+
+
+def chunk_body(ids_ref, pieces, gain_ref, head_ref, keyval_ref, query_ref, outs, waits, recv=None):
+    rows_ref, direct_ref, tail_ref = outs[:3]
     count = pieces[0].shape[0]
     half = rows_ref.shape[1]
-    core, segment = ids_ref[0], ids_ref[1]
+    core, segment, tp = ids_ref[0], ids_ref[1], ids_ref[3]
     columns = query_ref.shape[1]
     top = (iota((count, 1), 0) < count // 2).astype(jnp.int32)
     mask = (top ^ core) == 1
@@ -144,23 +147,37 @@
     keyval = jnp.dot(rows_ref[...], keyval_ref[...], preferred_element_type=F32)
     even = jnp.concatenate([keyval[:, :HEAD], keyval[:, 2 * HEAD:3 * HEAD]], axis=1)
     odd = jnp.concatenate([keyval[:, HEAD:2 * HEAD], keyval[:, 3 * HEAD:]], axis=1)
-    own_ref[...] = jnp.where(segment == 0, even, odd)
-    other = jnp.where(segment == 0, odd, even).astype(BF16)
-    if len(sends) == 1:
-        sends[0][:, columns:] = other
+    own = jnp.where(segment == 0, even, odd)
+    other = jnp.where(segment == 0, odd, even)
+    if recv is None:
+        own_ref, send_ref = outs[3:5]
+        own_ref[...] = own
+        if len(outs) > 5:
+            outs[5][...] = other.astype(BF16)
+        else:
+            send_ref[:, columns:] = other.astype(BF16)
     else:
-        sends[1][...] = other
+        send_ref, keep_ref, first_ref, second_ref, far_first_ref, far_second_ref = outs[3:]
+        low, high = split_slots(own + recv)
+        keep_ref[...] = jnp.where(tp == 3, high, low).astype(BF16)
+        first_ref[...] = jnp.where(tp < 2, high, low).astype(BF16)
+        second_ref[...] = jnp.where(tp == 2, high, low).astype(BF16)
+        low, high = split_slots(other)
+        far_first_ref[...] = jnp.where(tp < 2, high, low).astype(BF16)
+        far_second_ref[...] = jnp.where(tp < 2, low, high).astype(BF16)
     waits = waits[keyval_ref.shape[1] // BLOCK:]
     for index in range(columns // BLOCK):
         if waits:
             waits[index]()
         at = slice(index * BLOCK, (index + 1) * BLOCK)
-        sends[0][:, at] = jnp.dot(rows_ref[...], query_ref[:, at], preferred_element_type=F32).astype(BF16)
+        send_ref[:, at] = jnp.dot(rows_ref[...], query_ref[:, at], preferred_element_type=F32).astype(BF16)
 
 
 def first_chunk_kernel(ids_ref, near_ref, far_ref, gain_hbm, head_hbm, keyval_hbm, query_hbm, *refs):
-    outs, (gain_ref, head_ref, keyval_ref, query_ref), (part_ref, small_sems, sems) = refs[:5], refs[5:9], refs[9:]
-    half = outs[0].shape[1]
+    outs, (gain_ref, head_ref, keyval_ref, query_ref) = refs[:4], refs[4:8]
+    own_query_ref, own_out_ref, rows_ref, part_ref, small_sems, sems, own_sems = refs[8:]
+    outs = (rows_ref, *outs)
+    half = rows_ref.shape[1]
     segment, tp = ids_ref[1], ids_ref[3]
     small = [
         pltpu.make_async_copy(
@@ -170,7 +187,8 @@
     blocks = keyval_ref.shape[1] // BLOCK
     large = column_copies(keyval_hbm, 0, keyval_ref, sems)
     large += column_copies(query_hbm, (1 - segment) * query_ref.shape[1], query_ref, sems.at[pl.ds(blocks, query_ref.shape[1] // BLOCK)])
-    for copy in small + large:
+    owns = column_copies(query_hbm, segment * query_ref.shape[1], own_query_ref, own_sems)
+    for copy in small + large + owns:
         copy.start()
     for copy in small:
         copy.wait()
@@ -183,6 +201,7 @@
 
     chunk_body(ids_ref, (near_ref, far_ref), gain_ref, head_ref, keyval_ref, query_ref, outs,
                [copy.wait for copy in large])
+    own_body(rows_ref, own_query_ref, own_out_ref, [copy.wait for copy in owns])
 
 
 def next_chunk_kernel(ids_ref, *refs, chips):
@@ -190,52 +209,78 @@
     chunk_body(ids_ref, pieces, *refs[:4], refs[4:], [])
 
 
-def chunk_shapes(rows, half, widths):
-    return (
-        jax.ShapeDtypeStruct((rows, half), BF16),
-        jax.ShapeDtypeStruct((rows, 2 * HEAD), F32),
-        jax.ShapeDtypeStruct((rows, LANES), F32),
-        jax.ShapeDtypeStruct((8, LANES), F32),
-    ) + tuple(jax.ShapeDtypeStruct((rows, width), BF16) for width in widths)
+def last_chunk_kernel(ids_ref, *refs, start):
+    pieces, refs = refs[:2], refs[2:]
+    count = pieces[0].shape[0] * 2
+    chunk_body(ids_ref, pieces, *refs[:4], refs[5:], [], refs[4][start:start + count, :].astype(F32))
+
+
+def shape_of(*shape, kind=BF16):
+    return jax.ShapeDtypeStruct(shape, kind)
+
+
+def chunk_shapes(rows, half):
+    return (shape_of(rows, half), shape_of(rows, LANES, kind=F32), shape_of(8, LANES, kind=F32))
 
 
 def first_chunk(ids, near, far, gain, head, keyval, query):
     count, wide = near.shape
     half = wide - LANES
     columns = query.shape[1] // 2
-    shapes = chunk_shapes(2 * count, half, (columns + 2 * HEAD,)) + tuple(
-        jax.ShapeDtypeStruct(shape, BF16) for shape in ((1, half), (1, half), keyval.shape, (half, columns)))
+    rows = 2 * count
+    shapes = chunk_shapes(rows, half)[1:] + (
+        shape_of(rows, 2 * HEAD, kind=F32), shape_of(rows, columns + 2 * HEAD),
+        shape_of(1, half), shape_of(1, half), shape_of(*keyval.shape), shape_of(half, columns),
+        shape_of(half, columns), shape_of(rows, columns, kind=F32))
     out = pl.pallas_call(
         first_chunk_kernel,
         out_shape=shapes,
         in_specs=[whole(pltpu.SMEM), whole(), whole()] + [whole(pltpu.HBM)] * 4,
         out_specs=(whole(),) * len(shapes),
         scratch_shapes=[
+            pltpu.VMEM((rows, half), BF16),
             pltpu.VMEM(head.shape, BF16),
             pltpu.SemaphoreType.DMA((2,)),
             pltpu.SemaphoreType.DMA(((columns + keyval.shape[1]) // BLOCK,)),
+            pltpu.SemaphoreType.DMA((columns // BLOCK,)),
         ],
-        compiler_params=pltpu.CompilerParams(vmem_limit_bytes=24 << 20),
+        compiler_params=pltpu.CompilerParams(vmem_limit_bytes=14 << 20),
         name="first_chunk",
     )(ids, near, far, gain, head, keyval, query)
-    return out[:5], out[5:]
+    return out[:4], out[4:8], out[8], out[9]
 
 
 def next_chunk(ids, pieces, weights):
     count, wide = pieces[0].shape
     chips = len(pieces) // 2
-    shapes = chunk_shapes(2 * chips * count, wide - LANES, (weights[3].shape[1], 2 * HEAD))
+    rows = 2 * chips * count
+    shapes = chunk_shapes(rows, wide - LANES) + (
+        shape_of(rows, 2 * HEAD, kind=F32), shape_of(rows, weights[3].shape[1]), shape_of(rows, 2 * HEAD))
     return pl.pallas_call(
         functools.partial(next_chunk_kernel, chips=chips),
         out_shape=shapes,
         in_specs=[whole(pltpu.SMEM)] + [whole()] * (len(pieces) + 4),
         out_specs=(whole(),) * len(shapes),
-        compiler_params=pltpu.CompilerParams(vmem_limit_bytes=24 << 20),
+        compiler_params=pltpu.CompilerParams(vmem_limit_bytes=14 << 20),
         name="next_chunk",
     )(ids, *pieces, *weights)
 
 
-def own_body(rows_ref, query_ref, out_ref, waits):
+def last_chunk(ids, pieces, weights, recv, start):
+    count, wide = pieces[0].shape
+    rows = 2 * count
+    shapes = chunk_shapes(rows, wide - LANES) + (shape_of(rows, weights[3].shape[1]),) + (shape_of(rows, HEAD),) * 5
+    return pl.pallas_call(
+        functools.partial(last_chunk_kernel, start=start),
+        out_shape=shapes,
+        in_specs=[whole(pltpu.SMEM)] + [whole()] * (len(pieces) + 5),
+        out_specs=(whole(),) * len(shapes),
+        compiler_params=pltpu.CompilerParams(vmem_limit_bytes=14 << 20),
+        name="last_chunk",
+    )(ids, *pieces, *weights, recv)
+
+
+def own_body(rows_ref, query_ref, out_ref, waits=()):
     for index in range(query_ref.shape[1] // BLOCK):
         if waits:
             waits[index]()
@@ -243,42 +288,14 @@
         out_ref[:, at] = jnp.dot(rows_ref[...], query_ref[:, at], preferred_element_type=F32)
 
 
-def first_own_kernel(ids_ref, rows_ref, query_hbm, out_ref, query_ref, sems):
-    copies = column_copies(query_hbm, ids_ref[1] * query_ref.shape[1], query_ref, sems)
-    for copy in copies:
-        copy.start()
-    own_body(rows_ref, query_ref, out_ref, [copy.wait for copy in copies])
-
-
-def next_own_kernel(rows_ref, query_ref, out_ref):
-    own_body(rows_ref, query_ref, out_ref, [])
-
-
-def first_own(ids, rows, query):
-    count, half = rows.shape
-    columns = query.shape[1] // 2
+def own_queries(rows, query):
     return pl.pallas_call(
-        first_own_kernel,
-        out_shape=(
-            jax.ShapeDtypeStruct((count, columns), F32),
-            jax.ShapeDtypeStruct((half, columns), BF16),
-        ),
-        in_specs=[whole(pltpu.SMEM), whole(), whole(pltpu.HBM)],
-        out_specs=(whole(), whole()),
-        scratch_shapes=[pltpu.SemaphoreType.DMA((columns // BLOCK,))],
-        compiler_params=pltpu.CompilerParams(vmem_limit_bytes=16 << 20),
-        name="first_own",
-    )(ids, rows, query)
-
-
-def next_own(rows, query):
-    return pl.pallas_call(
-        next_own_kernel,
-        out_shape=jax.ShapeDtypeStruct((rows.shape[0], query.shape[1]), F32),
+        own_body,
+        out_shape=shape_of(rows.shape[0], query.shape[1], kind=F32),
         in_specs=[whole(), whole()],
         out_specs=whole(),
-        compiler_params=pltpu.CompilerParams(vmem_limit_bytes=16 << 20),
-        name="next_own",
+        compiler_params=pltpu.CompilerParams(vmem_limit_bytes=10 << 20),
+        name="own_queries",
     )(rows, query)
 
 
@@ -291,57 +308,50 @@
     return jnp.concatenate([part[pack * count:(pack + 1) * count] for part in parts], axis=0)
 
 
-def keyval_kernel(ids_ref, *refs, starts, recv_starts):
-    chips = len(starts)
-    owns, recvs = refs[:chips], refs[chips:2 * chips]
-    keep_ref, first_ref, second_ref = refs[2 * chips:]
+def keyval_kernel(ids_ref, own_ref, next_ref, recv_own_ref, recv_next_ref, keep_ref, first_ref, second_ref):
     tp = ids_ref[3]
-    count = keep_ref.shape[0] // chips
-    mine = slabs(owns, starts, count)
-    theirs = [slabs((ref,), (start,), count, slice(ref.shape[1] - 2 * HEAD, ref.shape[1]))[0]
-              for ref, start in zip(recvs, recv_starts)]
-    sums = [own + recv for own, recv in zip(mine, theirs)]
-    both = jnp.concatenate([by_pack(sums, pack) for pack in range(2)], axis=0)
-    low, high = both[:, :HEAD], both[:, HEAD:]
+    count = own_ref.shape[0]
+    mine, x_part, y_part = slabs((own_ref, next_ref, next_ref), (0, 0, count), count)
+    width = recv_next_ref.shape[1]
+    at = slice(width - 2 * HEAD, width)
+    sums = [mine + recv_own_ref[:count, :].astype(F32), x_part + recv_next_ref[:, at].astype(F32), y_part]
+    low, high = split_slots(jnp.concatenate([by_pack(sums, pack) for pack in range(2)], axis=0))
     keep_ref[...] = jnp.where(tp == 3, high, low).astype(BF16)
     first_ref[...] = jnp.where(tp < 2, high, low).astype(BF16)
     second_ref[...] = jnp.where(tp == 2, high, low).astype(BF16)
 
 
-def sum_keyval(ids, owns, starts, recvs, recv_starts, count):
-    shape = jax.ShapeDtypeStruct((len(owns) * count, HEAD), BF16)
+def sum_keyval(ids, own, pair, recv_own, recv_next):
+    shape = shape_of(own.shape[0] + pair.shape[0], HEAD)
     return pl.pallas_call(
-        functools.partial(keyval_kernel, starts=starts, recv_starts=recv_starts),
+        keyval_kernel,
         out_shape=(shape, shape, shape),
-        in_specs=[whole(pltpu.SMEM)] + [whole()] * (2 * len(owns)),
+        in_specs=[whole(pltpu.SMEM)] + [whole()] * 4,
         out_specs=(whole(),) * 3,
         compiler_params=pltpu.CompilerParams(vmem_limit_bytes=8 << 20),
         name="sum_keyval",
-    )(ids, *owns, *recvs)
+    )(ids, own, pair, recv_own, recv_next)
 
 
 def owner_of(row, pack, ids_ref, piece_rows):
     index = jnp.zeros_like(row)
     for step in range(1, 8):
         index = index + (row >= step * piece_rows).astype(jnp.int32)
-    slot, low = index >> 1, index & 1
-    chip = slot ^ (slot >> 1)
+    chip, low = index >> 1, index & 1
     shard = (((chip >> 1) ^ ids_ref[2]) * 2 + (low ^ pack)) * 2 + ((chip & 1) ^ ids_ref[1])
     return shard, row - index * piece_rows
 
 
-def attention_kernel(ids_ref, lengths_ref, tail_ref, *refs, slot, starts, recv_starts, more):
+def attention_kernel(ids_ref, lengths_ref, tail_ref, *refs, starts, recv_starts):
     chips = len(starts)
     owns, recvs, directs = (refs[index * chips:(index + 1) * chips] for index in range(3))
     refs = refs[3 * chips:]
-    firsts, lates, gain_ref = refs[0:3], refs[3:6], refs[6]
-    before_ref = refs[7] if more else None
-    out_ref, bias_ref = refs[7 + more:]
+    earlies, lates, fars, gain_ref = refs[0:3], refs[3:6], refs[6:8], refs[8]
+    out_ref, bias_ref = refs[9:]
     segment, tp = ids_ref[1], ids_ref[3]
     rows = bias_ref.shape[1]
     slab = rows // 2
     queries = bias_ref.shape[0]
-    base = slot * (slab // 2)
     piece_rows = rows // 8
     heads = owns[0].shape[1] // HEAD
     devices = out_ref.shape[0]
@@ -355,7 +365,14 @@
         return (jnp.where(tp == 0, keep, jnp.where(tp == 2, second, first)),
                 jnp.where(tp == 3, keep, jnp.where(tp == 1, second, first)))
 
-    early, late = chosen_keys(firsts), chosen_keys(lates)
+    def pack_part(part, pack):
+        count = part.shape[0] // 2
+        return part[pack * count:(pack + 1) * count]
+
+    far_first, far_second = (ref[...].astype(F32) for ref in fars)
+    odd = (tp & 1) == 1
+    far = (jnp.where(odd, far_first, far_second), jnp.where(odd, far_second, far_first))
+    early, late = chosen_keys(earlies), chosen_keys(lates)
     through = jnp.zeros((devices, wide), F32)
     direct = jnp.zeros((devices, wide), F32)
     for pack in range(2):
@@ -370,14 +387,16 @@
                 doc = doc + (position >= end).astype(jnp.int32)
             return position, doc
 
-        row_position, row_doc = place(iota((queries, 1), 0) + base)
+        row_position, row_doc = place(iota((queries, 1), 0))
         col_position, col_doc = place(iota((1, rows), 1))
         visible = jnp.logical_and(row_doc == col_doc, col_position <= row_position)
         bias_ref[...] = jnp.where(visible, 0.0, -1e30)
         keys, values = (
-            jnp.concatenate([part[pack * (part.shape[0] // 2):(pack + 1) * (part.shape[0] // 2)]
-                             for part in parts], axis=0).astype(BF16)
-            for parts in zip(early, late))
+            jnp.concatenate([
+                pack_part(at_once, pack)[:slab],
+                pack_part(at_once, pack)[slab:] + pack_part(far_part, pack),
+                pack_part(late_part, pack)], axis=0).astype(BF16)
+            for at_once, far_part, late_part in zip(early, far, late))
         values = jnp.concatenate([values, jnp.ones((rows, HEAD), BF16)], axis=1)
         total = jnp.zeros((queries, HEAD), F32)
         for head in range(heads):
@@ -392,8 +411,8 @@
             offset = pl.multiple_of(segment * heads * HEAD + head * HEAD, HEAD)
             total = total + both[:, :HEAD] / both[:, HEAD:] * gain_ref[:, pl.ds(offset, HEAD)].astype(F32)
 
-        _, inner = owner_of(iota((queries, 1), 0) + base, pack, ids_ref, piece_rows)
-        shard_row, _ = owner_of(iota((1, queries), 1) + base, pack, ids_ref, piece_rows)
+        _, inner = owner_of(iota((queries, 1), 0), pack, ids_ref, piece_rows)
+        shard_row, _ = owner_of(iota((1, queries), 1), pack, ids_ref, piece_rows)
         chosen = ((iota((devices, 1), 0) >> 2) == shard_row).astype(F32)
         hit = lane == inner + pack * piece_rows
 
@@ -402,27 +421,21 @@
 
         through = through + send(jnp.sum(total, axis=1, keepdims=True))
         direct = direct + send(jnp.sum(by_pack(slabs(directs, starts, slab), pack), axis=1, keepdims=True))
-    if more:
-        through = through + before_ref[:, :wide]
-        direct = direct + before_ref[:, wide:]
     out_ref[:, :wide] = through
     out_ref[:, wide:] = direct
 
 
-def attention(ids, lengths, tail, owns, starts, recvs, recv_starts, directs, firsts, lates, gain, devices,
-              slot, before):
-    rows = firsts[0].shape[0] // 2 + lates[0].shape[0] // 2
-    queries = len(owns) * (rows // 4)
+def attention(ids, lengths, tail, owns, starts, recvs, recv_starts, directs, early, late, far, gain, devices):
+    rows = early[0].shape[0] // 2 + late[0].shape[0] // 2
     return pl.pallas_call(
-        functools.partial(
-            attention_kernel, slot=slot, starts=starts, recv_starts=recv_starts, more=len(before)),
-        out_shape=jax.ShapeDtypeStruct((devices, 2 * LANES), F32),
-        in_specs=[whole(pltpu.SMEM), whole(pltpu.SMEM)] + [whole()] * (8 + 3 * len(owns) + len(before)),
+        functools.partial(attention_kernel, starts=starts, recv_starts=recv_starts),
+        out_shape=shape_of(devices, 2 * LANES, kind=F32),
+        in_specs=[whole(pltpu.SMEM), whole(pltpu.SMEM)] + [whole()] * (10 + 3 * len(owns)),
         out_specs=whole(),
-        scratch_shapes=[pltpu.VMEM((queries, rows), F32)],
-        compiler_params=pltpu.CompilerParams(vmem_limit_bytes=24 << 20),
+        scratch_shapes=[pltpu.VMEM((rows, rows), F32)],
+        compiler_params=pltpu.CompilerParams(vmem_limit_bytes=14 << 20),
         name="attend",
-    )(ids, lengths, tail, *owns, *recvs, *directs, *firsts, *lates, gain, *before)
+    )(ids, lengths, tail, *owns, *recvs, *directs, *early, *late, *far, gain)
 
 
 def finish_kernel(recv_ref, send_ref, out_ref):
@@ -481,43 +494,53 @@
     from_d = lax.ppermute(from_x, "branch", y_pairs)
 
     slab = 2 * mine.shape[0]
-    local, direct, query, received = {}, {}, {}, {}
-    for name, pieces in (("own", (mine,)), ("xy", (from_x, from_y)), ("d", (from_d,))):
-        pieces = [part for piece in pieces for part in (piece, swap(piece))]
-        if name == "own":
-            out, weights = first_chunk(ids, *pieces, attn_gain, head_weight, wkv, wq)
-        else:
-            out = next_chunk(ids, pieces, weights)
-        rows, local[name], direct[name], lengths, *sends = out
-        if name == "xy":
-            tail = lengths
-        for index, part in reversed(list(enumerate(sends))):
-            sends[index] = across(part)
-        received[name] = sends
-        if name == "own":
-            query[name], own_weights = first_own(ids, rows, wq)
-        else:
-            query[name] = next_own(rows, own_weights)
-
-    keep, first, second = sum_keyval(
-        ids, [local["own"], local["xy"], local["d"]], (0, 0, 0),
-        [received["xy"][1], received["own"][0], received["xy"][1]], (0, 0, slab), slab)
-    hand_first, hand_second = [(0, 1), (2, 0), (1, 3), (3, 2)], [(2, 1), (1, 2)]
-    first = lax.ppermute(first, "tp", hand_first)
-    second = lax.ppermute(second, "tp", hand_second)
+
+    def with_swapped(*pieces):
+        return [part for piece in pieces for part in (piece, swap(piece))]
+
+    pieces = with_swapped(mine)
+    (direct_own, _, local_own, part), weights, own_weights, query_own = first_chunk(
+        ids, *pieces, attn_gain, head_weight, wkv, wq)
+    received_own = across(part)
+
+    pieces = with_swapped(from_x, from_y)
+    rows, direct_xy, tail, local_xy, part, keyval = next_chunk(ids, pieces, weights)
+    keyval_xy = across(keyval)
+    received_xy = across(part)
+    query_xy = own_queries(rows, own_weights)
+
+    keep, first, second = sum_keyval(ids, local_own, local_xy, keyval_xy, received_own)
+    hand_first, hand_second = (1, 3, 0, 2), (0, 2, 1, 3)
+    n_tp = len(hand_first)
+
+    def hand(array, targets):
+        return lax.ppermute(array, "tp", [(i, to) for i, to in enumerate(targets) if i != to])
+
+    def hand_across(array, targets):
+        return lax.ppermute(array, ("segment", "tp"), [
+            (side * n_tp + i, (1 - side) * n_tp + to) for side in range(2) for i, to in enumerate(targets)])
+
+    first = hand(first, hand_first)
+    second = hand(second, hand_second)
     early = (keep, first, second)
-    keep, first, second = sum_keyval(
-        ids, [local["xy"]], (slab,), [received["d"][1]], (0,), slab)
-    first = lax.ppermute(first, "tp", hand_first)
-    second = lax.ppermute(second, "tp", hand_second)
+
+    pieces = with_swapped(from_d)
+    rows, direct_d, _, part, keep, first, second, far_first, far_second = last_chunk(
+        ids, pieces, weights, keyval_xy, slab)
+    far_first = hand_across(far_first, hand_first)
+    far_second = hand_across(far_second, hand_second)
+    received_d = across(part)
+    first = hand(first, hand_first)
+    second = hand(second, hand_second)
     late = (keep, first, second)
-    devices = n_branch * 2 * lax.axis_size("tp")
+    query_d = own_queries(rows, own_weights)
+    devices = n_branch * 2 * n_tp
     outgoing = attention(
         ids, seq_lengths, tail,
-        [query["own"], query["xy"], query["d"], query["xy"]], (0, 0, 0, slab),
-        [received["xy"][0], received["own"][0], received["xy"][0], received["d"][0]], (0, 0, slab, 0),
-        [direct["own"], direct["xy"], direct["d"], direct["xy"]],
-        early, late, head_attn, devices, 0, [])
+        [query_own, query_xy, query_xy, query_d], (0, 0, slab, 0),
+        [received_xy, received_own, received_d, received_xy], (0, 0, 0, slab),
+        [direct_own, direct_xy, direct_xy, direct_d],
+        early, late, (far_first, far_second), head_attn, devices)
     incoming = lax.all_to_all(outgoing, ALL_AXES, split_axis=0, concat_axis=0, tiled=True)
     return finish(incoming, packing, n_branch)
 

time: 119 us -> 119 us (level)
  starting transfers between devices: 19.4 us -> 24.5 us
  blocking collectives: 12.6 us -> 9.91 us
  waiting for transfers between devices: 49.5 us -> 48.2 us
    ppermute x4 -> x6, starting transfers between devices: 6.98 us -> 12.7 us  [the longest x4 6.85 us: hand(): lax.ppermute(array, 'tp', [(i, to) for i, to in enumerate(targets) if i !...]
    pallas_call x1, Pallas kernels: 8.99 us -> 14.3 us  [first_chunk(): pl.pallas_call(first_chunk_kernel, out_shape=shapes, in_specs=[whole(pltp...]
    pallas_call x2 -> x1, Pallas kernels: 8.53 us -> 4.81 us  [next_chunk(): pl.pallas_call(functools.partial(next_chunk_kernel, chips=chips), out_sha...]
    all_to_all x1, blocking collectives: 12.6 us -> 9.91 us  [paired(): lax.all_to_all(outgoing, ALL_AXES, split_axis=0, concat_axis=0, tiled=True)]
    pallas_call x6 -> x5, Pallas kernels: 16 us -> 13.5 us  [the longest x1 5.53 us: attention(): pl.pallas_call(functools.partial(attention_kernel, starts=starts, recv_st...]
    ppermute x6 -> x5, waiting for transfers between devices: 36.8 us -> 35.5 us  [across(): return lax.ppermute(part, 'segment', x_pairs)]
    ppermute x6 -> x5, starting transfers between devices: 8.6 us -> 8.03 us  [across(): return lax.ppermute(part, 'segment', x_pairs)]
  transfers between devices with their start and end apart: 16 -> 17, of which waited for: 4 -> 3; matrix products, arithmetic and copies ran while one was open for 0% -> 0% of each run, Pallas kernels for 24% -> 23%
where the time goes in v4:
time: 119 us
  waiting for transfers between devices  48.2 us (41%)
  Pallas kernels  36 us (30%)
  starting transfers between devices  24.5 us (21%)
  blocking collectives  9.91 us (8%)
    ppermute x5, waiting for transfers between devices, across(): return lax.ppermute(part, 'segment', x_pairs)  35.5 us
    pallas_call x1, Pallas kernels, first_chunk(): pl.pallas_call(first_chunk_kernel, out_shape=shapes, in_specs=[whole(pltp...  14.3 us
    ppermute x1, waiting for transfers between devices, paired(): from_d = lax.ppermute(from_x, 'branch', y_pairs)  12.6 us
    all_to_all x1, blocking collectives, paired(): lax.all_to_all(outgoing, ALL_AXES, split_axis=0, concat_axis=0, tiled=True)  9.91 us
    ppermute x5, starting transfers between devices, across(): return lax.ppermute(part, 'segment', x_pairs)  8.03 us
    ppermute x4, starting transfers between devices, hand(): lax.ppermute(array, 'tp', [(i, to) for i, to in enumerate(targets) if i !...  6.85 us
    ppermute x2, starting transfers between devices, hand_across(): lax.ppermute(array, ('segment', 'tp'), [(side * n_tp + i, (1 - side) * n_...  5.85 us
    pallas_call x1, Pallas kernels, attention(): pl.pallas_call(functools.partial(attention_kernel, starts=starts, recv_st...  5.53 us
  transfers between devices with their start and end apart: 17, of which 3 were waited for; matrix products, arithmetic and copies ran while one was open for 0% of the time, Pallas kernels for 23%

profile of v4, /device:TPU:0, one launch (start us, length us, event | category | flops | bytes accessed | tf_op | source)
XLA Modules:
  0.0 118.9 jit_solution(7280879913116560854)
XLA Ops:
  0.0 0.1 pad_add_fusion.ids_ref
  0.1 2.5 %prepare.1 = (bf16[72,4224]{1,0:T(8,128)(2,1)S(1)}, bf16[72,4224]{1,0:T(8,128)(2,1)S(1)}) custom-call(s32[4]{0:T(128)S(1)} %pad_add_fusion.ids_ref, s32[1,6]{1,0:T(1,128)} %lengths_ref.3, bf16[72,8192]{1,0:T(8,128)(2,1)} %rows_hbm.1, s32[1,72]{1,0:T(1,128)} %bitcast.13), custom_call_target="tpu_custom_call" | custom-call | tf_op jit(solution)/shard_map/prepare/pallas_call | solution.py:85
  2.6 3.0 %collective-permute-start = (bf16[72,4224]{1,0:T(8,128)(2,1)S(1)}, bf16[72,4224]{1,0:T(8,128)(2,1)S(1)}, u32[]{:S(2)}, u32[]{:S(2)}) collective-permute-start(bf16[72,4224]{1,0:T(8,128)(2,1)S(1)} %get-tuple-element.33), channel_id=1, source_target_pairs={{0,4},{4,0},{1,5},{5,1},{2,6},{6,2},{3,7},{7,3},{8,12},{12,8},{9,1... | collective-permute-start | bytes 1824776 | tf_op jit(solution)/shard_map/ppermute | solution.py:482
  5.6 1.5 %collective-permute-start.2 = (bf16[72,4224]{1,0:T(8,128)(2,1)S(1)}, bf16[72,4224]{1,0:T(8,128)(2,1)S(1)}, u32[]{:S(2)}, u32[]{:S(2)}) collective-permute-start(bf16[72,4224]{1,0:T(8,128)(2,1)S(1)} %get-tuple-element.34.near_ref), channel_id=1, source_target_pairs={{0,16},{8,24},{16,0},{24,8},{1,17},{9,25},{17,1},{25,9},{2,18},{10... | collective-permute-start | bytes 1824776 | tf_op jit(solution)/shard_map/ppermute | solution.py:493
  7.2 12.2 %collective-permute-done.refs_0_ = bf16[72,4224]{1,0:T(8,128)(2,1)S(1)} collective-permute-done((bf16[72,4224]{1,0:T(8,128)(2,1)S(1)}, bf16[72,4224]{1,0:T(8,128)(2,1)S(1)}, u32[]{:S(2)}, u32[]{:S(2)}) %collective-permute-start) | collective-permute-done | bytes 608288 | tf_op jit(solution)/shard_map/ppermute | solution.py:482
  19.4 1.8 %collective-permute-start.5 = (bf16[72,4224]{1,0:T(8,128)(2,1)S(1)}, bf16[72,4224]{1,0:T(8,128)(2,1)S(1)}, u32[]{:S(2)}, u32[]{:S(2)}) collective-permute-start(bf16[72,4224]{1,0:T(8,128)(2,1)S(1)} %collective-permute-done.refs_0_), channel_id=1, source_target_pairs={{0,16},{8,24},{16,0},{24,8},{1,17},{9,25},{17,1},{25,9},{2,18},{10... | collective-permute-start | bytes 1824776 | tf_op jit(solution)/shard_map/ppermute | solution.py:494
  21.1 0.0 collective-permute-start.4
  21.1 0.5 collective-permute-start.1
  21.6 0.0 collective-permute-done.2.refs_2_
  21.6 0.0 collective-permute-start.3
  21.7 12.6 %collective-permute-done.5.refs_0_ = bf16[72,4224]{1,0:T(8,128)(2,1)S(1)} collective-permute-done((bf16[72,4224]{1,0:T(8,128)(2,1)S(1)}, bf16[72,4224]{1,0:T(8,128)(2,1)S(1)}, u32[]{:S(2)}, u32[]{:S(2)}) %collective-permute-start.5) | collective-permute-done | bytes 608288 | tf_op jit(solution)/shard_map/ppermute | solution.py:494
  34.2 0.0 collective-permute-start.6
  34.2 0.0 collective-permute-done.4.far_ref
  34.3 14.3 %first_chunk.1 = (f32[144,128]{1,0:T(8,128)S(1)}, f32[8,128]{1,0:T(8,128)}, f32[144,256]{1,0:T(8,128)S(1)}, bf16[144,1280]{1,0:T(8,128)(2,1)S(1)}, bf16[1,4096]{...) custom-call(s32[4]{0:T(128)S(1)} %pad_add_fusion.ids_ref, ...), custom_call_target="tpu_custom_call" | custom-call | tf_op jit(solution)/shard_map/first_chunk/pallas_call | solution.py:235
  48.6 0.0 collective-permute-done.1.refs_1_
  48.6 0.0 collective-permute-done.3.refs_3_
  48.6 4.8 %next_chunk.1 = (bf16[288,4096]{1,0:T(8,128)(2,1)S(1)}, f32[288,128]{1,0:T(8,128)S(1)}, f32[8,128]{1,0:T(8,128)S(1)}, f32[288,256]{1,0:T(8,128)S(1)}, bf16[288,1...) custom-call(s32[4]{0:T(128)S(1)} %pad_add_fusion.ids_ref, bf16[72,4224]{1,0:T(8,128)(2,1)S(1)} %collective-permute-done.refs_0_, ...), custom_call_target="tpu_custom_call" | custom-call | tf_op jit(solution)/shard_map/next_chunk/pallas_call | solution.py:259
  53.4 1.5 %collective-permute-start.8 = (bf16[288,1024]{1,0:T(8,128)(2,1)S(1)}, bf16[288,1024]{1,0:T(8,128)(2,1)S(1)}, u32[]{:S(2)}, u32[]{:S(2)}) collective-permute-start(bf16[288,1024]{1,0:T(8,128)(2,1)S(1)} %get-tuple-element.45), channel_id=1, source_target_pairs={{0,4},{4,0},{1,5},{5,1},{2,6},{6,2},{3,7},{7,3},{8,12},{12,8},{9,1... | collective-permute-start | bytes 1769480 | tf_op jit(solution)/shard_map/ppermute | solution.py:482
  54.9 0.6 collective-permute-start.9
  55.5 1.5 %collective-permute-start.7 = (bf16[288,256]{1,0:T(8,128)(2,1)S(1)}, bf16[288,256]{1,0:T(8,128)(2,1)S(1)}, u32[]{:S(2)}, u32[]{:S(2)}) collective-permute-start(bf16[288,256]{1,0:T(8,128)(2,1)S(1)} %get-tuple-element.43), channel_id=1, source_target_pairs={{0,4},{4,0},{1,5},{5,1},{2,6},{6,2},{3,7},{7,3},{8,12},{12,8},{9,1... | collective-permute-start | bytes 442376 | tf_op jit(solution)/shard_map/ppermute | solution.py:482
  57.0 23.3 %collective-permute-done.7.refs_6_.recv_own_ref = bf16[288,256]{1,0:T(8,128)(2,1)S(1)} collective-permute-done((bf16[288,256]{1,0:T(8,128)(2,1)S(1)}, bf16[288,256]{1,0:T(8,128)(2,1)S(1)}, u32[]{:S(2)}, u32[]{:S(2)}) %collective-permute-start.7) | collective-permute-done | bytes 147488 | tf_op jit(solution)/shard_map/ppermute | solution.py:482
  80.3 0.0 collective-permute-done.6.refs_1_
  80.3 3.3 %last_chunk.1 = (bf16[144,4096]{1,0:T(8,128)(2,1)S(1)}, f32[144,128]{1,0:T(8,128)S(1)}, f32[8,128]{1,0:T(8,128)}, bf16[144,1024]{1,0:T(8,128)(2,1)S(1)}, bf16[14...) custom-call(s32[4]{0:T(128)S(1)} %pad_add_fusion.ids_ref, ...), custom_call_target="tpu_custom_call" | custom-call | tf_op jit(solution)/shard_map/last_chunk/pallas_call | solution.py:273
  83.6 1.5 %collective-permute-start.10 = (bf16[144,1024]{1,0:T(8,128)(2,1)S(1)}, bf16[144,1024]{1,0:T(8,128)(2,1)S(1)}, u32[]{:S(2)}, u32[]{:S(2)}) collective-permute-start(bf16[144,1024]{1,0:T(8,128)(2,1)S(1)} %get-tuple-element.47), channel_id=1, source_target_pairs={{0,4},{4,0},{1,5},{5,1},{2,6},{6,2},{3,7},{7,3},{8,12},{12,8},{9,1... | collective-permute-start | bytes 884744 | tf_op jit(solution)/shard_map/ppermute | solution.py:482
  85.0 0.0 collective-permute-done.9.recv_next_ref.refs_5_
  85.0 0.6 sum_keyval.1
  85.7 1.6 %collective-permute-start.11 = (bf16[432,128]{1,0:T(8,128)(2,1)S(1)}, bf16[432,128]{1,0:T(8,128)(2,1)S(1)}, u32[]{:S(2)}, u32[]{:S(2)}) collective-permute-start(bf16[432,128]{1,0:T(8,128)(2,1)S(1)} %get-tuple-element.54), channel_id=1, source_target_pairs={{0,1},{1,3},{2,0},{3,2},{4,5},{5,7},{6,4},{7,6},{8,9},{9,11},{10,8... | collective-permute-start | bytes 331784 | tf_op jit(solution)/shard_map/ppermute | solution.py:517
  87.3 0.7 collective-permute-start.12
  88.0 3.9 %collective-permute-start.13 = (bf16[144,128]{1,0:T(8,128)(2,1)S(1)}, bf16[144,128]{1,0:T(8,128)(2,1)S(1)}, u32[]{:S(2)}, u32[]{:S(2)}) collective-permute-start(bf16[144,128]{1,0:T(8,128)(2,1)S(1)} %get-tuple-element.57), channel_id=1, source_target_pairs={{0,1},{1,3},{2,0},{3,2},{4,5},{5,7},{6,4},{7,6},{8,9},{9,11},{10,8... | collective-permute-start | bytes 110600 | tf_op jit(solution)/shard_map/ppermute | solution.py:517
  91.9 0.0 collective-permute-done.11.refs_13_
  91.9 0.7 collective-permute-start.14
  92.5 0.0 collective-permute-done.12.refs_14_
  92.5 4.3 %collective-permute-start.15 = (bf16[144,128]{1,0:T(8,128)(2,1)S(1)}, bf16[144,128]{1,0:T(8,128)(2,1)S(1)}, u32[]{:S(2)}, u32[]{:S(2)}) collective-permute-start(bf16[144,128]{1,0:T(8,128)(2,1)S(1)} %get-tuple-element.59), channel_id=1, source_target_pairs={{0,5},{1,7},{2,4},{3,6},{4,1},{5,3},{6,0},{7,2},{8,13},{9,15},{10,... | collective-permute-start | bytes 110600 | tf_op jit(solution)/shard_map/ppermute | solution.py:520
  96.9 0.0 collective-permute-done.8.refs_4_.refs_7_
  96.9 1.5 %collective-permute-start.16 = (bf16[144,128]{1,0:T(8,128)(2,1)S(1)}, bf16[144,128]{1,0:T(8,128)(2,1)S(1)}, u32[]{:S(2)}, u32[]{:S(2)}) collective-permute-start(bf16[144,128]{1,0:T(8,128)(2,1)S(1)} %get-tuple-element.60), channel_id=1, source_target_pairs={{0,4},{1,6},{2,5},{3,7},{4,0},{5,2},{6,1},{7,3},{8,12},{9,14},{10,... | collective-permute-start | bytes 110600 | tf_op jit(solution)/shard_map/ppermute | solution.py:520
  98.4 2.6 %own_queries.2.refs_1_.refs_2_ = f32[288,1024]{1,0:T(8,128)S(1)} custom-call(bf16[288,4096]{1,0:T(8,128)(2,1)S(1)} %get-tuple-element.41.rows_ref, bf16[4096,1024]{1,0:T(8,128)(2,1)S(1)} %get-tuple-element.42.query_ref), custom_call_target="tpu_custom_call" | custom-call | tf_op jit(solution)/shard_map/own_queries/pallas_call | solution.py:292
  101.0 0.0 copy-start
  101.0 1.4 %own_queries.3.refs_3_ = f32[144,1024]{1,0:T(8,128)S(1)} custom-call(bf16[144,4096]{1,0:T(8,128)(2,1)S(1)} %get-tuple-element.44.rows_ref, bf16[4096,1024]{1,0:T(8,128)(2,1)S(1)} %get-tuple-element.42.query_ref), custom_call_target="tpu_custom_call" | custom-call | tf_op jit(solution)/shard_map/own_queries/pallas_call | solution.py:292
  102.4 0.0 copy-start.1
  102.4 0.0 collective-permute-done.13.refs_16_
  102.5 0.0 collective-permute-done.14.refs_17_
  102.5 0.0 collective-permute-done.15.refs_18_
  102.5 0.0 collective-permute-done.16.refs_19_
  102.5 0.0 collective-permute-done.10.refs_6_
  102.5 0.0 copy-done
  102.5 5.5 %attend.1 = f32[32,256]{1,0:T(8,128)S(1)} custom-call(s32[4]{0:T(128)S(1)} %pad_add_fusion.ids_ref, s32[1,6]{1,0:T(1,128)} %lengths_ref.3, f32[8,128]{1,0:T(8,128)S(1)} %get-tuple-element.39.tail_ref, f32[144,1024]{1,0:T(8,128)S(1)} %get-tuple-element.40.refs_0_, f32[288,1024]{1,0:T(8,128)S(1)} %own_queries.2.refs_1_.refs_2_, ...), custom_call_target="tpu_custom_call" | custom-call | tf_op jit(solution)/shard_map/attend/pallas_call | solution.py:430
  108.1 9.9 %all_to_all.11 = f32[32,1,256]{2,1,0:T(1,128)S(1)} all-to-all(f32[32,1,256]{2,1,0:T(1,128)S(1)} %copy.9), channel_id=1, replica_groups=mesh['branch'=4,'segment'=2,'tp'=4] {'branch','segment','tp'}, dimensions={0} | all-to-all | bytes 65536 | tf_op jit(solution)/shard_map/all_to_all | solution.py:544
  118.0 0.0 copy-done.1
  118.0 0.9 finish.1
  (2 shorter events, 0.0 us)
Async XLA Ops:
  2.6 16.8 %collective-permute-start = (bf16[72,4224]{1,0:T(8,128)(2,1)S(1)}, bf16[72,4224]{1,0:T(8,128)(2,1)S(1)}, u32[]{:S(2)}, u32[]{:S(2)}) collective-permute-start(bf16[72,4224]{1,0:T(8,128)(2,1)S(1)} %get-tuple-element.33), channel_id=1, source_target_pairs={{0,4},{4,0},{1,5},{5,1},{2,6},{6,2},{3,7},{7,3},{8,12},{12,8},{9,1... | collective-permute-start | bytes 1824776 | tf_op jit(solution)/shard_map/ppermute | solution.py:482
  5.6 16.0 %collective-permute-start.2 = (bf16[72,4224]{1,0:T(8,128)(2,1)S(1)}, bf16[72,4224]{1,0:T(8,128)(2,1)S(1)}, u32[]{:S(2)}, u32[]{:S(2)}) collective-permute-start(bf16[72,4224]{1,0:T(8,128)(2,1)S(1)} %get-tuple-element.34.near_ref), channel_id=1, source_target_pairs={{0,16},{8,24},{16,0},{24,8},{1,17},{9,25},{17,1},{25,9},{2,18},{10... | collective-permute-start | bytes 1824776 | tf_op jit(solution)/shard_map/ppermute | solution.py:493
  19.4 14.9 %collective-permute-start.5 = (bf16[72,4224]{1,0:T(8,128)(2,1)S(1)}, bf16[72,4224]{1,0:T(8,128)(2,1)S(1)}, u32[]{:S(2)}, u32[]{:S(2)}) collective-permute-start(bf16[72,4224]{1,0:T(8,128)(2,1)S(1)} %collective-permute-done.refs_0_), channel_id=1, source_target_pairs={{0,16},{8,24},{16,0},{24,8},{1,17},{9,25},{17,1},{25,9},{2,18},{10... | collective-permute-start | bytes 1824776 | tf_op jit(solution)/shard_map/ppermute | solution.py:494
  21.1 13.1 %collective-permute-start.4 = (bf16[72,4224]{1,0:T(8,128)(2,1)S(1)}, bf16[72,4224]{1,0:T(8,128)(2,1)S(1)}, u32[]{:S(2)}, u32[]{:S(2)}) collective-permute-start(bf16[72,4224]{1,0:T(8,128)(2,1)S(1)} %get-tuple-element.34.near_ref), channel_id=1, source_target_pairs={{0,8},{8,0},{16,24},{24,16},{1,9},{9,1},{17,25},{25,17},{2,10},{10... | collective-permute-start | bytes 1824776 | tf_op jit(solution)/shard_map/ppermute | solution.py:479
  21.1 27.4 %collective-permute-start.1 = (bf16[72,4224]{1,0:T(8,128)(2,1)S(1)}, bf16[72,4224]{1,0:T(8,128)(2,1)S(1)}, u32[]{:S(2)}, u32[]{:S(2)}) collective-permute-start(bf16[72,4224]{1,0:T(8,128)(2,1)S(1)} %collective-permute-done.refs_0_), channel_id=1, source_target_pairs={{0,8},{8,0},{16,24},{24,16},{1,9},{9,1},{17,25},{25,17},{2,10},{10... | collective-permute-start | bytes 1824776 | tf_op jit(solution)/shard_map/ppermute | solution.py:479
  21.6 26.9 %collective-permute-start.3 = (bf16[72,4224]{1,0:T(8,128)(2,1)S(1)}, bf16[72,4224]{1,0:T(8,128)(2,1)S(1)}, u32[]{:S(2)}, u32[]{:S(2)}) collective-permute-start(bf16[72,4224]{1,0:T(8,128)(2,1)S(1)} %collective-permute-done.2.refs_2_), channel_id=1, source_target_pairs={{0,8},{8,0},{16,24},{24,16},{1,9},{9,1},{17,25},{25,17},{2,10},{10... | collective-permute-start | bytes 1824776 | tf_op jit(solution)/shard_map/ppermute | solution.py:479
  34.2 46.0 %collective-permute-start.6 = (bf16[72,4224]{1,0:T(8,128)(2,1)S(1)}, bf16[72,4224]{1,0:T(8,128)(2,1)S(1)}, u32[]{:S(2)}, u32[]{:S(2)}) collective-permute-start(bf16[72,4224]{1,0:T(8,128)(2,1)S(1)} %collective-permute-done.5.refs_0_), channel_id=1, source_target_pairs={{0,8},{8,0},{16,24},{24,16},{1,9},{9,1},{17,25},{25,17},{2,10},{10... | collective-permute-start | bytes 1824776 | tf_op jit(solution)/shard_map/ppermute | solution.py:479
  53.4 43.5 %collective-permute-start.8 = (bf16[288,1024]{1,0:T(8,128)(2,1)S(1)}, bf16[288,1024]{1,0:T(8,128)(2,1)S(1)}, u32[]{:S(2)}, u32[]{:S(2)}) collective-permute-start(bf16[288,1024]{1,0:T(8,128)(2,1)S(1)} %get-tuple-element.45), channel_id=1, source_target_pairs={{0,4},{4,0},{1,5},{5,1},{2,6},{6,2},{3,7},{7,3},{8,12},{12,8},{9,1... | collective-permute-start | bytes 1769480 | tf_op jit(solution)/shard_map/ppermute | solution.py:482
  54.9 30.1 %collective-permute-start.9 = (bf16[144,1280]{1,0:T(8,128)(2,1)S(1)}, bf16[144,1280]{1,0:T(8,128)(2,1)S(1)}, u32[]{:S(2)}, u32[]{:S(2)}) collective-permute-start(bf16[144,1280]{1,0:T(8,128)(2,1)S(1)} %get-tuple-element.46), channel_id=1, source_target_pairs={{0,4},{4,0},{1,5},{5,1},{2,6},{6,2},{3,7},{7,3},{8,12},{12,8},{9,1... | collective-permute-start | bytes 1105928 | tf_op jit(solution)/shard_map/ppermute | solution.py:482
  55.5 24.8 %collective-permute-start.7 = (bf16[288,256]{1,0:T(8,128)(2,1)S(1)}, bf16[288,256]{1,0:T(8,128)(2,1)S(1)}, u32[]{:S(2)}, u32[]{:S(2)}) collective-permute-start(bf16[288,256]{1,0:T(8,128)(2,1)S(1)} %get-tuple-element.43), channel_id=1, source_target_pairs={{0,4},{4,0},{1,5},{5,1},{2,6},{6,2},{3,7},{7,3},{8,12},{12,8},{9,1... | collective-permute-start | bytes 442376 | tf_op jit(solution)/shard_map/ppermute | solution.py:482
  83.6 18.9 %collective-permute-start.10 = (bf16[144,1024]{1,0:T(8,128)(2,1)S(1)}, bf16[144,1024]{1,0:T(8,128)(2,1)S(1)}, u32[]{:S(2)}, u32[]{:S(2)}) collective-permute-start(bf16[144,1024]{1,0:T(8,128)(2,1)S(1)} %get-tuple-element.47), channel_id=1, source_target_pairs={{0,4},{4,0},{1,5},{5,1},{2,6},{6,2},{3,7},{7,3},{8,12},{12,8},{9,1... | collective-permute-start | bytes 884744 | tf_op jit(solution)/shard_map/ppermute | solution.py:482
  85.7 6.2 %collective-permute-start.11 = (bf16[432,128]{1,0:T(8,128)(2,1)S(1)}, bf16[432,128]{1,0:T(8,128)(2,1)S(1)}, u32[]{:S(2)}, u32[]{:S(2)}) collective-permute-start(bf16[432,128]{1,0:T(8,128)(2,1)S(1)} %get-tuple-element.54), channel_id=1, source_target_pairs={{0,1},{1,3},{2,0},{3,2},{4,5},{5,7},{6,4},{7,6},{8,9},{9,11},{10,8... | collective-permute-start | bytes 331784 | tf_op jit(solution)/shard_map/ppermute | solution.py:517
  87.3 5.2 %collective-permute-start.12 = (bf16[432,128]{1,0:T(8,128)(2,1)S(1)}, bf16[432,128]{1,0:T(8,128)(2,1)S(1)}, u32[]{:S(2)}, u32[]{:S(2)}) collective-permute-start(bf16[432,128]{1,0:T(8,128)(2,1)S(1)} %get-tuple-element.55), channel_id=1, source_target_pairs={{1,2},{2,1},{5,6},{6,5},{9,10},{10,9},{13,14},{14,13},{17,18},{18,... | collective-permute-start | bytes 331784 | tf_op jit(solution)/shard_map/ppermute | solution.py:517
  88.0 14.5 %collective-permute-start.13 = (bf16[144,128]{1,0:T(8,128)(2,1)S(1)}, bf16[144,128]{1,0:T(8,128)(2,1)S(1)}, u32[]{:S(2)}, u32[]{:S(2)}) collective-permute-start(bf16[144,128]{1,0:T(8,128)(2,1)S(1)} %get-tuple-element.57), channel_id=1, source_target_pairs={{0,1},{1,3},{2,0},{3,2},{4,5},{5,7},{6,4},{7,6},{8,9},{9,11},{10,8... | collective-permute-start | bytes 110600 | tf_op jit(solution)/shard_map/ppermute | solution.py:517
  91.9 10.6 %collective-permute-start.14 = (bf16[144,128]{1,0:T(8,128)(2,1)S(1)}, bf16[144,128]{1,0:T(8,128)(2,1)S(1)}, u32[]{:S(2)}, u32[]{:S(2)}) collective-permute-start(bf16[144,128]{1,0:T(8,128)(2,1)S(1)} %get-tuple-element.58), channel_id=1, source_target_pairs={{1,2},{2,1},{5,6},{6,5},{9,10},{10,9},{13,14},{14,13},{17,18},{18,... | collective-permute-start | bytes 110600 | tf_op jit(solution)/shard_map/ppermute | solution.py:517
  92.5 9.9 %collective-permute-start.15 = (bf16[144,128]{1,0:T(8,128)(2,1)S(1)}, bf16[144,128]{1,0:T(8,128)(2,1)S(1)}, u32[]{:S(2)}, u32[]{:S(2)}) collective-permute-start(bf16[144,128]{1,0:T(8,128)(2,1)S(1)} %get-tuple-element.59), channel_id=1, source_target_pairs={{0,5},{1,7},{2,4},{3,6},{4,1},{5,3},{6,0},{7,2},{8,13},{9,15},{10,... | collective-permute-start | bytes 110600 | tf_op jit(solution)/shard_map/ppermute | solution.py:520
  96.9 5.6 %collective-permute-start.16 = (bf16[144,128]{1,0:T(8,128)(2,1)S(1)}, bf16[144,128]{1,0:T(8,128)(2,1)S(1)}, u32[]{:S(2)}, u32[]{:S(2)}) collective-permute-start(bf16[144,128]{1,0:T(8,128)(2,1)S(1)} %get-tuple-element.60), channel_id=1, source_target_pairs={{0,4},{1,6},{2,5},{3,7},{4,0},{5,2},{6,1},{7,3},{8,12},{9,14},{10,... | collective-permute-start | bytes 110600 | tf_op jit(solution)/shard_map/ppermute | solution.py:520
  101.0 1.5 %copy-start = (bf16[1,2048]{1,0:T(2,128)(2,1)S(1)}, bf16[1,2048]{1,0:T(2,128)(2,1)}, u32[]{:S(2)}) copy-start(bf16[1,2048]{1,0:T(2,128)(2,1)} %refs_20_.1) | copy-start | bytes 12292
  102.4 15.6 %copy-start.1 = (s32[72]{0:T(128)S(1)}, s32[72]{0:T(128)}, u32[]{:S(2)}) copy-start(s32[72]{0:T(128)} %param.9) | copy-start | bytes 868

commit v5 on v4

--- a/solution.py
+++ b/solution.py
@@ -98,6 +98,7 @@
 
 
 BLOCK = 256
+IN_FLIGHT = 4
 
 
 def column_copies(source, first, target, sems):
@@ -188,8 +189,19 @@
     large = column_copies(keyval_hbm, 0, keyval_ref, sems)
     large += column_copies(query_hbm, (1 - segment) * query_ref.shape[1], query_ref, sems.at[pl.ds(blocks, query_ref.shape[1] // BLOCK)])
     owns = column_copies(query_hbm, segment * query_ref.shape[1], own_query_ref, own_sems)
-    for copy in small + large + owns:
+    copies = large + owns
+    for copy in small + copies[:IN_FLIGHT]:
         copy.start()
+
+    def waiter(index):
+        def wait():
+            copies[index].wait()
+            if index + IN_FLIGHT < len(copies):
+                copies[index + IN_FLIGHT].start()
+
+        return wait
+
+    waits = [waiter(index) for index in range(len(copies))]
     for copy in small:
         copy.wait()
     width = part_ref.shape[1]
@@ -200,8 +212,8 @@
         head_ref[:, pl.ds(pl.multiple_of((tp * width) % half, width), width)] = part_ref[...]
 
     chunk_body(ids_ref, (near_ref, far_ref), gain_ref, head_ref, keyval_ref, query_ref, outs,
-               [copy.wait for copy in large])
-    own_body(rows_ref, own_query_ref, own_out_ref, [copy.wait for copy in owns])
+               waits[:len(large)])
+    own_body(rows_ref, own_query_ref, own_out_ref, waits[len(large):])
 
 
 def next_chunk_kernel(ids_ref, *refs, chips):

time: 119 us -> 116 us (0.975)
  Pallas kernels: 36 us -> 32.9 us
    pallas_call x1, Pallas kernels: 14.3 us -> 11.2 us  [first_chunk(): pl.pallas_call(first_chunk_kernel, out_shape=shapes, in_specs=[whole(pltp...]
  transfers between devices with their start and end apart: 17 -> 17, of which waited for: 3 -> 3; matrix products, arithmetic and copies ran while one was open for 0% -> 0% of each run, Pallas kernels for 23% -> 21%
where the time goes in v5:
time: 116 us
  waiting for transfers between devices  48.1 us (41%)
  Pallas kernels  32.9 us (28%)
  starting transfers between devices  24.7 us (21%)
  blocking collectives  9.9 us (9%)
    ppermute x5, waiting for transfers between devices, across(): return lax.ppermute(part, 'segment', x_pairs)  35.5 us
    ppermute x1, waiting for transfers between devices, paired(): from_d = lax.ppermute(from_x, 'branch', y_pairs)  12.6 us
    pallas_call x1, Pallas kernels, first_chunk(): pl.pallas_call(first_chunk_kernel, out_shape=shapes, in_specs=[whole(pltp...  11.2 us
    all_to_all x1, blocking collectives, paired(): lax.all_to_all(outgoing, ALL_AXES, split_axis=0, concat_axis=0, tiled=True)  9.9 us
    ppermute x5, starting transfers between devices, across(): return lax.ppermute(part, 'segment', x_pairs)  8.16 us
    ppermute x4, starting transfers between devices, hand(): lax.ppermute(array, 'tp', [(i, to) for i, to in enumerate(targets) if i !...  6.84 us
    ppermute x2, starting transfers between devices, hand_across(): lax.ppermute(array, ('segment', 'tp'), [(side * n_tp + i, (1 - side) * n_...  5.85 us
    pallas_call x1, Pallas kernels, attention(): pl.pallas_call(functools.partial(attention_kernel, starts=starts, recv_st...  5.53 us
  transfers between devices with their start and end apart: 17, of which 3 were waited for; matrix products, arithmetic and copies ran while one was open for 0% of the time, Pallas kernels for 21%

profile of v5, /device:TPU:0, one launch (start us, length us, event | category | flops | bytes accessed | tf_op | source)
XLA Modules:
  0.0 115.9 jit_solution(9931762670390955771)
XLA Ops:
  0.0 0.1 pad_add_fusion.ids_ref
  0.1 2.5 %prepare.1 = (bf16[72,4224]{1,0:T(8,128)(2,1)S(1)}, bf16[72,4224]{1,0:T(8,128)(2,1)S(1)}) custom-call(s32[4]{0:T(128)S(1)} %pad_add_fusion.ids_ref, s32[1,6]{1,0:T(1,128)} %lengths_ref.3, bf16[72,8192]{1,0:T(8,128)(2,1)} %rows_hbm.1, s32[1,72]{1,0:T(1,128)} %bitcast.13), custom_call_target="tpu_custom_call" | custom-call | tf_op jit(solution)/shard_map/prepare/pallas_call | solution.py:85
  2.6 3.0 %collective-permute-start = (bf16[72,4224]{1,0:T(8,128)(2,1)S(1)}, bf16[72,4224]{1,0:T(8,128)(2,1)S(1)}, u32[]{:S(2)}, u32[]{:S(2)}) collective-permute-start(bf16[72,4224]{1,0:T(8,128)(2,1)S(1)} %get-tuple-element.33), channel_id=1, source_target_pairs={{0,4},{4,0},{1,5},{5,1},{2,6},{6,2},{3,7},{7,3},{8,12},{12,8},{9,1... | collective-permute-start | bytes 1824776 | tf_op jit(solution)/shard_map/ppermute | solution.py:494
  5.6 1.5 %collective-permute-start.2 = (bf16[72,4224]{1,0:T(8,128)(2,1)S(1)}, bf16[72,4224]{1,0:T(8,128)(2,1)S(1)}, u32[]{:S(2)}, u32[]{:S(2)}) collective-permute-start(bf16[72,4224]{1,0:T(8,128)(2,1)S(1)} %get-tuple-element.34.near_ref), channel_id=1, source_target_pairs={{0,16},{8,24},{16,0},{24,8},{1,17},{9,25},{17,1},{25,9},{2,18},{10... | collective-permute-start | bytes 1824776 | tf_op jit(solution)/shard_map/ppermute | solution.py:505
  7.2 12.2 %collective-permute-done.refs_0_ = bf16[72,4224]{1,0:T(8,128)(2,1)S(1)} collective-permute-done((bf16[72,4224]{1,0:T(8,128)(2,1)S(1)}, bf16[72,4224]{1,0:T(8,128)(2,1)S(1)}, u32[]{:S(2)}, u32[]{:S(2)}) %collective-permute-start) | collective-permute-done | bytes 608288 | tf_op jit(solution)/shard_map/ppermute | solution.py:494
  19.4 1.8 %collective-permute-start.5 = (bf16[72,4224]{1,0:T(8,128)(2,1)S(1)}, bf16[72,4224]{1,0:T(8,128)(2,1)S(1)}, u32[]{:S(2)}, u32[]{:S(2)}) collective-permute-start(bf16[72,4224]{1,0:T(8,128)(2,1)S(1)} %collective-permute-done.refs_0_), channel_id=1, source_target_pairs={{0,16},{8,24},{16,0},{24,8},{1,17},{9,25},{17,1},{25,9},{2,18},{10... | collective-permute-start | bytes 1824776 | tf_op jit(solution)/shard_map/ppermute | solution.py:506
  21.1 0.0 collective-permute-start.4
  21.1 0.5 collective-permute-start.1
  21.6 0.0 collective-permute-done.2.refs_2_
  21.6 0.0 collective-permute-start.3
  21.7 12.6 %collective-permute-done.5.refs_0_ = bf16[72,4224]{1,0:T(8,128)(2,1)S(1)} collective-permute-done((bf16[72,4224]{1,0:T(8,128)(2,1)S(1)}, bf16[72,4224]{1,0:T(8,128)(2,1)S(1)}, u32[]{:S(2)}, u32[]{:S(2)}) %collective-permute-start.5) | collective-permute-done | bytes 608288 | tf_op jit(solution)/shard_map/ppermute | solution.py:506
  34.2 0.0 collective-permute-start.6
  34.2 0.0 collective-permute-done.4.far_ref
  34.3 11.2 %first_chunk.1 = (f32[144,128]{1,0:T(8,128)S(1)}, f32[8,128]{1,0:T(8,128)}, f32[144,256]{1,0:T(8,128)S(1)}, bf16[144,1280]{1,0:T(8,128)(2,1)S(1)}, bf16[1,4096]{...) custom-call(s32[4]{0:T(128)S(1)} %pad_add_fusion.ids_ref, ...), custom_call_target="tpu_custom_call" | custom-call | tf_op jit(solution)/shard_map/first_chunk/pallas_call | solution.py:247
  45.5 0.0 collective-permute-done.1.refs_1_
  45.5 0.0 collective-permute-done.3.refs_3_
  45.5 4.8 %next_chunk.1 = (bf16[288,4096]{1,0:T(8,128)(2,1)S(1)}, f32[288,128]{1,0:T(8,128)S(1)}, f32[8,128]{1,0:T(8,128)S(1)}, f32[288,256]{1,0:T(8,128)S(1)}, bf16[288,1...) custom-call(s32[4]{0:T(128)S(1)} %pad_add_fusion.ids_ref, bf16[72,4224]{1,0:T(8,128)(2,1)S(1)} %collective-permute-done.refs_0_, ...), custom_call_target="tpu_custom_call" | custom-call | tf_op jit(solution)/shard_map/next_chunk/pallas_call | solution.py:271
  50.3 1.6 %collective-permute-start.8 = (bf16[288,1024]{1,0:T(8,128)(2,1)S(1)}, bf16[288,1024]{1,0:T(8,128)(2,1)S(1)}, u32[]{:S(2)}, u32[]{:S(2)}) collective-permute-start(bf16[288,1024]{1,0:T(8,128)(2,1)S(1)} %get-tuple-element.45), channel_id=1, source_target_pairs={{0,4},{4,0},{1,5},{5,1},{2,6},{6,2},{3,7},{7,3},{8,12},{12,8},{9,1... | collective-permute-start | bytes 1769480 | tf_op jit(solution)/shard_map/ppermute | solution.py:494
  51.9 0.5 collective-permute-start.9
  52.4 1.5 %collective-permute-start.7 = (bf16[288,256]{1,0:T(8,128)(2,1)S(1)}, bf16[288,256]{1,0:T(8,128)(2,1)S(1)}, u32[]{:S(2)}, u32[]{:S(2)}) collective-permute-start(bf16[288,256]{1,0:T(8,128)(2,1)S(1)} %get-tuple-element.43), channel_id=1, source_target_pairs={{0,4},{4,0},{1,5},{5,1},{2,6},{6,2},{3,7},{7,3},{8,12},{12,8},{9,1... | collective-permute-start | bytes 442376 | tf_op jit(solution)/shard_map/ppermute | solution.py:494
  53.9 23.3 %collective-permute-done.7.refs_6_.recv_own_ref = bf16[288,256]{1,0:T(8,128)(2,1)S(1)} collective-permute-done((bf16[288,256]{1,0:T(8,128)(2,1)S(1)}, bf16[288,256]{1,0:T(8,128)(2,1)S(1)}, u32[]{:S(2)}, u32[]{:S(2)}) %collective-permute-start.7) | collective-permute-done | bytes 147488 | tf_op jit(solution)/shard_map/ppermute | solution.py:494
  77.2 0.0 collective-permute-done.6.refs_1_
  77.2 3.3 %last_chunk.1 = (bf16[144,4096]{1,0:T(8,128)(2,1)S(1)}, f32[144,128]{1,0:T(8,128)S(1)}, f32[8,128]{1,0:T(8,128)}, bf16[144,1024]{1,0:T(8,128)(2,1)S(1)}, bf16[14...) custom-call(s32[4]{0:T(128)S(1)} %pad_add_fusion.ids_ref, ...), custom_call_target="tpu_custom_call" | custom-call | tf_op jit(solution)/shard_map/last_chunk/pallas_call | solution.py:285
  80.5 1.5 %collective-permute-start.10 = (bf16[144,1024]{1,0:T(8,128)(2,1)S(1)}, bf16[144,1024]{1,0:T(8,128)(2,1)S(1)}, u32[]{:S(2)}, u32[]{:S(2)}) collective-permute-start(bf16[144,1024]{1,0:T(8,128)(2,1)S(1)} %get-tuple-element.47), channel_id=1, source_target_pairs={{0,4},{4,0},{1,5},{5,1},{2,6},{6,2},{3,7},{7,3},{8,12},{12,8},{9,1... | collective-permute-start | bytes 884744 | tf_op jit(solution)/shard_map/ppermute | solution.py:494
  82.0 0.0 collective-permute-done.9.recv_next_ref.refs_5_
  82.0 0.6 sum_keyval.1
  82.6 1.6 %collective-permute-start.11 = (bf16[432,128]{1,0:T(8,128)(2,1)S(1)}, bf16[432,128]{1,0:T(8,128)(2,1)S(1)}, u32[]{:S(2)}, u32[]{:S(2)}) collective-permute-start(bf16[432,128]{1,0:T(8,128)(2,1)S(1)} %get-tuple-element.54), channel_id=1, source_target_pairs={{0,1},{1,3},{2,0},{3,2},{4,5},{5,7},{6,4},{7,6},{8,9},{9,11},{10,8... | collective-permute-start | bytes 331784 | tf_op jit(solution)/shard_map/ppermute | solution.py:529
  84.3 0.7 collective-permute-start.12
  84.9 3.9 %collective-permute-start.13 = (bf16[144,128]{1,0:T(8,128)(2,1)S(1)}, bf16[144,128]{1,0:T(8,128)(2,1)S(1)}, u32[]{:S(2)}, u32[]{:S(2)}) collective-permute-start(bf16[144,128]{1,0:T(8,128)(2,1)S(1)} %get-tuple-element.57), channel_id=1, source_target_pairs={{0,1},{1,3},{2,0},{3,2},{4,5},{5,7},{6,4},{7,6},{8,9},{9,11},{10,8... | collective-permute-start | bytes 110600 | tf_op jit(solution)/shard_map/ppermute | solution.py:529
  88.8 0.0 collective-permute-done.11.refs_13_
  88.8 0.7 collective-permute-start.14
  89.5 0.0 collective-permute-done.12.refs_14_
  89.5 4.3 %collective-permute-start.15 = (bf16[144,128]{1,0:T(8,128)(2,1)S(1)}, bf16[144,128]{1,0:T(8,128)(2,1)S(1)}, u32[]{:S(2)}, u32[]{:S(2)}) collective-permute-start(bf16[144,128]{1,0:T(8,128)(2,1)S(1)} %get-tuple-element.59), channel_id=1, source_target_pairs={{0,5},{1,7},{2,4},{3,6},{4,1},{5,3},{6,0},{7,2},{8,13},{9,15},{10,... | collective-permute-start | bytes 110600 | tf_op jit(solution)/shard_map/ppermute | solution.py:532
  93.8 0.0 collective-permute-done.8.refs_4_.refs_7_
  93.8 1.6 %collective-permute-start.16 = (bf16[144,128]{1,0:T(8,128)(2,1)S(1)}, bf16[144,128]{1,0:T(8,128)(2,1)S(1)}, u32[]{:S(2)}, u32[]{:S(2)}) collective-permute-start(bf16[144,128]{1,0:T(8,128)(2,1)S(1)} %get-tuple-element.60), channel_id=1, source_target_pairs={{0,4},{1,6},{2,5},{3,7},{4,0},{5,2},{6,1},{7,3},{8,12},{9,14},{10,... | collective-permute-start | bytes 110600 | tf_op jit(solution)/shard_map/ppermute | solution.py:532
  95.4 2.6 %own_queries.2.refs_1_.refs_2_ = f32[288,1024]{1,0:T(8,128)S(1)} custom-call(bf16[288,4096]{1,0:T(8,128)(2,1)S(1)} %get-tuple-element.41.rows_ref, bf16[4096,1024]{1,0:T(8,128)(2,1)S(1)} %get-tuple-element.42.query_ref), custom_call_target="tpu_custom_call" | custom-call | tf_op jit(solution)/shard_map/own_queries/pallas_call | solution.py:304
  98.0 0.0 copy-start
  98.0 1.4 %own_queries.3.refs_3_ = f32[144,1024]{1,0:T(8,128)S(1)} custom-call(bf16[144,4096]{1,0:T(8,128)(2,1)S(1)} %get-tuple-element.44.rows_ref, bf16[4096,1024]{1,0:T(8,128)(2,1)S(1)} %get-tuple-element.42.query_ref), custom_call_target="tpu_custom_call" | custom-call | tf_op jit(solution)/shard_map/own_queries/pallas_call | solution.py:304
  99.4 0.0 copy-start.1
  99.4 0.0 collective-permute-done.13.refs_16_
  99.4 0.0 collective-permute-done.14.refs_17_
  99.4 0.0 collective-permute-done.15.refs_18_
  99.5 0.0 collective-permute-done.16.refs_19_
  99.5 0.0 collective-permute-done.10.refs_6_
  99.5 0.0 copy-done
  99.5 5.5 %attend.1 = f32[32,256]{1,0:T(8,128)S(1)} custom-call(s32[4]{0:T(128)S(1)} %pad_add_fusion.ids_ref, s32[1,6]{1,0:T(1,128)} %lengths_ref.3, f32[8,128]{1,0:T(8,128)S(1)} %get-tuple-element.39.tail_ref, f32[144,1024]{1,0:T(8,128)S(1)} %get-tuple-element.40.refs_0_, f32[288,1024]{1,0:T(8,128)S(1)} %own_queries.2.refs_1_.refs_2_, ...), custom_call_target="tpu_custom_call" | custom-call | tf_op jit(solution)/shard_map/attend/pallas_call | solution.py:442
  105.1 9.9 %all_to_all.11 = f32[32,1,256]{2,1,0:T(1,128)S(1)} all-to-all(f32[32,1,256]{2,1,0:T(1,128)S(1)} %copy.9), channel_id=1, replica_groups=mesh['branch'=4,'segment'=2,'tp'=4] {'branch','segment','tp'}, dimensions={0} | all-to-all | bytes 65536 | tf_op jit(solution)/shard_map/all_to_all | solution.py:556
  115.0 0.0 copy-done.1
  115.0 0.9 finish.1
  (2 shorter events, 0.0 us)
Async XLA Ops:
  2.6 16.8 %collective-permute-start = (bf16[72,4224]{1,0:T(8,128)(2,1)S(1)}, bf16[72,4224]{1,0:T(8,128)(2,1)S(1)}, u32[]{:S(2)}, u32[]{:S(2)}) collective-permute-start(bf16[72,4224]{1,0:T(8,128)(2,1)S(1)} %get-tuple-element.33), channel_id=1, source_target_pairs={{0,4},{4,0},{1,5},{5,1},{2,6},{6,2},{3,7},{7,3},{8,12},{12,8},{9,1... | collective-permute-start | bytes 1824776 | tf_op jit(solution)/shard_map/ppermute | solution.py:494
  5.6 16.0 %collective-permute-start.2 = (bf16[72,4224]{1,0:T(8,128)(2,1)S(1)}, bf16[72,4224]{1,0:T(8,128)(2,1)S(1)}, u32[]{:S(2)}, u32[]{:S(2)}) collective-permute-start(bf16[72,4224]{1,0:T(8,128)(2,1)S(1)} %get-tuple-element.34.near_ref), channel_id=1, source_target_pairs={{0,16},{8,24},{16,0},{24,8},{1,17},{9,25},{17,1},{25,9},{2,18},{10... | collective-permute-start | bytes 1824776 | tf_op jit(solution)/shard_map/ppermute | solution.py:505
  19.4 14.9 %collective-permute-start.5 = (bf16[72,4224]{1,0:T(8,128)(2,1)S(1)}, bf16[72,4224]{1,0:T(8,128)(2,1)S(1)}, u32[]{:S(2)}, u32[]{:S(2)}) collective-permute-start(bf16[72,4224]{1,0:T(8,128)(2,1)S(1)} %collective-permute-done.refs_0_), channel_id=1, source_target_pairs={{0,16},{8,24},{16,0},{24,8},{1,17},{9,25},{17,1},{25,9},{2,18},{10... | collective-permute-start | bytes 1824776 | tf_op jit(solution)/shard_map/ppermute | solution.py:506
  21.1 13.1 %collective-permute-start.4 = (bf16[72,4224]{1,0:T(8,128)(2,1)S(1)}, bf16[72,4224]{1,0:T(8,128)(2,1)S(1)}, u32[]{:S(2)}, u32[]{:S(2)}) collective-permute-start(bf16[72,4224]{1,0:T(8,128)(2,1)S(1)} %get-tuple-element.34.near_ref), channel_id=1, source_target_pairs={{0,8},{8,0},{16,24},{24,16},{1,9},{9,1},{17,25},{25,17},{2,10},{10... | collective-permute-start | bytes 1824776 | tf_op jit(solution)/shard_map/ppermute | solution.py:491
  21.1 24.3 %collective-permute-start.1 = (bf16[72,4224]{1,0:T(8,128)(2,1)S(1)}, bf16[72,4224]{1,0:T(8,128)(2,1)S(1)}, u32[]{:S(2)}, u32[]{:S(2)}) collective-permute-start(bf16[72,4224]{1,0:T(8,128)(2,1)S(1)} %collective-permute-done.refs_0_), channel_id=1, source_target_pairs={{0,8},{8,0},{16,24},{24,16},{1,9},{9,1},{17,25},{25,17},{2,10},{10... | collective-permute-start | bytes 1824776 | tf_op jit(solution)/shard_map/ppermute | solution.py:491
  21.6 23.8 %collective-permute-start.3 = (bf16[72,4224]{1,0:T(8,128)(2,1)S(1)}, bf16[72,4224]{1,0:T(8,128)(2,1)S(1)}, u32[]{:S(2)}, u32[]{:S(2)}) collective-permute-start(bf16[72,4224]{1,0:T(8,128)(2,1)S(1)} %collective-permute-done.2.refs_2_), channel_id=1, source_target_pairs={{0,8},{8,0},{16,24},{24,16},{1,9},{9,1},{17,25},{25,17},{2,10},{10... | collective-permute-start | bytes 1824776 | tf_op jit(solution)/shard_map/ppermute | solution.py:491
  34.2 42.9 %collective-permute-start.6 = (bf16[72,4224]{1,0:T(8,128)(2,1)S(1)}, bf16[72,4224]{1,0:T(8,128)(2,1)S(1)}, u32[]{:S(2)}, u32[]{:S(2)}) collective-permute-start(bf16[72,4224]{1,0:T(8,128)(2,1)S(1)} %collective-permute-done.5.refs_0_), channel_id=1, source_target_pairs={{0,8},{8,0},{16,24},{24,16},{1,9},{9,1},{17,25},{25,17},{2,10},{10... | collective-permute-start | bytes 1824776 | tf_op jit(solution)/shard_map/ppermute | solution.py:491
  50.3 43.5 %collective-permute-start.8 = (bf16[288,1024]{1,0:T(8,128)(2,1)S(1)}, bf16[288,1024]{1,0:T(8,128)(2,1)S(1)}, u32[]{:S(2)}, u32[]{:S(2)}) collective-permute-start(bf16[288,1024]{1,0:T(8,128)(2,1)S(1)} %get-tuple-element.45), channel_id=1, source_target_pairs={{0,4},{4,0},{1,5},{5,1},{2,6},{6,2},{3,7},{7,3},{8,12},{12,8},{9,1... | collective-permute-start | bytes 1769480 | tf_op jit(solution)/shard_map/ppermute | solution.py:494
  51.9 30.1 %collective-permute-start.9 = (bf16[144,1280]{1,0:T(8,128)(2,1)S(1)}, bf16[144,1280]{1,0:T(8,128)(2,1)S(1)}, u32[]{:S(2)}, u32[]{:S(2)}) collective-permute-start(bf16[144,1280]{1,0:T(8,128)(2,1)S(1)} %get-tuple-element.46), channel_id=1, source_target_pairs={{0,4},{4,0},{1,5},{5,1},{2,6},{6,2},{3,7},{7,3},{8,12},{12,8},{9,1... | collective-permute-start | bytes 1105928 | tf_op jit(solution)/shard_map/ppermute | solution.py:494
  52.4 24.8 %collective-permute-start.7 = (bf16[288,256]{1,0:T(8,128)(2,1)S(1)}, bf16[288,256]{1,0:T(8,128)(2,1)S(1)}, u32[]{:S(2)}, u32[]{:S(2)}) collective-permute-start(bf16[288,256]{1,0:T(8,128)(2,1)S(1)} %get-tuple-element.43), channel_id=1, source_target_pairs={{0,4},{4,0},{1,5},{5,1},{2,6},{6,2},{3,7},{7,3},{8,12},{12,8},{9,1... | collective-permute-start | bytes 442376 | tf_op jit(solution)/shard_map/ppermute | solution.py:494
  80.5 19.0 %collective-permute-start.10 = (bf16[144,1024]{1,0:T(8,128)(2,1)S(1)}, bf16[144,1024]{1,0:T(8,128)(2,1)S(1)}, u32[]{:S(2)}, u32[]{:S(2)}) collective-permute-start(bf16[144,1024]{1,0:T(8,128)(2,1)S(1)} %get-tuple-element.47), channel_id=1, source_target_pairs={{0,4},{4,0},{1,5},{5,1},{2,6},{6,2},{3,7},{7,3},{8,12},{12,8},{9,1... | collective-permute-start | bytes 884744 | tf_op jit(solution)/shard_map/ppermute | solution.py:494
  82.6 6.2 %collective-permute-start.11 = (bf16[432,128]{1,0:T(8,128)(2,1)S(1)}, bf16[432,128]{1,0:T(8,128)(2,1)S(1)}, u32[]{:S(2)}, u32[]{:S(2)}) collective-permute-start(bf16[432,128]{1,0:T(8,128)(2,1)S(1)} %get-tuple-element.54), channel_id=1, source_target_pairs={{0,1},{1,3},{2,0},{3,2},{4,5},{5,7},{6,4},{7,6},{8,9},{9,11},{10,8... | collective-permute-start | bytes 331784 | tf_op jit(solution)/shard_map/ppermute | solution.py:529
  84.3 5.2 %collective-permute-start.12 = (bf16[432,128]{1,0:T(8,128)(2,1)S(1)}, bf16[432,128]{1,0:T(8,128)(2,1)S(1)}, u32[]{:S(2)}, u32[]{:S(2)}) collective-permute-start(bf16[432,128]{1,0:T(8,128)(2,1)S(1)} %get-tuple-element.55), channel_id=1, source_target_pairs={{1,2},{2,1},{5,6},{6,5},{9,10},{10,9},{13,14},{14,13},{17,18},{18,... | collective-permute-start | bytes 331784 | tf_op jit(solution)/shard_map/ppermute | solution.py:529
  84.9 14.5 %collective-permute-start.13 = (bf16[144,128]{1,0:T(8,128)(2,1)S(1)}, bf16[144,128]{1,0:T(8,128)(2,1)S(1)}, u32[]{:S(2)}, u32[]{:S(2)}) collective-permute-start(bf16[144,128]{1,0:T(8,128)(2,1)S(1)} %get-tuple-element.57), channel_id=1, source_target_pairs={{0,1},{1,3},{2,0},{3,2},{4,5},{5,7},{6,4},{7,6},{8,9},{9,11},{10,8... | collective-permute-start | bytes 110600 | tf_op jit(solution)/shard_map/ppermute | solution.py:529
  88.8 10.6 %collective-permute-start.14 = (bf16[144,128]{1,0:T(8,128)(2,1)S(1)}, bf16[144,128]{1,0:T(8,128)(2,1)S(1)}, u32[]{:S(2)}, u32[]{:S(2)}) collective-permute-start(bf16[144,128]{1,0:T(8,128)(2,1)S(1)} %get-tuple-element.58), channel_id=1, source_target_pairs={{1,2},{2,1},{5,6},{6,5},{9,10},{10,9},{13,14},{14,13},{17,18},{18,... | collective-permute-start | bytes 110600 | tf_op jit(solution)/shard_map/ppermute | solution.py:529
  89.5 9.9 %collective-permute-start.15 = (bf16[144,128]{1,0:T(8,128)(2,1)S(1)}, bf16[144,128]{1,0:T(8,128)(2,1)S(1)}, u32[]{:S(2)}, u32[]{:S(2)}) collective-permute-start(bf16[144,128]{1,0:T(8,128)(2,1)S(1)} %get-tuple-element.59), channel_id=1, source_target_pairs={{0,5},{1,7},{2,4},{3,6},{4,1},{5,3},{6,0},{7,2},{8,13},{9,15},{10,... | collective-permute-start | bytes 110600 | tf_op jit(solution)/shard_map/ppermute | solution.py:532
  93.8 5.6 %collective-permute-start.16 = (bf16[144,128]{1,0:T(8,128)(2,1)S(1)}, bf16[144,128]{1,0:T(8,128)(2,1)S(1)}, u32[]{:S(2)}, u32[]{:S(2)}) collective-permute-start(bf16[144,128]{1,0:T(8,128)(2,1)S(1)} %get-tuple-element.60), channel_id=1, source_target_pairs={{0,4},{1,6},{2,5},{3,7},{4,0},{5,2},{6,1},{7,3},{8,12},{9,14},{10,... | collective-permute-start | bytes 110600 | tf_op jit(solution)/shard_map/ppermute | solution.py:532
  98.0 1.5 %copy-start = (bf16[1,2048]{1,0:T(2,128)(2,1)S(1)}, bf16[1,2048]{1,0:T(2,128)(2,1)}, u32[]{:S(2)}) copy-start(bf16[1,2048]{1,0:T(2,128)(2,1)} %refs_20_.1) | copy-start | bytes 12292
  99.4 15.6 %copy-start.1 = (s32[72]{0:T(128)S(1)}, s32[72]{0:T(128)}, u32[]{:S(2)}) copy-start(s32[72]{0:T(128)} %param.9) | copy-start | bytes 868

commit v6 on v5

--- a/solution.py
+++ b/solution.py
@@ -115,7 +115,7 @@
 
 
 def chunk_body(ids_ref, pieces, gain_ref, head_ref, keyval_ref, query_ref, outs, waits, recv=None):
-    rows_ref, direct_ref, tail_ref = outs[:3]
+    rows_ref, direct_ref = outs[:2]
     count = pieces[0].shape[0]
     half = rows_ref.shape[1]
     core, segment, tp = ids_ref[0], ids_ref[1], ids_ref[3]
@@ -141,7 +141,6 @@
             direct = direct + rows[:, lane:lane + LANES] * weight[:, lane:lane + LANES]
         rows_ref[:, at] = (rows * scale * gain_ref[:, at].astype(F32)).astype(BF16)
     direct_ref[...] = direct
-    tail_ref[...] = pieces[0][:, half:].astype(F32)[:8]
 
     for wait in waits[:keyval_ref.shape[1] // BLOCK]:
         wait()
@@ -151,15 +150,21 @@
     own = jnp.where(segment == 0, even, odd)
     other = jnp.where(segment == 0, odd, even)
     if recv is None:
-        own_ref, send_ref = outs[3:5]
+        own_ref, send_ref = outs[2:4]
         own_ref[...] = own
-        if len(outs) > 5:
-            outs[5][...] = other.astype(BF16)
+        if len(outs) > 4:
+            outs[4][...] = other.astype(BF16)
         else:
             send_ref[:, columns:] = other.astype(BF16)
     else:
-        send_ref, keep_ref, first_ref, second_ref, far_first_ref, far_second_ref = outs[3:]
-        low, high = split_slots(own + recv)
+        send_ref, keep_ref, first_ref, second_ref, far_first_ref, far_second_ref = outs[2:]
+        own_part_ref, pair_part_ref, recv_own_ref, recv_next_ref = recv
+        slab = 2 * count
+        mine, x_part, y_part = slabs((own_part_ref, pair_part_ref, pair_part_ref), (0, 0, slab), slab)
+        at = slice(columns, columns + 2 * HEAD)
+        sums = [mine + recv_own_ref[:slab, :].astype(F32), x_part + recv_next_ref[:, at].astype(F32), y_part,
+                own + recv_own_ref[slab:, :].astype(F32)]
+        low, high = split_slots(jnp.concatenate([by_pack(sums, pack) for pack in range(2)], axis=0))
         keep_ref[...] = jnp.where(tp == 3, high, low).astype(BF16)
         first_ref[...] = jnp.where(tp < 2, high, low).astype(BF16)
         second_ref[...] = jnp.where(tp == 2, high, low).astype(BF16)
@@ -176,8 +181,8 @@
 
 def first_chunk_kernel(ids_ref, near_ref, far_ref, gain_hbm, head_hbm, keyval_hbm, query_hbm, *refs):
     outs, (gain_ref, head_ref, keyval_ref, query_ref) = refs[:4], refs[4:8]
-    own_query_ref, own_out_ref, rows_ref, part_ref, small_sems, sems, own_sems = refs[8:]
-    outs = (rows_ref, *outs)
+    own_query_ref, part_ref, small_sems, sems, own_sems = refs[8:]
+    rows_ref = outs[0]
     half = rows_ref.shape[1]
     segment, tp = ids_ref[1], ids_ref[3]
     small = [
@@ -213,7 +218,8 @@
 
     chunk_body(ids_ref, (near_ref, far_ref), gain_ref, head_ref, keyval_ref, query_ref, outs,
                waits[:len(large)])
-    own_body(rows_ref, own_query_ref, own_out_ref, waits[len(large):])
+    for wait in waits[len(large):]:
+        wait()
 
 
 def next_chunk_kernel(ids_ref, *refs, chips):
@@ -221,10 +227,8 @@
     chunk_body(ids_ref, pieces, *refs[:4], refs[4:], [])
 
 
-def last_chunk_kernel(ids_ref, *refs, start):
-    pieces, refs = refs[:2], refs[2:]
-    count = pieces[0].shape[0] * 2
-    chunk_body(ids_ref, pieces, *refs[:4], refs[5:], [], refs[4][start:start + count, :].astype(F32))
+def last_chunk_kernel(ids_ref, *refs):
+    chunk_body(ids_ref, refs[:2], *refs[2:6], refs[10:], [], refs[6:10])
 
 
 def shape_of(*shape, kind=BF16):
@@ -232,7 +236,7 @@
 
 
 def chunk_shapes(rows, half):
-    return (shape_of(rows, half), shape_of(rows, LANES, kind=F32), shape_of(8, LANES, kind=F32))
+    return (shape_of(rows, half), shape_of(rows, LANES, kind=F32))
 
 
 def first_chunk(ids, near, far, gain, head, keyval, query):
@@ -240,17 +244,16 @@
     half = wide - LANES
     columns = query.shape[1] // 2
     rows = 2 * count
-    shapes = chunk_shapes(rows, half)[1:] + (
+    shapes = chunk_shapes(rows, half) + (
         shape_of(rows, 2 * HEAD, kind=F32), shape_of(rows, columns + 2 * HEAD),
         shape_of(1, half), shape_of(1, half), shape_of(*keyval.shape), shape_of(half, columns),
-        shape_of(half, columns), shape_of(rows, columns, kind=F32))
+        shape_of(half, columns))
     out = pl.pallas_call(
         first_chunk_kernel,
         out_shape=shapes,
         in_specs=[whole(pltpu.SMEM), whole(), whole()] + [whole(pltpu.HBM)] * 4,
         out_specs=(whole(),) * len(shapes),
         scratch_shapes=[
-            pltpu.VMEM((rows, half), BF16),
             pltpu.VMEM(head.shape, BF16),
             pltpu.SemaphoreType.DMA((2,)),
             pltpu.SemaphoreType.DMA(((columns + keyval.shape[1]) // BLOCK,)),
@@ -259,7 +262,7 @@
         compiler_params=pltpu.CompilerParams(vmem_limit_bytes=14 << 20),
         name="first_chunk",
     )(ids, near, far, gain, head, keyval, query)
-    return out[:4], out[4:8], out[8], out[9]
+    return out[:4], out[4:8], out[8]
 
 
 def next_chunk(ids, pieces, weights):
@@ -278,18 +281,19 @@
     )(ids, *pieces, *weights)
 
 
-def last_chunk(ids, pieces, weights, recv, start):
+def last_chunk(ids, pieces, weights, parts):
     count, wide = pieces[0].shape
     rows = 2 * count
-    shapes = chunk_shapes(rows, wide - LANES) + (shape_of(rows, weights[3].shape[1]),) + (shape_of(rows, HEAD),) * 5
+    shapes = chunk_shapes(rows, wide - LANES) + (
+        shape_of(rows, weights[3].shape[1]),) + (shape_of(4 * rows, HEAD),) * 3 + (shape_of(rows, HEAD),) * 2
     return pl.pallas_call(
-        functools.partial(last_chunk_kernel, start=start),
+        last_chunk_kernel,
         out_shape=shapes,
-        in_specs=[whole(pltpu.SMEM)] + [whole()] * (len(pieces) + 5),
+        in_specs=[whole(pltpu.SMEM)] + [whole()] * (len(pieces) + 8),
         out_specs=(whole(),) * len(shapes),
         compiler_params=pltpu.CompilerParams(vmem_limit_bytes=14 << 20),
         name="last_chunk",
-    )(ids, *pieces, *weights, recv)
+    )(ids, *pieces, *weights, *parts)
 
 
 def own_body(rows_ref, query_ref, out_ref, waits=()):
@@ -320,31 +324,6 @@
     return jnp.concatenate([part[pack * count:(pack + 1) * count] for part in parts], axis=0)
 
 
-def keyval_kernel(ids_ref, own_ref, next_ref, recv_own_ref, recv_next_ref, keep_ref, first_ref, second_ref):
-    tp = ids_ref[3]
-    count = own_ref.shape[0]
-    mine, x_part, y_part = slabs((own_ref, next_ref, next_ref), (0, 0, count), count)
-    width = recv_next_ref.shape[1]
-    at = slice(width - 2 * HEAD, width)
-    sums = [mine + recv_own_ref[:count, :].astype(F32), x_part + recv_next_ref[:, at].astype(F32), y_part]
-    low, high = split_slots(jnp.concatenate([by_pack(sums, pack) for pack in range(2)], axis=0))
-    keep_ref[...] = jnp.where(tp == 3, high, low).astype(BF16)
-    first_ref[...] = jnp.where(tp < 2, high, low).astype(BF16)
-    second_ref[...] = jnp.where(tp == 2, high, low).astype(BF16)
-
-
-def sum_keyval(ids, own, pair, recv_own, recv_next):
-    shape = shape_of(own.shape[0] + pair.shape[0], HEAD)
-    return pl.pallas_call(
-        keyval_kernel,
-        out_shape=(shape, shape, shape),
-        in_specs=[whole(pltpu.SMEM)] + [whole()] * 4,
-        out_specs=(whole(),) * 3,
-        compiler_params=pltpu.CompilerParams(vmem_limit_bytes=8 << 20),
-        name="sum_keyval",
-    )(ids, own, pair, recv_own, recv_next)
-
-
 def owner_of(row, pack, ids_ref, piece_rows):
     index = jnp.zeros_like(row)
     for step in range(1, 8):
@@ -354,39 +333,11 @@
     return shard, row - index * piece_rows
 
 
-def attention_kernel(ids_ref, lengths_ref, tail_ref, *refs, starts, recv_starts):
-    chips = len(starts)
-    owns, recvs, directs = (refs[index * chips:(index + 1) * chips] for index in range(3))
-    refs = refs[3 * chips:]
-    earlies, lates, fars, gain_ref = refs[0:3], refs[3:6], refs[6:8], refs[8]
-    out_ref, bias_ref = refs[9:]
-    segment, tp = ids_ref[1], ids_ref[3]
-    rows = bias_ref.shape[1]
-    slab = rows // 2
-    queries = bias_ref.shape[0]
+def mask_kernel(ids_ref, lengths_ref, near_ref, out_ref):
+    segment = ids_ref[1]
+    rows = out_ref.shape[1]
     piece_rows = rows // 8
-    heads = owns[0].shape[1] // HEAD
-    devices = out_ref.shape[0]
-    wide = out_ref.shape[1] // 2
-    scale = math.log2(math.e) / math.sqrt(HEAD)
-    tail = tail_ref[:1, :].astype(jnp.int32)
-    lane = iota((queries, wide), 1)
-
-    def chosen_keys(refs):
-        keep, first, second = (ref[...].astype(F32) for ref in refs)
-        return (jnp.where(tp == 0, keep, jnp.where(tp == 2, second, first)),
-                jnp.where(tp == 3, keep, jnp.where(tp == 1, second, first)))
-
-    def pack_part(part, pack):
-        count = part.shape[0] // 2
-        return part[pack * count:(pack + 1) * count]
-
-    far_first, far_second = (ref[...].astype(F32) for ref in fars)
-    odd = (tp & 1) == 1
-    far = (jnp.where(odd, far_first, far_second), jnp.where(odd, far_second, far_first))
-    early, late = chosen_keys(earlies), chosen_keys(lates)
-    through = jnp.zeros((devices, wide), F32)
-    direct = jnp.zeros((devices, wide), F32)
+    tail = near_ref[:, near_ref.shape[1] - LANES:].astype(F32)[:1].astype(jnp.int32)
     for pack in range(2):
         def place(row):
             shard, inner = owner_of(row, pack, ids_ref, piece_rows)
@@ -399,16 +350,61 @@
                 doc = doc + (position >= end).astype(jnp.int32)
             return position, doc
 
-        row_position, row_doc = place(iota((queries, 1), 0))
+        row_position, row_doc = place(iota((rows, 1), 0))
         col_position, col_doc = place(iota((1, rows), 1))
         visible = jnp.logical_and(row_doc == col_doc, col_position <= row_position)
-        bias_ref[...] = jnp.where(visible, 0.0, -1e30)
+        out_ref[pack * rows:(pack + 1) * rows, :] = jnp.where(visible, 0.0, -1e30)
+
+
+def masks(ids, lengths, near, rows):
+    return pl.pallas_call(
+        mask_kernel,
+        out_shape=shape_of(2 * rows, rows, kind=F32),
+        in_specs=[whole(pltpu.SMEM), whole(pltpu.SMEM), whole()],
+        out_specs=whole(),
+        compiler_params=pltpu.CompilerParams(vmem_limit_bytes=4 << 20),
+        name="masks",
+    )(ids, lengths, near)
+
+
+def attention_kernel(ids_ref, bias_ref, *refs, starts, recv_starts):
+    chips = len(starts)
+    owns, recvs, directs = (refs[index * chips:(index + 1) * chips] for index in range(3))
+    refs = refs[3 * chips:]
+    nears, fars, gain_ref, out_ref = refs[0:3], refs[3:5], refs[5], refs[6]
+    segment, tp = ids_ref[1], ids_ref[3]
+    rows = bias_ref.shape[1]
+    slab = rows // 2
+    queries = rows
+    piece_rows = rows // 8
+    heads = owns[0].shape[1] // HEAD
+    devices = out_ref.shape[0]
+    wide = out_ref.shape[1] // 2
+    scale = math.log2(math.e) / math.sqrt(HEAD)
+    lane = iota((queries, wide), 1)
+
+    def chosen_keys(refs):
+        keep, first, second = (ref[...].astype(F32) for ref in refs)
+        return (jnp.where(tp == 0, keep, jnp.where(tp == 2, second, first)),
+                jnp.where(tp == 3, keep, jnp.where(tp == 1, second, first)))
+
+    def pack_part(part, pack):
+        count = part.shape[0] // 2
+        return part[pack * count:(pack + 1) * count]
+
+    far_first, far_second = (ref[...].astype(F32) for ref in fars)
+    odd = (tp & 1) == 1
+    far = (jnp.where(odd, far_first, far_second), jnp.where(odd, far_second, far_first))
+    near = chosen_keys(nears)
+    through = jnp.zeros((devices, wide), F32)
+    direct = jnp.zeros((devices, wide), F32)
+    for pack in range(2):
         keys, values = (
             jnp.concatenate([
-                pack_part(at_once, pack)[:slab],
-                pack_part(at_once, pack)[slab:] + pack_part(far_part, pack),
-                pack_part(late_part, pack)], axis=0).astype(BF16)
-            for at_once, far_part, late_part in zip(early, far, late))
+                pack_part(near_part, pack)[:slab],
+                pack_part(near_part, pack)[slab:slab + slab // 2] + pack_part(far_part, pack),
+                pack_part(near_part, pack)[slab + slab // 2:]], axis=0).astype(BF16)
+            for near_part, far_part in zip(near, far))
         values = jnp.concatenate([values, jnp.ones((rows, HEAD), BF16)], axis=1)
         total = jnp.zeros((queries, HEAD), F32)
         for head in range(heads):
@@ -417,7 +413,7 @@
                 slabs(owns, starts, slab, at), slabs(recvs, recv_starts, slab, at))]
             query = (by_pack(parts, pack) * scale).astype(BF16)
             logits = lax.dot_general(query, keys, (((1,), (1,)), ((), ())), preferred_element_type=F32)
-            logits = logits + bias_ref[...]
+            logits = logits + bias_ref[pack * rows:(pack + 1) * rows, :]
             expo = jnp.exp2(logits - jnp.max(logits, axis=1, keepdims=True)).astype(BF16)
             both = jnp.dot(expo, values, preferred_element_type=F32)
             offset = pl.multiple_of(segment * heads * HEAD + head * HEAD, HEAD)
@@ -437,17 +433,15 @@
     out_ref[:, wide:] = direct
 
 
-def attention(ids, lengths, tail, owns, starts, recvs, recv_starts, directs, early, late, far, gain, devices):
-    rows = early[0].shape[0] // 2 + late[0].shape[0] // 2
+def attention(ids, bias, owns, starts, recvs, recv_starts, directs, near, far, gain, devices):
     return pl.pallas_call(
         functools.partial(attention_kernel, starts=starts, recv_starts=recv_starts),
         out_shape=shape_of(devices, 2 * LANES, kind=F32),
-        in_specs=[whole(pltpu.SMEM), whole(pltpu.SMEM)] + [whole()] * (10 + 3 * len(owns)),
+        in_specs=[whole(pltpu.SMEM)] + [whole()] * (7 + 3 * len(owns)),
         out_specs=whole(),
-        scratch_shapes=[pltpu.VMEM((rows, rows), F32)],
         compiler_params=pltpu.CompilerParams(vmem_limit_bytes=14 << 20),
         name="attend",
-    )(ids, lengths, tail, *owns, *recvs, *directs, *early, *late, *far, gain)
+    )(ids, bias, *owns, *recvs, *directs, *near, *far, gain)
 
 
 def finish_kernel(recv_ref, send_ref, out_ref):
@@ -511,17 +505,18 @@
         return [part for piece in pieces for part in (piece, swap(piece))]
 
     pieces = with_swapped(mine)
-    (direct_own, _, local_own, part), weights, own_weights, query_own = first_chunk(
+    (rows, direct_own, local_own, part), weights, own_weights = first_chunk(
         ids, *pieces, attn_gain, head_weight, wkv, wq)
     received_own = across(part)
+    query_own = own_queries(rows, own_weights)
+    bias = masks(ids, seq_lengths, from_x, 2 * slab)
 
     pieces = with_swapped(from_x, from_y)
-    rows, direct_xy, tail, local_xy, part, keyval = next_chunk(ids, pieces, weights)
+    rows, direct_xy, local_xy, part, keyval = next_chunk(ids, pieces, weights)
     keyval_xy = across(keyval)
     received_xy = across(part)
     query_xy = own_queries(rows, own_weights)
 
-    keep, first, second = sum_keyval(ids, local_own, local_xy, keyval_xy, received_own)
     hand_first, hand_second = (1, 3, 0, 2), (0, 2, 1, 3)
     n_tp = len(hand_first)
 
@@ -532,27 +527,21 @@
         return lax.ppermute(array, ("segment", "tp"), [
             (side * n_tp + i, (1 - side) * n_tp + to) for side in range(2) for i, to in enumerate(targets)])
 
-    first = hand(first, hand_first)
-    second = hand(second, hand_second)
-    early = (keep, first, second)
-
     pieces = with_swapped(from_d)
-    rows, direct_d, _, part, keep, first, second, far_first, far_second = last_chunk(
-        ids, pieces, weights, keyval_xy, slab)
-    far_first = hand_across(far_first, hand_first)
-    far_second = hand_across(far_second, hand_second)
+    rows, direct_d, part, keep, first, second, far_first, far_second = last_chunk(
+        ids, pieces, weights, (local_own, local_xy, keyval_xy, received_own))
     received_d = across(part)
     first = hand(first, hand_first)
     second = hand(second, hand_second)
-    late = (keep, first, second)
+    far_first = hand_across(far_first, hand_first)
+    far_second = hand_across(far_second, hand_second)
     query_d = own_queries(rows, own_weights)
     devices = n_branch * 2 * n_tp
     outgoing = attention(
-        ids, seq_lengths, tail,
-        [query_own, query_xy, query_xy, query_d], (0, 0, slab, 0),
+        ids, bias, [query_own, query_xy, query_xy, query_d], (0, 0, slab, 0),
         [received_xy, received_own, received_d, received_xy], (0, 0, 0, slab),
         [direct_own, direct_xy, direct_xy, direct_d],
-        early, late, (far_first, far_second), head_attn, devices)
+        (keep, first, second), (far_first, far_second), head_attn, devices)
     incoming = lax.all_to_all(outgoing, ALL_AXES, split_axis=0, concat_axis=0, tiled=True)
     return finish(incoming, packing, n_branch)
 

time: 116 us -> 107 us (0.922)
  waiting for transfers between devices: 48.1 us -> 43.1 us
  starting transfers between devices: 24.7 us -> 19.9 us
  blocking collectives: 9.9 us -> 11.2 us
    ppermute x5, waiting for transfers between devices: 35.5 us -> 30.4 us  [across(): return lax.ppermute(part, 'segment', x_pairs)]
    ppermute x4 -> x2, starting transfers between devices: 6.84 us -> 2.24 us  [hand(): lax.ppermute(array, 'tp', [(i, to) for i, to in enumerate(targets) if i !...]
    pallas_call x1, Pallas kernels: 11.2 us -> 8.92 us  [first_chunk(): pl.pallas_call(first_chunk_kernel, out_shape=shapes, in_specs=[whole(pltp...]
    pallas_call x2 -> x3, Pallas kernels: 4.02 us -> 5.47 us  [own_queries(): pl.pallas_call(own_body, out_shape=shape_of(rows.shape[0], query.shape[1]...]
    all_to_all x1, blocking collectives: 9.9 us -> 11.2 us  [paired(): lax.all_to_all(outgoing, ALL_AXES, split_axis=0, concat_axis=0, tiled=True)]
  transfers between devices with their start and end apart: 17 -> 15, of which waited for: 3 -> 4; matrix products, arithmetic and copies ran while one was open for 0% -> 0% of each run, Pallas kernels for 21% -> 22%
where the time goes in v6:
time: 107 us
  waiting for transfers between devices  43.1 us (40%)
  Pallas kernels  32.1 us (30%)
  starting transfers between devices  19.9 us (19%)
  blocking collectives  11.2 us (10%)
    ppermute x5, waiting for transfers between devices, across(): return lax.ppermute(part, 'segment', x_pairs)  30.4 us
    ppermute x1, waiting for transfers between devices, paired(): from_d = lax.ppermute(from_x, 'branch', y_pairs)  12.6 us
    all_to_all x1, blocking collectives, paired(): lax.all_to_all(outgoing, ALL_AXES, split_axis=0, concat_axis=0, tiled=True)  11.2 us
    pallas_call x1, Pallas kernels, first_chunk(): pl.pallas_call(first_chunk_kernel, out_shape=shapes, in_specs=[whole(pltp...  8.92 us
    ppermute x5, starting transfers between devices, across(): return lax.ppermute(part, 'segment', x_pairs)  8.28 us
    ppermute x2, starting transfers between devices, hand_across(): lax.ppermute(array, ('segment', 'tp'), [(side * n_tp + i, (1 - side) * n_...  5.55 us
    pallas_call x3, Pallas kernels, own_queries(): pl.pallas_call(own_body, out_shape=shape_of(rows.shape[0], query.shape[1]...  5.47 us
    pallas_call x1, Pallas kernels, attention(): pl.pallas_call(functools.partial(attention_kernel, starts=starts, recv_st...  5.24 us
  transfers between devices with their start and end apart: 15, of which 4 were waited for; matrix products, arithmetic and copies ran while one was open for 0% of the time, Pallas kernels for 22%

profile of v6, /device:TPU:0, one launch (start us, length us, event | category | flops | bytes accessed | tf_op | source)
XLA Modules:
  0.0 106.6 jit_solution(12858271047430156335)
XLA Ops:
  0.0 0.1 pad_add_fusion.ids_ref
  0.1 2.5 %prepare.1 = (bf16[72,4224]{1,0:T(8,128)(2,1)S(1)}, bf16[72,4224]{1,0:T(8,128)(2,1)S(1)}) custom-call(s32[4]{0:T(128)S(1)} %pad_add_fusion.ids_ref, s32[1,6]{1,0:T(1,128)} %lengths_ref.3, bf16[72,8192]{1,0:T(8,128)(2,1)} %rows_hbm.1, s32[1,72]{1,0:T(1,128)} %bitcast.13), custom_call_target="tpu_custom_call" | custom-call | tf_op jit(solution)/shard_map/prepare/pallas_call | solution.py:85
  2.6 3.0 %collective-permute-start = (bf16[72,4224]{1,0:T(8,128)(2,1)S(1)}, bf16[72,4224]{1,0:T(8,128)(2,1)S(1)}, u32[]{:S(2)}, u32[]{:S(2)}) collective-permute-start(bf16[72,4224]{1,0:T(8,128)(2,1)S(1)} %get-tuple-element.29), channel_id=1, source_target_pairs={{0,4},{4,0},{1,5},{5,1},{2,6},{6,2},{3,7},{7,3},{8,12},{12,8},{9,1... | collective-permute-start | bytes 1824776 | tf_op jit(solution)/shard_map/ppermute | solution.py:488
  5.6 1.5 %collective-permute-start.3 = (bf16[72,4224]{1,0:T(8,128)(2,1)S(1)}, bf16[72,4224]{1,0:T(8,128)(2,1)S(1)}, u32[]{:S(2)}, u32[]{:S(2)}) collective-permute-start(bf16[72,4224]{1,0:T(8,128)(2,1)S(1)} %get-tuple-element.30.near_ref), channel_id=1, source_target_pairs={{0,16},{8,24},{16,0},{24,8},{1,17},{9,25},{17,1},{25,9},{2,18},{10... | collective-permute-start | bytes 1824776 | tf_op jit(solution)/shard_map/ppermute | solution.py:499
  7.2 12.2 %collective-permute-done.near_ref.refs_0_ = bf16[72,4224]{1,0:T(8,128)(2,1)S(1)} collective-permute-done((bf16[72,4224]{1,0:T(8,128)(2,1)S(1)}, bf16[72,4224]{1,0:T(8,128)(2,1)S(1)}, u32[]{:S(2)}, u32[]{:S(2)}) %collective-permute-start) | collective-permute-done | bytes 608288 | tf_op jit(solution)/shard_map/ppermute | solution.py:488
  19.4 1.8 %collective-permute-start.5 = (bf16[72,4224]{1,0:T(8,128)(2,1)S(1)}, bf16[72,4224]{1,0:T(8,128)(2,1)S(1)}, u32[]{:S(2)}, u32[]{:S(2)}) collective-permute-start(bf16[72,4224]{1,0:T(8,128)(2,1)S(1)} %collective-permute-done.near_ref.refs_0_), channel_id=1, source_target_pairs={{0,16},{8,24},{16,0},{24,8},{1,17},{9,25},{17,1},{25,9},{2,18},{10... | collective-permute-start | bytes 1824776 | tf_op jit(solution)/shard_map/ppermute | solution.py:500
  21.1 0.0 collective-permute-start.1
  21.1 0.5 collective-permute-start.2
  21.6 0.0 collective-permute-done.3.refs_2_
  21.6 0.0 collective-permute-start.4
  21.7 12.6 %collective-permute-done.5.refs_0_ = bf16[72,4224]{1,0:T(8,128)(2,1)S(1)} collective-permute-done((bf16[72,4224]{1,0:T(8,128)(2,1)S(1)}, bf16[72,4224]{1,0:T(8,128)(2,1)S(1)}, u32[]{:S(2)}, u32[]{:S(2)}) %collective-permute-start.5) | collective-permute-done | bytes 608288 | tf_op jit(solution)/shard_map/ppermute | solution.py:500
  34.2 0.0 collective-permute-start.6
  34.2 0.0 collective-permute-done.1.far_ref
  34.3 8.9 %first_chunk.1 = (bf16[144,4096]{1,0:T(8,128)(2,1)S(1)}, f32[144,128]{1,0:T(8,128)S(1)}, f32[144,256]{1,0:T(8,128)S(1)}, bf16[144,1280]{1,0:T(8,128)(2,1)S(1)}, ...) custom-call(s32[4]{0:T(128)S(1)} %pad_add_fusion.ids_ref, ...), custom_call_target="tpu_custom_call" | custom-call | tf_op jit(solution)/shard_map/first_chunk/pallas_call | solution.py:251
  43.2 1.6 %collective-permute-start.8 = (bf16[144,1280]{1,0:T(8,128)(2,1)S(1)}, bf16[144,1280]{1,0:T(8,128)(2,1)S(1)}, u32[]{:S(2)}, u32[]{:S(2)}) collective-permute-start(bf16[144,1280]{1,0:T(8,128)(2,1)S(1)} %get-tuple-element.41), channel_id=1, source_target_pairs={{0,4},{4,0},{1,5},{5,1},{2,6},{6,2},{3,7},{7,3},{8,12},{12,8},{9,1... | collective-permute-start | bytes 1105928 | tf_op jit(solution)/shard_map/ppermute | solution.py:488
  44.8 0.0 collective-permute-done.2.refs_1_
  44.8 0.0 collective-permute-done.4.refs_3_
  44.8 4.9 %next_chunk.1 = (bf16[288,4096]{1,0:T(8,128)(2,1)S(1)}, f32[288,128]{1,0:T(8,128)S(1)}, f32[288,256]{1,0:T(8,128)S(1)}, bf16[288,1024]{1,0:T(8,128)(2,1)S(1)}, bf16[288,256]{1,0:T(8,128)(2,1)S(1)}) custom-call(s32[4]{0:T(128)S(1)} %pad_add_fusion.ids_ref, bf16[72,4224]{1,0:T(8,128)(2,1)S(1)} %collective-permute-done.near_ref.refs_0_, ...), custom_call_target="tpu_custom_call" | custom-call | tf_op jit(solution)/shard_map/next_chunk/pallas_call | solution.py:274
  49.7 0.6 collective-permute-start.9
  50.3 1.5 %collective-permute-start.7 = (bf16[288,256]{1,0:T(8,128)(2,1)S(1)}, bf16[288,256]{1,0:T(8,128)(2,1)S(1)}, u32[]{:S(2)}, u32[]{:S(2)}) collective-permute-start(bf16[288,256]{1,0:T(8,128)(2,1)S(1)} %get-tuple-element.40), channel_id=1, source_target_pairs={{0,4},{4,0},{1,5},{5,1},{2,6},{6,2},{3,7},{7,3},{8,12},{12,8},{9,1... | collective-permute-start | bytes 442376 | tf_op jit(solution)/shard_map/ppermute | solution.py:488
  51.8 2.9 %collective-permute-done.8.refs_9_.refs_5_ = bf16[144,1280]{1,0:T(8,128)(2,1)S(1)} collective-permute-done((bf16[144,1280]{1,0:T(8,128)(2,1)S(1)}, bf16[144,1280]{1,0:T(8,128)(2,1)S(1)}, u32[]{:S(2)}, u32[]{:S(2)}) %collective-permute-start.8) | collective-permute-done | bytes 368672 | tf_op jit(solution)/shard_map/ppermute | solution.py:488
  54.7 15.3 %collective-permute-done.7.refs_8_ = bf16[288,256]{1,0:T(8,128)(2,1)S(1)} collective-permute-done((bf16[288,256]{1,0:T(8,128)(2,1)S(1)}, bf16[288,256]{1,0:T(8,128)(2,1)S(1)}, u32[]{:S(2)}, u32[]{:S(2)}) %collective-permute-start.7) | collective-permute-done | bytes 147488 | tf_op jit(solution)/shard_map/ppermute | solution.py:488
  70.0 0.0 collective-permute-done.6.refs_1_
  70.0 3.1 %last_chunk.1 = (bf16[144,4096]{1,0:T(8,128)(2,1)S(1)}, f32[144,128]{1,0:T(8,128)S(1)}, bf16[144,1024]{1,0:T(8,128)(2,1)S(1)}, bf16[576,128]{1,0:T(8,128)(2,1)S(...) custom-call(s32[4]{0:T(128)S(1)} %pad_add_fusion.ids_ref, ...), custom_call_target="tpu_custom_call" | custom-call | tf_op jit(solution)/shard_map/last_chunk/pallas_call | solution.py:289
  73.1 1.6 %collective-permute-start.10 = (bf16[144,1024]{1,0:T(8,128)(2,1)S(1)}, bf16[144,1024]{1,0:T(8,128)(2,1)S(1)}, u32[]{:S(2)}, u32[]{:S(2)}) collective-permute-start(bf16[144,1024]{1,0:T(8,128)(2,1)S(1)} %get-tuple-element.44), channel_id=1, source_target_pairs={{0,4},{4,0},{1,5},{5,1},{2,6},{6,2},{3,7},{7,3},{8,12},{12,8},{9,1... | collective-permute-start | bytes 884744 | tf_op jit(solution)/shard_map/ppermute | solution.py:488
  74.7 1.6 %collective-permute-start.11 = (bf16[576,128]{1,0:T(8,128)(2,1)S(1)}, bf16[576,128]{1,0:T(8,128)(2,1)S(1)}, u32[]{:S(2)}, u32[]{:S(2)}) collective-permute-start(bf16[576,128]{1,0:T(8,128)(2,1)S(1)} %get-tuple-element.49), channel_id=1, source_target_pairs={{0,1},{1,3},{2,0},{3,2},{4,5},{5,7},{6,4},{7,6},{8,9},{9,11},{10,8... | collective-permute-start | bytes 442376 | tf_op jit(solution)/shard_map/ppermute | solution.py:524
  76.3 0.7 collective-permute-start.12
  77.0 4.0 %collective-permute-start.13 = (bf16[144,128]{1,0:T(8,128)(2,1)S(1)}, bf16[144,128]{1,0:T(8,128)(2,1)S(1)}, u32[]{:S(2)}, u32[]{:S(2)}) collective-permute-start(bf16[144,128]{1,0:T(8,128)(2,1)S(1)} %get-tuple-element.51), channel_id=1, source_target_pairs={{0,5},{1,7},{2,4},{3,6},{4,1},{5,3},{6,0},{7,2},{8,13},{9,15},{10,... | collective-permute-start | bytes 110600 | tf_op jit(solution)/shard_map/ppermute | solution.py:527
  80.9 0.0 collective-permute-done.9.refs_4_.refs_7_
  80.9 1.6 %collective-permute-start.14 = (bf16[144,128]{1,0:T(8,128)(2,1)S(1)}, bf16[144,128]{1,0:T(8,128)(2,1)S(1)}, u32[]{:S(2)}, u32[]{:S(2)}) collective-permute-start(bf16[144,128]{1,0:T(8,128)(2,1)S(1)} %get-tuple-element.52), channel_id=1, source_target_pairs={{0,4},{1,6},{2,5},{3,7},{4,0},{5,2},{6,1},{7,3},{8,12},{9,14},{10,... | collective-permute-start | bytes 110600 | tf_op jit(solution)/shard_map/ppermute | solution.py:527
  82.5 1.4 %own_queries.3.refs_0_ = f32[144,1024]{1,0:T(8,128)S(1)} custom-call(bf16[144,4096]{1,0:T(8,128)(2,1)S(1)} %get-tuple-element.31.rows_ref, bf16[4096,1024]{1,0:T(8,128)(2,1)S(1)} %get-tuple-element.32.query_ref), custom_call_target="tpu_custom_call" | custom-call | tf_op jit(solution)/shard_map/own_queries/pallas_call | solution.py:308
  84.0 1.1 masks.1.bias_ref
  85.0 2.6 %own_queries.4.refs_1_.refs_2_ = f32[288,1024]{1,0:T(8,128)S(1)} custom-call(bf16[288,4096]{1,0:T(8,128)(2,1)S(1)} %get-tuple-element.37.rows_ref, bf16[4096,1024]{1,0:T(8,128)(2,1)S(1)} %get-tuple-element.32.query_ref), custom_call_target="tpu_custom_call" | custom-call | tf_op jit(solution)/shard_map/own_queries/pallas_call | solution.py:308
  87.6 0.0 copy-start
  87.6 1.4 %own_queries.5.refs_3_ = f32[144,1024]{1,0:T(8,128)S(1)} custom-call(bf16[144,4096]{1,0:T(8,128)(2,1)S(1)} %get-tuple-element.42.rows_ref, bf16[4096,1024]{1,0:T(8,128)(2,1)S(1)} %get-tuple-element.32.query_ref), custom_call_target="tpu_custom_call" | custom-call | tf_op jit(solution)/shard_map/own_queries/pallas_call | solution.py:308
  89.1 0.0 copy-start.1
  89.1 0.0 collective-permute-done.13.refs_15_
  89.1 0.0 collective-permute-done.14.refs_16_
  89.1 0.0 collective-permute-done.11.refs_13_
  89.1 0.0 collective-permute-done.12.refs_14_
  89.1 0.0 collective-permute-done.10.refs_6_
  89.1 0.0 copy-done
  89.1 5.2 %attend.1 = f32[32,256]{1,0:T(8,128)S(1)} custom-call(s32[4]{0:T(128)S(1)} %pad_add_fusion.ids_ref, f32[576,288]{1,0:T(8,128)S(1)} %masks.1.bias_ref, f32[144,1024]{1,0:T(8,128)S(1)} %own_queries.3.refs_0_, f32[288,1024]{1,0:T(8,128)S(1)} %own_queries.4.refs_1_.refs_2_, f32[288,1024]{1,0:T(8,128)S(1)} %own_queries.4.refs_1_.refs_2_, ...), custom_call_target="tpu_custom_call" | custom-call | tf_op jit(solution)/shard_map/attend/pallas_call | solution.py:437
  94.4 11.2 %all_to_all.11 = f32[32,1,256]{2,1,0:T(1,128)S(1)} all-to-all(f32[32,1,256]{2,1,0:T(1,128)S(1)} %copy.9), channel_id=1, replica_groups=mesh['branch'=4,'segment'=2,'tp'=4] {'branch','segment','tp'}, dimensions={0} | all-to-all | bytes 65536 | tf_op jit(solution)/shard_map/all_to_all | solution.py:545
  105.7 0.0 copy-done.1
  105.7 0.9 finish.1
  (2 shorter events, 0.0 us)
Async XLA Ops:
  2.6 16.8 %collective-permute-start = (bf16[72,4224]{1,0:T(8,128)(2,1)S(1)}, bf16[72,4224]{1,0:T(8,128)(2,1)S(1)}, u32[]{:S(2)}, u32[]{:S(2)}) collective-permute-start(bf16[72,4224]{1,0:T(8,128)(2,1)S(1)} %get-tuple-element.29), channel_id=1, source_target_pairs={{0,4},{4,0},{1,5},{5,1},{2,6},{6,2},{3,7},{7,3},{8,12},{12,8},{9,1... | collective-permute-start | bytes 1824776 | tf_op jit(solution)/shard_map/ppermute | solution.py:488
  5.6 16.0 %collective-permute-start.3 = (bf16[72,4224]{1,0:T(8,128)(2,1)S(1)}, bf16[72,4224]{1,0:T(8,128)(2,1)S(1)}, u32[]{:S(2)}, u32[]{:S(2)}) collective-permute-start(bf16[72,4224]{1,0:T(8,128)(2,1)S(1)} %get-tuple-element.30.near_ref), channel_id=1, source_target_pairs={{0,16},{8,24},{16,0},{24,8},{1,17},{9,25},{17,1},{25,9},{2,18},{10... | collective-permute-start | bytes 1824776 | tf_op jit(solution)/shard_map/ppermute | solution.py:499
  19.4 14.9 %collective-permute-start.5 = (bf16[72,4224]{1,0:T(8,128)(2,1)S(1)}, bf16[72,4224]{1,0:T(8,128)(2,1)S(1)}, u32[]{:S(2)}, u32[]{:S(2)}) collective-permute-start(bf16[72,4224]{1,0:T(8,128)(2,1)S(1)} %collective-permute-done.near_ref.refs_0_), channel_id=1, source_target_pairs={{0,16},{8,24},{16,0},{24,8},{1,17},{9,25},{17,1},{25,9},{2,18},{10... | collective-permute-start | bytes 1824776 | tf_op jit(solution)/shard_map/ppermute | solution.py:500
  21.1 13.1 %collective-permute-start.1 = (bf16[72,4224]{1,0:T(8,128)(2,1)S(1)}, bf16[72,4224]{1,0:T(8,128)(2,1)S(1)}, u32[]{:S(2)}, u32[]{:S(2)}) collective-permute-start(bf16[72,4224]{1,0:T(8,128)(2,1)S(1)} %get-tuple-element.30.near_ref), channel_id=1, source_target_pairs={{0,8},{8,0},{16,24},{24,16},{1,9},{9,1},{17,25},{25,17},{2,10},{10... | collective-permute-start | bytes 1824776 | tf_op jit(solution)/shard_map/ppermute | solution.py:485
  21.1 23.6 %collective-permute-start.2 = (bf16[72,4224]{1,0:T(8,128)(2,1)S(1)}, bf16[72,4224]{1,0:T(8,128)(2,1)S(1)}, u32[]{:S(2)}, u32[]{:S(2)}) collective-permute-start(bf16[72,4224]{1,0:T(8,128)(2,1)S(1)} %collective-permute-done.near_ref.refs_0_), channel_id=1, source_target_pairs={{0,8},{8,0},{16,24},{24,16},{1,9},{9,1},{17,25},{25,17},{2,10},{10... | collective-permute-start | bytes 1824776 | tf_op jit(solution)/shard_map/ppermute | solution.py:485
  21.6 23.1 %collective-permute-start.4 = (bf16[72,4224]{1,0:T(8,128)(2,1)S(1)}, bf16[72,4224]{1,0:T(8,128)(2,1)S(1)}, u32[]{:S(2)}, u32[]{:S(2)}) collective-permute-start(bf16[72,4224]{1,0:T(8,128)(2,1)S(1)} %collective-permute-done.3.refs_2_), channel_id=1, source_target_pairs={{0,8},{8,0},{16,24},{24,16},{1,9},{9,1},{17,25},{25,17},{2,10},{10... | collective-permute-start | bytes 1824776 | tf_op jit(solution)/shard_map/ppermute | solution.py:485
  34.2 35.8 %collective-permute-start.6 = (bf16[72,4224]{1,0:T(8,128)(2,1)S(1)}, bf16[72,4224]{1,0:T(8,128)(2,1)S(1)}, u32[]{:S(2)}, u32[]{:S(2)}) collective-permute-start(bf16[72,4224]{1,0:T(8,128)(2,1)S(1)} %collective-permute-done.5.refs_0_), channel_id=1, source_target_pairs={{0,8},{8,0},{16,24},{24,16},{1,9},{9,1},{17,25},{25,17},{2,10},{10... | collective-permute-start | bytes 1824776 | tf_op jit(solution)/shard_map/ppermute | solution.py:485
  43.2 11.5 %collective-permute-start.8 = (bf16[144,1280]{1,0:T(8,128)(2,1)S(1)}, bf16[144,1280]{1,0:T(8,128)(2,1)S(1)}, u32[]{:S(2)}, u32[]{:S(2)}) collective-permute-start(bf16[144,1280]{1,0:T(8,128)(2,1)S(1)} %get-tuple-element.41), channel_id=1, source_target_pairs={{0,4},{4,0},{1,5},{5,1},{2,6},{6,2},{3,7},{7,3},{8,12},{12,8},{9,1... | collective-permute-start | bytes 1105928 | tf_op jit(solution)/shard_map/ppermute | solution.py:488
  49.7 31.2 %collective-permute-start.9 = (bf16[288,1024]{1,0:T(8,128)(2,1)S(1)}, bf16[288,1024]{1,0:T(8,128)(2,1)S(1)}, u32[]{:S(2)}, u32[]{:S(2)}) collective-permute-start(bf16[288,1024]{1,0:T(8,128)(2,1)S(1)} %get-tuple-element.43), channel_id=1, source_target_pairs={{0,4},{4,0},{1,5},{5,1},{2,6},{6,2},{3,7},{7,3},{8,12},{12,8},{9,1... | collective-permute-start | bytes 1769480 | tf_op jit(solution)/shard_map/ppermute | solution.py:488
  50.3 19.7 %collective-permute-start.7 = (bf16[288,256]{1,0:T(8,128)(2,1)S(1)}, bf16[288,256]{1,0:T(8,128)(2,1)S(1)}, u32[]{:S(2)}, u32[]{:S(2)}) collective-permute-start(bf16[288,256]{1,0:T(8,128)(2,1)S(1)} %get-tuple-element.40), channel_id=1, source_target_pairs={{0,4},{4,0},{1,5},{5,1},{2,6},{6,2},{3,7},{7,3},{8,12},{12,8},{9,1... | collective-permute-start | bytes 442376 | tf_op jit(solution)/shard_map/ppermute | solution.py:488
  73.1 16.0 %collective-permute-start.10 = (bf16[144,1024]{1,0:T(8,128)(2,1)S(1)}, bf16[144,1024]{1,0:T(8,128)(2,1)S(1)}, u32[]{:S(2)}, u32[]{:S(2)}) collective-permute-start(bf16[144,1024]{1,0:T(8,128)(2,1)S(1)} %get-tuple-element.44), channel_id=1, source_target_pairs={{0,4},{4,0},{1,5},{5,1},{2,6},{6,2},{3,7},{7,3},{8,12},{12,8},{9,1... | collective-permute-start | bytes 884744 | tf_op jit(solution)/shard_map/ppermute | solution.py:488
  74.7 14.4 %collective-permute-start.11 = (bf16[576,128]{1,0:T(8,128)(2,1)S(1)}, bf16[576,128]{1,0:T(8,128)(2,1)S(1)}, u32[]{:S(2)}, u32[]{:S(2)}) collective-permute-start(bf16[576,128]{1,0:T(8,128)(2,1)S(1)} %get-tuple-element.49), channel_id=1, source_target_pairs={{0,1},{1,3},{2,0},{3,2},{4,5},{5,7},{6,4},{7,6},{8,9},{9,11},{10,8... | collective-permute-start | bytes 442376 | tf_op jit(solution)/shard_map/ppermute | solution.py:524
  76.3 12.8 %collective-permute-start.12 = (bf16[576,128]{1,0:T(8,128)(2,1)S(1)}, bf16[576,128]{1,0:T(8,128)(2,1)S(1)}, u32[]{:S(2)}, u32[]{:S(2)}) collective-permute-start(bf16[576,128]{1,0:T(8,128)(2,1)S(1)} %get-tuple-element.50), channel_id=1, source_target_pairs={{1,2},{2,1},{5,6},{6,5},{9,10},{10,9},{13,14},{14,13},{17,18},{18,... | collective-permute-start | bytes 442376 | tf_op jit(solution)/shard_map/ppermute | solution.py:524
  77.0 12.1 %collective-permute-start.13 = (bf16[144,128]{1,0:T(8,128)(2,1)S(1)}, bf16[144,128]{1,0:T(8,128)(2,1)S(1)}, u32[]{:S(2)}, u32[]{:S(2)}) collective-permute-start(bf16[144,128]{1,0:T(8,128)(2,1)S(1)} %get-tuple-element.51), channel_id=1, source_target_pairs={{0,5},{1,7},{2,4},{3,6},{4,1},{5,3},{6,0},{7,2},{8,13},{9,15},{10,... | collective-permute-start | bytes 110600 | tf_op jit(solution)/shard_map/ppermute | solution.py:527
  80.9 8.2 %collective-permute-start.14 = (bf16[144,128]{1,0:T(8,128)(2,1)S(1)}, bf16[144,128]{1,0:T(8,128)(2,1)S(1)}, u32[]{:S(2)}, u32[]{:S(2)}) collective-permute-start(bf16[144,128]{1,0:T(8,128)(2,1)S(1)} %get-tuple-element.52), channel_id=1, source_target_pairs={{0,4},{1,6},{2,5},{3,7},{4,0},{5,2},{6,1},{7,3},{8,12},{9,14},{10,... | collective-permute-start | bytes 110600 | tf_op jit(solution)/shard_map/ppermute | solution.py:527
  87.6 1.5 %copy-start = (bf16[1,2048]{1,0:T(2,128)(2,1)S(1)}, bf16[1,2048]{1,0:T(2,128)(2,1)}, u32[]{:S(2)}) copy-start(bf16[1,2048]{1,0:T(2,128)(2,1)} %refs_17_.1) | copy-start | bytes 12292
  89.1 16.6 %copy-start.1 = (s32[72]{0:T(128)S(1)}, s32[72]{0:T(128)}, u32[]{:S(2)}) copy-start(s32[72]{0:T(128)} %param.9) | copy-start | bytes 868

commit v7 on v6

--- a/solution.py
+++ b/solution.py
@@ -27,16 +27,22 @@
     return pl.BlockSpec(memory_space=memory_space)
 
 
+def position():
+    branch = lax.axis_index("branch")
+    return branch & 1, lax.axis_index("segment"), branch >> 1, lax.axis_index("tp")
+
+
 def iota(shape, dimension):
     return lax.broadcasted_iota(jnp.int32, shape, dimension)
 
 
-def prepare_kernel(ids_ref, lengths_ref, rows_hbm, send_hbm, mine_ref, theirs_ref, rows_ref, send_ref, sems):
+def prepare_kernel(lengths_ref, rows_hbm, send_hbm, mine_ref, theirs_ref, rows_ref, send_ref, sems):
+    ids = position()
     count, width = rows_ref.shape
     half = width // 2
     parts = sems.shape[0] - 1
     step = width // parts
-    core, segment = ids_ref[0], ids_ref[1]
+    core, segment = ids[0], ids[1]
     copies = [pltpu.make_async_copy(send_hbm, send_ref, sems.at[parts])]
     for part in range(parts):
         at = pl.ds(part * step, step)
@@ -79,13 +85,13 @@
     mine_ref[:, half:] = tail
 
 
-def prepare(ids, lengths, rows, send):
+def prepare(lengths, rows, send):
     count, width = rows.shape
     shape = jax.ShapeDtypeStruct((count, width // 2 + LANES), BF16)
     return pl.pallas_call(
         prepare_kernel,
         out_shape=(shape, shape),
-        in_specs=[whole(pltpu.SMEM), whole(pltpu.SMEM), whole(pltpu.HBM), whole(pltpu.HBM)],
+        in_specs=[whole(pltpu.SMEM), whole(pltpu.HBM), whole(pltpu.HBM)],
         out_specs=(whole(), whole()),
         scratch_shapes=[
             pltpu.VMEM((count, width), BF16),
@@ -94,7 +100,7 @@
         ],
         compiler_params=pltpu.CompilerParams(vmem_limit_bytes=12 << 20),
         name="prepare",
-    )(ids, lengths, rows, send)
+    )(lengths, rows, send)
 
 
 BLOCK = 256
@@ -114,11 +120,11 @@
     return values[:, :HEAD], values[:, HEAD:]
 
 
-def chunk_body(ids_ref, pieces, gain_ref, head_ref, keyval_ref, query_ref, outs, waits, recv=None):
+def chunk_body(pieces, gain_ref, head_ref, keyval_ref, query_ref, outs, waits, recv=None):
     rows_ref, direct_ref = outs[:2]
     count = pieces[0].shape[0]
     half = rows_ref.shape[1]
-    core, segment, tp = ids_ref[0], ids_ref[1], ids_ref[3]
+    core, segment, _, tp = position()
     columns = query_ref.shape[1]
     top = (iota((count, 1), 0) < count // 2).astype(jnp.int32)
     mask = (top ^ core) == 1
@@ -179,12 +185,12 @@
         send_ref[:, at] = jnp.dot(rows_ref[...], query_ref[:, at], preferred_element_type=F32).astype(BF16)
 
 
-def first_chunk_kernel(ids_ref, near_ref, far_ref, gain_hbm, head_hbm, keyval_hbm, query_hbm, *refs):
+def first_chunk_kernel(near_ref, far_ref, gain_hbm, head_hbm, keyval_hbm, query_hbm, *refs):
     outs, (gain_ref, head_ref, keyval_ref, query_ref) = refs[:4], refs[4:8]
     own_query_ref, part_ref, small_sems, sems, own_sems = refs[8:]
     rows_ref = outs[0]
     half = rows_ref.shape[1]
-    segment, tp = ids_ref[1], ids_ref[3]
+    _, segment, _, tp = position()
     small = [
         pltpu.make_async_copy(
             gain_hbm.at[:, pl.ds(pl.multiple_of(segment * half, half), half)], gain_ref, small_sems.at[0]),
@@ -216,19 +222,19 @@
     def _():
         head_ref[:, pl.ds(pl.multiple_of((tp * width) % half, width), width)] = part_ref[...]
 
-    chunk_body(ids_ref, (near_ref, far_ref), gain_ref, head_ref, keyval_ref, query_ref, outs,
+    chunk_body((near_ref, far_ref), gain_ref, head_ref, keyval_ref, query_ref, outs,
                waits[:len(large)])
     for wait in waits[len(large):]:
         wait()
 
 
-def next_chunk_kernel(ids_ref, *refs, chips):
+def next_chunk_kernel(*refs, chips):
     pieces, refs = refs[:2 * chips], refs[2 * chips:]
-    chunk_body(ids_ref, pieces, *refs[:4], refs[4:], [])
-
-
-def last_chunk_kernel(ids_ref, *refs):
-    chunk_body(ids_ref, refs[:2], *refs[2:6], refs[10:], [], refs[6:10])
+    chunk_body(pieces, *refs[:4], refs[4:], [])
+
+
+def last_chunk_kernel(*refs):
+    chunk_body(refs[:2], *refs[2:6], refs[10:], [], refs[6:10])
 
 
 def shape_of(*shape, kind=BF16):
@@ -239,7 +245,7 @@
     return (shape_of(rows, half), shape_of(rows, LANES, kind=F32))
 
 
-def first_chunk(ids, near, far, gain, head, keyval, query):
+def first_chunk(near, far, gain, head, keyval, query):
     count, wide = near.shape
     half = wide - LANES
     columns = query.shape[1] // 2
@@ -251,7 +257,7 @@
     out = pl.pallas_call(
         first_chunk_kernel,
         out_shape=shapes,
-        in_specs=[whole(pltpu.SMEM), whole(), whole()] + [whole(pltpu.HBM)] * 4,
+        in_specs=[whole(), whole()] + [whole(pltpu.HBM)] * 4,
         out_specs=(whole(),) * len(shapes),
         scratch_shapes=[
             pltpu.VMEM(head.shape, BF16),
@@ -261,11 +267,11 @@
         ],
         compiler_params=pltpu.CompilerParams(vmem_limit_bytes=14 << 20),
         name="first_chunk",
-    )(ids, near, far, gain, head, keyval, query)
+    )(near, far, gain, head, keyval, query)
     return out[:4], out[4:8], out[8]
 
 
-def next_chunk(ids, pieces, weights):
+def next_chunk(pieces, weights):
     count, wide = pieces[0].shape
     chips = len(pieces) // 2
     rows = 2 * chips * count
@@ -274,14 +280,14 @@
     return pl.pallas_call(
         functools.partial(next_chunk_kernel, chips=chips),
         out_shape=shapes,
-        in_specs=[whole(pltpu.SMEM)] + [whole()] * (len(pieces) + 4),
+        in_specs=[whole()] * (len(pieces) + 4),
         out_specs=(whole(),) * len(shapes),
         compiler_params=pltpu.CompilerParams(vmem_limit_bytes=14 << 20),
         name="next_chunk",
-    )(ids, *pieces, *weights)
-
-
-def last_chunk(ids, pieces, weights, parts):
+    )(*pieces, *weights)
+
+
+def last_chunk(pieces, weights, parts):
     count, wide = pieces[0].shape
     rows = 2 * count
     shapes = chunk_shapes(rows, wide - LANES) + (
@@ -289,11 +295,11 @@
     return pl.pallas_call(
         last_chunk_kernel,
         out_shape=shapes,
-        in_specs=[whole(pltpu.SMEM)] + [whole()] * (len(pieces) + 8),
+        in_specs=[whole()] * (len(pieces) + 8),
         out_specs=(whole(),) * len(shapes),
         compiler_params=pltpu.CompilerParams(vmem_limit_bytes=14 << 20),
         name="last_chunk",
-    )(ids, *pieces, *weights, *parts)
+    )(*pieces, *weights, *parts)
 
 
 def own_body(rows_ref, query_ref, out_ref, waits=()):
@@ -324,31 +330,32 @@
     return jnp.concatenate([part[pack * count:(pack + 1) * count] for part in parts], axis=0)
 
 
-def owner_of(row, pack, ids_ref, piece_rows):
+def owner_of(row, pack, ids, piece_rows):
     index = jnp.zeros_like(row)
     for step in range(1, 8):
         index = index + (row >= step * piece_rows).astype(jnp.int32)
     chip, low = index >> 1, index & 1
-    shard = (((chip >> 1) ^ ids_ref[2]) * 2 + (low ^ pack)) * 2 + ((chip & 1) ^ ids_ref[1])
+    shard = (((chip >> 1) ^ ids[2]) * 2 + (low ^ pack)) * 2 + ((chip & 1) ^ ids[1])
     return shard, row - index * piece_rows
 
 
-def mask_kernel(ids_ref, lengths_ref, near_ref, out_ref):
-    segment = ids_ref[1]
+def mask_kernel(lengths_ref, near_ref, out_ref):
+    ids = position()
+    segment = ids[1]
     rows = out_ref.shape[1]
     piece_rows = rows // 8
     tail = near_ref[:, near_ref.shape[1] - LANES:].astype(F32)[:1].astype(jnp.int32)
     for pack in range(2):
         def place(row):
-            shard, inner = owner_of(row, pack, ids_ref, piece_rows)
-            position = shard * piece_rows + inner
+            shard, inner = owner_of(row, pack, ids, piece_rows)
+            place_in_pack = shard * piece_rows + inner
             end = jnp.zeros((1, 1), jnp.int32)
-            doc = jnp.zeros_like(position)
+            doc = jnp.zeros_like(place_in_pack)
             for index in range(lengths_ref.shape[1]):
                 at = LENGTHS_AT + index
                 end = end + jnp.where(segment == pack, lengths_ref[0, index], tail[:, at:at + 1])
-                doc = doc + (position >= end).astype(jnp.int32)
-            return position, doc
+                doc = doc + (place_in_pack >= end).astype(jnp.int32)
+            return place_in_pack, doc
 
         row_position, row_doc = place(iota((rows, 1), 0))
         col_position, col_doc = place(iota((1, rows), 1))
@@ -356,23 +363,24 @@
         out_ref[pack * rows:(pack + 1) * rows, :] = jnp.where(visible, 0.0, -1e30)
 
 
-def masks(ids, lengths, near, rows):
+def masks(lengths, near, rows):
     return pl.pallas_call(
         mask_kernel,
         out_shape=shape_of(2 * rows, rows, kind=F32),
-        in_specs=[whole(pltpu.SMEM), whole(pltpu.SMEM), whole()],
+        in_specs=[whole(pltpu.SMEM), whole()],
         out_specs=whole(),
         compiler_params=pltpu.CompilerParams(vmem_limit_bytes=4 << 20),
         name="masks",
-    )(ids, lengths, near)
-
-
-def attention_kernel(ids_ref, bias_ref, *refs, starts, recv_starts):
+    )(lengths, near)
+
+
+def attention_kernel(bias_ref, *refs, starts, recv_starts):
     chips = len(starts)
     owns, recvs, directs = (refs[index * chips:(index + 1) * chips] for index in range(3))
     refs = refs[3 * chips:]
     nears, fars, gain_ref, out_ref = refs[0:3], refs[3:5], refs[5], refs[6]
-    segment, tp = ids_ref[1], ids_ref[3]
+    ids = position()
+    segment, tp = ids[1], ids[3]
     rows = bias_ref.shape[1]
     slab = rows // 2
     queries = rows
@@ -419,8 +427,8 @@
             offset = pl.multiple_of(segment * heads * HEAD + head * HEAD, HEAD)
             total = total + both[:, :HEAD] / both[:, HEAD:] * gain_ref[:, pl.ds(offset, HEAD)].astype(F32)
 
-        _, inner = owner_of(iota((queries, 1), 0), pack, ids_ref, piece_rows)
-        shard_row, _ = owner_of(iota((1, queries), 1), pack, ids_ref, piece_rows)
+        _, inner = owner_of(iota((queries, 1), 0), pack, ids, piece_rows)
+        shard_row, _ = owner_of(iota((1, queries), 1), pack, ids, piece_rows)
         chosen = ((iota((devices, 1), 0) >> 2) == shard_row).astype(F32)
         hit = lane == inner + pack * piece_rows
 
@@ -433,15 +441,15 @@
     out_ref[:, wide:] = direct
 
 
-def attention(ids, bias, owns, starts, recvs, recv_starts, directs, near, far, gain, devices):
+def attention(bias, owns, starts, recvs, recv_starts, directs, near, far, gain, devices):
     return pl.pallas_call(
         functools.partial(attention_kernel, starts=starts, recv_starts=recv_starts),
         out_shape=shape_of(devices, 2 * LANES, kind=F32),
-        in_specs=[whole(pltpu.SMEM)] + [whole()] * (7 + 3 * len(owns)),
+        in_specs=[whole()] * (7 + 3 * len(owns)),
         out_specs=whole(),
         compiler_params=pltpu.CompilerParams(vmem_limit_bytes=14 << 20),
         name="attend",
-    )(ids, bias, *owns, *recvs, *directs, *near, *far, gain)
+    )(bias, *owns, *recvs, *directs, *near, *far, gain)
 
 
 def finish_kernel(recv_ref, send_ref, out_ref):
@@ -471,11 +479,7 @@
 
 def paired(rollout, send_rows, seq_lengths, attn_gain, w_query, w_keyval, head_weight, head_attn):
     n_branch = lax.axis_size("branch")
-    branch = lax.axis_index("branch")
-    segment = lax.axis_index("segment")
-    tp = lax.axis_index("tp")
     send = send_rows.reshape(1, -1)
-    ids = jnp.stack([branch & 1, segment, branch >> 1, tp]).astype(jnp.int32)
 
     core_pairs = [(i, i ^ 1) for i in range(n_branch)]
     y_pairs = [(i, i ^ 2) for i in range(n_branch)]
@@ -494,7 +498,7 @@
     rollout, send, attn_gain, head_weight, seq_lengths = map(
         in_hbm, (rollout, send, attn_gain, head_weight, seq_lengths))
     wq, wkv = in_hbm(w_query[0]), in_hbm(w_keyval[0])
-    mine, theirs = prepare(ids, seq_lengths, rollout, send)
+    mine, theirs = prepare(seq_lengths, rollout, send)
     from_x = across(theirs)
     from_y = lax.ppermute(mine, "branch", y_pairs)
     from_d = lax.ppermute(from_x, "branch", y_pairs)
@@ -506,13 +510,13 @@
 
     pieces = with_swapped(mine)
     (rows, direct_own, local_own, part), weights, own_weights = first_chunk(
-        ids, *pieces, attn_gain, head_weight, wkv, wq)
+        *pieces, attn_gain, head_weight, wkv, wq)
     received_own = across(part)
     query_own = own_queries(rows, own_weights)
-    bias = masks(ids, seq_lengths, from_x, 2 * slab)
-
-    pieces = with_swapped(from_x, from_y)
-    rows, direct_xy, local_xy, part, keyval = next_chunk(ids, pieces, weights)
+    bias = masks(seq_lengths, from_x, 2 * slab)
+
+    pieces = with_swapped(from_x) + with_swapped(from_y)
+    rows, direct_xy, local_xy, part, keyval = next_chunk(pieces, weights)
     keyval_xy = across(keyval)
     received_xy = across(part)
     query_xy = own_queries(rows, own_weights)
@@ -529,7 +533,7 @@
 
     pieces = with_swapped(from_d)
     rows, direct_d, part, keep, first, second, far_first, far_second = last_chunk(
-        ids, pieces, weights, (local_own, local_xy, keyval_xy, received_own))
+        pieces, weights, (local_own, local_xy, keyval_xy, received_own))
     received_d = across(part)
     first = hand(first, hand_first)
     second = hand(second, hand_second)
@@ -538,7 +542,7 @@
     query_d = own_queries(rows, own_weights)
     devices = n_branch * 2 * n_tp
     outgoing = attention(
-        ids, bias, [query_own, query_xy, query_xy, query_d], (0, 0, slab, 0),
+        bias, [query_own, query_xy, query_xy, query_d], (0, 0, slab, 0),
         [received_xy, received_own, received_d, received_xy], (0, 0, 0, slab),
         [direct_own, direct_xy, direct_xy, direct_d],
         (keep, first, second), (far_first, far_second), head_attn, devices)

time: 107 us -> 105 us (0.981)
  Pallas kernels: 32.1 us -> 29.6 us
    pallas_call x2, Pallas kernels: 12 us -> 10.8 us  [the longest x1 8.38 us: first_chunk(): pl.pallas_call(first_chunk_kernel, out_shape=shapes, in_specs=[whole(), w...]
  transfers between devices with their start and end apart: 15 -> 15, of which waited for: 4 -> 4; matrix products, arithmetic and copies ran while one was open for 0% -> 0% of each run, Pallas kernels for 22% -> 21%
where the time goes in v7:
time: 105 us
  waiting for transfers between devices  43.8 us (42%)
  Pallas kernels  29.6 us (28%)
  starting transfers between devices  19.8 us (19%)
  blocking collectives  11.2 us (11%)
    ppermute x5, waiting for transfers between devices, across(): return lax.ppermute(part, 'segment', x_pairs)  31.1 us
    ppermute x1, waiting for transfers between devices, paired(): from_d = lax.ppermute(from_x, 'branch', y_pairs)  12.6 us
    all_to_all x1, blocking collectives, paired(): lax.all_to_all(outgoing, ALL_AXES, split_axis=0, concat_axis=0, tiled=True)  11.2 us
    pallas_call x1, Pallas kernels, first_chunk(): pl.pallas_call(first_chunk_kernel, out_shape=shapes, in_specs=[whole(), w...  8.38 us
    ppermute x5, starting transfers between devices, across(): return lax.ppermute(part, 'segment', x_pairs)  8.27 us
    ppermute x2, starting transfers between devices, hand_across(): lax.ppermute(array, ('segment', 'tp'), [(side * n_tp + i, (1 - side) * n_...  5.55 us
    pallas_call x3, Pallas kernels, own_queries(): pl.pallas_call(own_body, out_shape=shape_of(rows.shape[0], query.shape[1]...  5.46 us
    pallas_call x1, Pallas kernels, attention(): pl.pallas_call(functools.partial(attention_kernel, starts=starts, recv_st...  4.6 us
  transfers between devices with their start and end apart: 15, of which 4 were waited for; matrix products, arithmetic and copies ran while one was open for 0% of the time, Pallas kernels for 21%

profile of v7, /device:TPU:0, one launch (start us, length us, event | category | flops | bytes accessed | tf_op | source)
XLA Modules:
  0.0 104.6 jit_solution(9449420262123666684)
XLA Ops:
  0.0 2.5 %prepare.1 = (bf16[72,4224]{1,0:T(8,128)(2,1)S(1)}, bf16[72,4224]{1,0:T(8,128)(2,1)S(1)}) custom-call(s32[1,6]{1,0:T(1,128)} %lengths_ref.3, bf16[72,8192]{1,0:T(8,128)(2,1)} %rows_hbm.1, s32[1,72]{1,0:T(1,128)} %bitcast.9), custom_call_target="tpu_custom_call" | custom-call | tf_op jit(solution)/shard_map/prepare/pallas_call | solution.py:91
  2.5 3.0 %collective-permute-start = (bf16[72,4224]{1,0:T(8,128)(2,1)S(1)}, bf16[72,4224]{1,0:T(8,128)(2,1)S(1)}, u32[]{:S(2)}, u32[]{:S(2)}) collective-permute-start(bf16[72,4224]{1,0:T(8,128)(2,1)S(1)} %get-tuple-element.29), channel_id=1, source_target_pairs={{0,4},{4,0},{1,5},{5,1},{2,6},{6,2},{3,7},{7,3},{8,12},{12,8},{9,1... | collective-permute-start | bytes 1824776 | tf_op jit(solution)/shard_map/ppermute | solution.py:492
  5.6 1.5 %collective-permute-start.3 = (bf16[72,4224]{1,0:T(8,128)(2,1)S(1)}, bf16[72,4224]{1,0:T(8,128)(2,1)S(1)}, u32[]{:S(2)}, u32[]{:S(2)}) collective-permute-start(bf16[72,4224]{1,0:T(8,128)(2,1)S(1)} %get-tuple-element.30.near_ref), channel_id=1, source_target_pairs={{0,16},{8,24},{16,0},{24,8},{1,17},{9,25},{17,1},{25,9},{2,18},{10... | collective-permute-start | bytes 1824776 | tf_op jit(solution)/shard_map/ppermute | solution.py:503
  7.1 12.2 %collective-permute-done.near_ref.refs_0_ = bf16[72,4224]{1,0:T(8,128)(2,1)S(1)} collective-permute-done((bf16[72,4224]{1,0:T(8,128)(2,1)S(1)}, bf16[72,4224]{1,0:T(8,128)(2,1)S(1)}, u32[]{:S(2)}, u32[]{:S(2)}) %collective-permute-start) | collective-permute-done | bytes 608288 | tf_op jit(solution)/shard_map/ppermute | solution.py:492
  19.3 1.8 %collective-permute-start.5 = (bf16[72,4224]{1,0:T(8,128)(2,1)S(1)}, bf16[72,4224]{1,0:T(8,128)(2,1)S(1)}, u32[]{:S(2)}, u32[]{:S(2)}) collective-permute-start(bf16[72,4224]{1,0:T(8,128)(2,1)S(1)} %collective-permute-done.near_ref.refs_0_), channel_id=1, source_target_pairs={{0,16},{8,24},{16,0},{24,8},{1,17},{9,25},{17,1},{25,9},{2,18},{10... | collective-permute-start | bytes 1824776 | tf_op jit(solution)/shard_map/ppermute | solution.py:504
  21.0 0.0 collective-permute-start.1
  21.1 0.5 collective-permute-start.2
  21.6 0.0 collective-permute-done.3.refs_2_
  21.6 0.0 collective-permute-start.4
  21.6 12.6 %collective-permute-done.5.refs_0_ = bf16[72,4224]{1,0:T(8,128)(2,1)S(1)} collective-permute-done((bf16[72,4224]{1,0:T(8,128)(2,1)S(1)}, bf16[72,4224]{1,0:T(8,128)(2,1)S(1)}, u32[]{:S(2)}, u32[]{:S(2)}) %collective-permute-start.5) | collective-permute-done | bytes 608288 | tf_op jit(solution)/shard_map/ppermute | solution.py:504
  34.2 0.0 collective-permute-start.6
  34.2 0.0 collective-permute-done.1.far_ref
  34.2 8.4 %first_chunk.1 = (bf16[144,4096]{1,0:T(8,128)(2,1)S(1)}, f32[144,128]{1,0:T(8,128)S(1)}, f32[144,256]{1,0:T(8,128)S(1)}, bf16[144,1280]{1,0:T(8,128)(2,1)S(1)}, ...) custom-call(bf16[72,4224]{1,0:T(8,128)(2,1)S(1)} %get-tuple-element., ...), custom_call_target="tpu_custom_call" | custom-call | tf_op jit(solution)/shard_map/first_chunk/pallas_call | solution.py:257
  42.6 1.6 %collective-permute-start.8 = (bf16[144,1280]{1,0:T(8,128)(2,1)S(1)}, bf16[144,1280]{1,0:T(8,128)(2,1)S(1)}, u32[]{:S(2)}, u32[]{:S(2)}) collective-permute-start(bf16[144,1280]{1,0:T(8,128)(2,1)S(1)} %get-tuple-element.41), channel_id=1, source_target_pairs={{0,4},{4,0},{1,5},{5,1},{2,6},{6,2},{3,7},{7,3},{8,12},{12,8},{9,1... | collective-permute-start | bytes 1105928 | tf_op jit(solution)/shard_map/ppermute | solution.py:492
  44.1 0.0 collective-permute-done.2.refs_1_
  44.1 0.0 collective-permute-done.4.refs_3_
  44.1 4.3 %next_chunk.1 = (bf16[288,4096]{1,0:T(8,128)(2,1)S(1)}, f32[288,128]{1,0:T(8,128)S(1)}, f32[288,256]{1,0:T(8,128)S(1)}, bf16[288,1024]{1,0:T(8,128)(2,1)S(1)}, bf16[288,256]{1,0:T(8,128)(2,1)S(1)}) custom-call(bf16[72,4224]{1,0:T(8,128)(2,1)S(1)} %collective-permute-done.near_ref.refs_0_, bf16[72,4224]{1,0:T(8,128)(2,1)S(1)} %collective-permute-done.2.refs_1_, ...), custom_call_target="tpu_custom_call" | custom-call | tf_op jit(solution)/shard_map/next_chunk/pallas_call | solution.py:280
  48.4 0.6 collective-permute-start.9
  49.0 1.5 %collective-permute-start.7 = (bf16[288,256]{1,0:T(8,128)(2,1)S(1)}, bf16[288,256]{1,0:T(8,128)(2,1)S(1)}, u32[]{:S(2)}, u32[]{:S(2)}) collective-permute-start(bf16[288,256]{1,0:T(8,128)(2,1)S(1)} %get-tuple-element.40), channel_id=1, source_target_pairs={{0,4},{4,0},{1,5},{5,1},{2,6},{6,2},{3,7},{7,3},{8,12},{12,8},{9,1... | collective-permute-start | bytes 442376 | tf_op jit(solution)/shard_map/ppermute | solution.py:492
  50.5 3.6 %collective-permute-done.8.refs_9_.refs_5_ = bf16[144,1280]{1,0:T(8,128)(2,1)S(1)} collective-permute-done((bf16[144,1280]{1,0:T(8,128)(2,1)S(1)}, bf16[144,1280]{1,0:T(8,128)(2,1)S(1)}, u32[]{:S(2)}, u32[]{:S(2)}) %collective-permute-start.8) | collective-permute-done | bytes 368672 | tf_op jit(solution)/shard_map/ppermute | solution.py:492
  54.1 15.3 %collective-permute-done.7.refs_8_ = bf16[288,256]{1,0:T(8,128)(2,1)S(1)} collective-permute-done((bf16[288,256]{1,0:T(8,128)(2,1)S(1)}, bf16[288,256]{1,0:T(8,128)(2,1)S(1)}, u32[]{:S(2)}, u32[]{:S(2)}) %collective-permute-start.7) | collective-permute-done | bytes 147488 | tf_op jit(solution)/shard_map/ppermute | solution.py:492
  69.4 0.0 collective-permute-done.6.refs_1_
  69.4 2.4 %last_chunk.1 = (bf16[144,4096]{1,0:T(8,128)(2,1)S(1)}, f32[144,128]{1,0:T(8,128)S(1)}, bf16[144,1024]{1,0:T(8,128)(2,1)S(1)}, bf16[576,128]{1,0:T(8,128)(2,1)S(...) custom-call(bf16[72,4224]{1,0:T(8,128)(2,1)S(1)} %collective-permute, ...), custom_call_target="tpu_custom_call" | custom-call | tf_op jit(solution)/shard_map/last_chunk/pallas_call | solution.py:295
  71.9 1.6 %collective-permute-start.10 = (bf16[144,1024]{1,0:T(8,128)(2,1)S(1)}, bf16[144,1024]{1,0:T(8,128)(2,1)S(1)}, u32[]{:S(2)}, u32[]{:S(2)}) collective-permute-start(bf16[144,1024]{1,0:T(8,128)(2,1)S(1)} %get-tuple-element.44), channel_id=1, source_target_pairs={{0,4},{4,0},{1,5},{5,1},{2,6},{6,2},{3,7},{7,3},{8,12},{12,8},{9,1... | collective-permute-start | bytes 884744 | tf_op jit(solution)/shard_map/ppermute | solution.py:492
  73.4 1.6 %collective-permute-start.11 = (bf16[576,128]{1,0:T(8,128)(2,1)S(1)}, bf16[576,128]{1,0:T(8,128)(2,1)S(1)}, u32[]{:S(2)}, u32[]{:S(2)}) collective-permute-start(bf16[576,128]{1,0:T(8,128)(2,1)S(1)} %get-tuple-element.49), channel_id=1, source_target_pairs={{0,1},{1,3},{2,0},{3,2},{4,5},{5,7},{6,4},{7,6},{8,9},{9,11},{10,8... | collective-permute-start | bytes 442376 | tf_op jit(solution)/shard_map/ppermute | solution.py:528
  75.0 0.7 collective-permute-start.12
  75.7 4.0 %collective-permute-start.13 = (bf16[144,128]{1,0:T(8,128)(2,1)S(1)}, bf16[144,128]{1,0:T(8,128)(2,1)S(1)}, u32[]{:S(2)}, u32[]{:S(2)}) collective-permute-start(bf16[144,128]{1,0:T(8,128)(2,1)S(1)} %get-tuple-element.51), channel_id=1, source_target_pairs={{0,5},{1,7},{2,4},{3,6},{4,1},{5,3},{6,0},{7,2},{8,13},{9,15},{10,... | collective-permute-start | bytes 110600 | tf_op jit(solution)/shard_map/ppermute | solution.py:531
  79.7 0.0 collective-permute-done.9.refs_4_.refs_7_
  79.7 1.6 %collective-permute-start.14 = (bf16[144,128]{1,0:T(8,128)(2,1)S(1)}, bf16[144,128]{1,0:T(8,128)(2,1)S(1)}, u32[]{:S(2)}, u32[]{:S(2)}) collective-permute-start(bf16[144,128]{1,0:T(8,128)(2,1)S(1)} %get-tuple-element.52), channel_id=1, source_target_pairs={{0,4},{1,6},{2,5},{3,7},{4,0},{5,2},{6,1},{7,3},{8,12},{9,14},{10,... | collective-permute-start | bytes 110600 | tf_op jit(solution)/shard_map/ppermute | solution.py:531
  81.2 1.4 %own_queries.3.refs_0_ = f32[144,1024]{1,0:T(8,128)S(1)} custom-call(bf16[144,4096]{1,0:T(8,128)(2,1)S(1)} %get-tuple-element.31.rows_ref, bf16[4096,1024]{1,0:T(8,128)(2,1)S(1)} %get-tuple-element.32.query_ref), custom_call_target="tpu_custom_call" | custom-call | tf_op jit(solution)/shard_map/own_queries/pallas_call | solution.py:314
  82.7 1.0 %masks.1.bias_ref = f32[576,288]{1,0:T(8,128)S(1)} custom-call(s32[1,6]{1,0:T(1,128)} %lengths_ref.3, bf16[72,4224]{1,0:T(8,128)(2,1)S(1)} %collective-permute-done.near_ref.refs_0_), custom_call_target="tpu_custom_call" | custom-call | tf_op jit(solution)/shard_map/masks/pallas_call | solution.py:367
  83.7 2.6 %own_queries.4.refs_1_.refs_2_ = f32[288,1024]{1,0:T(8,128)S(1)} custom-call(bf16[288,4096]{1,0:T(8,128)(2,1)S(1)} %get-tuple-element.37.rows_ref, bf16[4096,1024]{1,0:T(8,128)(2,1)S(1)} %get-tuple-element.32.query_ref), custom_call_target="tpu_custom_call" | custom-call | tf_op jit(solution)/shard_map/own_queries/pallas_call | solution.py:314
  86.3 0.0 copy-start
  86.3 1.4 %own_queries.5.refs_3_ = f32[144,1024]{1,0:T(8,128)S(1)} custom-call(bf16[144,4096]{1,0:T(8,128)(2,1)S(1)} %get-tuple-element.42.rows_ref, bf16[4096,1024]{1,0:T(8,128)(2,1)S(1)} %get-tuple-element.32.query_ref), custom_call_target="tpu_custom_call" | custom-call | tf_op jit(solution)/shard_map/own_queries/pallas_call | solution.py:314
  87.8 0.0 copy-start.1
  87.8 0.0 collective-permute-done.13.refs_15_
  87.8 0.0 collective-permute-done.14.refs_16_
  87.8 0.0 collective-permute-done.11.refs_13_
  87.8 0.0 collective-permute-done.12.refs_14_
  87.8 0.0 collective-permute-done.10.refs_6_
  87.8 0.0 copy-done
  87.8 4.6 %attend.1 = f32[32,256]{1,0:T(8,128)S(1)} custom-call(f32[576,288]{1,0:T(8,128)S(1)} %masks.1.bias_ref, f32[144,1024]{1,0:T(8,128)S(1)} %own_queries.3.refs_0_, f32[288,1024]{1,0:T(8,128)S(1)} %own_queries.4.refs_1_.refs_2_, f32[288,1024]{1,0:T(8,128)S(1)} %own_queries.4.refs_1_.refs_2_, f32[144,1024]{1,0:T(8,128)S(1)} %own_queries.5.refs_3_, ...), custom_call_target="tpu_custom_call" | custom-call | tf_op jit(solution)/shard_map/attend/pallas_call | solution.py:445
  92.5 11.2 %all_to_all.11 = f32[32,1,256]{2,1,0:T(1,128)S(1)} all-to-all(f32[32,1,256]{2,1,0:T(1,128)S(1)} %copy.9), channel_id=1, replica_groups=mesh['branch'=4,'segment'=2,'tp'=4] {'branch','segment','tp'}, dimensions={0} | all-to-all | bytes 65536 | tf_op jit(solution)/shard_map/all_to_all | solution.py:549
  103.7 0.0 copy-done.1
  103.7 0.9 finish.1
  (2 shorter events, 0.0 us)
Async XLA Ops:
  2.5 16.8 %collective-permute-start = (bf16[72,4224]{1,0:T(8,128)(2,1)S(1)}, bf16[72,4224]{1,0:T(8,128)(2,1)S(1)}, u32[]{:S(2)}, u32[]{:S(2)}) collective-permute-start(bf16[72,4224]{1,0:T(8,128)(2,1)S(1)} %get-tuple-element.29), channel_id=1, source_target_pairs={{0,4},{4,0},{1,5},{5,1},{2,6},{6,2},{3,7},{7,3},{8,12},{12,8},{9,1... | collective-permute-start | bytes 1824776 | tf_op jit(solution)/shard_map/ppermute | solution.py:492
  5.6 16.0 %collective-permute-start.3 = (bf16[72,4224]{1,0:T(8,128)(2,1)S(1)}, bf16[72,4224]{1,0:T(8,128)(2,1)S(1)}, u32[]{:S(2)}, u32[]{:S(2)}) collective-permute-start(bf16[72,4224]{1,0:T(8,128)(2,1)S(1)} %get-tuple-element.30.near_ref), channel_id=1, source_target_pairs={{0,16},{8,24},{16,0},{24,8},{1,17},{9,25},{17,1},{25,9},{2,18},{10... | collective-permute-start | bytes 1824776 | tf_op jit(solution)/shard_map/ppermute | solution.py:503
  19.3 14.9 %collective-permute-start.5 = (bf16[72,4224]{1,0:T(8,128)(2,1)S(1)}, bf16[72,4224]{1,0:T(8,128)(2,1)S(1)}, u32[]{:S(2)}, u32[]{:S(2)}) collective-permute-start(bf16[72,4224]{1,0:T(8,128)(2,1)S(1)} %collective-permute-done.near_ref.refs_0_), channel_id=1, source_target_pairs={{0,16},{8,24},{16,0},{24,8},{1,17},{9,25},{17,1},{25,9},{2,18},{10... | collective-permute-start | bytes 1824776 | tf_op jit(solution)/shard_map/ppermute | solution.py:504
  21.0 13.1 %collective-permute-start.1 = (bf16[72,4224]{1,0:T(8,128)(2,1)S(1)}, bf16[72,4224]{1,0:T(8,128)(2,1)S(1)}, u32[]{:S(2)}, u32[]{:S(2)}) collective-permute-start(bf16[72,4224]{1,0:T(8,128)(2,1)S(1)} %get-tuple-element.30.near_ref), channel_id=1, source_target_pairs={{0,8},{8,0},{16,24},{24,16},{1,9},{9,1},{17,25},{25,17},{2,10},{10... | collective-permute-start | bytes 1824776 | tf_op jit(solution)/shard_map/ppermute | solution.py:489
  21.1 23.1 %collective-permute-start.2 = (bf16[72,4224]{1,0:T(8,128)(2,1)S(1)}, bf16[72,4224]{1,0:T(8,128)(2,1)S(1)}, u32[]{:S(2)}, u32[]{:S(2)}) collective-permute-start(bf16[72,4224]{1,0:T(8,128)(2,1)S(1)} %collective-permute-done.near_ref.refs_0_), channel_id=1, source_target_pairs={{0,8},{8,0},{16,24},{24,16},{1,9},{9,1},{17,25},{25,17},{2,10},{10... | collective-permute-start | bytes 1824776 | tf_op jit(solution)/shard_map/ppermute | solution.py:489
  21.6 22.6 %collective-permute-start.4 = (bf16[72,4224]{1,0:T(8,128)(2,1)S(1)}, bf16[72,4224]{1,0:T(8,128)(2,1)S(1)}, u32[]{:S(2)}, u32[]{:S(2)}) collective-permute-start(bf16[72,4224]{1,0:T(8,128)(2,1)S(1)} %collective-permute-done.3.refs_2_), channel_id=1, source_target_pairs={{0,8},{8,0},{16,24},{24,16},{1,9},{9,1},{17,25},{25,17},{2,10},{10... | collective-permute-start | bytes 1824776 | tf_op jit(solution)/shard_map/ppermute | solution.py:489
  34.2 35.3 %collective-permute-start.6 = (bf16[72,4224]{1,0:T(8,128)(2,1)S(1)}, bf16[72,4224]{1,0:T(8,128)(2,1)S(1)}, u32[]{:S(2)}, u32[]{:S(2)}) collective-permute-start(bf16[72,4224]{1,0:T(8,128)(2,1)S(1)} %collective-permute-done.5.refs_0_), channel_id=1, source_target_pairs={{0,8},{8,0},{16,24},{24,16},{1,9},{9,1},{17,25},{25,17},{2,10},{10... | collective-permute-start | bytes 1824776 | tf_op jit(solution)/shard_map/ppermute | solution.py:489
  42.6 11.5 %collective-permute-start.8 = (bf16[144,1280]{1,0:T(8,128)(2,1)S(1)}, bf16[144,1280]{1,0:T(8,128)(2,1)S(1)}, u32[]{:S(2)}, u32[]{:S(2)}) collective-permute-start(bf16[144,1280]{1,0:T(8,128)(2,1)S(1)} %get-tuple-element.41), channel_id=1, source_target_pairs={{0,4},{4,0},{1,5},{5,1},{2,6},{6,2},{3,7},{7,3},{8,12},{12,8},{9,1... | collective-permute-start | bytes 1105928 | tf_op jit(solution)/shard_map/ppermute | solution.py:492
  48.4 31.2 %collective-permute-start.9 = (bf16[288,1024]{1,0:T(8,128)(2,1)S(1)}, bf16[288,1024]{1,0:T(8,128)(2,1)S(1)}, u32[]{:S(2)}, u32[]{:S(2)}) collective-permute-start(bf16[288,1024]{1,0:T(8,128)(2,1)S(1)} %get-tuple-element.43), channel_id=1, source_target_pairs={{0,4},{4,0},{1,5},{5,1},{2,6},{6,2},{3,7},{7,3},{8,12},{12,8},{9,1... | collective-permute-start | bytes 1769480 | tf_op jit(solution)/shard_map/ppermute | solution.py:492
  49.0 20.4 %collective-permute-start.7 = (bf16[288,256]{1,0:T(8,128)(2,1)S(1)}, bf16[288,256]{1,0:T(8,128)(2,1)S(1)}, u32[]{:S(2)}, u32[]{:S(2)}) collective-permute-start(bf16[288,256]{1,0:T(8,128)(2,1)S(1)} %get-tuple-element.40), channel_id=1, source_target_pairs={{0,4},{4,0},{1,5},{5,1},{2,6},{6,2},{3,7},{7,3},{8,12},{12,8},{9,1... | collective-permute-start | bytes 442376 | tf_op jit(solution)/shard_map/ppermute | solution.py:492
  71.9 16.0 %collective-permute-start.10 = (bf16[144,1024]{1,0:T(8,128)(2,1)S(1)}, bf16[144,1024]{1,0:T(8,128)(2,1)S(1)}, u32[]{:S(2)}, u32[]{:S(2)}) collective-permute-start(bf16[144,1024]{1,0:T(8,128)(2,1)S(1)} %get-tuple-element.44), channel_id=1, source_target_pairs={{0,4},{4,0},{1,5},{5,1},{2,6},{6,2},{3,7},{7,3},{8,12},{12,8},{9,1... | collective-permute-start | bytes 884744 | tf_op jit(solution)/shard_map/ppermute | solution.py:492
  73.4 14.4 %collective-permute-start.11 = (bf16[576,128]{1,0:T(8,128)(2,1)S(1)}, bf16[576,128]{1,0:T(8,128)(2,1)S(1)}, u32[]{:S(2)}, u32[]{:S(2)}) collective-permute-start(bf16[576,128]{1,0:T(8,128)(2,1)S(1)} %get-tuple-element.49), channel_id=1, source_target_pairs={{0,1},{1,3},{2,0},{3,2},{4,5},{5,7},{6,4},{7,6},{8,9},{9,11},{10,8... | collective-permute-start | bytes 442376 | tf_op jit(solution)/shard_map/ppermute | solution.py:528
  75.0 12.8 %collective-permute-start.12 = (bf16[576,128]{1,0:T(8,128)(2,1)S(1)}, bf16[576,128]{1,0:T(8,128)(2,1)S(1)}, u32[]{:S(2)}, u32[]{:S(2)}) collective-permute-start(bf16[576,128]{1,0:T(8,128)(2,1)S(1)} %get-tuple-element.50), channel_id=1, source_target_pairs={{1,2},{2,1},{5,6},{6,5},{9,10},{10,9},{13,14},{14,13},{17,18},{18,... | collective-permute-start | bytes 442376 | tf_op jit(solution)/shard_map/ppermute | solution.py:528
  75.7 12.1 %collective-permute-start.13 = (bf16[144,128]{1,0:T(8,128)(2,1)S(1)}, bf16[144,128]{1,0:T(8,128)(2,1)S(1)}, u32[]{:S(2)}, u32[]{:S(2)}) collective-permute-start(bf16[144,128]{1,0:T(8,128)(2,1)S(1)} %get-tuple-element.51), channel_id=1, source_target_pairs={{0,5},{1,7},{2,4},{3,6},{4,1},{5,3},{6,0},{7,2},{8,13},{9,15},{10,... | collective-permute-start | bytes 110600 | tf_op jit(solution)/shard_map/ppermute | solution.py:531
  79.7 8.1 %collective-permute-start.14 = (bf16[144,128]{1,0:T(8,128)(2,1)S(1)}, bf16[144,128]{1,0:T(8,128)(2,1)S(1)}, u32[]{:S(2)}, u32[]{:S(2)}) collective-permute-start(bf16[144,128]{1,0:T(8,128)(2,1)S(1)} %get-tuple-element.52), channel_id=1, source_target_pairs={{0,4},{1,6},{2,5},{3,7},{4,0},{5,2},{6,1},{7,3},{8,12},{9,14},{10,... | collective-permute-start | bytes 110600 | tf_op jit(solution)/shard_map/ppermute | solution.py:531
  86.3 1.5 %copy-start = (bf16[1,2048]{1,0:T(2,128)(2,1)S(1)}, bf16[1,2048]{1,0:T(2,128)(2,1)}, u32[]{:S(2)}) copy-start(bf16[1,2048]{1,0:T(2,128)(2,1)} %refs_17_.1) | copy-start | bytes 12292
  87.8 16.0 %copy-start.1 = (s32[72]{0:T(128)S(1)}, s32[72]{0:T(128)}, u32[]{:S(2)}) copy-start(s32[72]{0:T(128)} %param.9) | copy-start | bytes 868

commit v8 on v7

--- a/solution.py
+++ b/solution.py
@@ -36,18 +36,19 @@
     return lax.broadcasted_iota(jnp.int32, shape, dimension)
 
 
-def prepare_kernel(lengths_ref, rows_hbm, send_hbm, mine_ref, theirs_ref, rows_ref, send_ref, sems):
+def prepare_kernel(lengths_hbm, rows_hbm, send_hbm, mine_ref, theirs_ref, rows_ref, send_ref, lengths_ref, sems):
     ids = position()
     count, width = rows_ref.shape
     half = width // 2
-    parts = sems.shape[0] - 1
+    parts = sems.shape[0] - 2
     step = width // parts
     core, segment = ids[0], ids[1]
     copies = [pltpu.make_async_copy(send_hbm, send_ref, sems.at[parts])]
     for part in range(parts):
         at = pl.ds(part * step, step)
         copies.append(pltpu.make_async_copy(rows_hbm.at[:, at], rows_ref.at[:, at], sems.at[part]))
-    for copy in copies:
+    lengths_copy = pltpu.make_async_copy(lengths_hbm, lengths_ref, sems.at[parts + 1])
+    for copy in copies + [lengths_copy]:
         copy.start()
     copies[0].wait()
     send = send_ref[...]
@@ -78,6 +79,7 @@
     lane = iota((count, LANES), 1)
     tail = jnp.where(lane == 0, high, jnp.where(lane == 1, middle, jnp.where(lane == 2, low, 0.0)))
     tail = ordered(tail.astype(BF16))
+    lengths_copy.wait()
     for index in range(lengths_ref.shape[1]):
         length = lengths_ref[0, index].astype(F32).astype(BF16)
         tail = jnp.where(lane == LENGTHS_AT + index, length, tail)
@@ -91,12 +93,13 @@
     return pl.pallas_call(
         prepare_kernel,
         out_shape=(shape, shape),
-        in_specs=[whole(pltpu.SMEM), whole(pltpu.HBM), whole(pltpu.HBM)],
+        in_specs=[whole(pltpu.HBM)] * 3,
         out_specs=(whole(), whole()),
         scratch_shapes=[
             pltpu.VMEM((count, width), BF16),
             pltpu.VMEM((1, count), jnp.int32),
-            pltpu.SemaphoreType.DMA((5,)),
+            pltpu.SMEM(lengths.shape, jnp.int32),
+            pltpu.SemaphoreType.DMA((6,)),
         ],
         compiler_params=pltpu.CompilerParams(vmem_limit_bytes=12 << 20),
         name="prepare",
@@ -339,10 +342,14 @@
     return shard, row - index * piece_rows
 
 
+def padded(rows):
+    return -(-rows // LANES) * LANES
+
+
 def mask_kernel(lengths_ref, near_ref, out_ref):
     ids = position()
     segment = ids[1]
-    rows = out_ref.shape[1]
+    rows = out_ref.shape[0] // 2
     piece_rows = rows // 8
     tail = near_ref[:, near_ref.shape[1] - LANES:].astype(F32)[:1].astype(jnp.int32)
     for pack in range(2):
@@ -358,15 +365,17 @@
             return place_in_pack, doc
 
         row_position, row_doc = place(iota((rows, 1), 0))
-        col_position, col_doc = place(iota((1, rows), 1))
+        column = iota((1, out_ref.shape[1]), 1)
+        col_position, col_doc = place(column)
         visible = jnp.logical_and(row_doc == col_doc, col_position <= row_position)
+        visible = jnp.logical_and(visible, column < rows)
         out_ref[pack * rows:(pack + 1) * rows, :] = jnp.where(visible, 0.0, -1e30)
 
 
 def masks(lengths, near, rows):
     return pl.pallas_call(
         mask_kernel,
-        out_shape=shape_of(2 * rows, rows, kind=F32),
+        out_shape=shape_of(2 * rows, padded(rows), kind=F32),
         in_specs=[whole(pltpu.SMEM), whole()],
         out_specs=whole(),
         compiler_params=pltpu.CompilerParams(vmem_limit_bytes=4 << 20),
@@ -379,17 +388,22 @@
     owns, recvs, directs = (refs[index * chips:(index + 1) * chips] for index in range(3))
     refs = refs[3 * chips:]
     nears, fars, gain_ref, out_ref = refs[0:3], refs[3:5], refs[5], refs[6]
+    expo_ref, weight_ref = refs[7:]
     ids = position()
     segment, tp = ids[1], ids[3]
-    rows = bias_ref.shape[1]
+    rows = bias_ref.shape[0] // 2
+    keys_wide = bias_ref.shape[1]
     slab = rows // 2
-    queries = rows
     piece_rows = rows // 8
     heads = owns[0].shape[1] // HEAD
     devices = out_ref.shape[0]
     wide = out_ref.shape[1] // 2
     scale = math.log2(math.e) / math.sqrt(HEAD)
-    lane = iota((queries, wide), 1)
+    lane = iota((rows, wide), 1)
+    used = lane < 2 * heads
+    gains = [gain_ref[:, pl.ds(pl.multiple_of((segment * heads + head) * HEAD, HEAD), HEAD)].astype(F32)
+             for head in range(heads)]
+    gains = jnp.concatenate(gains * 2 + [jnp.zeros((LANES - 2 * heads, HEAD), F32)], axis=0).astype(BF16)
 
     def chosen_keys(refs):
         keep, first, second = (ref[...].astype(F32) for ref in refs)
@@ -411,24 +425,35 @@
             jnp.concatenate([
                 pack_part(near_part, pack)[:slab],
                 pack_part(near_part, pack)[slab:slab + slab // 2] + pack_part(far_part, pack),
-                pack_part(near_part, pack)[slab + slab // 2:]], axis=0).astype(BF16)
+                pack_part(near_part, pack)[slab + slab // 2:]], axis=0)
             for near_part, far_part in zip(near, far))
-        values = jnp.concatenate([values, jnp.ones((rows, HEAD), BF16)], axis=1)
-        total = jnp.zeros((queries, HEAD), F32)
+        keys = jnp.concatenate([keys, jnp.zeros((keys_wide - rows, HEAD), F32)], axis=0).astype(BF16)
+        high = values.astype(BF16)
+        rest = (values - high.astype(F32)).astype(BF16)
+        product = (((1,), (1,)), ((), ()))
+        score = (lax.dot_general(high, gains, product, preferred_element_type=F32)
+                 + lax.dot_general(rest, gains, product, preferred_element_type=F32))
+        high = score.astype(BF16).astype(F32)
+        score = jnp.where(lane < heads, high, score - high)
         for head in range(heads):
+            here = jnp.logical_and(used, (lane & (heads - 1)) == head)
+            block = jnp.concatenate([jnp.where(here, score, 0.0), jnp.where(here, 1.0, 0.0)], axis=1)
+            block = jnp.concatenate([block, jnp.zeros((keys_wide - rows, 2 * LANES), F32)], axis=0)
+            weight_ref[head * keys_wide:(head + 1) * keys_wide, :] = block.astype(BF16)
+
             at = slice(head * HEAD, (head + 1) * HEAD)
             parts = [own + recv for own, recv in zip(
                 slabs(owns, starts, slab, at), slabs(recvs, recv_starts, slab, at))]
             query = (by_pack(parts, pack) * scale).astype(BF16)
-            logits = lax.dot_general(query, keys, (((1,), (1,)), ((), ())), preferred_element_type=F32)
+            logits = lax.dot_general(query, keys, product, preferred_element_type=F32)
             logits = logits + bias_ref[pack * rows:(pack + 1) * rows, :]
             expo = jnp.exp2(logits - jnp.max(logits, axis=1, keepdims=True)).astype(BF16)
-            both = jnp.dot(expo, values, preferred_element_type=F32)
-            offset = pl.multiple_of(segment * heads * HEAD + head * HEAD, HEAD)
-            total = total + both[:, :HEAD] / both[:, HEAD:] * gain_ref[:, pl.ds(offset, HEAD)].astype(F32)
-
-        _, inner = owner_of(iota((queries, 1), 0), pack, ids, piece_rows)
-        shard_row, _ = owner_of(iota((1, queries), 1), pack, ids, piece_rows)
+            expo_ref[:, head * keys_wide:(head + 1) * keys_wide] = expo
+        both = jnp.dot(expo_ref[...], weight_ref[...], preferred_element_type=F32)
+        total = both[:, :LANES] / jnp.where(used, both[:, LANES:], 1.0)
+
+        _, inner = owner_of(iota((rows, 1), 0), pack, ids, piece_rows)
+        shard_row, _ = owner_of(iota((1, rows), 1), pack, ids, piece_rows)
         chosen = ((iota((devices, 1), 0) >> 2) == shard_row).astype(F32)
         hit = lane == inner + pack * piece_rows
 
@@ -442,11 +467,16 @@
 
 
 def attention(bias, owns, starts, recvs, recv_starts, directs, near, far, gain, devices):
+    heads = owns[0].shape[1] // HEAD
     return pl.pallas_call(
         functools.partial(attention_kernel, starts=starts, recv_starts=recv_starts),
         out_shape=shape_of(devices, 2 * LANES, kind=F32),
         in_specs=[whole()] * (7 + 3 * len(owns)),
         out_specs=whole(),
+        scratch_shapes=[
+            pltpu.VMEM((bias.shape[0] // 2, heads * bias.shape[1]), BF16),
+            pltpu.VMEM((heads * bias.shape[1], 2 * LANES), BF16),
+        ],
         compiler_params=pltpu.CompilerParams(vmem_limit_bytes=14 << 20),
         name="attend",
     )(bias, *owns, *recvs, *directs, *near, *far, gain)

time: 105 us -> 103 us (0.981)
  Pallas kernels: 29.6 us -> 27.8 us
    pallas_call x1, Pallas kernels: 4.6 us -> 3.46 us  [attention(): pl.pallas_call(functools.partial(attention_kernel, starts=starts, recv_st...]
where the time goes in v8:
time: 103 us
  waiting for transfers between devices  43.7 us (42%)
  Pallas kernels  27.8 us (27%)
  starting transfers between devices  19.9 us (19%)
  blocking collectives  11.2 us (11%)
    ppermute x5, waiting for transfers between devices, across(): return lax.ppermute(part, 'segment', x_pairs)  31.1 us
    ppermute x1, waiting for transfers between devices, paired(): from_d = lax.ppermute(from_x, 'branch', y_pairs)  12.6 us
    all_to_all x1, blocking collectives, paired(): lax.all_to_all(outgoing, ALL_AXES, split_axis=0, concat_axis=0, tiled=True)  11.2 us
    pallas_call x1, Pallas kernels, first_chunk(): pl.pallas_call(first_chunk_kernel, out_shape=shapes, in_specs=[whole(), w...  8.38 us
    ppermute x5, starting transfers between devices, across(): return lax.ppermute(part, 'segment', x_pairs)  8.27 us
    ppermute x2, starting transfers between devices, hand_across(): lax.ppermute(array, ('segment', 'tp'), [(side * n_tp + i, (1 - side) * n_...  5.55 us
    pallas_call x3, Pallas kernels, own_queries(): pl.pallas_call(own_body, out_shape=shape_of(rows.shape[0], query.shape[1]...  5.46 us
    pallas_call x1, Pallas kernels, next_chunk(): pl.pallas_call(functools.partial(next_chunk_kernel, chips=chips), out_sha...  4.27 us
  transfers between devices with their start and end apart: 15, of which 4 were waited for; matrix products, arithmetic and copies ran while one was open for 0% of the time, Pallas kernels for 21%

profile of v8, /device:TPU:0, one launch (start us, length us, event | category | flops | bytes accessed | tf_op | source)
XLA Modules:
  0.0 102.9 jit_solution(9755062564080328265)
XLA Ops:
  0.0 1.9 %prepare.1 = (bf16[72,4224]{1,0:T(8,128)(2,1)S(1)}, bf16[72,4224]{1,0:T(8,128)(2,1)S(1)}) custom-call(s32[1,6]{1,0:T(1,128)} %lengths_ref.1, bf16[72,8192]{1,0:T(8,128)(2,1)} %rows_hbm.1, s32[1,72]{1,0:T(1,128)} %bitcast.9), custom_call_target="tpu_custom_call" | custom-call | tf_op jit(solution)/shard_map/prepare/pallas_call | solution.py:93
  1.9 3.0 %collective-permute-start = (bf16[72,4224]{1,0:T(8,128)(2,1)S(1)}, bf16[72,4224]{1,0:T(8,128)(2,1)S(1)}, u32[]{:S(2)}, u32[]{:S(2)}) collective-permute-start(bf16[72,4224]{1,0:T(8,128)(2,1)S(1)} %get-tuple-element.29), channel_id=1, source_target_pairs={{0,4},{4,0},{1,5},{5,1},{2,6},{6,2},{3,7},{7,3},{8,12},{12,8},{9,1... | collective-permute-start | bytes 1824776 | tf_op jit(solution)/shard_map/ppermute | solution.py:522
  4.9 1.5 %collective-permute-start.3 = (bf16[72,4224]{1,0:T(8,128)(2,1)S(1)}, bf16[72,4224]{1,0:T(8,128)(2,1)S(1)}, u32[]{:S(2)}, u32[]{:S(2)}) collective-permute-start(bf16[72,4224]{1,0:T(8,128)(2,1)S(1)} %get-tuple-element.30.near_ref), channel_id=1, source_target_pairs={{0,16},{8,24},{16,0},{24,8},{1,17},{9,25},{17,1},{25,9},{2,18},{10... | collective-permute-start | bytes 1824776 | tf_op jit(solution)/shard_map/ppermute | solution.py:533
  6.5 12.2 %collective-permute-done.near_ref.refs_0_ = bf16[72,4224]{1,0:T(8,128)(2,1)S(1)} collective-permute-done((bf16[72,4224]{1,0:T(8,128)(2,1)S(1)}, bf16[72,4224]{1,0:T(8,128)(2,1)S(1)}, u32[]{:S(2)}, u32[]{:S(2)}) %collective-permute-start) | collective-permute-done | bytes 608288 | tf_op jit(solution)/shard_map/ppermute | solution.py:522
  18.7 1.8 %collective-permute-start.5 = (bf16[72,4224]{1,0:T(8,128)(2,1)S(1)}, bf16[72,4224]{1,0:T(8,128)(2,1)S(1)}, u32[]{:S(2)}, u32[]{:S(2)}) collective-permute-start(bf16[72,4224]{1,0:T(8,128)(2,1)S(1)} %collective-permute-done.near_ref.refs_0_), channel_id=1, source_target_pairs={{0,16},{8,24},{16,0},{24,8},{1,17},{9,25},{17,1},{25,9},{2,18},{10... | collective-permute-start | bytes 1824776 | tf_op jit(solution)/shard_map/ppermute | solution.py:534
  20.4 0.0 collective-permute-start.1
  20.4 0.5 collective-permute-start.2
  20.9 0.0 collective-permute-done.3.refs_2_
  20.9 0.0 collective-permute-start.4
  20.9 12.6 %collective-permute-done.5.refs_0_ = bf16[72,4224]{1,0:T(8,128)(2,1)S(1)} collective-permute-done((bf16[72,4224]{1,0:T(8,128)(2,1)S(1)}, bf16[72,4224]{1,0:T(8,128)(2,1)S(1)}, u32[]{:S(2)}, u32[]{:S(2)}) %collective-permute-start.5) | collective-permute-done | bytes 608288 | tf_op jit(solution)/shard_map/ppermute | solution.py:534
  33.5 0.0 collective-permute-start.6
  33.5 0.0 collective-permute-done.1.far_ref
  33.6 8.4 %first_chunk.1 = (bf16[144,4096]{1,0:T(8,128)(2,1)S(1)}, f32[144,128]{1,0:T(8,128)S(1)}, f32[144,256]{1,0:T(8,128)S(1)}, bf16[144,1280]{1,0:T(8,128)(2,1)S(1)}, ...) custom-call(bf16[72,4224]{1,0:T(8,128)(2,1)S(1)} %get-tuple-element., ...), custom_call_target="tpu_custom_call" | custom-call | tf_op jit(solution)/shard_map/first_chunk/pallas_call | solution.py:260
  41.9 1.6 %collective-permute-start.8 = (bf16[144,1280]{1,0:T(8,128)(2,1)S(1)}, bf16[144,1280]{1,0:T(8,128)(2,1)S(1)}, u32[]{:S(2)}, u32[]{:S(2)}) collective-permute-start(bf16[144,1280]{1,0:T(8,128)(2,1)S(1)} %get-tuple-element.41), channel_id=1, source_target_pairs={{0,4},{4,0},{1,5},{5,1},{2,6},{6,2},{3,7},{7,3},{8,12},{12,8},{9,1... | collective-permute-start | bytes 1105928 | tf_op jit(solution)/shard_map/ppermute | solution.py:522
  43.5 0.0 collective-permute-done.2.refs_1_
  43.5 0.0 collective-permute-done.4.refs_3_
  43.5 4.3 %next_chunk.1 = (bf16[288,4096]{1,0:T(8,128)(2,1)S(1)}, f32[288,128]{1,0:T(8,128)S(1)}, f32[288,256]{1,0:T(8,128)S(1)}, bf16[288,1024]{1,0:T(8,128)(2,1)S(1)}, bf16[288,256]{1,0:T(8,128)(2,1)S(1)}) custom-call(bf16[72,4224]{1,0:T(8,128)(2,1)S(1)} %collective-permute-done.near_ref.refs_0_, bf16[72,4224]{1,0:T(8,128)(2,1)S(1)} %collective-permute-done.2.refs_1_, ...), custom_call_target="tpu_custom_call" | custom-call | tf_op jit(solution)/shard_map/next_chunk/pallas_call | solution.py:283
  47.8 0.6 collective-permute-start.9
  48.4 1.5 %collective-permute-start.7 = (bf16[288,256]{1,0:T(8,128)(2,1)S(1)}, bf16[288,256]{1,0:T(8,128)(2,1)S(1)}, u32[]{:S(2)}, u32[]{:S(2)}) collective-permute-start(bf16[288,256]{1,0:T(8,128)(2,1)S(1)} %get-tuple-element.40), channel_id=1, source_target_pairs={{0,4},{4,0},{1,5},{5,1},{2,6},{6,2},{3,7},{7,3},{8,12},{12,8},{9,1... | collective-permute-start | bytes 442376 | tf_op jit(solution)/shard_map/ppermute | solution.py:522
  49.9 3.6 %collective-permute-done.8.refs_9_.refs_5_ = bf16[144,1280]{1,0:T(8,128)(2,1)S(1)} collective-permute-done((bf16[144,1280]{1,0:T(8,128)(2,1)S(1)}, bf16[144,1280]{1,0:T(8,128)(2,1)S(1)}, u32[]{:S(2)}, u32[]{:S(2)}) %collective-permute-start.8) | collective-permute-done | bytes 368672 | tf_op jit(solution)/shard_map/ppermute | solution.py:522
  53.5 15.3 %collective-permute-done.7.refs_8_ = bf16[288,256]{1,0:T(8,128)(2,1)S(1)} collective-permute-done((bf16[288,256]{1,0:T(8,128)(2,1)S(1)}, bf16[288,256]{1,0:T(8,128)(2,1)S(1)}, u32[]{:S(2)}, u32[]{:S(2)}) %collective-permute-start.7) | collective-permute-done | bytes 147488 | tf_op jit(solution)/shard_map/ppermute | solution.py:522
  68.8 0.0 collective-permute-done.6.refs_1_
  68.8 2.4 %last_chunk.1 = (bf16[144,4096]{1,0:T(8,128)(2,1)S(1)}, f32[144,128]{1,0:T(8,128)S(1)}, bf16[144,1024]{1,0:T(8,128)(2,1)S(1)}, bf16[576,128]{1,0:T(8,128)(2,1)S(...) custom-call(bf16[72,4224]{1,0:T(8,128)(2,1)S(1)} %collective-permute, ...), custom_call_target="tpu_custom_call" | custom-call | tf_op jit(solution)/shard_map/last_chunk/pallas_call | solution.py:298
  71.2 1.6 %collective-permute-start.10 = (bf16[144,1024]{1,0:T(8,128)(2,1)S(1)}, bf16[144,1024]{1,0:T(8,128)(2,1)S(1)}, u32[]{:S(2)}, u32[]{:S(2)}) collective-permute-start(bf16[144,1024]{1,0:T(8,128)(2,1)S(1)} %get-tuple-element.44), channel_id=1, source_target_pairs={{0,4},{4,0},{1,5},{5,1},{2,6},{6,2},{3,7},{7,3},{8,12},{12,8},{9,1... | collective-permute-start | bytes 884744 | tf_op jit(solution)/shard_map/ppermute | solution.py:522
  72.8 1.6 %collective-permute-start.11 = (bf16[576,128]{1,0:T(8,128)(2,1)S(1)}, bf16[576,128]{1,0:T(8,128)(2,1)S(1)}, u32[]{:S(2)}, u32[]{:S(2)}) collective-permute-start(bf16[576,128]{1,0:T(8,128)(2,1)S(1)} %get-tuple-element.49), channel_id=1, source_target_pairs={{0,1},{1,3},{2,0},{3,2},{4,5},{5,7},{6,4},{7,6},{8,9},{9,11},{10,8... | collective-permute-start | bytes 442376 | tf_op jit(solution)/shard_map/ppermute | solution.py:558
  74.4 0.7 collective-permute-start.12
  75.0 4.0 %collective-permute-start.13 = (bf16[144,128]{1,0:T(8,128)(2,1)S(1)}, bf16[144,128]{1,0:T(8,128)(2,1)S(1)}, u32[]{:S(2)}, u32[]{:S(2)}) collective-permute-start(bf16[144,128]{1,0:T(8,128)(2,1)S(1)} %get-tuple-element.51), channel_id=1, source_target_pairs={{0,5},{1,7},{2,4},{3,6},{4,1},{5,3},{6,0},{7,2},{8,13},{9,15},{10,... | collective-permute-start | bytes 110600 | tf_op jit(solution)/shard_map/ppermute | solution.py:561
  79.0 0.0 collective-permute-done.9.refs_4_.refs_7_
  79.0 1.6 %collective-permute-start.14 = (bf16[144,128]{1,0:T(8,128)(2,1)S(1)}, bf16[144,128]{1,0:T(8,128)(2,1)S(1)}, u32[]{:S(2)}, u32[]{:S(2)}) collective-permute-start(bf16[144,128]{1,0:T(8,128)(2,1)S(1)} %get-tuple-element.52), channel_id=1, source_target_pairs={{0,4},{1,6},{2,5},{3,7},{4,0},{5,2},{6,1},{7,3},{8,12},{9,14},{10,... | collective-permute-start | bytes 110600 | tf_op jit(solution)/shard_map/ppermute | solution.py:561
  80.6 1.4 %own_queries.3.refs_0_ = f32[144,1024]{1,0:T(8,128)S(1)} custom-call(bf16[144,4096]{1,0:T(8,128)(2,1)S(1)} %get-tuple-element.31.rows_ref, bf16[4096,1024]{1,0:T(8,128)(2,1)S(1)} %get-tuple-element.32.query_ref), custom_call_target="tpu_custom_call" | custom-call | tf_op jit(solution)/shard_map/own_queries/pallas_call | solution.py:317
  82.0 1.1 %masks.1.bias_ref = f32[576,384]{1,0:T(8,128)S(1)} custom-call(s32[1,6]{1,0:T(1,128)} %lengths_ref.1, bf16[72,4224]{1,0:T(8,128)(2,1)S(1)} %collective-permute-done.near_ref.refs_0_), custom_call_target="tpu_custom_call" | custom-call | tf_op jit(solution)/shard_map/masks/pallas_call | solution.py:376
  83.1 2.6 %own_queries.4.refs_1_.refs_2_ = f32[288,1024]{1,0:T(8,128)S(1)} custom-call(bf16[288,4096]{1,0:T(8,128)(2,1)S(1)} %get-tuple-element.37.rows_ref, bf16[4096,1024]{1,0:T(8,128)(2,1)S(1)} %get-tuple-element.32.query_ref), custom_call_target="tpu_custom_call" | custom-call | tf_op jit(solution)/shard_map/own_queries/pallas_call | solution.py:317
  85.7 0.0 copy-start
  85.7 1.4 %own_queries.5.refs_3_ = f32[144,1024]{1,0:T(8,128)S(1)} custom-call(bf16[144,4096]{1,0:T(8,128)(2,1)S(1)} %get-tuple-element.42.rows_ref, bf16[4096,1024]{1,0:T(8,128)(2,1)S(1)} %get-tuple-element.32.query_ref), custom_call_target="tpu_custom_call" | custom-call | tf_op jit(solution)/shard_map/own_queries/pallas_call | solution.py:317
  87.2 0.0 copy-start.1
  87.2 0.0 collective-permute-done.13.refs_15_
  87.2 0.0 collective-permute-done.14.refs_16_
  87.2 0.0 collective-permute-done.11.refs_13_
  87.2 0.0 collective-permute-done.12.refs_14_
  87.2 0.0 collective-permute-done.10.refs_6_
  87.2 0.0 copy-done
  87.2 3.5 %attend.1 = f32[32,256]{1,0:T(8,128)S(1)} custom-call(f32[576,384]{1,0:T(8,128)S(1)} %masks.1.bias_ref, f32[144,1024]{1,0:T(8,128)S(1)} %own_queries.3.refs_0_, f32[288,1024]{1,0:T(8,128)S(1)} %own_queries.4.refs_1_.refs_2_, f32[288,1024]{1,0:T(8,128)S(1)} %own_queries.4.refs_1_.refs_2_, f32[144,1024]{1,0:T(8,128)S(1)} %own_queries.5.refs_3_, ...), custom_call_target="tpu_custom_call" | custom-call | tf_op jit(solution)/shard_map/attend/pallas_call | solution.py:471
  90.7 11.2 %all_to_all.11 = f32[32,1,256]{2,1,0:T(1,128)S(1)} all-to-all(f32[32,1,256]{2,1,0:T(1,128)S(1)} %copy.9), channel_id=1, replica_groups=mesh['branch'=4,'segment'=2,'tp'=4] {'branch','segment','tp'}, dimensions={0} | all-to-all | bytes 65536 | tf_op jit(solution)/shard_map/all_to_all | solution.py:579
  102.0 0.0 copy-done.1
  102.0 0.9 finish.1
  (2 shorter events, 0.0 us)
Async XLA Ops:
  1.9 16.8 %collective-permute-start = (bf16[72,4224]{1,0:T(8,128)(2,1)S(1)}, bf16[72,4224]{1,0:T(8,128)(2,1)S(1)}, u32[]{:S(2)}, u32[]{:S(2)}) collective-permute-start(bf16[72,4224]{1,0:T(8,128)(2,1)S(1)} %get-tuple-element.29), channel_id=1, source_target_pairs={{0,4},{4,0},{1,5},{5,1},{2,6},{6,2},{3,7},{7,3},{8,12},{12,8},{9,1... | collective-permute-start | bytes 1824776 | tf_op jit(solution)/shard_map/ppermute | solution.py:522
  4.9 16.0 %collective-permute-start.3 = (bf16[72,4224]{1,0:T(8,128)(2,1)S(1)}, bf16[72,4224]{1,0:T(8,128)(2,1)S(1)}, u32[]{:S(2)}, u32[]{:S(2)}) collective-permute-start(bf16[72,4224]{1,0:T(8,128)(2,1)S(1)} %get-tuple-element.30.near_ref), channel_id=1, source_target_pairs={{0,16},{8,24},{16,0},{24,8},{1,17},{9,25},{17,1},{25,9},{2,18},{10... | collective-permute-start | bytes 1824776 | tf_op jit(solution)/shard_map/ppermute | solution.py:533
  18.7 14.9 %collective-permute-start.5 = (bf16[72,4224]{1,0:T(8,128)(2,1)S(1)}, bf16[72,4224]{1,0:T(8,128)(2,1)S(1)}, u32[]{:S(2)}, u32[]{:S(2)}) collective-permute-start(bf16[72,4224]{1,0:T(8,128)(2,1)S(1)} %collective-permute-done.near_ref.refs_0_), channel_id=1, source_target_pairs={{0,16},{8,24},{16,0},{24,8},{1,17},{9,25},{17,1},{25,9},{2,18},{10... | collective-permute-start | bytes 1824776 | tf_op jit(solution)/shard_map/ppermute | solution.py:534
  20.4 13.1 %collective-permute-start.1 = (bf16[72,4224]{1,0:T(8,128)(2,1)S(1)}, bf16[72,4224]{1,0:T(8,128)(2,1)S(1)}, u32[]{:S(2)}, u32[]{:S(2)}) collective-permute-start(bf16[72,4224]{1,0:T(8,128)(2,1)S(1)} %get-tuple-element.30.near_ref), channel_id=1, source_target_pairs={{0,8},{8,0},{16,24},{24,16},{1,9},{9,1},{17,25},{25,17},{2,10},{10... | collective-permute-start | bytes 1824776 | tf_op jit(solution)/shard_map/ppermute | solution.py:519
  20.4 23.1 %collective-permute-start.2 = (bf16[72,4224]{1,0:T(8,128)(2,1)S(1)}, bf16[72,4224]{1,0:T(8,128)(2,1)S(1)}, u32[]{:S(2)}, u32[]{:S(2)}) collective-permute-start(bf16[72,4224]{1,0:T(8,128)(2,1)S(1)} %collective-permute-done.near_ref.refs_0_), channel_id=1, source_target_pairs={{0,8},{8,0},{16,24},{24,16},{1,9},{9,1},{17,25},{25,17},{2,10},{10... | collective-permute-start | bytes 1824776 | tf_op jit(solution)/shard_map/ppermute | solution.py:519
  20.9 22.6 %collective-permute-start.4 = (bf16[72,4224]{1,0:T(8,128)(2,1)S(1)}, bf16[72,4224]{1,0:T(8,128)(2,1)S(1)}, u32[]{:S(2)}, u32[]{:S(2)}) collective-permute-start(bf16[72,4224]{1,0:T(8,128)(2,1)S(1)} %collective-permute-done.3.refs_2_), channel_id=1, source_target_pairs={{0,8},{8,0},{16,24},{24,16},{1,9},{9,1},{17,25},{25,17},{2,10},{10... | collective-permute-start | bytes 1824776 | tf_op jit(solution)/shard_map/ppermute | solution.py:519
  33.5 35.3 %collective-permute-start.6 = (bf16[72,4224]{1,0:T(8,128)(2,1)S(1)}, bf16[72,4224]{1,0:T(8,128)(2,1)S(1)}, u32[]{:S(2)}, u32[]{:S(2)}) collective-permute-start(bf16[72,4224]{1,0:T(8,128)(2,1)S(1)} %collective-permute-done.5.refs_0_), channel_id=1, source_target_pairs={{0,8},{8,0},{16,24},{24,16},{1,9},{9,1},{17,25},{25,17},{2,10},{10... | collective-permute-start | bytes 1824776 | tf_op jit(solution)/shard_map/ppermute | solution.py:519
  41.9 11.5 %collective-permute-start.8 = (bf16[144,1280]{1,0:T(8,128)(2,1)S(1)}, bf16[144,1280]{1,0:T(8,128)(2,1)S(1)}, u32[]{:S(2)}, u32[]{:S(2)}) collective-permute-start(bf16[144,1280]{1,0:T(8,128)(2,1)S(1)} %get-tuple-element.41), channel_id=1, source_target_pairs={{0,4},{4,0},{1,5},{5,1},{2,6},{6,2},{3,7},{7,3},{8,12},{12,8},{9,1... | collective-permute-start | bytes 1105928 | tf_op jit(solution)/shard_map/ppermute | solution.py:522
  47.8 31.2 %collective-permute-start.9 = (bf16[288,1024]{1,0:T(8,128)(2,1)S(1)}, bf16[288,1024]{1,0:T(8,128)(2,1)S(1)}, u32[]{:S(2)}, u32[]{:S(2)}) collective-permute-start(bf16[288,1024]{1,0:T(8,128)(2,1)S(1)} %get-tuple-element.43), channel_id=1, source_target_pairs={{0,4},{4,0},{1,5},{5,1},{2,6},{6,2},{3,7},{7,3},{8,12},{12,8},{9,1... | collective-permute-start | bytes 1769480 | tf_op jit(solution)/shard_map/ppermute | solution.py:522
  48.4 20.4 %collective-permute-start.7 = (bf16[288,256]{1,0:T(8,128)(2,1)S(1)}, bf16[288,256]{1,0:T(8,128)(2,1)S(1)}, u32[]{:S(2)}, u32[]{:S(2)}) collective-permute-start(bf16[288,256]{1,0:T(8,128)(2,1)S(1)} %get-tuple-element.40), channel_id=1, source_target_pairs={{0,4},{4,0},{1,5},{5,1},{2,6},{6,2},{3,7},{7,3},{8,12},{12,8},{9,1... | collective-permute-start | bytes 442376 | tf_op jit(solution)/shard_map/ppermute | solution.py:522
  71.2 16.0 %collective-permute-start.10 = (bf16[144,1024]{1,0:T(8,128)(2,1)S(1)}, bf16[144,1024]{1,0:T(8,128)(2,1)S(1)}, u32[]{:S(2)}, u32[]{:S(2)}) collective-permute-start(bf16[144,1024]{1,0:T(8,128)(2,1)S(1)} %get-tuple-element.44), channel_id=1, source_target_pairs={{0,4},{4,0},{1,5},{5,1},{2,6},{6,2},{3,7},{7,3},{8,12},{12,8},{9,1... | collective-permute-start | bytes 884744 | tf_op jit(solution)/shard_map/ppermute | solution.py:522
  72.8 14.4 %collective-permute-start.11 = (bf16[576,128]{1,0:T(8,128)(2,1)S(1)}, bf16[576,128]{1,0:T(8,128)(2,1)S(1)}, u32[]{:S(2)}, u32[]{:S(2)}) collective-permute-start(bf16[576,128]{1,0:T(8,128)(2,1)S(1)} %get-tuple-element.49), channel_id=1, source_target_pairs={{0,1},{1,3},{2,0},{3,2},{4,5},{5,7},{6,4},{7,6},{8,9},{9,11},{10,8... | collective-permute-start | bytes 442376 | tf_op jit(solution)/shard_map/ppermute | solution.py:558
  74.4 12.8 %collective-permute-start.12 = (bf16[576,128]{1,0:T(8,128)(2,1)S(1)}, bf16[576,128]{1,0:T(8,128)(2,1)S(1)}, u32[]{:S(2)}, u32[]{:S(2)}) collective-permute-start(bf16[576,128]{1,0:T(8,128)(2,1)S(1)} %get-tuple-element.50), channel_id=1, source_target_pairs={{1,2},{2,1},{5,6},{6,5},{9,10},{10,9},{13,14},{14,13},{17,18},{18,... | collective-permute-start | bytes 442376 | tf_op jit(solution)/shard_map/ppermute | solution.py:558
  75.0 12.1 %collective-permute-start.13 = (bf16[144,128]{1,0:T(8,128)(2,1)S(1)}, bf16[144,128]{1,0:T(8,128)(2,1)S(1)}, u32[]{:S(2)}, u32[]{:S(2)}) collective-permute-start(bf16[144,128]{1,0:T(8,128)(2,1)S(1)} %get-tuple-element.51), channel_id=1, source_target_pairs={{0,5},{1,7},{2,4},{3,6},{4,1},{5,3},{6,0},{7,2},{8,13},{9,15},{10,... | collective-permute-start | bytes 110600 | tf_op jit(solution)/shard_map/ppermute | solution.py:561
  79.0 8.1 %collective-permute-start.14 = (bf16[144,128]{1,0:T(8,128)(2,1)S(1)}, bf16[144,128]{1,0:T(8,128)(2,1)S(1)}, u32[]{:S(2)}, u32[]{:S(2)}) collective-permute-start(bf16[144,128]{1,0:T(8,128)(2,1)S(1)} %get-tuple-element.52), channel_id=1, source_target_pairs={{0,4},{1,6},{2,5},{3,7},{4,0},{5,2},{6,1},{7,3},{8,12},{9,14},{10,... | collective-permute-start | bytes 110600 | tf_op jit(solution)/shard_map/ppermute | solution.py:561
  85.7 1.5 %copy-start = (bf16[1,2048]{1,0:T(2,128)(2,1)S(1)}, bf16[1,2048]{1,0:T(2,128)(2,1)}, u32[]{:S(2)}) copy-start(bf16[1,2048]{1,0:T(2,128)(2,1)} %refs_17_.1) | copy-start | bytes 12292
  87.2 14.8 %copy-start.1 = (s32[72]{0:T(128)S(1)}, s32[72]{0:T(128)}, u32[]{:S(2)}) copy-start(s32[72]{0:T(128)} %param.9) | copy-start | bytes 868

commit v9 on v8

--- a/solution.py
+++ b/solution.py
@@ -45,8 +45,10 @@
     core, segment = ids[0], ids[1]
     copies = [pltpu.make_async_copy(send_hbm, send_ref, sems.at[parts])]
     for part in range(parts):
-        at = pl.ds(part * step, step)
-        copies.append(pltpu.make_async_copy(rows_hbm.at[:, at], rows_ref.at[:, at], sems.at[part]))
+        first = (1 - segment) * half if part < parts // 2 else segment * half
+        source = pl.ds(pl.multiple_of(first + part % (parts // 2) * step, step), step)
+        copies.append(pltpu.make_async_copy(
+            rows_hbm.at[:, source], rows_ref.at[:, pl.ds(part * step, step)], sems.at[part]))
     lengths_copy = pltpu.make_async_copy(lengths_hbm, lengths_ref, sems.at[parts + 1])
     for copy in copies + [lengths_copy]:
         copy.start()
@@ -61,17 +63,16 @@
         return out.astype(BF16)
 
     lanes = jnp.zeros((count, LANES), F32)
+    chunk = 512
     for part in range(parts):
         copies[1 + part].wait()
-        square = rows_ref[:, part * step:(part + 1) * step].astype(F32)
-        square = square * square
-        for lane in range(0, step, LANES):
-            lanes = lanes + square[:, lane:lane + LANES]
-    chunk = 1024
-    for start in range(0, half, chunk):
-        for out_ref, which in ((theirs_ref, 1 - segment), (mine_ref, segment)):
-            at = pl.multiple_of(which * half + start, chunk)
-            out_ref[:, start:start + chunk] = ordered(rows_ref[:, pl.ds(at, chunk)])
+        out_ref = theirs_ref if part < parts // 2 else mine_ref
+        for start in range(part * step, (part + 1) * step, chunk):
+            rows = rows_ref[:, start:start + chunk]
+            out_ref[:, start % half:start % half + chunk] = ordered(rows)
+            for lane in range(0, chunk, LANES):
+                square = rows[:, lane:lane + LANES].astype(F32)
+                lanes = lanes + square * square
     scale = lax.rsqrt(jnp.sum(lanes, axis=1, keepdims=True) * (1.0 / width) + epsilon)
     high = scale.astype(BF16).astype(F32)
     middle = (scale - high).astype(BF16).astype(F32)
@@ -383,20 +384,61 @@
     )(lengths, near)
 
 
+def place_rows(chosen, spread):
+    high = spread.astype(BF16)
+    rest = spread - high.astype(F32)
+    middle = rest.astype(BF16)
+    low = (rest - middle.astype(F32)).astype(BF16)
+    parts = jnp.concatenate([high, middle, low], axis=1)
+    placed = jnp.dot(chosen, parts, preferred_element_type=F32)
+    wide = spread.shape[1]
+    return placed[:, :wide] + placed[:, wide:2 * wide] + placed[:, 2 * wide:]
+
+
+def placement_kernel(*refs, starts):
+    directs, (direct_ref, chosen_ref, hit_ref) = refs[:-3], refs[-3:]
+    ids = position()
+    devices = direct_ref.shape[0]
+    rows = hit_ref.shape[0] // 2
+    slab = rows // 2
+    piece_rows = rows // 8
+    lane = iota((rows, LANES), 1)
+    for pack in range(2):
+        _, inner = owner_of(iota((rows, 1), 0), pack, ids, piece_rows)
+        shard_row, _ = owner_of(iota((1, rows), 1), pack, ids, piece_rows)
+        chosen = jnp.where((iota((devices, 1), 0) >> 2) == shard_row, 1.0, 0.0).astype(BF16)
+        hit = jnp.where(lane == inner + pack * piece_rows, 1.0, 0.0)
+        column = jnp.sum(by_pack(slabs(directs, starts, slab), pack), axis=1, keepdims=True)
+        placed = place_rows(chosen, hit * column)
+        direct_ref[...] = placed if pack == 0 else direct_ref[...] + placed
+        chosen_ref[:, pack * rows:(pack + 1) * rows] = chosen
+        hit_ref[pack * rows:(pack + 1) * rows, :] = hit
+
+
+def placement(directs, starts, rows, devices):
+    return pl.pallas_call(
+        functools.partial(placement_kernel, starts=starts),
+        out_shape=(
+            shape_of(devices, LANES, kind=F32), shape_of(devices, 2 * rows), shape_of(2 * rows, LANES, kind=F32)),
+        in_specs=[whole()] * len(directs),
+        out_specs=(whole(),) * 3,
+        compiler_params=pltpu.CompilerParams(vmem_limit_bytes=6 << 20),
+        name="placement",
+    )(*directs)
+
+
 def attention_kernel(bias_ref, *refs, starts, recv_starts):
     chips = len(starts)
-    owns, recvs, directs = (refs[index * chips:(index + 1) * chips] for index in range(3))
-    refs = refs[3 * chips:]
-    nears, fars, gain_ref, out_ref = refs[0:3], refs[3:5], refs[5], refs[6]
-    expo_ref, weight_ref = refs[7:]
+    owns, recvs, refs = refs[:chips], refs[chips:2 * chips], refs[2 * chips:]
+    direct_ref, chosen_ref, hit_ref = refs[:3]
+    nears, fars, gain_ref, out_ref = refs[3:6], refs[6:8], refs[8], refs[9]
+    expo_ref, weight_ref = refs[10:]
     ids = position()
     segment, tp = ids[1], ids[3]
     rows = bias_ref.shape[0] // 2
     keys_wide = bias_ref.shape[1]
     slab = rows // 2
-    piece_rows = rows // 8
     heads = owns[0].shape[1] // HEAD
-    devices = out_ref.shape[0]
     wide = out_ref.shape[1] // 2
     scale = math.log2(math.e) / math.sqrt(HEAD)
     lane = iota((rows, wide), 1)
@@ -418,8 +460,7 @@
     odd = (tp & 1) == 1
     far = (jnp.where(odd, far_first, far_second), jnp.where(odd, far_second, far_first))
     near = chosen_keys(nears)
-    through = jnp.zeros((devices, wide), F32)
-    direct = jnp.zeros((devices, wide), F32)
+    totals = []
     for pack in range(2):
         keys, values = (
             jnp.concatenate([
@@ -452,26 +493,18 @@
         both = jnp.dot(expo_ref[...], weight_ref[...], preferred_element_type=F32)
         total = both[:, :LANES] / jnp.where(used, both[:, LANES:], 1.0)
 
-        _, inner = owner_of(iota((rows, 1), 0), pack, ids, piece_rows)
-        shard_row, _ = owner_of(iota((1, rows), 1), pack, ids, piece_rows)
-        chosen = ((iota((devices, 1), 0) >> 2) == shard_row).astype(F32)
-        hit = lane == inner + pack * piece_rows
-
-        def send(column):
-            return jnp.dot(chosen, jnp.where(hit, column, 0.0), precision=HIGHEST, preferred_element_type=F32)
-
-        through = through + send(jnp.sum(total, axis=1, keepdims=True))
-        direct = direct + send(jnp.sum(by_pack(slabs(directs, starts, slab), pack), axis=1, keepdims=True))
-    out_ref[:, :wide] = through
-    out_ref[:, wide:] = direct
-
-
-def attention(bias, owns, starts, recvs, recv_starts, directs, near, far, gain, devices):
+        totals.append(jnp.sum(total, axis=1, keepdims=True))
+    spread = hit_ref[...] * jnp.concatenate(totals, axis=0)
+    out_ref[:, :wide] = place_rows(chosen_ref[...], spread)
+    out_ref[:, wide:] = direct_ref[...]
+
+
+def attention(bias, owns, starts, recvs, recv_starts, places, near, far, gain, devices):
     heads = owns[0].shape[1] // HEAD
     return pl.pallas_call(
         functools.partial(attention_kernel, starts=starts, recv_starts=recv_starts),
         out_shape=shape_of(devices, 2 * LANES, kind=F32),
-        in_specs=[whole()] * (7 + 3 * len(owns)),
+        in_specs=[whole()] * (10 + 2 * len(owns)),
         out_specs=whole(),
         scratch_shapes=[
             pltpu.VMEM((bias.shape[0] // 2, heads * bias.shape[1]), BF16),
@@ -479,7 +512,7 @@
         ],
         compiler_params=pltpu.CompilerParams(vmem_limit_bytes=14 << 20),
         name="attend",
-    )(bias, *owns, *recvs, *directs, *near, *far, gain)
+    )(bias, *owns, *recvs, *places, *near, *far, gain)
 
 
 def finish_kernel(recv_ref, send_ref, out_ref):
@@ -571,11 +604,11 @@
     far_second = hand_across(far_second, hand_second)
     query_d = own_queries(rows, own_weights)
     devices = n_branch * 2 * n_tp
+    places = placement([direct_own, direct_xy, direct_xy, direct_d], (0, 0, slab, 0), 2 * slab, devices)
     outgoing = attention(
         bias, [query_own, query_xy, query_xy, query_d], (0, 0, slab, 0),
         [received_xy, received_own, received_d, received_xy], (0, 0, 0, slab),
-        [direct_own, direct_xy, direct_xy, direct_d],
-        (keep, first, second), (far_first, far_second), head_attn, devices)
+        places, (keep, first, second), (far_first, far_second), head_attn, devices)
     incoming = lax.all_to_all(outgoing, ALL_AXES, split_axis=0, concat_axis=0, tiled=True)
     return finish(incoming, packing, n_branch)
 

time: 103 us -> 103 us (level)
  no operation moved by 1% of the time
where the time goes in v9:
time: 103 us
  waiting for transfers between devices  43.7 us (42%)
  Pallas kernels  28 us (27%)
  starting transfers between devices  19.8 us (19%)
  blocking collectives  11.3 us (11%)
    ppermute x5, waiting for transfers between devices, across(): return lax.ppermute(part, 'segment', x_pairs)  31.1 us
    ppermute x1, waiting for transfers between devices, paired(): from_d = lax.ppermute(from_x, 'branch', y_pairs)  12.6 us
    all_to_all x1, blocking collectives, paired(): lax.all_to_all(outgoing, ALL_AXES, split_axis=0, concat_axis=0, tiled=True)  11.3 us
    pallas_call x1, Pallas kernels, first_chunk(): pl.pallas_call(first_chunk_kernel, out_shape=shapes, in_specs=[whole(), w...  8.38 us
    ppermute x5, starting transfers between devices, across(): return lax.ppermute(part, 'segment', x_pairs)  8.27 us
    ppermute x2, starting transfers between devices, hand_across(): lax.ppermute(array, ('segment', 'tp'), [(side * n_tp + i, (1 - side) * n_...  5.53 us
    pallas_call x3, Pallas kernels, own_queries(): pl.pallas_call(own_body, out_shape=shape_of(rows.shape[0], query.shape[1]...  5.46 us
    pallas_call x1, Pallas kernels, next_chunk(): pl.pallas_call(functools.partial(next_chunk_kernel, chips=chips), out_sha...  4.27 us
  transfers between devices with their start and end apart: 15, of which 4 were waited for; matrix products, arithmetic and copies ran while one was open for 0% of the time, Pallas kernels for 21%

profile of v9, /device:TPU:0, one launch (start us, length us, event | category | flops | bytes accessed | tf_op | source)
XLA Modules:
  0.0 103.0 jit_solution(16716083197520495697)
XLA Ops:
  0.0 2.1 %prepare.1 = (bf16[72,4224]{1,0:T(8,128)(2,1)S(1)}, bf16[72,4224]{1,0:T(8,128)(2,1)S(1)}) custom-call(s32[1,6]{1,0:T(1,128)} %lengths_ref.1, bf16[72,8192]{1,0:T(8,128)(2,1)} %rows_hbm.1, s32[1,72]{1,0:T(1,128)} %bitcast.9), custom_call_target="tpu_custom_call" | custom-call | tf_op jit(solution)/shard_map/prepare/pallas_call | solution.py:94
  2.2 3.0 %collective-permute-start = (bf16[72,4224]{1,0:T(8,128)(2,1)S(1)}, bf16[72,4224]{1,0:T(8,128)(2,1)S(1)}, u32[]{:S(2)}, u32[]{:S(2)}) collective-permute-start(bf16[72,4224]{1,0:T(8,128)(2,1)S(1)} %get-tuple-element.32), channel_id=1, source_target_pairs={{0,4},{4,0},{1,5},{5,1},{2,6},{6,2},{3,7},{7,3},{8,12},{12,8},{9,1... | collective-permute-start | bytes 1824776 | tf_op jit(solution)/shard_map/ppermute | solution.py:555
  5.2 1.5 %collective-permute-start.3 = (bf16[72,4224]{1,0:T(8,128)(2,1)S(1)}, bf16[72,4224]{1,0:T(8,128)(2,1)S(1)}, u32[]{:S(2)}, u32[]{:S(2)}) collective-permute-start(bf16[72,4224]{1,0:T(8,128)(2,1)S(1)} %get-tuple-element.33.near_ref), channel_id=1, source_target_pairs={{0,16},{8,24},{16,0},{24,8},{1,17},{9,25},{17,1},{25,9},{2,18},{10... | collective-permute-start | bytes 1824776 | tf_op jit(solution)/shard_map/ppermute | solution.py:566
  6.7 12.2 %collective-permute-done.near_ref.refs_0_ = bf16[72,4224]{1,0:T(8,128)(2,1)S(1)} collective-permute-done((bf16[72,4224]{1,0:T(8,128)(2,1)S(1)}, bf16[72,4224]{1,0:T(8,128)(2,1)S(1)}, u32[]{:S(2)}, u32[]{:S(2)}) %collective-permute-start) | collective-permute-done | bytes 608288 | tf_op jit(solution)/shard_map/ppermute | solution.py:555
  18.9 1.8 %collective-permute-start.5 = (bf16[72,4224]{1,0:T(8,128)(2,1)S(1)}, bf16[72,4224]{1,0:T(8,128)(2,1)S(1)}, u32[]{:S(2)}, u32[]{:S(2)}) collective-permute-start(bf16[72,4224]{1,0:T(8,128)(2,1)S(1)} %collective-permute-done.near_ref.refs_0_), channel_id=1, source_target_pairs={{0,16},{8,24},{16,0},{24,8},{1,17},{9,25},{17,1},{25,9},{2,18},{10... | collective-permute-start | bytes 1824776 | tf_op jit(solution)/shard_map/ppermute | solution.py:567
  20.7 0.0 collective-permute-start.1
  20.7 0.5 collective-permute-start.2
  21.2 0.0 collective-permute-done.3.refs_2_
  21.2 0.0 collective-permute-start.4
  21.2 12.6 %collective-permute-done.5.refs_0_ = bf16[72,4224]{1,0:T(8,128)(2,1)S(1)} collective-permute-done((bf16[72,4224]{1,0:T(8,128)(2,1)S(1)}, bf16[72,4224]{1,0:T(8,128)(2,1)S(1)}, u32[]{:S(2)}, u32[]{:S(2)}) %collective-permute-start.5) | collective-permute-done | bytes 608288 | tf_op jit(solution)/shard_map/ppermute | solution.py:567
  33.8 0.0 collective-permute-start.6
  33.8 0.0 collective-permute-done.1.far_ref
  33.8 8.4 %first_chunk.1 = (bf16[144,4096]{1,0:T(8,128)(2,1)S(1)}, f32[144,128]{1,0:T(8,128)S(1)}, f32[144,256]{1,0:T(8,128)S(1)}, bf16[144,1280]{1,0:T(8,128)(2,1)S(1)}, ...) custom-call(bf16[72,4224]{1,0:T(8,128)(2,1)S(1)} %get-tuple-element., ...), custom_call_target="tpu_custom_call" | custom-call | tf_op jit(solution)/shard_map/first_chunk/pallas_call | solution.py:261
  42.2 1.6 %collective-permute-start.8 = (bf16[144,1280]{1,0:T(8,128)(2,1)S(1)}, bf16[144,1280]{1,0:T(8,128)(2,1)S(1)}, u32[]{:S(2)}, u32[]{:S(2)}) collective-permute-start(bf16[144,1280]{1,0:T(8,128)(2,1)S(1)} %get-tuple-element.44), channel_id=1, source_target_pairs={{0,4},{4,0},{1,5},{5,1},{2,6},{6,2},{3,7},{7,3},{8,12},{12,8},{9,1... | collective-permute-start | bytes 1105928 | tf_op jit(solution)/shard_map/ppermute | solution.py:555
  43.8 0.0 collective-permute-done.2.refs_1_
  43.8 0.0 collective-permute-done.4.refs_3_
  43.8 4.3 %next_chunk.1 = (bf16[288,4096]{1,0:T(8,128)(2,1)S(1)}, f32[288,128]{1,0:T(8,128)S(1)}, f32[288,256]{1,0:T(8,128)S(1)}, bf16[288,1024]{1,0:T(8,128)(2,1)S(1)}, bf16[288,256]{1,0:T(8,128)(2,1)S(1)}) custom-call(bf16[72,4224]{1,0:T(8,128)(2,1)S(1)} %collective-permute-done.near_ref.refs_0_, bf16[72,4224]{1,0:T(8,128)(2,1)S(1)} %collective-permute-done.2.refs_1_, ...), custom_call_target="tpu_custom_call" | custom-call | tf_op jit(solution)/shard_map/next_chunk/pallas_call | solution.py:284
  48.0 0.6 collective-permute-start.9
  48.6 1.5 %collective-permute-start.7 = (bf16[288,256]{1,0:T(8,128)(2,1)S(1)}, bf16[288,256]{1,0:T(8,128)(2,1)S(1)}, u32[]{:S(2)}, u32[]{:S(2)}) collective-permute-start(bf16[288,256]{1,0:T(8,128)(2,1)S(1)} %get-tuple-element.43), channel_id=1, source_target_pairs={{0,4},{4,0},{1,5},{5,1},{2,6},{6,2},{3,7},{7,3},{8,12},{12,8},{9,1... | collective-permute-start | bytes 442376 | tf_op jit(solution)/shard_map/ppermute | solution.py:555
  50.1 3.6 %collective-permute-done.8.refs_9_.refs_5_ = bf16[144,1280]{1,0:T(8,128)(2,1)S(1)} collective-permute-done((bf16[144,1280]{1,0:T(8,128)(2,1)S(1)}, bf16[144,1280]{1,0:T(8,128)(2,1)S(1)}, u32[]{:S(2)}, u32[]{:S(2)}) %collective-permute-start.8) | collective-permute-done | bytes 368672 | tf_op jit(solution)/shard_map/ppermute | solution.py:555
  53.7 15.3 %collective-permute-done.7.refs_8_ = bf16[288,256]{1,0:T(8,128)(2,1)S(1)} collective-permute-done((bf16[288,256]{1,0:T(8,128)(2,1)S(1)}, bf16[288,256]{1,0:T(8,128)(2,1)S(1)}, u32[]{:S(2)}, u32[]{:S(2)}) %collective-permute-start.7) | collective-permute-done | bytes 147488 | tf_op jit(solution)/shard_map/ppermute | solution.py:555
  69.1 0.0 collective-permute-done.6.refs_1_
  69.1 2.4 %last_chunk.1 = (bf16[144,4096]{1,0:T(8,128)(2,1)S(1)}, f32[144,128]{1,0:T(8,128)S(1)}, bf16[144,1024]{1,0:T(8,128)(2,1)S(1)}, bf16[576,128]{1,0:T(8,128)(2,1)S(...) custom-call(bf16[72,4224]{1,0:T(8,128)(2,1)S(1)} %collective-permute, ...), custom_call_target="tpu_custom_call" | custom-call | tf_op jit(solution)/shard_map/last_chunk/pallas_call | solution.py:299
  71.5 1.6 %collective-permute-start.10 = (bf16[144,1024]{1,0:T(8,128)(2,1)S(1)}, bf16[144,1024]{1,0:T(8,128)(2,1)S(1)}, u32[]{:S(2)}, u32[]{:S(2)}) collective-permute-start(bf16[144,1024]{1,0:T(8,128)(2,1)S(1)} %get-tuple-element.47), channel_id=1, source_target_pairs={{0,4},{4,0},{1,5},{5,1},{2,6},{6,2},{3,7},{7,3},{8,12},{12,8},{9,1... | collective-permute-start | bytes 884744 | tf_op jit(solution)/shard_map/ppermute | solution.py:555
  73.1 1.6 %collective-permute-start.11 = (bf16[576,128]{1,0:T(8,128)(2,1)S(1)}, bf16[576,128]{1,0:T(8,128)(2,1)S(1)}, u32[]{:S(2)}, u32[]{:S(2)}) collective-permute-start(bf16[576,128]{1,0:T(8,128)(2,1)S(1)} %get-tuple-element.55), channel_id=1, source_target_pairs={{0,1},{1,3},{2,0},{3,2},{4,5},{5,7},{6,4},{7,6},{8,9},{9,11},{10,8... | collective-permute-start | bytes 442376 | tf_op jit(solution)/shard_map/ppermute | solution.py:591
  74.6 0.7 collective-permute-start.12
  75.3 4.0 %collective-permute-start.13 = (bf16[144,128]{1,0:T(8,128)(2,1)S(1)}, bf16[144,128]{1,0:T(8,128)(2,1)S(1)}, u32[]{:S(2)}, u32[]{:S(2)}) collective-permute-start(bf16[144,128]{1,0:T(8,128)(2,1)S(1)} %get-tuple-element.57), channel_id=1, source_target_pairs={{0,5},{1,7},{2,4},{3,6},{4,1},{5,3},{6,0},{7,2},{8,13},{9,15},{10,... | collective-permute-start | bytes 110600 | tf_op jit(solution)/shard_map/ppermute | solution.py:594
  79.3 0.0 collective-permute-done.9.refs_4_.refs_7_
  79.3 1.5 %collective-permute-start.14 = (bf16[144,128]{1,0:T(8,128)(2,1)S(1)}, bf16[144,128]{1,0:T(8,128)(2,1)S(1)}, u32[]{:S(2)}, u32[]{:S(2)}) collective-permute-start(bf16[144,128]{1,0:T(8,128)(2,1)S(1)} %get-tuple-element.58), channel_id=1, source_target_pairs={{0,4},{1,6},{2,5},{3,7},{4,0},{5,2},{6,1},{7,3},{8,12},{9,14},{10,... | collective-permute-start | bytes 110600 | tf_op jit(solution)/shard_map/ppermute | solution.py:594
  80.8 1.4 %own_queries.3.refs_0_ = f32[144,1024]{1,0:T(8,128)S(1)} custom-call(bf16[144,4096]{1,0:T(8,128)(2,1)S(1)} %get-tuple-element.34.rows_ref, bf16[4096,1024]{1,0:T(8,128)(2,1)S(1)} %get-tuple-element.35.query_ref), custom_call_target="tpu_custom_call" | custom-call | tf_op jit(solution)/shard_map/own_queries/pallas_call | solution.py:318
  82.3 1.1 %masks.1.bias_ref = f32[576,384]{1,0:T(8,128)S(1)} custom-call(s32[1,6]{1,0:T(1,128)} %lengths_ref.1, bf16[72,4224]{1,0:T(8,128)(2,1)S(1)} %collective-permute-done.near_ref.refs_0_), custom_call_target="tpu_custom_call" | custom-call | tf_op jit(solution)/shard_map/masks/pallas_call | solution.py:377
  83.3 2.6 %own_queries.4.refs_1_.refs_2_ = f32[288,1024]{1,0:T(8,128)S(1)} custom-call(bf16[288,4096]{1,0:T(8,128)(2,1)S(1)} %get-tuple-element.40.rows_ref, bf16[4096,1024]{1,0:T(8,128)(2,1)S(1)} %get-tuple-element.35.query_ref), custom_call_target="tpu_custom_call" | custom-call | tf_op jit(solution)/shard_map/own_queries/pallas_call | solution.py:318
  85.9 0.0 copy-start
  85.9 1.4 %own_queries.5.refs_3_ = f32[144,1024]{1,0:T(8,128)S(1)} custom-call(bf16[144,4096]{1,0:T(8,128)(2,1)S(1)} %get-tuple-element.45.rows_ref, bf16[4096,1024]{1,0:T(8,128)(2,1)S(1)} %get-tuple-element.35.query_ref), custom_call_target="tpu_custom_call" | custom-call | tf_op jit(solution)/shard_map/own_queries/pallas_call | solution.py:318
  87.4 0.0 copy-start.1
  87.4 0.3 placement.1
  87.7 0.0 collective-permute-done.13.refs_14_
  87.7 0.0 collective-permute-done.14.refs_15_
  87.7 0.0 collective-permute-done.11.refs_12_
  87.7 0.0 collective-permute-done.12.refs_13_
  87.7 0.0 collective-permute-done.10.refs_6_
  87.8 0.0 copy-done
  87.8 3.0 %attend.1 = f32[32,256]{1,0:T(8,128)S(1)} custom-call(f32[576,384]{1,0:T(8,128)S(1)} %masks.1.bias_ref, f32[144,1024]{1,0:T(8,128)S(1)} %own_queries.3.refs_0_, f32[288,1024]{1,0:T(8,128)S(1)} %own_queries.4.refs_1_.refs_2_, f32[288,1024]{1,0:T(8,128)S(1)} %own_queries.4.refs_1_.refs_2_, f32[144,1024]{1,0:T(8,128)S(1)} %own_queries.5.refs_3_, ...), custom_call_target="tpu_custom_call" | custom-call | tf_op jit(solution)/shard_map/attend/pallas_call | solution.py:504
  90.9 11.3 %all_to_all.11 = f32[32,1,256]{2,1,0:T(1,128)S(1)} all-to-all(f32[32,1,256]{2,1,0:T(1,128)S(1)} %copy.9), channel_id=1, replica_groups=mesh['branch'=4,'segment'=2,'tp'=4] {'branch','segment','tp'}, dimensions={0} | all-to-all | bytes 65536 | tf_op jit(solution)/shard_map/all_to_all | solution.py:612
  102.1 0.0 copy-done.1
  102.1 0.9 finish.1
  (2 shorter events, 0.0 us)
Async XLA Ops:
  2.2 16.8 %collective-permute-start = (bf16[72,4224]{1,0:T(8,128)(2,1)S(1)}, bf16[72,4224]{1,0:T(8,128)(2,1)S(1)}, u32[]{:S(2)}, u32[]{:S(2)}) collective-permute-start(bf16[72,4224]{1,0:T(8,128)(2,1)S(1)} %get-tuple-element.32), channel_id=1, source_target_pairs={{0,4},{4,0},{1,5},{5,1},{2,6},{6,2},{3,7},{7,3},{8,12},{12,8},{9,1... | collective-permute-start | bytes 1824776 | tf_op jit(solution)/shard_map/ppermute | solution.py:555
  5.2 16.0 %collective-permute-start.3 = (bf16[72,4224]{1,0:T(8,128)(2,1)S(1)}, bf16[72,4224]{1,0:T(8,128)(2,1)S(1)}, u32[]{:S(2)}, u32[]{:S(2)}) collective-permute-start(bf16[72,4224]{1,0:T(8,128)(2,1)S(1)} %get-tuple-element.33.near_ref), channel_id=1, source_target_pairs={{0,16},{8,24},{16,0},{24,8},{1,17},{9,25},{17,1},{25,9},{2,18},{10... | collective-permute-start | bytes 1824776 | tf_op jit(solution)/shard_map/ppermute | solution.py:566
  18.9 14.9 %collective-permute-start.5 = (bf16[72,4224]{1,0:T(8,128)(2,1)S(1)}, bf16[72,4224]{1,0:T(8,128)(2,1)S(1)}, u32[]{:S(2)}, u32[]{:S(2)}) collective-permute-start(bf16[72,4224]{1,0:T(8,128)(2,1)S(1)} %collective-permute-done.near_ref.refs_0_), channel_id=1, source_target_pairs={{0,16},{8,24},{16,0},{24,8},{1,17},{9,25},{17,1},{25,9},{2,18},{10... | collective-permute-start | bytes 1824776 | tf_op jit(solution)/shard_map/ppermute | solution.py:567
  20.7 13.1 %collective-permute-start.1 = (bf16[72,4224]{1,0:T(8,128)(2,1)S(1)}, bf16[72,4224]{1,0:T(8,128)(2,1)S(1)}, u32[]{:S(2)}, u32[]{:S(2)}) collective-permute-start(bf16[72,4224]{1,0:T(8,128)(2,1)S(1)} %get-tuple-element.33.near_ref), channel_id=1, source_target_pairs={{0,8},{8,0},{16,24},{24,16},{1,9},{9,1},{17,25},{25,17},{2,10},{10... | collective-permute-start | bytes 1824776 | tf_op jit(solution)/shard_map/ppermute | solution.py:552
  20.7 23.1 %collective-permute-start.2 = (bf16[72,4224]{1,0:T(8,128)(2,1)S(1)}, bf16[72,4224]{1,0:T(8,128)(2,1)S(1)}, u32[]{:S(2)}, u32[]{:S(2)}) collective-permute-start(bf16[72,4224]{1,0:T(8,128)(2,1)S(1)} %collective-permute-done.near_ref.refs_0_), channel_id=1, source_target_pairs={{0,8},{8,0},{16,24},{24,16},{1,9},{9,1},{17,25},{25,17},{2,10},{10... | collective-permute-start | bytes 1824776 | tf_op jit(solution)/shard_map/ppermute | solution.py:552
  21.2 22.6 %collective-permute-start.4 = (bf16[72,4224]{1,0:T(8,128)(2,1)S(1)}, bf16[72,4224]{1,0:T(8,128)(2,1)S(1)}, u32[]{:S(2)}, u32[]{:S(2)}) collective-permute-start(bf16[72,4224]{1,0:T(8,128)(2,1)S(1)} %collective-permute-done.3.refs_2_), channel_id=1, source_target_pairs={{0,8},{8,0},{16,24},{24,16},{1,9},{9,1},{17,25},{25,17},{2,10},{10... | collective-permute-start | bytes 1824776 | tf_op jit(solution)/shard_map/ppermute | solution.py:552
  33.8 35.3 %collective-permute-start.6 = (bf16[72,4224]{1,0:T(8,128)(2,1)S(1)}, bf16[72,4224]{1,0:T(8,128)(2,1)S(1)}, u32[]{:S(2)}, u32[]{:S(2)}) collective-permute-start(bf16[72,4224]{1,0:T(8,128)(2,1)S(1)} %collective-permute-done.5.refs_0_), channel_id=1, source_target_pairs={{0,8},{8,0},{16,24},{24,16},{1,9},{9,1},{17,25},{25,17},{2,10},{10... | collective-permute-start | bytes 1824776 | tf_op jit(solution)/shard_map/ppermute | solution.py:552
  42.2 11.5 %collective-permute-start.8 = (bf16[144,1280]{1,0:T(8,128)(2,1)S(1)}, bf16[144,1280]{1,0:T(8,128)(2,1)S(1)}, u32[]{:S(2)}, u32[]{:S(2)}) collective-permute-start(bf16[144,1280]{1,0:T(8,128)(2,1)S(1)} %get-tuple-element.44), channel_id=1, source_target_pairs={{0,4},{4,0},{1,5},{5,1},{2,6},{6,2},{3,7},{7,3},{8,12},{12,8},{9,1... | collective-permute-start | bytes 1105928 | tf_op jit(solution)/shard_map/ppermute | solution.py:555
  48.0 31.2 %collective-permute-start.9 = (bf16[288,1024]{1,0:T(8,128)(2,1)S(1)}, bf16[288,1024]{1,0:T(8,128)(2,1)S(1)}, u32[]{:S(2)}, u32[]{:S(2)}) collective-permute-start(bf16[288,1024]{1,0:T(8,128)(2,1)S(1)} %get-tuple-element.46), channel_id=1, source_target_pairs={{0,4},{4,0},{1,5},{5,1},{2,6},{6,2},{3,7},{7,3},{8,12},{12,8},{9,1... | collective-permute-start | bytes 1769480 | tf_op jit(solution)/shard_map/ppermute | solution.py:555
  48.6 20.4 %collective-permute-start.7 = (bf16[288,256]{1,0:T(8,128)(2,1)S(1)}, bf16[288,256]{1,0:T(8,128)(2,1)S(1)}, u32[]{:S(2)}, u32[]{:S(2)}) collective-permute-start(bf16[288,256]{1,0:T(8,128)(2,1)S(1)} %get-tuple-element.43), channel_id=1, source_target_pairs={{0,4},{4,0},{1,5},{5,1},{2,6},{6,2},{3,7},{7,3},{8,12},{12,8},{9,1... | collective-permute-start | bytes 442376 | tf_op jit(solution)/shard_map/ppermute | solution.py:555
  71.5 16.3 %collective-permute-start.10 = (bf16[144,1024]{1,0:T(8,128)(2,1)S(1)}, bf16[144,1024]{1,0:T(8,128)(2,1)S(1)}, u32[]{:S(2)}, u32[]{:S(2)}) collective-permute-start(bf16[144,1024]{1,0:T(8,128)(2,1)S(1)} %get-tuple-element.47), channel_id=1, source_target_pairs={{0,4},{4,0},{1,5},{5,1},{2,6},{6,2},{3,7},{7,3},{8,12},{12,8},{9,1... | collective-permute-start | bytes 884744 | tf_op jit(solution)/shard_map/ppermute | solution.py:555
  73.1 14.7 %collective-permute-start.11 = (bf16[576,128]{1,0:T(8,128)(2,1)S(1)}, bf16[576,128]{1,0:T(8,128)(2,1)S(1)}, u32[]{:S(2)}, u32[]{:S(2)}) collective-permute-start(bf16[576,128]{1,0:T(8,128)(2,1)S(1)} %get-tuple-element.55), channel_id=1, source_target_pairs={{0,1},{1,3},{2,0},{3,2},{4,5},{5,7},{6,4},{7,6},{8,9},{9,11},{10,8... | collective-permute-start | bytes 442376 | tf_op jit(solution)/shard_map/ppermute | solution.py:591
  74.6 13.1 %collective-permute-start.12 = (bf16[576,128]{1,0:T(8,128)(2,1)S(1)}, bf16[576,128]{1,0:T(8,128)(2,1)S(1)}, u32[]{:S(2)}, u32[]{:S(2)}) collective-permute-start(bf16[576,128]{1,0:T(8,128)(2,1)S(1)} %get-tuple-element.56), channel_id=1, source_target_pairs={{1,2},{2,1},{5,6},{6,5},{9,10},{10,9},{13,14},{14,13},{17,18},{18,... | collective-permute-start | bytes 442376 | tf_op jit(solution)/shard_map/ppermute | solution.py:591
  75.3 12.4 %collective-permute-start.13 = (bf16[144,128]{1,0:T(8,128)(2,1)S(1)}, bf16[144,128]{1,0:T(8,128)(2,1)S(1)}, u32[]{:S(2)}, u32[]{:S(2)}) collective-permute-start(bf16[144,128]{1,0:T(8,128)(2,1)S(1)} %get-tuple-element.57), channel_id=1, source_target_pairs={{0,5},{1,7},{2,4},{3,6},{4,1},{5,3},{6,0},{7,2},{8,13},{9,15},{10,... | collective-permute-start | bytes 110600 | tf_op jit(solution)/shard_map/ppermute | solution.py:594
  79.3 8.4 %collective-permute-start.14 = (bf16[144,128]{1,0:T(8,128)(2,1)S(1)}, bf16[144,128]{1,0:T(8,128)(2,1)S(1)}, u32[]{:S(2)}, u32[]{:S(2)}) collective-permute-start(bf16[144,128]{1,0:T(8,128)(2,1)S(1)} %get-tuple-element.58), channel_id=1, source_target_pairs={{0,4},{1,6},{2,5},{3,7},{4,0},{5,2},{6,1},{7,3},{8,12},{9,14},{10,... | collective-permute-start | bytes 110600 | tf_op jit(solution)/shard_map/ppermute | solution.py:594
  85.9 1.8 %copy-start = (bf16[1,2048]{1,0:T(2,128)(2,1)S(1)}, bf16[1,2048]{1,0:T(2,128)(2,1)}, u32[]{:S(2)}) copy-start(bf16[1,2048]{1,0:T(2,128)(2,1)} %refs_16_.1) | copy-start | bytes 12292
  87.4 14.7 %copy-start.1 = (s32[72]{0:T(128)S(1)}, s32[72]{0:T(128)}, u32[]{:S(2)}) copy-start(s32[72]{0:T(128)} %param.9) | copy-start | bytes 868

commit v10 on v9

--- a/solution.py
+++ b/solution.py
@@ -45,10 +45,8 @@
     core, segment = ids[0], ids[1]
     copies = [pltpu.make_async_copy(send_hbm, send_ref, sems.at[parts])]
     for part in range(parts):
-        first = (1 - segment) * half if part < parts // 2 else segment * half
-        source = pl.ds(pl.multiple_of(first + part % (parts // 2) * step, step), step)
-        copies.append(pltpu.make_async_copy(
-            rows_hbm.at[:, source], rows_ref.at[:, pl.ds(part * step, step)], sems.at[part]))
+        at = pl.ds(part * step, step)
+        copies.append(pltpu.make_async_copy(rows_hbm.at[:, at], rows_ref.at[:, at], sems.at[part]))
     lengths_copy = pltpu.make_async_copy(lengths_hbm, lengths_ref, sems.at[parts + 1])
     for copy in copies + [lengths_copy]:
         copy.start()
@@ -63,16 +61,17 @@
         return out.astype(BF16)
 
     lanes = jnp.zeros((count, LANES), F32)
-    chunk = 512
     for part in range(parts):
         copies[1 + part].wait()
-        out_ref = theirs_ref if part < parts // 2 else mine_ref
-        for start in range(part * step, (part + 1) * step, chunk):
-            rows = rows_ref[:, start:start + chunk]
-            out_ref[:, start % half:start % half + chunk] = ordered(rows)
-            for lane in range(0, chunk, LANES):
-                square = rows[:, lane:lane + LANES].astype(F32)
-                lanes = lanes + square * square
+        square = rows_ref[:, part * step:(part + 1) * step].astype(F32)
+        square = square * square
+        for lane in range(0, step, LANES):
+            lanes = lanes + square[:, lane:lane + LANES]
+    chunk = 1024
+    for start in range(0, half, chunk):
+        for out_ref, which in ((theirs_ref, 1 - segment), (mine_ref, segment)):
+            at = pl.multiple_of(which * half + start, chunk)
+            out_ref[:, start:start + chunk] = ordered(rows_ref[:, pl.ds(at, chunk)])
     scale = lax.rsqrt(jnp.sum(lanes, axis=1, keepdims=True) * (1.0 / width) + epsilon)
     high = scale.astype(BF16).astype(F32)
     middle = (scale - high).astype(BF16).astype(F32)

time: 103 us -> 103 us (level)
  no operation moved by 1% of the time
where the time goes in v10:
time: 103 us
  waiting for transfers between devices  43.7 us (42%)
  Pallas kernels  27.7 us (27%)
  starting transfers between devices  19.9 us (19%)
  blocking collectives  11.2 us (11%)
    ppermute x5, waiting for transfers between devices, across(): return lax.ppermute(part, 'segment', x_pairs)  31.1 us
    ppermute x1, waiting for transfers between devices, paired(): from_d = lax.ppermute(from_x, 'branch', y_pairs)  12.6 us
    all_to_all x1, blocking collectives, paired(): lax.all_to_all(outgoing, ALL_AXES, split_axis=0, concat_axis=0, tiled=True)  11.2 us
    pallas_call x1, Pallas kernels, first_chunk(): pl.pallas_call(first_chunk_kernel, out_shape=shapes, in_specs=[whole(), w...  8.38 us
    ppermute x5, starting transfers between devices, across(): return lax.ppermute(part, 'segment', x_pairs)  8.27 us
    ppermute x2, starting transfers between devices, hand_across(): lax.ppermute(array, ('segment', 'tp'), [(side * n_tp + i, (1 - side) * n_...  5.55 us
    pallas_call x3, Pallas kernels, own_queries(): pl.pallas_call(own_body, out_shape=shape_of(rows.shape[0], query.shape[1]...  5.46 us
    pallas_call x1, Pallas kernels, next_chunk(): pl.pallas_call(functools.partial(next_chunk_kernel, chips=chips), out_sha...  4.28 us
  transfers between devices with their start and end apart: 15, of which 4 were waited for; matrix products, arithmetic and copies ran while one was open for 0% of the time, Pallas kernels for 21%

profile of v10, /device:TPU:0, one launch (start us, length us, event | category | flops | bytes accessed | tf_op | source)
XLA Modules:
  0.0 102.8 jit_solution(13101862934296114181)
XLA Ops:
  0.0 1.9 %prepare.1 = (bf16[72,4224]{1,0:T(8,128)(2,1)S(1)}, bf16[72,4224]{1,0:T(8,128)(2,1)S(1)}) custom-call(s32[1,6]{1,0:T(1,128)} %lengths_ref.1, bf16[72,8192]{1,0:T(8,128)(2,1)} %rows_hbm.1, s32[1,72]{1,0:T(1,128)} %bitcast.9), custom_call_target="tpu_custom_call" | custom-call | tf_op jit(solution)/shard_map/prepare/pallas_call | solution.py:93
  1.9 3.0 %collective-permute-start = (bf16[72,4224]{1,0:T(8,128)(2,1)S(1)}, bf16[72,4224]{1,0:T(8,128)(2,1)S(1)}, u32[]{:S(2)}, u32[]{:S(2)}) collective-permute-start(bf16[72,4224]{1,0:T(8,128)(2,1)S(1)} %get-tuple-element.32), channel_id=1, source_target_pairs={{0,4},{4,0},{1,5},{5,1},{2,6},{6,2},{3,7},{7,3},{8,12},{12,8},{9,1... | collective-permute-start | bytes 1824776 | tf_op jit(solution)/shard_map/ppermute | solution.py:554
  4.9 1.5 %collective-permute-start.3 = (bf16[72,4224]{1,0:T(8,128)(2,1)S(1)}, bf16[72,4224]{1,0:T(8,128)(2,1)S(1)}, u32[]{:S(2)}, u32[]{:S(2)}) collective-permute-start(bf16[72,4224]{1,0:T(8,128)(2,1)S(1)} %get-tuple-element.33.near_ref), channel_id=1, source_target_pairs={{0,16},{8,24},{16,0},{24,8},{1,17},{9,25},{17,1},{25,9},{2,18},{10... | collective-permute-start | bytes 1824776 | tf_op jit(solution)/shard_map/ppermute | solution.py:565
  6.5 12.2 %collective-permute-done.near_ref.refs_0_ = bf16[72,4224]{1,0:T(8,128)(2,1)S(1)} collective-permute-done((bf16[72,4224]{1,0:T(8,128)(2,1)S(1)}, bf16[72,4224]{1,0:T(8,128)(2,1)S(1)}, u32[]{:S(2)}, u32[]{:S(2)}) %collective-permute-start) | collective-permute-done | bytes 608288 | tf_op jit(solution)/shard_map/ppermute | solution.py:554
  18.7 1.8 %collective-permute-start.5 = (bf16[72,4224]{1,0:T(8,128)(2,1)S(1)}, bf16[72,4224]{1,0:T(8,128)(2,1)S(1)}, u32[]{:S(2)}, u32[]{:S(2)}) collective-permute-start(bf16[72,4224]{1,0:T(8,128)(2,1)S(1)} %collective-permute-done.near_ref.refs_0_), channel_id=1, source_target_pairs={{0,16},{8,24},{16,0},{24,8},{1,17},{9,25},{17,1},{25,9},{2,18},{10... | collective-permute-start | bytes 1824776 | tf_op jit(solution)/shard_map/ppermute | solution.py:566
  20.4 0.0 collective-permute-start.1
  20.4 0.5 collective-permute-start.2
  20.9 0.0 collective-permute-done.3.refs_2_
  20.9 0.0 collective-permute-start.4
  20.9 12.6 %collective-permute-done.5.refs_0_ = bf16[72,4224]{1,0:T(8,128)(2,1)S(1)} collective-permute-done((bf16[72,4224]{1,0:T(8,128)(2,1)S(1)}, bf16[72,4224]{1,0:T(8,128)(2,1)S(1)}, u32[]{:S(2)}, u32[]{:S(2)}) %collective-permute-start.5) | collective-permute-done | bytes 608288 | tf_op jit(solution)/shard_map/ppermute | solution.py:566
  33.5 0.0 collective-permute-start.6
  33.5 0.0 collective-permute-done.1.far_ref
  33.6 8.4 %first_chunk.1 = (bf16[144,4096]{1,0:T(8,128)(2,1)S(1)}, f32[144,128]{1,0:T(8,128)S(1)}, f32[144,256]{1,0:T(8,128)S(1)}, bf16[144,1280]{1,0:T(8,128)(2,1)S(1)}, ...) custom-call(bf16[72,4224]{1,0:T(8,128)(2,1)S(1)} %get-tuple-element., ...), custom_call_target="tpu_custom_call" | custom-call | tf_op jit(solution)/shard_map/first_chunk/pallas_call | solution.py:260
  41.9 1.6 %collective-permute-start.8 = (bf16[144,1280]{1,0:T(8,128)(2,1)S(1)}, bf16[144,1280]{1,0:T(8,128)(2,1)S(1)}, u32[]{:S(2)}, u32[]{:S(2)}) collective-permute-start(bf16[144,1280]{1,0:T(8,128)(2,1)S(1)} %get-tuple-element.44), channel_id=1, source_target_pairs={{0,4},{4,0},{1,5},{5,1},{2,6},{6,2},{3,7},{7,3},{8,12},{12,8},{9,1... | collective-permute-start | bytes 1105928 | tf_op jit(solution)/shard_map/ppermute | solution.py:554
  43.5 0.0 collective-permute-done.2.refs_1_
  43.5 0.0 collective-permute-done.4.refs_3_
  43.5 4.3 %next_chunk.1 = (bf16[288,4096]{1,0:T(8,128)(2,1)S(1)}, f32[288,128]{1,0:T(8,128)S(1)}, f32[288,256]{1,0:T(8,128)S(1)}, bf16[288,1024]{1,0:T(8,128)(2,1)S(1)}, bf16[288,256]{1,0:T(8,128)(2,1)S(1)}) custom-call(bf16[72,4224]{1,0:T(8,128)(2,1)S(1)} %collective-permute-done.near_ref.refs_0_, bf16[72,4224]{1,0:T(8,128)(2,1)S(1)} %collective-permute-done.2.refs_1_, ...), custom_call_target="tpu_custom_call" | custom-call | tf_op jit(solution)/shard_map/next_chunk/pallas_call | solution.py:283
  47.8 0.6 collective-permute-start.9
  48.4 1.5 %collective-permute-start.7 = (bf16[288,256]{1,0:T(8,128)(2,1)S(1)}, bf16[288,256]{1,0:T(8,128)(2,1)S(1)}, u32[]{:S(2)}, u32[]{:S(2)}) collective-permute-start(bf16[288,256]{1,0:T(8,128)(2,1)S(1)} %get-tuple-element.43), channel_id=1, source_target_pairs={{0,4},{4,0},{1,5},{5,1},{2,6},{6,2},{3,7},{7,3},{8,12},{12,8},{9,1... | collective-permute-start | bytes 442376 | tf_op jit(solution)/shard_map/ppermute | solution.py:554
  49.9 3.6 %collective-permute-done.8.refs_9_.refs_5_ = bf16[144,1280]{1,0:T(8,128)(2,1)S(1)} collective-permute-done((bf16[144,1280]{1,0:T(8,128)(2,1)S(1)}, bf16[144,1280]{1,0:T(8,128)(2,1)S(1)}, u32[]{:S(2)}, u32[]{:S(2)}) %collective-permute-start.8) | collective-permute-done | bytes 368672 | tf_op jit(solution)/shard_map/ppermute | solution.py:554
  53.5 15.3 %collective-permute-done.7.refs_8_ = bf16[288,256]{1,0:T(8,128)(2,1)S(1)} collective-permute-done((bf16[288,256]{1,0:T(8,128)(2,1)S(1)}, bf16[288,256]{1,0:T(8,128)(2,1)S(1)}, u32[]{:S(2)}, u32[]{:S(2)}) %collective-permute-start.7) | collective-permute-done | bytes 147488 | tf_op jit(solution)/shard_map/ppermute | solution.py:554
  68.8 0.0 collective-permute-done.6.refs_1_
  68.8 2.4 %last_chunk.1 = (bf16[144,4096]{1,0:T(8,128)(2,1)S(1)}, f32[144,128]{1,0:T(8,128)S(1)}, bf16[144,1024]{1,0:T(8,128)(2,1)S(1)}, bf16[576,128]{1,0:T(8,128)(2,1)S(...) custom-call(bf16[72,4224]{1,0:T(8,128)(2,1)S(1)} %collective-permute, ...), custom_call_target="tpu_custom_call" | custom-call | tf_op jit(solution)/shard_map/last_chunk/pallas_call | solution.py:298
  71.2 1.6 %collective-permute-start.10 = (bf16[144,1024]{1,0:T(8,128)(2,1)S(1)}, bf16[144,1024]{1,0:T(8,128)(2,1)S(1)}, u32[]{:S(2)}, u32[]{:S(2)}) collective-permute-start(bf16[144,1024]{1,0:T(8,128)(2,1)S(1)} %get-tuple-element.47), channel_id=1, source_target_pairs={{0,4},{4,0},{1,5},{5,1},{2,6},{6,2},{3,7},{7,3},{8,12},{12,8},{9,1... | collective-permute-start | bytes 884744 | tf_op jit(solution)/shard_map/ppermute | solution.py:554
  72.8 1.6 %collective-permute-start.11 = (bf16[576,128]{1,0:T(8,128)(2,1)S(1)}, bf16[576,128]{1,0:T(8,128)(2,1)S(1)}, u32[]{:S(2)}, u32[]{:S(2)}) collective-permute-start(bf16[576,128]{1,0:T(8,128)(2,1)S(1)} %get-tuple-element.55), channel_id=1, source_target_pairs={{0,1},{1,3},{2,0},{3,2},{4,5},{5,7},{6,4},{7,6},{8,9},{9,11},{10,8... | collective-permute-start | bytes 442376 | tf_op jit(solution)/shard_map/ppermute | solution.py:590
  74.4 0.7 collective-permute-start.12
  75.0 4.0 %collective-permute-start.13 = (bf16[144,128]{1,0:T(8,128)(2,1)S(1)}, bf16[144,128]{1,0:T(8,128)(2,1)S(1)}, u32[]{:S(2)}, u32[]{:S(2)}) collective-permute-start(bf16[144,128]{1,0:T(8,128)(2,1)S(1)} %get-tuple-element.57), channel_id=1, source_target_pairs={{0,5},{1,7},{2,4},{3,6},{4,1},{5,3},{6,0},{7,2},{8,13},{9,15},{10,... | collective-permute-start | bytes 110600 | tf_op jit(solution)/shard_map/ppermute | solution.py:593
  79.0 0.0 collective-permute-done.9.refs_4_.refs_7_
  79.0 1.6 %collective-permute-start.14 = (bf16[144,128]{1,0:T(8,128)(2,1)S(1)}, bf16[144,128]{1,0:T(8,128)(2,1)S(1)}, u32[]{:S(2)}, u32[]{:S(2)}) collective-permute-start(bf16[144,128]{1,0:T(8,128)(2,1)S(1)} %get-tuple-element.58), channel_id=1, source_target_pairs={{0,4},{1,6},{2,5},{3,7},{4,0},{5,2},{6,1},{7,3},{8,12},{9,14},{10,... | collective-permute-start | bytes 110600 | tf_op jit(solution)/shard_map/ppermute | solution.py:593
  80.6 1.4 %own_queries.3.refs_0_ = f32[144,1024]{1,0:T(8,128)S(1)} custom-call(bf16[144,4096]{1,0:T(8,128)(2,1)S(1)} %get-tuple-element.34.rows_ref, bf16[4096,1024]{1,0:T(8,128)(2,1)S(1)} %get-tuple-element.35.query_ref), custom_call_target="tpu_custom_call" | custom-call | tf_op jit(solution)/shard_map/own_queries/pallas_call | solution.py:317
  82.0 1.1 %masks.1.bias_ref = f32[576,384]{1,0:T(8,128)S(1)} custom-call(s32[1,6]{1,0:T(1,128)} %lengths_ref.1, bf16[72,4224]{1,0:T(8,128)(2,1)S(1)} %collective-permute-done.near_ref.refs_0_), custom_call_target="tpu_custom_call" | custom-call | tf_op jit(solution)/shard_map/masks/pallas_call | solution.py:376
  83.1 2.6 %own_queries.4.refs_1_.refs_2_ = f32[288,1024]{1,0:T(8,128)S(1)} custom-call(bf16[288,4096]{1,0:T(8,128)(2,1)S(1)} %get-tuple-element.40.rows_ref, bf16[4096,1024]{1,0:T(8,128)(2,1)S(1)} %get-tuple-element.35.query_ref), custom_call_target="tpu_custom_call" | custom-call | tf_op jit(solution)/shard_map/own_queries/pallas_call | solution.py:317
  85.7 0.0 copy-start
  85.7 1.4 %own_queries.5.refs_3_ = f32[144,1024]{1,0:T(8,128)S(1)} custom-call(bf16[144,4096]{1,0:T(8,128)(2,1)S(1)} %get-tuple-element.45.rows_ref, bf16[4096,1024]{1,0:T(8,128)(2,1)S(1)} %get-tuple-element.35.query_ref), custom_call_target="tpu_custom_call" | custom-call | tf_op jit(solution)/shard_map/own_queries/pallas_call | solution.py:317
  87.2 0.0 copy-start.1
  87.2 0.3 placement.1
  87.5 0.0 collective-permute-done.13.refs_14_
  87.5 0.0 collective-permute-done.14.refs_15_
  87.5 0.0 collective-permute-done.11.refs_12_
  87.5 0.0 collective-permute-done.12.refs_13_
  87.5 0.0 collective-permute-done.10.refs_6_
  87.5 0.0 copy-done
  87.5 3.0 %attend.1 = f32[32,256]{1,0:T(8,128)S(1)} custom-call(f32[576,384]{1,0:T(8,128)S(1)} %masks.1.bias_ref, f32[144,1024]{1,0:T(8,128)S(1)} %own_queries.3.refs_0_, f32[288,1024]{1,0:T(8,128)S(1)} %own_queries.4.refs_1_.refs_2_, f32[288,1024]{1,0:T(8,128)S(1)} %own_queries.4.refs_1_.refs_2_, f32[144,1024]{1,0:T(8,128)S(1)} %own_queries.5.refs_3_, ...), custom_call_target="tpu_custom_call" | custom-call | tf_op jit(solution)/shard_map/attend/pallas_call | solution.py:503
  90.6 11.2 %all_to_all.11 = f32[32,1,256]{2,1,0:T(1,128)S(1)} all-to-all(f32[32,1,256]{2,1,0:T(1,128)S(1)} %copy.9), channel_id=1, replica_groups=mesh['branch'=4,'segment'=2,'tp'=4] {'branch','segment','tp'}, dimensions={0} | all-to-all | bytes 65536 | tf_op jit(solution)/shard_map/all_to_all | solution.py:611
  101.9 0.0 copy-done.1
  101.9 0.9 finish.1
  (2 shorter events, 0.0 us)
Async XLA Ops:
  1.9 16.8 %collective-permute-start = (bf16[72,4224]{1,0:T(8,128)(2,1)S(1)}, bf16[72,4224]{1,0:T(8,128)(2,1)S(1)}, u32[]{:S(2)}, u32[]{:S(2)}) collective-permute-start(bf16[72,4224]{1,0:T(8,128)(2,1)S(1)} %get-tuple-element.32), channel_id=1, source_target_pairs={{0,4},{4,0},{1,5},{5,1},{2,6},{6,2},{3,7},{7,3},{8,12},{12,8},{9,1... | collective-permute-start | bytes 1824776 | tf_op jit(solution)/shard_map/ppermute | solution.py:554
  4.9 16.0 %collective-permute-start.3 = (bf16[72,4224]{1,0:T(8,128)(2,1)S(1)}, bf16[72,4224]{1,0:T(8,128)(2,1)S(1)}, u32[]{:S(2)}, u32[]{:S(2)}) collective-permute-start(bf16[72,4224]{1,0:T(8,128)(2,1)S(1)} %get-tuple-element.33.near_ref), channel_id=1, source_target_pairs={{0,16},{8,24},{16,0},{24,8},{1,17},{9,25},{17,1},{25,9},{2,18},{10... | collective-permute-start | bytes 1824776 | tf_op jit(solution)/shard_map/ppermute | solution.py:565
  18.7 14.9 %collective-permute-start.5 = (bf16[72,4224]{1,0:T(8,128)(2,1)S(1)}, bf16[72,4224]{1,0:T(8,128)(2,1)S(1)}, u32[]{:S(2)}, u32[]{:S(2)}) collective-permute-start(bf16[72,4224]{1,0:T(8,128)(2,1)S(1)} %collective-permute-done.near_ref.refs_0_), channel_id=1, source_target_pairs={{0,16},{8,24},{16,0},{24,8},{1,17},{9,25},{17,1},{25,9},{2,18},{10... | collective-permute-start | bytes 1824776 | tf_op jit(solution)/shard_map/ppermute | solution.py:566
  20.4 13.1 %collective-permute-start.1 = (bf16[72,4224]{1,0:T(8,128)(2,1)S(1)}, bf16[72,4224]{1,0:T(8,128)(2,1)S(1)}, u32[]{:S(2)}, u32[]{:S(2)}) collective-permute-start(bf16[72,4224]{1,0:T(8,128)(2,1)S(1)} %get-tuple-element.33.near_ref), channel_id=1, source_target_pairs={{0,8},{8,0},{16,24},{24,16},{1,9},{9,1},{17,25},{25,17},{2,10},{10... | collective-permute-start | bytes 1824776 | tf_op jit(solution)/shard_map/ppermute | solution.py:551
  20.4 23.1 %collective-permute-start.2 = (bf16[72,4224]{1,0:T(8,128)(2,1)S(1)}, bf16[72,4224]{1,0:T(8,128)(2,1)S(1)}, u32[]{:S(2)}, u32[]{:S(2)}) collective-permute-start(bf16[72,4224]{1,0:T(8,128)(2,1)S(1)} %collective-permute-done.near_ref.refs_0_), channel_id=1, source_target_pairs={{0,8},{8,0},{16,24},{24,16},{1,9},{9,1},{17,25},{25,17},{2,10},{10... | collective-permute-start | bytes 1824776 | tf_op jit(solution)/shard_map/ppermute | solution.py:551
  20.9 22.6 %collective-permute-start.4 = (bf16[72,4224]{1,0:T(8,128)(2,1)S(1)}, bf16[72,4224]{1,0:T(8,128)(2,1)S(1)}, u32[]{:S(2)}, u32[]{:S(2)}) collective-permute-start(bf16[72,4224]{1,0:T(8,128)(2,1)S(1)} %collective-permute-done.3.refs_2_), channel_id=1, source_target_pairs={{0,8},{8,0},{16,24},{24,16},{1,9},{9,1},{17,25},{25,17},{2,10},{10... | collective-permute-start | bytes 1824776 | tf_op jit(solution)/shard_map/ppermute | solution.py:551
  33.5 35.3 %collective-permute-start.6 = (bf16[72,4224]{1,0:T(8,128)(2,1)S(1)}, bf16[72,4224]{1,0:T(8,128)(2,1)S(1)}, u32[]{:S(2)}, u32[]{:S(2)}) collective-permute-start(bf16[72,4224]{1,0:T(8,128)(2,1)S(1)} %collective-permute-done.5.refs_0_), channel_id=1, source_target_pairs={{0,8},{8,0},{16,24},{24,16},{1,9},{9,1},{17,25},{25,17},{2,10},{10... | collective-permute-start | bytes 1824776 | tf_op jit(solution)/shard_map/ppermute | solution.py:551
  41.9 11.5 %collective-permute-start.8 = (bf16[144,1280]{1,0:T(8,128)(2,1)S(1)}, bf16[144,1280]{1,0:T(8,128)(2,1)S(1)}, u32[]{:S(2)}, u32[]{:S(2)}) collective-permute-start(bf16[144,1280]{1,0:T(8,128)(2,1)S(1)} %get-tuple-element.44), channel_id=1, source_target_pairs={{0,4},{4,0},{1,5},{5,1},{2,6},{6,2},{3,7},{7,3},{8,12},{12,8},{9,1... | collective-permute-start | bytes 1105928 | tf_op jit(solution)/shard_map/ppermute | solution.py:554
  47.8 31.2 %collective-permute-start.9 = (bf16[288,1024]{1,0:T(8,128)(2,1)S(1)}, bf16[288,1024]{1,0:T(8,128)(2,1)S(1)}, u32[]{:S(2)}, u32[]{:S(2)}) collective-permute-start(bf16[288,1024]{1,0:T(8,128)(2,1)S(1)} %get-tuple-element.46), channel_id=1, source_target_pairs={{0,4},{4,0},{1,5},{5,1},{2,6},{6,2},{3,7},{7,3},{8,12},{12,8},{9,1... | collective-permute-start | bytes 1769480 | tf_op jit(solution)/shard_map/ppermute | solution.py:554
  48.4 20.4 %collective-permute-start.7 = (bf16[288,256]{1,0:T(8,128)(2,1)S(1)}, bf16[288,256]{1,0:T(8,128)(2,1)S(1)}, u32[]{:S(2)}, u32[]{:S(2)}) collective-permute-start(bf16[288,256]{1,0:T(8,128)(2,1)S(1)} %get-tuple-element.43), channel_id=1, source_target_pairs={{0,4},{4,0},{1,5},{5,1},{2,6},{6,2},{3,7},{7,3},{8,12},{12,8},{9,1... | collective-permute-start | bytes 442376 | tf_op jit(solution)/shard_map/ppermute | solution.py:554
  71.2 16.3 %collective-permute-start.10 = (bf16[144,1024]{1,0:T(8,128)(2,1)S(1)}, bf16[144,1024]{1,0:T(8,128)(2,1)S(1)}, u32[]{:S(2)}, u32[]{:S(2)}) collective-permute-start(bf16[144,1024]{1,0:T(8,128)(2,1)S(1)} %get-tuple-element.47), channel_id=1, source_target_pairs={{0,4},{4,0},{1,5},{5,1},{2,6},{6,2},{3,7},{7,3},{8,12},{12,8},{9,1... | collective-permute-start | bytes 884744 | tf_op jit(solution)/shard_map/ppermute | solution.py:554
  72.8 14.7 %collective-permute-start.11 = (bf16[576,128]{1,0:T(8,128)(2,1)S(1)}, bf16[576,128]{1,0:T(8,128)(2,1)S(1)}, u32[]{:S(2)}, u32[]{:S(2)}) collective-permute-start(bf16[576,128]{1,0:T(8,128)(2,1)S(1)} %get-tuple-element.55), channel_id=1, source_target_pairs={{0,1},{1,3},{2,0},{3,2},{4,5},{5,7},{6,4},{7,6},{8,9},{9,11},{10,8... | collective-permute-start | bytes 442376 | tf_op jit(solution)/shard_map/ppermute | solution.py:590
  74.4 13.1 %collective-permute-start.12 = (bf16[576,128]{1,0:T(8,128)(2,1)S(1)}, bf16[576,128]{1,0:T(8,128)(2,1)S(1)}, u32[]{:S(2)}, u32[]{:S(2)}) collective-permute-start(bf16[576,128]{1,0:T(8,128)(2,1)S(1)} %get-tuple-element.56), channel_id=1, source_target_pairs={{1,2},{2,1},{5,6},{6,5},{9,10},{10,9},{13,14},{14,13},{17,18},{18,... | collective-permute-start | bytes 442376 | tf_op jit(solution)/shard_map/ppermute | solution.py:590
  75.0 12.4 %collective-permute-start.13 = (bf16[144,128]{1,0:T(8,128)(2,1)S(1)}, bf16[144,128]{1,0:T(8,128)(2,1)S(1)}, u32[]{:S(2)}, u32[]{:S(2)}) collective-permute-start(bf16[144,128]{1,0:T(8,128)(2,1)S(1)} %get-tuple-element.57), channel_id=1, source_target_pairs={{0,5},{1,7},{2,4},{3,6},{4,1},{5,3},{6,0},{7,2},{8,13},{9,15},{10,... | collective-permute-start | bytes 110600 | tf_op jit(solution)/shard_map/ppermute | solution.py:593
  79.0 8.4 %collective-permute-start.14 = (bf16[144,128]{1,0:T(8,128)(2,1)S(1)}, bf16[144,128]{1,0:T(8,128)(2,1)S(1)}, u32[]{:S(2)}, u32[]{:S(2)}) collective-permute-start(bf16[144,128]{1,0:T(8,128)(2,1)S(1)} %get-tuple-element.58), channel_id=1, source_target_pairs={{0,4},{1,6},{2,5},{3,7},{4,0},{5,2},{6,1},{7,3},{8,12},{9,14},{10,... | collective-permute-start | bytes 110600 | tf_op jit(solution)/shard_map/ppermute | solution.py:593
  85.7 1.8 %copy-start = (bf16[1,2048]{1,0:T(2,128)(2,1)S(1)}, bf16[1,2048]{1,0:T(2,128)(2,1)}, u32[]{:S(2)}) copy-start(bf16[1,2048]{1,0:T(2,128)(2,1)} %refs_16_.1) | copy-start | bytes 12292
  87.2 14.7 %copy-start.1 = (s32[72]{0:T(128)S(1)}, s32[72]{0:T(128)}, u32[]{:S(2)}) copy-start(s32[72]{0:T(128)} %param.9) | copy-start | bytes 868
